TPU v7x, 128 devices: a whole 4x4x4 slice. The times are simulated.
128 devices in a mesh: req: 4 (over x), tp: 32 (over z, y, core).
Axes of the slice: x: 4, y: 4, z: 4, core: 2. Of those that a mesh axis runs over, the one named last changes fastest.
Arguments:
- step_inputs: bfloat16 [4, 256, 1536], P(None, ('req', 'tp')), may hold values from -6 to 6
- qkv_weight: bfloat16 [1536, 2048], replicated, may hold values from -0.15625 to 0.15625
- qkv_bias: float32 [2048], replicated, may hold values from -8 to 8
- out_weight: bfloat16 [1536, 1536], P('tp'), may hold values from -0.15625 to 0.15625
- gate_weight: bfloat16 [1536, 8960], P(None, 'tp'), may hold values from -0.15625 to 0.15625
- up_weight: bfloat16 [1536, 8960], P(None, 'tp'), may hold values from -0.15625 to 0.15625
- down_weight: bfloat16 [8960, 1536], P('tp'), may hold values from -0.0625 to 0.0625
- cache_keys: bfloat16 [256, 4096, 256], P(('req', 'tp')), may hold values from -60 to 60
- cache_values: bfloat16 [256, 4096, 256], P(('req', 'tp')), may hold values from -24 to 24
- lengths: int32 [32, 8], replicated, may hold values from 1 to 4096, as said below
- parents: int32 [4, 32, 8], replicated, may hold values from 0 to 7
- slot_request: int32 [32], replicated, may hold values from 0 to 31, each once
Outputs:
- outputs: bfloat16 [4, 256, 1536], P(None, ('req', 'tp'))
Inputs may be any that keep to these rules, and one draw needn't show every extreme that they name: lengths[r, c] is the number of cached positions of beam c of request r; some beam has exactly 4096. parents[t, r, b] names a beam of the same request r. `slot_request`: a permutation of the requests; slots 8 * i to 8 * i + 7 are rows of index i of req.
All inputs are finite; a program needn't handle non-finite values.
Results may differ from a plain program's by a relative error of at most 0.022.
The roundings to bfloat16 on the way count: a program that leaves them out, or rounds other values in their place, can miss the bound.
Values may be sent and summed in bfloat16 or wider, within the bound.
No kernel may reach another device: no remote copies, remote signals or barrier semaphores. Data moves between devices by JAX's collectives and lax.ppermute only.
A program may use at most 128 MiB of HBM per device.

v0:
```python
import jax
import jax.numpy as jnp
from jax import lax
from jax.sharding import PartitionSpec as P

Q_HEADS = 12
KV_HEADS = 2


theta_base = 1000000.0
norm_eps = 1e-06
masked_score = -1e30


def rms_normed(values):
    values = values.astype(jnp.float32)
    factor = lax.rsqrt(jnp.mean(values * values, axis=-1, keepdims=True) + norm_eps)
    return (values * factor).astype(jnp.bfloat16)


def rotate(vectors, positions):
    half = vectors.shape[-1] // 2
    freqs = theta_base ** (-jnp.arange(half, dtype=jnp.float32) * 2.0 / vectors.shape[-1])
    angles = positions.astype(jnp.float32)[:, None] * freqs[None, :]
    cosine = jnp.cos(angles)[:, None, :]
    sine = jnp.sin(angles)[:, None, :]
    values = vectors.astype(jnp.float32)
    first = values[..., :half]
    second = values[..., half:]
    return jnp.concatenate(
        [first * cosine - second * sine, second * cosine + first * sine], axis=-1
    ).astype(jnp.bfloat16)


def owner_rows(flat, owned_count, beams, inverse):
    owned_global = flat * owned_count + jnp.arange(owned_count, dtype=jnp.int32)
    owned_request = owned_global // beams
    owned_beam = owned_global % beams
    beam_range = jnp.arange(beams, dtype=jnp.int32)
    query_rows = (inverse[owned_request][:, None] * beams + beam_range[None, :]).reshape(-1)
    return (owned_request, owned_beam, query_rows)


def owned_attention(
    every_query, keys, values, owned_request, owned_beam, query_rows, root_all, lengths
):
    owned_rows, context, kv_width = keys.shape
    beams = root_all.shape[1]
    head_dim = kv_width // KV_HEADS
    group = Q_HEADS // KV_HEADS
    grouped = jnp.take(every_query, query_rows, axis=0).reshape(
        owned_rows, beams, KV_HEADS, group, head_dim
    )
    keys = keys.reshape(owned_rows, context, KV_HEADS, head_dim)
    values = values.reshape(owned_rows, context, KV_HEADS, head_dim)
    scores = jnp.einsum(
        "jbkgd,jpkd->jbkgp", grouped, keys, preferred_element_type=jnp.float32
    ) * head_dim ** (-0.5)
    limits = lengths[owned_request, owned_beam]
    live = (jnp.arange(context, dtype=jnp.int32)[None, :] < limits[:, None])[:, None, None, None, :]
    scores = jnp.where(live, scores, masked_score)
    peak = jnp.max(scores, axis=-1)
    weights = jnp.where(live, jnp.exp(scores - peak[..., None]), 0.0)
    total = jnp.sum(weights, axis=-1)
    output = jnp.einsum(
        "jbkgp,jpkd->jbkgd",
        weights.astype(jnp.bfloat16),
        values,
        preferred_element_type=jnp.float32,
    )
    chosen = (root_all[owned_request] == owned_beam[:, None])[:, :, None, None]
    peak = jnp.where(chosen, peak, 0.0).reshape(owned_rows * beams, KV_HEADS, group)
    total = jnp.where(chosen, total, 0.0).reshape(owned_rows * beams, KV_HEADS, group)
    output = jnp.where(chosen[..., None], output, 0.0).reshape(
        owned_rows * beams, KV_HEADS, group, head_dim
    )
    return (peak, total, output)


def spread_rows(pieces, target_rows, row_count):
    return tuple(
        (
            jnp.zeros((row_count,) + piece.shape[1:], jnp.float32).at[target_rows].add(piece)
            for piece in pieces
        )
    )


def per_device(
    step_inputs,
    qkv_weight,
    qkv_bias,
    out_weight,
    gate_weight,
    up_weight,
    down_weight,
    cache_keys,
    cache_values,
    lengths,
    parents,
    slot_request,
):
    steps_count, rows_dev, width = step_inputs.shape
    beams = parents.shape[2]
    requests = slot_request.shape[0]
    req_count = lax.axis_size("req")
    tp_count = lax.axis_size("tp")
    group_requests = requests // req_count
    group_rows = group_requests * beams
    total_rows = requests * beams
    owned_count = cache_keys.shape[0]
    kv_width = cache_keys.shape[2]
    head_dim = kv_width // KV_HEADS
    group = Q_HEADS // KV_HEADS
    attn_width = Q_HEADS * head_dim
    req_index = lax.axis_index("req")
    tp_index = lax.axis_index("tp")
    flat_index = req_index * tp_count + tp_index
    my_requests = lax.dynamic_slice_in_dim(slot_request, req_index * group_requests, group_requests)
    inverse = (
        jnp.zeros((requests,), jnp.int32)
        .at[slot_request]
        .set(jnp.arange(requests, dtype=jnp.int32))
    )
    owned_request, owned_beam, query_rows = owner_rows(flat_index, owned_count, beams, inverse)
    beam_range = jnp.arange(beams, dtype=jnp.int32)
    root_all = jnp.broadcast_to(beam_range[None, :], (requests, beams))
    gen_keys = jnp.zeros((steps_count, group_rows, kv_width), jnp.bfloat16)
    gen_values = jnp.zeros((steps_count, group_rows, kv_width), jnp.bfloat16)
    base_rows = (jnp.arange(group_requests, dtype=jnp.int32) * beams)[:, None]
    column_width = out_weight.shape[0]
    results = []
    for step in range(steps_count):
        root_all = jnp.take_along_axis(root_all, parents[step], axis=1)
        reorder = (base_rows + parents[step][my_requests]).reshape(-1)
        gen_keys = jnp.take(gen_keys, reorder, axis=1)
        gen_values = jnp.take(gen_values, reorder, axis=1)
        inputs = step_inputs[step]
        normed = rms_normed(inputs)
        qkv = (
            jnp.dot(
                lax.all_gather(normed, "tp", axis=0, tiled=True),
                qkv_weight,
                preferred_element_type=jnp.float32,
            )
            + qkv_bias
        ).astype(jnp.bfloat16)
        my_roots = root_all[my_requests]
        positions = (jnp.take_along_axis(lengths[my_requests], my_roots, axis=1) + step).reshape(-1)
        queries = rotate(qkv[:, :attn_width].reshape(group_rows, Q_HEADS, head_dim), positions)
        new_keys = rotate(
            qkv[:, attn_width : attn_width + kv_width].reshape(group_rows, KV_HEADS, head_dim),
            positions,
        )
        gen_keys = gen_keys.at[step].set(new_keys.reshape(group_rows, kv_width))
        gen_values = gen_values.at[step].set(qkv[:, attn_width + kv_width :])
        every_query = lax.all_gather(
            queries.reshape(group_rows, attn_width), "req", axis=0, tiled=True
        )
        part_peak, part_total, part_output = owned_attention(
            every_query,
            cache_keys,
            cache_values,
            owned_request,
            owned_beam,
            query_rows,
            root_all,
            lengths,
        )
        all_peak, all_total, all_output = spread_rows(
            (part_peak, part_total, part_output), query_rows, total_rows
        )
        sum_peak, sum_total, sum_output = lax.psum((all_peak, all_total, all_output), ("req", "tp"))
        peak = lax.dynamic_slice_in_dim(sum_peak, req_index * group_rows, group_rows, 0)
        total = lax.dynamic_slice_in_dim(sum_total, req_index * group_rows, group_rows, 0)
        output = lax.dynamic_slice_in_dim(sum_output, req_index * group_rows, group_rows, 0)
        grouped = queries.reshape(group_rows, KV_HEADS, group, head_dim)
        past_keys = gen_keys[: step + 1].reshape(step + 1, group_rows, KV_HEADS, head_dim)
        past_values = gen_values[: step + 1].reshape(step + 1, group_rows, KV_HEADS, head_dim)
        recent_scores = jnp.einsum(
            "bkgd,sbkd->bkgs", grouped, past_keys, preferred_element_type=jnp.float32
        ) * head_dim ** (-0.5)
        top = jnp.maximum(peak, jnp.max(recent_scores, axis=-1))
        factor = jnp.exp(peak - top)
        recent_weights = jnp.exp(recent_scores - top[..., None])
        denominator = total * factor + jnp.sum(recent_weights, axis=-1)
        numerator = output * factor[..., None] + jnp.einsum(
            "bkgs,sbkd->bkgd",
            recent_weights.astype(jnp.bfloat16),
            past_values,
            preferred_element_type=jnp.float32,
        )
        attention = (
            (numerator / denominator[..., None])
            .reshape(group_rows, attn_width)
            .astype(jnp.bfloat16)
        )
        columns = lax.dynamic_slice_in_dim(attention, tp_index * column_width, column_width, 1)
        attended = lax.psum_scatter(
            jnp.dot(columns, out_weight, preferred_element_type=jnp.float32).astype(jnp.bfloat16),
            "tp",
            scatter_dimension=0,
            tiled=True,
        ).astype(jnp.float32)
        middle = inputs.astype(jnp.float32) + attended
        mixed_in = rms_normed(middle)
        piece = lax.all_gather(mixed_in, "tp", axis=0, tiled=True)
        gate = jnp.dot(piece, gate_weight, preferred_element_type=jnp.float32)
        upward = jnp.dot(piece, up_weight, preferred_element_type=jnp.float32)
        hidden = (jax.nn.silu(gate) * upward).astype(jnp.bfloat16)
        lowered = lax.psum_scatter(
            jnp.dot(hidden, down_weight, preferred_element_type=jnp.float32).astype(jnp.bfloat16),
            "tp",
            scatter_dimension=0,
            tiled=True,
        ).astype(jnp.float32)
        results.append((middle + lowered).astype(jnp.bfloat16))
    return jnp.stack(results)


def solution(mesh):
    in_specs = (
        P(None, ("req", "tp"), None),
        P(),
        P(),
        P("tp", None),
        P(None, "tp"),
        P(None, "tp"),
        P("tp", None),
        P(("req", "tp"), None, None),
        P(("req", "tp"), None, None),
        P(),
        P(),
        P(),
    )
    out_specs = P(None, ("req", "tp"), None)
    return jax.shard_map(
        per_device, mesh=mesh, in_specs=in_specs, out_specs=out_specs, check_vma=False
    )
```

profile of v0, /device:TPU:0, one launch (start us, length us, event | category | flops | bytes accessed | tf_op | source)
XLA Modules:
  0.0 1171.8 jit_solution(9988134711650191990)
XLA Ops:
  9.8 1.9 gather_fusion.15
  12.0 1.9 gather_fusion.18
  15.5 1.9 gather_fusion.24
  18.3 1.9 gather_fusion.29
  28.1 26.4 %all-gather = bf16[32,2,1536]{2,1,0:T(2,128)(2,1)S(1)} all-gather(bf16[1,2,1536]{2,1,0:T(2,128)(2,1)S(1)} %fusion.170), channel_id=1, replica_groups=mesh['req'=4,'tp'=32] {'tp'}, dimensions={0}, use_global_device_ids=true | all-gather | bytes 202752 | tf_op jit(solution)/shard_map/all_gather | solution.py:142
  54.6 4.0 fusion.28
  60.3 14.1 %all_gather.37 = bf16[256,1536]{1,0:T(8,128)(2,1)S(1)} all-gather(bf16[64,1536]{1,0:T(8,128)(2,1)S(1)} %bitcast.314), channel_id=1, replica_groups=mesh['req'=4,'tp'=32] {'req'}, dimensions={0}, use_global_device_ids=true | all-gather | bytes 983040 | tf_op jit(solution)/shard_map/all_gather | solution.py:157
  75.1 7.0 reshape.1079
  82.1 6.9 reshape.1080
  89.7 4.0 fusion.204
  99.8 2.6 fusion.20
  109.7 65.5 %all-reduce.9 = (f32[256,2,6]{0,1,2:T(2,128)S(1)}, f32[256,2,6]{0,1,2:T(2,128)S(1)}) all-reduce(f32[256,2,6]{0,1,2:T(2,128)S(1)} %copy.328, f32[256,2,6]{0,1,2:T(2,128)S(1)} %copy.335), channel_id=1, replica_groups=mesh['req'=4,'tp'=32] {'req','tp'}, use_global_device_ids=true, to_apply=%region_6.10 | all-reduce | flops 6144 | bytes 49152 | tf_op jit(solution)/shard_map/psum | solution.py:173
  185.3 63.5 %all-reduce.20.cloned.1.call-done = f32[256,2,6,128]{3,1,2,0:T(2,128)} async-done(((f32[256,2,6,128]{3,1,2,0:T(2,128)}), f32[256,2,6,128]{3,1,2,0:T(2,128)}) %all-reduce.20.cloned.1.call-update) | async-done | bytes 1572880 | tf_op jit(solution)/shard_map/psum | solution.py:173
  248.8 2.9 fusion.98
  253.1 98.7 %all-reduce.22.cloned.1.call-done = bf16[64,1536]{1,0:T(8,128)(2,1)} async-done(((bf16[64,1536]{1,0:T(8,128)(2,1)}), bf16[64,1536]{1,0:T(8,128)(2,1)}) %all-reduce.22.cloned.1.call-update) | async-done | bytes 196624
  354.1 23.7 %all-gather.4 = bf16[32,2,1536]{2,1,0:T(2,128)(2,1)S(1)} all-gather(bf16[1,2,1536]{2,1,0:T(2,128)(2,1)S(1)} %get-tuple-element.172), channel_id=1, replica_groups=mesh['req'=4,'tp'=32] {'tp'}, dimensions={0}, use_global_device_ids=true | all-gather | bytes 202752 | tf_op jit(solution)/shard_map/all_gather | solution.py:142
  377.9 4.0 fusion.30
  382.6 23.3 %all-gather.2 = bf16[32,2,1536]{2,1,0:T(2,128)(2,1)S(1)} all-gather(bf16[1,2,1536]{2,1,0:T(2,128)(2,1)S(1)} %get-tuple-element.171), channel_id=1, replica_groups=mesh['req'=4,'tp'=32] {'tp'}, dimensions={0}, use_global_device_ids=true | all-gather | bytes 202752 | tf_op jit(solution)/shard_map/all_gather | solution.py:142
  406.0 4.0 fusion.29
  413.4 23.7 %all-gather.6 = bf16[32,2,1536]{2,1,0:T(2,128)(2,1)S(1)} all-gather(bf16[1,2,1536]{2,1,0:T(2,128)(2,1)S(1)} %get-tuple-element.173), channel_id=1, replica_groups=mesh['req'=4,'tp'=32] {'tp'}, dimensions={0}, use_global_device_ids=true | all-gather | bytes 202752 | tf_op jit(solution)/shard_map/all_gather | solution.py:142
  437.3 4.0 fusion.31
  442.3 14.0 %all_gather.46 = bf16[256,1536]{1,0:T(8,128)(2,1)S(1)} all-gather(bf16[64,1536]{1,0:T(8,128)(2,1)S(1)} %bitcast.315), channel_id=1, replica_groups=mesh['req'=4,'tp'=32] {'req'}, dimensions={0}, use_global_device_ids=true | all-gather | bytes 983040 | tf_op jit(solution)/shard_map/all_gather | solution.py:157
  459.0 14.3 %all_gather.40 = bf16[256,1536]{1,0:T(8,128)(2,1)S(1)} all-gather(bf16[64,1536]{1,0:T(8,128)(2,1)S(1)} %bitcast.316), channel_id=1, replica_groups=mesh['req'=4,'tp'=32] {'req'}, dimensions={0}, use_global_device_ids=true | all-gather | bytes 983040 | tf_op jit(solution)/shard_map/all_gather | solution.py:157
  475.0 13.9 %all_gather.43 = bf16[256,1536]{1,0:T(8,128)(2,1)S(1)} all-gather(bf16[64,1536]{1,0:T(8,128)(2,1)S(1)} %bitcast.317), channel_id=1, replica_groups=mesh['req'=4,'tp'=32] {'req'}, dimensions={0}, use_global_device_ids=true | all-gather | bytes 983040 | tf_op jit(solution)/shard_map/all_gather | solution.py:157
  490.5 4.0 fusion.206
  494.5 1.6 fusion.207
  498.4 1.7 fusion.83
  500.1 1.7 fusion.93
  501.8 2.1 fusion.22
  504.0 1.7 fusion.73
  526.8 1.6 copy.365
  534.0 1.6 copy.343
  545.6 1.8 copy.348
  555.7 1.9 select_bitcast_fusion
  557.7 22.9 %all-gather.1 = bf16[32,2,1536]{2,1,0:T(2,128)(2,1)S(1)} all-gather(bf16[1,2,1536]{2,1,0:T(2,128)(2,1)S(1)} %copy-done.66), channel_id=1, replica_groups=mesh['req'=4,'tp'=32] {'tp'}, dimensions={0}, use_global_device_ids=true | all-gather | bytes 202752 | tf_op jit(solution)/shard_map/all_gather | solution.py:207
  580.7 2.2 scatter.55
  587.7 119.7 %all-reduce.24.cloned.1.call-done = (f32[256,2,6]{2,1,0:T(2,128)}, f32[256,2,6]{2,1,0:T(2,128)}, f32[256,2,6]{2,1,0:T(2,128)}, f32[256,2,6]{2,1,0:T(2,128)}, f32[256,2,6]{2,1,0:T(2,128)}, /*index=5*/f32[256,2,6]{2,1,0:T(2,128)}) async-done(((f32[256,2,6]{2,1,0:T(2,128)}, f32[256,2,6]{2,1,0:T(2,128)}, f32[256,2,6]{2,1,0:T(2,128)}, f32[256,2,6]{2,1,0:T(2,128)}, f32[256,2,6]{2,1,0:T(2,128)}, ...) | async-done | bytes 73744 | tf_op jit(solution)/shard_map/psum | solution.py:173
  714.4 155.2 %all-reduce.26.cloned.1.call-done = (f32[256,2,6,128]{3,2,1,0:T(8,128)}, f32[256,2,6,128]{3,2,1,0:T(8,128)}, f32[256,2,6,128]{3,2,1,0:T(8,128)}) async-done(((f32[256,2,6,128]{3,2,1,0:T(8,128)}, f32[256,2,6,128]{3,2,1,0:T(8,128)}, f32[256,2,6,128]{3,2,1,0:T(8,128)}), (f32[256,2,6,128]{3,2,1,0:T(8,128)}, f32[256,2,6,128]{3,2,1,0:T(8,128)}, f32[256,2,6,128]{3,2,1,0:T(8,128)})) %all-reduce.26.cloned.1.call-update) | async-done | bytes 4718608 | tf_op jit(solution)/shard_map/psum | solution.py:173
  875.2 1.7 fusion.53
  878.6 1.6 convolution_convert_fusion.6
  880.3 99.7 %all-reduce.30.cloned.1.call-done = (bf16[64,1536]{1,0:T(8,128)(2,1)}, bf16[64,1536]{1,0:T(8,128)(2,1)}, bf16[64,1536]{1,0:T(8,128)(2,1)}) async-done(((bf16[64,1536]{1,0:T(8,128)(2,1)}, bf16[64,1536]{1,0:T(8,128)(2,1)}, bf16[64,1536]{1,0:T(8,128)(2,1)}), (bf16[64,1536]{1,0:T(8,128)(2,1)}, bf16[64,1536]{1,0:T(8,128)(2,1)}, bf16[64,1536]{1,0:T(8,128)(2,1)})) %all-reduce.30.cloned.1.call-update) | async-done | bytes 589840
  981.8 24.7 %all-gather.3 = bf16[32,2,1536]{2,1,0:T(2,128)(2,1)S(1)} all-gather(bf16[1,2,1536]{2,1,0:T(2,128)(2,1)S(1)} %get-tuple-element.174), channel_id=1, replica_groups=mesh['req'=4,'tp'=32] {'tp'}, dimensions={0}, use_global_device_ids=true | all-gather | bytes 202752 | tf_op jit(solution)/shard_map/all_gather | solution.py:207
  1007.0 1.6 convolution_convert_fusion.4
  1008.6 22.5 %all-gather.5 = bf16[32,2,1536]{2,1,0:T(2,128)(2,1)S(1)} all-gather(bf16[1,2,1536]{2,1,0:T(2,128)(2,1)S(1)} %get-tuple-element.176), channel_id=1, replica_groups=mesh['req'=4,'tp'=32] {'tp'}, dimensions={0}, use_global_device_ids=true | all-gather | bytes 202752 | tf_op jit(solution)/shard_map/all_gather | solution.py:207
  1031.7 1.6 convolution_convert_fusion.2
  1033.3 24.1 %all-gather.7 = bf16[32,2,1536]{2,1,0:T(2,128)(2,1)S(1)} all-gather(bf16[1,2,1536]{2,1,0:T(2,128)(2,1)S(1)} %get-tuple-element.175), channel_id=1, replica_groups=mesh['req'=4,'tp'=32] {'tp'}, dimensions={0}, use_global_device_ids=true | all-gather | bytes 202752 | tf_op jit(solution)/shard_map/all_gather | solution.py:207
  1057.9 1.7 convolution_convert_fusion
  1059.6 103.3 %all-reduce.28.cloned.1.call-done = (bf16[64,1536]{1,0:T(8,128)(2,1)}, bf16[64,1536]{1,0:T(8,128)(2,1)}, bf16[64,1536]{1,0:T(8,128)(2,1)}, bf16[64,1536]{1,0:T(8,128)(2,1)}) async-done(((bf16[64,1536]{1,0:T(8,128)(2,1)}, bf16[64,1536]{1,0:T(8,128)(2,1)}, bf16[64,1536]{1,0:T(8,128)(2,1)}, bf16[64,1536]{1,0:T(8,128)(2,1)}), (bf16[64,1536]{1,0:T(8,128)(2,1)}, bf16[64,1536]{1,0:T(8,128)(2,1)}, ...) | async-done | bytes 786448
  (478 shorter events, 124.4 us)
Async XLA Ops:
  6.5 872.1 %copy-start = (bf16[280,1536]{1,0:T(8,128)(2,1)S(1)}, bf16[280,1536]{1,0:T(8,128)(2,1)}, u32[]{:S(2)}) copy-start(bf16[280,1536]{1,0:T(8,128)(2,1)} %param.42) | copy-start | bytes 2580484
  6.5 242.2 %all-reduce.20.cloned.1.call-start = ((), (), s32[]{:S(2)}) async-start(), calls=%async_computation | async-start | bytes 3145728 | tf_op jit(solution)/shard_map/psum | solution.py:173
  8.8 80.8 %copy-start.68 = (pred[16]{0:T(512)(128)(4,1)}, pred[16]{0:T(512)(128)(4,1)S(1)}, u32[]{:S(2)}) copy-start(pred[16]{0:T(512)(128)(4,1)S(1)} %compare_and_fusion.4) | copy-start | bytes 52
  26.7 27.9 %copy-start.53 = (f32[2048]{0:T(1024)S(1)}, f32[2048]{0:T(1024)}, u32[]{:S(2)}) copy-start(f32[2048]{0:T(1024)} %param.38) | copy-start | bytes 24580
  59.8 22.3 %copy-start.42 = (f32[64,64]{1,0:T(8,128)}, f32[64,64]{1,0:T(8,128)S(1)}, u32[]{:S(2)}) copy-start(f32[64,64]{1,0:T(8,128)S(1)} %get-tuple-element.217) | copy-start | bytes 49156
  59.8 22.3 %copy-start.44 = (f32[64,64]{1,0:T(8,128)}, f32[64,64]{1,0:T(8,128)S(1)}, u32[]{:S(2)}) copy-start(f32[64,64]{1,0:T(8,128)S(1)} %get-tuple-element.218) | copy-start | bytes 49156
  74.4 14.6 %copy-start.67 = (s32[1024]{0:T(1024)}, s32[1024]{0:T(1024)S(1)}, u32[]{:S(2)}) copy-start(s32[1024]{0:T(1024)S(1)} %pad_clamp_fusion.4) | copy-start | bytes 12292
  96.8 6.4 copy-start.43
  99.4 252.3 %all-reduce.22.cloned.1.call-start = ((), (), s32[]{:S(2)}) async-start(), calls=%async_computation.1 | async-start | bytes 393216
  103.2 77.1 %copy-start.75 = (pred[2,8]{1,0:T(4,128)(4,1)S(1)}, pred[2,8]{1,0:T(4,128)(4,1)}, u32[]{:S(2)}) copy-start(pred[2,8]{1,0:T(4,128)(4,1)} %get-tuple-element.206) | copy-start | bytes 52
  103.2 77.6 %copy-start.73 = (pred[2,8]{1,0:T(4,128)(4,1)S(1)}, pred[2,8]{1,0:T(4,128)(4,1)}, u32[]{:S(2)}) copy-start(pred[2,8]{1,0:T(4,128)(4,1)} %get-tuple-element.208) | copy-start | bytes 52
  103.2 78.2 %copy-start.71 = (pred[2,8]{1,0:T(4,128)(4,1)S(1)}, pred[2,8]{1,0:T(4,128)(4,1)}, u32[]{:S(2)}) copy-start(pred[2,8]{1,0:T(4,128)(4,1)} %get-tuple-element.207) | copy-start | bytes 52
  103.2 78.8 %copy-start.79 = (u32[128]{0:T(128)S(1)}, u32[128]{0:T(128)}, u32[]{:S(2)}) copy-start(u32[128]{0:T(128)} %constant.501) | copy-start | bytes 1540
  108.4 143.6 %copy-start.9 = (bf16[48,1536]{1,0:T(8,128)(2,1)S(1)}, bf16[48,1536]{1,0:T(8,128)(2,1)}, u32[]{:S(2)}) copy-start(bf16[48,1536]{1,0:T(8,128)(2,1)} %param.39) | copy-start | bytes 442372
  253.0 454.4 %all-reduce.24.cloned.1.call-start = ((), (), s32[]{:S(2)}) async-start(), calls=%async_computation.2 | async-start | bytes 3145728 | tf_op jit(solution)/shard_map/psum | solution.py:173
  457.7 31.9 %copy-start.69 = (pred[16]{0:T(512)(128)(4,1)S(1)}, pred[16]{0:T(512)(128)(4,1)}, u32[]{:S(2)}) copy-start(pred[16]{0:T(512)(128)(4,1)} %copy-done.68) | copy-start | bytes 52
  503.9 5.5 copy-start.41
  504.0 6.5 copy-start.50
  504.0 6.5 copy-start.36
  504.0 6.5 copy-start.37
  505.7 6.9 copy-start.21
  505.7 8.6 copy-start.18
  505.7 9.5 copy-start.19
  505.7 17.5 %copy-start.55 = (bf16[1,64,256]{2,1,0:T(8,128)(2,1)S(1)}, bf16[1,64,256]{2,1,0:T(8,128)(2,1)}, u32[]{:S(2)}) copy-start(bf16[1,64,256]{2,1,0:T(8,128)(2,1)} %get-tuple-element.151) | copy-start | bytes 98308
  511.8 13.1 %copy-start.25 = (bf16[4,64,256]{2,0,1:T(4,128)(2,1)}, bf16[4,64,256]{2,0,1:T(4,128)(2,1)S(1)}, u32[]{:S(2)}) copy-start(bf16[4,64,256]{2,0,1:T(4,128)(2,1)S(1)} %scatter.36) | copy-start | bytes 393220
  513.5 11.3 copy-start.22
  520.4 8.1 copy-start.58
  532.5 10.8 copy-start.33
  532.5 10.8 copy-start.35
  533.9 14.3 %copy-start.61 = (f32[16,2,6]{2,1,0:T(2,128)S(1)}, f32[16,2,6]{2,1,0:T(2,128)}, u32[]{:S(2)}) copy-start(f32[16,2,6]{2,1,0:T(2,128)} %copy.379) | copy-start | bytes 2308
  534.0 15.7 %copy-start.60 = (f32[16,2,6]{2,1,0:T(2,128)S(1)}, f32[16,2,6]{2,1,0:T(2,128)}, u32[]{:S(2)}) copy-start(f32[16,2,6]{2,1,0:T(2,128)} %copy.367) | copy-start | bytes 2308
  535.6 11.7 %copy-start.17 = (bf16[64,12,64]{2,0,1:T(8,128)(2,1)S(1)}, bf16[64,12,64]{2,0,1:T(8,128)(2,1)}, u32[]{:S(2)}) copy-start(bf16[64,12,64]{2,0,1:T(8,128)(2,1)} %copy.347) | copy-start | bytes 294916
  535.6 15.3 %copy-start.63 = (f32[16,2,6]{2,1,0:T(2,128)S(1)}, f32[16,2,6]{2,1,0:T(2,128)}, u32[]{:S(2)}) copy-start(f32[16,2,6]{2,1,0:T(2,128)} %copy.399) | copy-start | bytes 2308
  535.6 16.5 %copy-start.62 = (f32[16,2,6]{2,1,0:T(2,128)S(1)}, f32[16,2,6]{2,1,0:T(2,128)}, u32[]{:S(2)}) copy-start(f32[16,2,6]{2,1,0:T(2,128)} %copy.387) | copy-start | bytes 2308
  535.6 17.7 %copy-start.65 = (f32[16,2,6]{2,1,0:T(2,128)S(1)}, f32[16,2,6]{2,1,0:T(2,128)}, u32[]{:S(2)}) copy-start(f32[16,2,6]{2,1,0:T(2,128)} %copy.359) | copy-start | bytes 2308
  535.6 18.9 %copy-start.64 = (f32[16,2,6]{2,1,0:T(2,128)S(1)}, f32[16,2,6]{2,1,0:T(2,128)}, u32[]{:S(2)}) copy-start(f32[16,2,6]{2,1,0:T(2,128)} %copy.345) | copy-start | bytes 2308
  537.4 7.0 copy-start.30
  543.3 14.4 %copy-start.66 = (bf16[1,2,1536]{2,1,0:T(2,128)(2,1)S(1)}, bf16[1,2,1536]{2,1,0:T(2,128)(2,1)}, u32[]{:S(2)}) copy-start(bf16[1,2,1536]{2,1,0:T(2,128)(2,1)} %get-tuple-element.170) | copy-start | bytes 18436
  544.3 36.4 %copy-start.52 = (bf16[1,64,256]{2,0,1:T(2,128)(2,1)S(1)}, bf16[1,64,256]{2,0,1:T(2,128)(2,1)}, u32[]{:S(2)}) copy-start(bf16[1,64,256]{2,0,1:T(2,128)(2,1)} %copy.395) | copy-start | bytes 98308
  544.4 11.2 copy-start.27
  549.6 8.0 copy-start.11
  550.8 6.8 copy-start.12
  552.0 5.6 copy-start.13
  557.6 312.0 %all-reduce.26.cloned.1.call-start = ((), (), s32[]{:S(2)}) async-start(), calls=%async_computation.3 | async-start | bytes 12582912 | tf_op jit(solution)/shard_map/psum | solution.py:173
  584.6 285.0 %copy-start.29 = (bf16[4,64,256]{2,0,1:T(4,128)(2,1)S(1)}, bf16[4,64,256]{2,0,1:T(4,128)(2,1)}, u32[]{:S(2)}) copy-start(bf16[4,64,256]{2,0,1:T(4,128)(2,1)} %copy-done.28) | copy-start | bytes 393220
  584.6 395.3 %all-reduce.30.cloned.1.call-start = ((), (), s32[]{:S(2)}) async-start(), calls=%async_computation.5 | async-start | bytes 1179648
  586.8 284.5 %copy-start.57 = (f32[64,2,6,2]{2,3,1,0:T(2,128)}, f32[64,2,6,2]{2,3,1,0:T(2,128)S(1)}, u32[]{:S(2)}) copy-start(f32[64,2,6,2]{2,3,1,0:T(2,128)S(1)} %get-tuple-element.230) | copy-start | bytes 18436
  878.1 284.8 %all-reduce.28.cloned.1.call-start = ((), (), s32[]{:S(2)}) async-start(), calls=%async_computation.4 | async-start | bytes 1572864
  (38 other events, 119.1 us)
Sparse Core Ops, SparseCore 0:
  99.5 149.2 all-reduce.19
  253.1 98.5 all-reduce.21
  557.8 149.5 all-reduce.23
  712.4 157.1 all-reduce.25
  878.2 101.6 all-reduce.29
  1059.7 103.1 all-reduce.27
where the time goes:
time: 1180 us; the launch traced here: 1170 us
  waiting for transfers between devices  640 us (54%)
  blocking collectives  313 us (27%)
  local copies, waits for them, and re-layouts  95.5 us (8%)
  other arithmetic  53.3 us (5%)
  matrix products  52.6 us (4%)
  between operations  16.5 us (1%)
    psum x3, waiting for transfers between devices, per_device(): lax.psum((all_peak, all_total, all_output), ('req', 'tp'))  338 us
    unnamed x9, waiting for transfers between devices  302 us
    all_gather x4, blocking collectives, per_device(): lax.all_gather(normed, 'tp', axis=0, tiled=True)  97.2 us
    all_gather x4, blocking collectives, per_device(): piece = lax.all_gather(mixed_in, 'tp', axis=0, tiled=True)  94.2 us
    psum x1, blocking collectives, per_device(): lax.psum((all_peak, all_total, all_output), ('req', 'tp'))  65.5 us
    all_gather x4, blocking collectives, per_device(): lax.all_gather(queries.reshape(group_rows, attn_width), 'req', axis=0, ti...  56.3 us
  transfers between devices with their start and end apart: 6, of which 6 were waited for; matrix products, arithmetic and copies ran while one was open for 3% of the time, Pallas kernels for 0%

commit v1 on v0

v1 whole, which is shorter than its diff:
```python
import jax
import jax.numpy as jnp
from jax import lax
from jax.sharding import Mesh
from jax.sharding import PartitionSpec as P

Q_HEADS = 12
KV_HEADS = 2

theta_base = 1000000.0
norm_eps = 1e-06
masked_score = -1e30

ALL = ("req", "tpo", "tpi")
TP = ("tpo", "tpi")


def rms_normed(values):
    values = values.astype(jnp.float32)
    factor = lax.rsqrt(jnp.mean(values * values, axis=-1, keepdims=True) + norm_eps)
    return (values * factor).astype(jnp.bfloat16)


def rotate(vectors, positions):
    half = vectors.shape[-1] // 2
    freqs = theta_base ** (-jnp.arange(half, dtype=jnp.float32) * 2.0 / vectors.shape[-1])
    angles = positions.astype(jnp.float32)[..., None] * freqs
    cosine = jnp.cos(angles)[..., None, :]
    sine = jnp.sin(angles)[..., None, :]
    values = vectors.astype(jnp.float32)
    first = values[..., :half]
    second = values[..., half:]
    return jnp.concatenate(
        [first * cosine - second * sine, second * cosine + first * sine], axis=-1
    ).astype(jnp.bfloat16)


def per_device(
    step_inputs,
    qkv_weight,
    qkv_bias,
    out_weight,
    gate_weight,
    up_weight,
    down_weight,
    cache_keys,
    cache_values,
    lengths,
    parents,
    slot_request,
):
    steps, rows_dev, width = step_inputs.shape
    beams = parents.shape[2]
    requests = slot_request.shape[0]
    n_req = lax.axis_size("req")
    n_o = lax.axis_size("tpo")
    n_i = lax.axis_size("tpi")
    tp_count = n_o * n_i
    group_requests = requests // n_req
    group_rows = group_requests * beams
    owned, context, kv_width = cache_keys.shape
    head_dim = kv_width // KV_HEADS
    group = Q_HEADS // KV_HEADS
    attn_width = Q_HEADS * head_dim
    scale = head_dim ** (-0.5)
    assert owned * n_i == beams

    req_index = lax.axis_index("req")
    tp_index = lax.axis_index("tpo") * n_i + lax.axis_index("tpi")
    j = lax.axis_index("tpi")
    flat = req_index * tp_count + tp_index
    r = flat // n_i

    inverse = (
        jnp.zeros((requests,), jnp.int32)
        .at[slot_request]
        .set(jnp.arange(requests, dtype=jnp.int32))
    )

    x_all = lax.all_gather(jnp.swapaxes(step_inputs, 0, 1), ALL, axis=0, tiled=True)

    x_req = lax.dynamic_slice_in_dim(x_all, inverse[r] * beams, beams, 0)
    normed = rms_normed(x_req)
    qkv = (
        jnp.dot(normed, qkv_weight, preferred_element_type=jnp.float32) + qkv_bias
    ).astype(jnp.bfloat16)

    par = parents[:, r, :]
    root = jnp.arange(beams, dtype=jnp.int32)
    roots = []
    for t in range(steps):
        root = root[par[t]]
        roots.append(root)
    roots = jnp.stack(roots, axis=1)
    len_r = lengths[r]
    positions = len_r[roots] + jnp.arange(steps, dtype=jnp.int32)[None, :]

    queries = rotate(qkv[..., :attn_width].reshape(beams, steps, Q_HEADS, head_dim), positions)
    new_keys = rotate(
        qkv[..., attn_width : attn_width + kv_width].reshape(beams, steps, KV_HEADS, head_dim),
        positions,
    )
    new_values = qkv[..., attn_width + kv_width :].reshape(beams, steps, KV_HEADS, head_dim)

    keys = cache_keys.reshape(owned, context, KV_HEADS, head_dim)
    values = cache_values.reshape(owned, context, KV_HEADS, head_dim)
    qg = queries.reshape(beams, steps, KV_HEADS, group, head_dim)
    scores = jnp.einsum(
        "btkgd,cpkd->cbtkgp", qg, keys, preferred_element_type=jnp.float32
    ) * scale
    my_beams = j * owned + jnp.arange(owned, dtype=jnp.int32)
    limits = len_r[my_beams]
    live = (jnp.arange(context, dtype=jnp.int32)[None, :] < limits[:, None])[
        :, None, None, None, None, :
    ]
    scores = jnp.where(live, scores, masked_score)
    peak = jnp.max(scores, axis=-1)
    weights = jnp.where(live, jnp.exp(scores - peak[..., None]), 0.0)
    total = jnp.sum(weights, axis=-1)
    output = jnp.einsum(
        "cbtkgp,cpkd->cbtkgd",
        weights.astype(jnp.bfloat16),
        values,
        preferred_element_type=jnp.float32,
    )
    chosen = (roots[None, :, :] == my_beams[:, None, None])[..., None, None]
    peak = jnp.sum(jnp.where(chosen, peak, 0.0), axis=0)
    total = jnp.sum(jnp.where(chosen, total, 0.0), axis=0)
    output = jnp.sum(jnp.where(chosen[..., None], output, 0.0), axis=0)
    packed = jnp.concatenate([output, peak[..., None], total[..., None]], axis=-1)
    packed = packed.reshape(n_i, owned, steps, KV_HEADS, group, head_dim + 2)
    packed = lax.psum_scatter(packed, "tpi", scatter_dimension=0, tiled=True)[0]
    part_output = packed[..., :head_dim]
    part_peak = packed[..., head_dim]
    part_total = packed[..., head_dim + 1]

    anc = []
    for t in range(steps):
        cur = jnp.arange(beams, dtype=jnp.int32)
        row = [None] * steps
        row[t] = cur
        for step in range(t, 0, -1):
            cur = par[step][cur]
            row[step - 1] = cur
        for u in range(t + 1, steps):
            row[u] = jnp.arange(beams, dtype=jnp.int32)
        anc.append(jnp.stack(row, axis=0))
    anc = jnp.stack(anc, axis=0)
    anc_mine = lax.dynamic_slice_in_dim(anc, j * owned, owned, 2)
    anc_mine = jnp.transpose(anc_mine, (2, 0, 1))
    u_index = jnp.broadcast_to(jnp.arange(steps, dtype=jnp.int32), anc_mine.shape)
    hist_keys = new_keys[anc_mine, u_index]
    hist_values = new_values[anc_mine, u_index]
    q_mine = lax.dynamic_slice_in_dim(qg, j * owned, owned, 0)
    recent_scores = jnp.einsum(
        "ctkgd,ctukd->ctkgu", q_mine, hist_keys, preferred_element_type=jnp.float32
    ) * scale
    causal = (
        jnp.arange(steps, dtype=jnp.int32)[None, :] <= jnp.arange(steps, dtype=jnp.int32)[:, None]
    )[None, :, None, None, :]
    recent_scores = jnp.where(causal, recent_scores, masked_score)
    top = jnp.maximum(part_peak, jnp.max(recent_scores, axis=-1))
    factor = jnp.exp(part_peak - top)
    recent_weights = jnp.where(causal, jnp.exp(recent_scores - top[..., None]), 0.0)
    denominator = part_total * factor + jnp.sum(recent_weights, axis=-1)
    numerator = part_output * factor[..., None] + jnp.einsum(
        "ctkgu,ctukd->ctkgd",
        recent_weights.astype(jnp.bfloat16),
        hist_values,
        preferred_element_type=jnp.float32,
    )
    attention = (
        (numerator / denominator[..., None]).reshape(owned, steps, attn_width).astype(jnp.bfloat16)
    )

    att_all = lax.all_gather(attention, ALL, axis=0, tiled=True)
    my_requests = lax.dynamic_slice_in_dim(slot_request, req_index * group_requests, group_requests)
    att_group = att_all.reshape(requests, beams, steps, attn_width)[my_requests].reshape(
        group_rows, steps, attn_width
    )
    x_group = lax.dynamic_slice_in_dim(x_all, req_index * group_rows, group_rows, 0)

    full_out = lax.all_gather(out_weight, TP, axis=0, tiled=True)
    middle = x_group.astype(jnp.float32) + jnp.dot(
        att_group, full_out, preferred_element_type=jnp.float32
    )
    mixed_in = rms_normed(middle)
    gate = jnp.dot(mixed_in, gate_weight, preferred_element_type=jnp.float32)
    upward = jnp.dot(mixed_in, up_weight, preferred_element_type=jnp.float32)
    hidden = (jax.nn.silu(gate) * upward).astype(jnp.bfloat16)
    lowered = lax.psum_scatter(
        jnp.dot(hidden, down_weight, preferred_element_type=jnp.float32).astype(jnp.bfloat16),
        TP,
        scatter_dimension=0,
        tiled=True,
    ).astype(jnp.float32)
    middle_mine = lax.dynamic_slice_in_dim(middle, tp_index * rows_dev, rows_dev, 0)
    result = (middle_mine + lowered).astype(jnp.bfloat16)
    return jnp.swapaxes(result, 0, 1)


def solution(mesh):
    n_req = mesh.shape["req"]
    n_tp = mesh.shape["tp"]
    inner = 4
    devices = mesh.devices.reshape(n_req, n_tp // inner, inner)
    sub = Mesh(devices, ALL)
    rows = P(None, ALL, None)
    in_specs = (
        rows,
        P(),
        P(),
        P(TP, None),
        P(None, TP),
        P(None, TP),
        P(TP, None),
        P(ALL, None, None),
        P(ALL, None, None),
        P(),
        P(),
        P(),
    )
    return jax.shard_map(per_device, mesh=sub, in_specs=in_specs, out_specs=rows, check_vma=False)
```

time: 1180 us -> 353 us (0.30)
  waiting for transfers between devices: 640 us -> 263 us
  blocking collectives: 313 us -> 0 us
  local copies, waits for them, and re-layouts: 95.5 us -> 43.4 us
  other arithmetic: 53.3 us -> 12.6 us
  matrix products: 52.6 us -> 17.5 us
    psum x3 -> x0, waiting for transfers between devices: 338 us -> none  [per_device(): lax.psum((all_peak, all_total, all_output), ('req', 'tp'))]
    all_gather x12 -> x0, blocking collectives: 248 us -> none  [the longest x4 97.2 us: per_device(): lax.all_gather(normed, 'tp', axis=0, tiled=True)]
    unnamed x9 -> x6, waiting for transfers between devices: 302 us -> 103 us
    all_gather x0 -> x3, waiting for transfers between devices: none -> 146 us  [the longest x1 64.1 us: per_device(): att_all = lax.all_gather(attention, ALL, axis=0, tiled=True)]
    psum x1 -> x0, blocking collectives: 65.5 us -> none  [per_device(): lax.psum((all_peak, all_total, all_output), ('req', 'tp'))]
    dot_general x27 -> x7, matrix products: 46 us -> 15.1 us  [the longest x1 4.27 us: per_device(): jnp.dot(att_group, full_out, preferred_element_type=jnp.float32)]
    gather x50 -> x16, local copies, waits for them, and re-layouts: 30.3 us -> 12.6 us  [the longest x6 3.87 us: per_device(): cur = par[step][cur]]
    scatter-add x12 -> x0, other arithmetic: 14.9 us -> none  [spread_rows(): jnp.zeros((row_count,) + piece.shape[1:], jnp.float32).at[target_rows]]
  transfers between devices with their start and end apart: 6 -> 5, of which waited for: 6 -> 5; matrix products, arithmetic and copies ran while one was open for 3% -> 11% of each run, Pallas kernels for 0% -> 0%
where the time goes in v1:
time: 353 us; the launch traced here: 352 us
  waiting for transfers between devices  263 us (75%)
  local copies, waits for them, and re-layouts  43.4 us (12%)
  matrix products  17.5 us (5%)
  between operations  14.8 us (4%)
  other arithmetic  12.6 us (4%)
    unnamed x6, waiting for transfers between devices  103 us
    all_gather x1, waiting for transfers between devices, per_device(): att_all = lax.all_gather(attention, ALL, axis=0, tiled=True)  64.1 us
    all_gather x1, waiting for transfers between devices, per_device(): lax.all_gather(jnp.swapaxes(step_inputs, 0, 1), ALL, axis=0, tiled=True)  43.4 us
    all_gather x1, waiting for transfers between devices, per_device(): full_out = lax.all_gather(out_weight, TP, axis=0, tiled=True)  38.6 us
    reduce_scatter x1, waiting for transfers between devices, per_device(): packed = lax.psum_scatter(packed, 'tpi', scatter_dimension=0, tiled=True)[0]  13.5 us
  transfers between devices with their start and end apart: 5, of which 5 were waited for; matrix products, arithmetic and copies ran while one was open for 11% of the time, Pallas kernels for 0%

profile of v1, /device:TPU:0, one launch (start us, length us, event | category | flops | bytes accessed | tf_op | source)
XLA Modules:
  0.0 351.5 jit_solution(14179320280636789039)
XLA Ops:
  6.5 1.4 copy.169
  8.1 0.7 compare_select_fusion.6
  8.7 0.7 scatter_custom_fusion
  9.4 0.6 dynamic_slice.30
  10.7 1.0 dynamic-slice_reduce_fusion
  11.6 0.6 gather_fusion.7
  12.3 0.6 gather_fusion.9
  12.9 0.6 gather_fusion.6
  13.6 0.6 gather_fusion
  14.3 0.6 gather_fusion.1
  14.9 0.6 gather_fusion.2
  15.6 0.6 gather_fusion.3
  16.4 0.9 dynamic-slice_reduce_fusion.4
  17.3 0.7 gather_fusion.5
  18.3 0.6 gather_fusion.4
  19.0 6.9 %reshape.449 = bf16[2,4096,2,128]{3,2,1,0:T(2,128)(2,1)} reshape(bf16[2,4096,256]{2,1,0:T(8,128)(2,1)} %param.19) | data formatting | bytes 8388608 | tf_op jit(solution)/shard_map/reshape | solution.py:105
  25.9 6.9 %reshape.450 = bf16[2,4096,2,128]{3,2,1,0:T(2,128)(2,1)} reshape(bf16[2,4096,256]{2,1,0:T(8,128)(2,1)} %param.20) | data formatting | bytes 8388608 | tf_op jit(solution)/shard_map/reshape | solution.py:106
  33.0 0.6 gather_fusion.10
  33.6 0.6 gather_fusion.11
  34.3 0.6 gather_fusion.8
  35.4 43.4 %all-gather.4.cloned.1.call-done = bf16[256,4,1536]{2,1,0:T(4,128)(2,1)} async-done(((bf16[2,4,1536]{2,1,0:T(4,128)(2,1)}), bf16[256,4,1536]{2,1,0:T(4,128)(2,1)}) %all-gather.4.cloned.1.call-update) | async-done | bytes 3145744 | tf_op jit(solution)/shard_map/all_gather | solution.py:80
  78.8 1.2 fusion.48
  80.0 1.1 fusion.49
  81.1 3.9 %fusion.19 = bf16[8,4,2048]{2,0,1:T(8,128)(2,1)S(1)} fusion(bf16[1536,2048]{1,0:T(8,128)(2,1)} %param.13, f32[2048]{0:T(1024)S(1)} %copy-done.4, bf16[8,4,1536]{2,1,0:T(4,128)(2,1)S(1)} %fusion.49), kind=kOutput, calls=%fused_computation.35 | convolution fusion | flops 201457664 | bytes 6529024 | tf_op jit(solution)/shard_map/dot_general | solution.py:85
  85.3 2.4 bitcast_reduce_fusion
  87.7 4.6 %fusion.3 = (bf16[2,8,4,2,6,4096]{5,1,0,4,2,3:T(8,128)(2,1)S(1)}, f32[2,8,4,2,6]{1,0,4,2,3:T(2,128)S(1)}) fusion(f32[2,8,4,6,2,4096]{5,1,4,3,2,0:T(8,128)S(1)} %get-tuple-element.28, f32[2,8,4,2,6]{1,0,4,2,3:T(2,128)S(1)} %get-tuple-element.27, pred[2,4096]{1,0:T(4,128)(4,1)S(1)} %iota_compare_fusion), kind=kLoop, calls=%fused_computation.22 | loop fusion | flops 18873600 | bytes 18888704 | tf_op jit(solution)/shard_map/convert_element_type | solution.py:122
  92.3 1.8 fusion.28
  95.6 0.9 pad_maximum_fusion
  96.8 0.7 gather_fusion.12
  98.0 0.7 gather_fusion.13
  98.6 13.5 %reduce-scatter.2.cloned.1.call-done = f32[1,2,4,2,6,130]{5,4,3,2,1,0:T(8,128)} async-done(((f32[4,2,4,2,6,130]{5,4,3,2,1,0:T(8,128)}), f32[1,2,4,2,6,130]{5,4,3,2,1,0:T(8,128)}) %reduce-scatter.2.cloned.1.call-update) | async-done | bytes 49936 | tf_op jit(solution)/shard_map/reduce_scatter | solution.py:132
  112.2 0.9 fusion.57
  113.4 1.1 fusion.68
  114.5 1.2 fusion.34
  115.7 0.6 convert_element_type.74
  117.3 2.3 constant_dynamic-slice_fusion.1
  119.6 64.1 %all-gather.6.cloned.1.call-done = bf16[256,4,1536]{2,1,0:T(4,128)(2,1)} async-done(((bf16[2,4,1536]{2,1,0:T(4,128)(2,1)}), bf16[256,4,1536]{2,1,0:T(4,128)(2,1)}) %all-gather.6.cloned.1.call-update) | async-done | bytes 3145744 | tf_op jit(solution)/shard_map/all_gather | solution.py:176
  183.7 4.4 %copy.99 = bf16[32,8,4,1536]{3,1,2,0:T(8,128)(2,1)} copy(bf16[32,8,4,1536]{3,2,1,0:T(4,128)(2,1)} %bitcast.148) | data formatting | bytes 6291456 | tf_op jit(solution)/shard_map/reshape | solution.py:178
  188.1 3.4 gather_fusion.14
  191.5 38.6 %all-gather.8.cloned.1.call-done = bf16[1536,1536]{1,0:T(8,128)(2,1)} async-done(((bf16[48,1536]{1,0:T(8,128)(2,1)}), bf16[1536,1536]{1,0:T(8,128)(2,1)}) %all-gather.8.cloned.1.call-update) | async-done | bytes 4718608 | tf_op jit(solution)/shard_map/all_gather | solution.py:183
  230.1 4.3 %multiply_reduce_fusion = (f32[64,4]{0,1:T(4,128)S(1)}, f32[64,4,1536]{2,0,1:T(8,128)S(1)}) fusion(bf16[1536,1536]{1,0:T(8,128)(2,1)} %all-gather.8.cloned.1.call-done, bf16[8,8,4,1536]{3,1,2,0:T(8,128)(2,1)} %gather_fusion.14, bf16[64,4,1536]{2,1,0:T(4,128)(2,1)} %constant_dynamic-slice_fusion.1), kind=kOutput, calls=%fused_computation.37 | convolution fusion | flops 1209532160 | bytes 7865344 | tf_op jit(solution)/shard_map/dot_general | solution.py:184
  234.4 1.3 fusion.39
  235.7 2.4 convolution_convert_fusion
  238.1 1.5 copy.101
  239.7 0.6 dynamic-slice
  240.9 102.7 %all-reduce.3.cloned.1.call-done = bf16[64,4,1536]{2,1,0:T(4,128)(2,1)} async-done(((bf16[64,4,1536]{2,1,0:T(4,128)(2,1)}), bf16[64,4,1536]{2,1,0:T(4,128)(2,1)}) %all-reduce.3.cloned.1.call-update) | async-done | bytes 786448
  343.6 0.7 constant_dynamic-slice_fusion.2
  344.4 0.6 fusion.58
  (86 shorter events, 4.8 us)
Async XLA Ops:
  6.5 229.2 %copy-start = (bf16[280,1536]{1,0:T(8,128)(2,1)S(1)}, bf16[280,1536]{1,0:T(8,128)(2,1)}, u32[]{:S(2)}) copy-start(bf16[280,1536]{1,0:T(8,128)(2,1)} %param.18) | copy-start | bytes 2580484
  6.5 72.3 %all-gather.4.cloned.1.call-start = ((), (), s32[]{:S(2)}) async-start(), calls=%async_computation.1 | async-start | bytes 3170304 | tf_op jit(solution)/shard_map/all_gather | solution.py:80
  8.0 104.2 %reduce-scatter.2.cloned.1.call-start = ((), (), s32[]{:S(2)}) async-start(), calls=%async_computation.2 | async-start | bytes 655360 | tf_op jit(solution)/shard_map/reduce_scatter | solution.py:132
  25.9 55.2 %copy-start.4 = (f32[2048]{0:T(1024)S(1)}, f32[2048]{0:T(1024)}, u32[]{:S(2)}) copy-start(f32[2048]{0:T(1024)} %param.14) | copy-start | bytes 24580
  78.8 6.4 %copy-start.1 = (bf16[2,4096,2,128]{3,2,1,0:T(2,128)(2,1)S(1)}, bf16[2,4096,2,128]{3,2,1,0:T(2,128)(2,1)}, u32[]{:S(2)}) copy-start(bf16[2,4096,2,128]{3,2,1,0:T(2,128)(2,1)} %reshape.449) | copy-start | bytes 12582916
  87.7 4.6 %copy-start.2 = (bf16[2,4096,2,128]{3,2,1,0:T(2,128)(2,1)S(1)}, bf16[2,4096,2,128]{3,2,1,0:T(2,128)(2,1)}, u32[]{:S(2)}) copy-start(bf16[2,4096,2,128]{3,2,1,0:T(2,128)(2,1)} %reshape.450) | copy-start | bytes 12582916
  94.1 23.1 %copy-start.5 = (s32[32]{0:T(128)S(1)}, s32[32]{0:T(128)}, u32[]{:S(2)}) copy-start(s32[32]{0:T(128)} %param.23) | copy-start | bytes 388
  96.5 87.2 %all-gather.6.cloned.1.call-start = ((), (), s32[]{:S(2)}) async-start(), calls=%async_computation.3 | async-start | bytes 3170304 | tf_op jit(solution)/shard_map/all_gather | solution.py:176
  116.4 113.7 %all-gather.8.cloned.1.call-start = ((), (), s32[]{:S(2)}) async-start(), calls=%async_computation.4 | async-start | bytes 4866048 | tf_op jit(solution)/shard_map/all_gather | solution.py:183
  117.0 226.7 %all-reduce.3.cloned.1.call-start = ((), (), s32[]{:S(2)}) async-start(), calls=%async_computation.5 | async-start | bytes 1572864
  191.5 42.9 %copy-start.3 = (bf16[1536,280]{0,1:T(8,128)(2,1)S(1)}, bf16[1536,280]{0,1:T(8,128)(2,1)}, u32[]{:S(2)}) copy-start(bf16[1536,280]{0,1:T(8,128)(2,1)} %param.16) | copy-start | bytes 2580484
  235.7 4.0 %copy-start.6 = (u32[128]{0:T(128)S(1)}, u32[128]{0:T(128)}, u32[]{:S(2)}) copy-start(u32[128]{0:T(128)} %constant.119) | copy-start | bytes 1540
Sparse Core Ops, SparseCore 0:
  10.4 68.3 all-gather.3
  96.7 15.4 reduce-scatter.1
  116.5 67.1 all-gather.5
  185.8 44.2 all-gather.7
  239.8 103.7 all-reduce.2

commit v2 on v1

--- a/solution.py
+++ b/solution.py
@@ -77,9 +77,13 @@
         .set(jnp.arange(requests, dtype=jnp.int32))
     )
 
-    x_all = lax.all_gather(jnp.swapaxes(step_inputs, 0, 1), ALL, axis=0, tiled=True)
-
-    x_req = lax.dynamic_slice_in_dim(x_all, inverse[r] * beams, beams, 0)
+    x_plane = lax.all_gather(jnp.swapaxes(step_inputs, 0, 1), ("req", "tpo"), axis=0, tiled=False)
+    my_slots = lax.dynamic_slice_in_dim(x_plane, req_index * group_requests, group_requests, 0)
+    carry = jnp.concatenate([x_plane[inverse[r]][None], my_slots], axis=0)
+    carry = lax.all_gather(carry, "tpi", axis=0, tiled=False)
+    x_req = carry[:, 0].reshape(beams, steps, width)
+    x_group = jnp.swapaxes(carry[:, 1:], 0, 1).reshape(group_rows, steps, width)
+
     normed = rms_normed(x_req)
     qkv = (
         jnp.dot(normed, qkv_weight, preferred_element_type=jnp.float32) + qkv_bias
@@ -102,12 +106,14 @@
     )
     new_values = qkv[..., attn_width + kv_width :].reshape(beams, steps, KV_HEADS, head_dim)
 
-    keys = cache_keys.reshape(owned, context, KV_HEADS, head_dim)
-    values = cache_values.reshape(owned, context, KV_HEADS, head_dim)
     qg = queries.reshape(beams, steps, KV_HEADS, group, head_dim)
-    scores = jnp.einsum(
-        "btkgd,cpkd->cbtkgp", qg, keys, preferred_element_type=jnp.float32
-    ) * scale
+    score_parts = []
+    for k in range(KV_HEADS):
+        keys_k = cache_keys[:, :, k * head_dim : (k + 1) * head_dim]
+        score_parts.append(
+            jnp.einsum("btgd,cpd->cbtgp", qg[:, :, k], keys_k, preferred_element_type=jnp.float32)
+        )
+    scores = jnp.stack(score_parts, axis=3) * scale
     my_beams = j * owned + jnp.arange(owned, dtype=jnp.int32)
     limits = len_r[my_beams]
     live = (jnp.arange(context, dtype=jnp.int32)[None, :] < limits[:, None])[
@@ -117,11 +123,18 @@
     peak = jnp.max(scores, axis=-1)
     weights = jnp.where(live, jnp.exp(scores - peak[..., None]), 0.0)
     total = jnp.sum(weights, axis=-1)
-    output = jnp.einsum(
-        "cbtkgp,cpkd->cbtkgd",
-        weights.astype(jnp.bfloat16),
-        values,
-        preferred_element_type=jnp.float32,
+    weights = weights.astype(jnp.bfloat16)
+    output = jnp.stack(
+        [
+            jnp.einsum(
+                "cbtgp,cpd->cbtgd",
+                weights[:, :, :, k],
+                cache_values[:, :, k * head_dim : (k + 1) * head_dim],
+                preferred_element_type=jnp.float32,
+            )
+            for k in range(KV_HEADS)
+        ],
+        axis=3,
     )
     chosen = (roots[None, :, :] == my_beams[:, None, None])[..., None, None]
     peak = jnp.sum(jnp.where(chosen, peak, 0.0), axis=0)
@@ -173,12 +186,11 @@
         (numerator / denominator[..., None]).reshape(owned, steps, attn_width).astype(jnp.bfloat16)
     )
 
-    att_all = lax.all_gather(attention, ALL, axis=0, tiled=True)
+    att_plane = lax.all_gather(attention, ("req", "tpo"), axis=0, tiled=False)
     my_requests = lax.dynamic_slice_in_dim(slot_request, req_index * group_requests, group_requests)
-    att_group = att_all.reshape(requests, beams, steps, attn_width)[my_requests].reshape(
-        group_rows, steps, attn_width
-    )
-    x_group = lax.dynamic_slice_in_dim(x_all, req_index * group_rows, group_rows, 0)
+    att_mine = att_plane[my_requests]
+    att_group = lax.all_gather(att_mine, "tpi", axis=0, tiled=False)
+    att_group = jnp.swapaxes(att_group, 0, 1).reshape(group_rows, steps, attn_width)
 
     full_out = lax.all_gather(out_weight, TP, axis=0, tiled=True)
     middle = x_group.astype(jnp.float32) + jnp.dot(
@@ -188,12 +200,10 @@
     gate = jnp.dot(mixed_in, gate_weight, preferred_element_type=jnp.float32)
     upward = jnp.dot(mixed_in, up_weight, preferred_element_type=jnp.float32)
     hidden = (jax.nn.silu(gate) * upward).astype(jnp.bfloat16)
-    lowered = lax.psum_scatter(
-        jnp.dot(hidden, down_weight, preferred_element_type=jnp.float32).astype(jnp.bfloat16),
-        TP,
-        scatter_dimension=0,
-        tiled=True,
-    ).astype(jnp.float32)
+    partial = jnp.dot(hidden, down_weight, preferred_element_type=jnp.float32)
+    partial = partial.reshape(tp_count, rows_dev * steps, width)
+    lowered = lax.psum_scatter(partial, TP, scatter_dimension=0, tiled=True)
+    lowered = lowered.reshape(rows_dev, steps, width)
     middle_mine = lax.dynamic_slice_in_dim(middle, tp_index * rows_dev, rows_dev, 0)
     result = (middle_mine + lowered).astype(jnp.bfloat16)
     return jnp.swapaxes(result, 0, 1)

time: 353 us -> 382 us (1.082)
  blocking collectives: 0 us -> 216 us
  waiting for transfers between devices: 263 us -> 76.4 us
  local copies, waits for them, and re-layouts: 43.4 us -> 30.7 us
  matrix products: 17.5 us -> 23.2 us
  other arithmetic: 12.6 us -> 17.3 us
    all_gather x0 -> x4, blocking collectives: none -> 216 us  [the longest x1 101 us: per_device(): lax.all_gather(jnp.swapaxes(step_inputs, 0, 1), ('req', 'tpo'), axis=0, t...]
    all_gather x2 -> x0, waiting for transfers between devices: 108 us -> none  [the longest x1 64.1 us: per_device(): att_all = lax.all_gather(attention, ALL, axis=0, tiled=True)]
    unnamed x6 -> x3, waiting for transfers between devices: 103 us -> 0.55 us
    reduce_scatter x0 -> x1, waiting for transfers between devices: none -> 73.6 us  [per_device(): lowered = lax.psum_scatter(partial, TP, scatter_dimension=0, tiled=True)]
    all_gather x1, waiting for transfers between devices: 38.6 us -> 0.03 us  [per_device(): full_out = lax.all_gather(out_weight, TP, axis=0, tiled=True)]
    reshape x3, local copies, waits for them, and re-layouts: 18.3 us -> 3.88 us  [the longest x1 2.77 us: per_device(): partial = partial.reshape(tp_count, rows_dev * steps, width)]
    reduce_scatter x1, waiting for transfers between devices: 13.5 us -> 2.28 us  [per_device(): packed = lax.psum_scatter(packed, 'tpi', scatter_dimension=0, tiled=True)[0]]
    reduce_max x0 -> x1, other arithmetic: none -> 6.32 us  [per_device(): peak = jnp.max(scores, axis=-1)]
  transfers between devices with their start and end apart: 5 -> 3, of which waited for: 5 -> 2; matrix products, arithmetic and copies ran while one was open for 11% -> 4% of each run, Pallas kernels for 0% -> 0%
where the time goes in v2:
time: 382 us; the launch traced here: 381 us
  blocking collectives  216 us (57%)
  waiting for transfers between devices  76.4 us (20%)
  local copies, waits for them, and re-layouts  30.7 us (8%)
  matrix products  23.2 us (6%)
  other arithmetic  17.3 us (5%)
  between operations  17.3 us (5%)
    all_gather x1, blocking collectives, per_device(): lax.all_gather(jnp.swapaxes(step_inputs, 0, 1), ('req', 'tpo'), axis=0, t...  101 us
    all_gather x1, blocking collectives, per_device(): att_plane = lax.all_gather(attention, ('req', 'tpo'), axis=0, tiled=False)  99.1 us
    reduce_scatter x1, waiting for transfers between devices, per_device(): lowered = lax.psum_scatter(partial, TP, scatter_dimension=0, tiled=True)  73.6 us
    all_gather x1, blocking collectives, per_device(): carry = lax.all_gather(carry, 'tpi', axis=0, tiled=False)  8.37 us
  transfers between devices with their start and end apart: 3, of which 2 were waited for; matrix products, arithmetic and copies ran while one was open for 4% of the time, Pallas kernels for 0%

profile of v2, /device:TPU:0, one launch (start us, length us, event | category | flops | bytes accessed | tf_op | source)
XLA Modules:
  0.0 381.0 jit_solution(18272524326881148084)
XLA Ops:
  7.4 0.7 compare_select_fusion.11
  8.1 0.7 scatter_custom_fusion
  10.7 0.8 copy.135
  11.4 100.7 %all-gather = bf16[64,4,1536]{2,1,0:T(4,128)(2,1)S(1)} all-gather(bf16[2,4,1536]{2,1,0:T(4,128)(2,1)S(1)} %bitcast.211), channel_id=2, replica_groups=mesh['req'=4,'tpo'=8,'tpi'=4] {'req','tpo'}, dimensions={0}, use_global_device_ids=true | all-gather | bytes 811008 | tf_op jit(solution)/shard_map/all_gather | solution.py:80
  113.1 8.4 %all-gather.1 = bf16[36,2,4,1536]{3,2,1,0:T(4,128)(2,1)S(1)} all-gather(bf16[9,2,4,1536]{3,2,1,0:T(4,128)(2,1)S(1)} %pad_maximum_fusion.1), channel_id=3, replica_groups=mesh['req'=4,'tpo'=8,'tpi'=4] {'tpi'}, dimensions={0}, use_global_device_ids=true | all-gather | bytes 1105920 | tf_op jit(solution)/shard_map/all_gather | solution.py:83
  121.6 0.9 dynamic-slice_reduce_fusion
  122.6 0.6 gather_fusion
  123.3 0.6 gather_fusion.1
  123.9 0.6 gather_fusion.2
  124.6 0.6 gather_fusion.3
  125.6 0.7 gather_fusion.5
  126.7 4.1 %fusion.18 = bf16[8,4,2048]{2,0,1:T(8,128)(2,1)S(1)} fusion(bf16[1536,2048]{1,0:T(8,128)(2,1)} %param.13, f32[2048]{0:T(1024)S(1)} %copy-done.4, f32[8,4,1536]{2,1,0:T(4,128)S(1)} %bitcast.205, f32[8,4]{0,1:T(4,128)S(1)} %copy.55), kind=kOutput, calls=%fused_computation.36 | convolution fusion | flops 201555968 | bytes 6627456 | tf_op jit(solution)/shard_map/dot_general | solution.py:89
  131.0 3.7 convolution_bitcast_fusion.1
  134.7 3.7 convolution_bitcast_fusion
  138.4 0.6 gather_fusion.4
  139.2 6.3 %fusion.5 = f32[2,8,4,2,6]{1,0,4,2,3:T(2,128)S(1)} fusion(f32[2,8,4,1,6,4096]{5,1,0,4,2,3:T(8,128)} %convolution_bitcast_fusion, f32[2,8,4,1,6,4096]{5,1,0,4,2,3:T(8,128)} %convolution_bitcast_fusion.1, pred[2,4096]{1,0:T(4,128)(4,1)S(1)} %iota_compare_fusion), kind=kLoop, calls=%fused_computation.25 | loop fusion | flops 12582144 | bytes 12594176 | tf_op jit(solution)/shard_map/reduce_max | solution.py:123
  145.5 1.3 slice-done
  146.8 0.7 slice-done.1
  147.5 4.6 %fusion.2 = (bf16[2,8,4,2,6,4096]{5,1,0,4,2,3:T(8,128)(2,1)S(1)}, f32[2,8,4,2,6]{1,0,4,2,3:T(2,128)S(1)}) fusion(f32[2,8,4,2,6]{1,0,4,2,3:T(2,128)S(1)} %fusion.5, pred[2,4096]{1,0:T(4,128)(4,1)S(1)} %iota_compare_fusion, f32[2,8,4,1,6,4096]{5,1,0,4,2,3:T(8,128)S(1)} %copy-done.1, f32[2,8,4,1,6,4096]{5,1,0,4,2,3:T(8,128)S(1)} %bitcast.190), kind=kLoop, calls=%fused_computation.20 | loop fusion | flops 22019328 | bytes 18888704 | tf_op jit(solution)/shard_map/convert_element_type | solution.py:126
  152.1 0.8 slice_bitcast_fusion.1
  152.9 1.4 copy-done.6
  154.3 1.0 fusion.30
  155.3 1.0 fusion.35
  157.9 1.0 pad_maximum_fusion
  159.7 0.6 gather_fusion.7
  160.4 0.6 gather_fusion.9
  161.0 0.6 gather_fusion.6
  161.7 0.6 gather_fusion.10
  162.3 0.6 gather_fusion.11
  163.0 0.6 gather_fusion.8
  164.2 0.7 gather_fusion.12
  165.4 0.7 gather_fusion.13
  166.2 0.8 copy.54
  167.1 2.3 reshape.474
  169.4 2.3 reduce-scatter.3.cloned.1.call-done
  171.7 0.9 fusion.70
  172.9 1.1 fusion.82
  174.0 1.2 fusion.42
  175.3 99.1 %all_gather.29 = bf16[32,2,4,1536]{3,2,1,0:T(4,128)(2,1)S(1)} all-gather(bf16[1,2,4,1536]{3,2,1,0:T(4,128)(2,1)S(1)} %convert_element_type.91), channel_id=1, replica_groups=mesh['req'=4,'tpo'=8,'tpi'=4] {'req','tpo'}, dimensions={0}, use_global_device_ids=true | all-gather | bytes 811008 | tf_op jit(solution)/shard_map/all_gather | solution.py:189
  274.4 0.7 gather_fusion.14
  275.1 7.6 %all-gather.2 = bf16[32,2,4,1536]{3,2,1,0:T(4,128)(2,1)S(1)} all-gather(bf16[8,2,4,1536]{3,2,1,0:T(4,128)(2,1)S(1)} %gather_fusion.14), channel_id=4, replica_groups=mesh['req'=4,'tpo'=8,'tpi'=4] {'tpi'}, dimensions={0}, use_global_device_ids=true | all-gather | bytes 983040 | tf_op jit(solution)/shard_map/all_gather | solution.py:192
  283.6 4.4 %multiply_reduce_fusion = (f32[64,4]{0,1:T(4,128)S(1)}, f32[64,4,1536]{2,0,1:T(8,128)S(1)}) fusion(f32[64,4,1536]{2,0,1:T(8,128)} %reshape.474, bf16[64,4,1536]{2,0,1:T(8,128)(2,1)S(1)} %reshape.471, bf16[1536,1536]{1,0:T(8,128)(2,1)} %all-gather.5.cloned.1.call-done), kind=kOutput, calls=%fused_computation.47 | convolution fusion | flops 1209138944 | bytes 8651776 | tf_op jit(solution)/shard_map/dot_general | solution.py:196
  288.6 3.5 fusion.40
  292.1 3.6 copy.82
  295.7 2.8 reshape.472
  298.5 73.6 %reduce-scatter.5.cloned.1.call-done = f32[1,8,1536]{2,1,0:T(8,128)} async-done(((f32[32,8,1536]{2,1,0:T(8,128)}), f32[1,8,1536]{2,1,0:T(8,128)}) %reduce-scatter.5.cloned.1.call-update) | async-done | bytes 49168 | tf_op jit(solution)/shard_map/reduce_scatter | solution.py:205
  372.1 0.8 reshape.473
  372.9 0.6 fusion.72
  (101 shorter events, 7.8 us)
Async XLA Ops:
  7.4 281.3 %copy-start = (bf16[280,1536]{1,0:T(8,128)(2,1)S(1)}, bf16[280,1536]{1,0:T(8,128)(2,1)}, u32[]{:S(2)}) copy-start(bf16[280,1536]{1,0:T(8,128)(2,1)} %param.18) | copy-start | bytes 2580484
  7.4 118.0 %copy-start.5 = (s32[32,8]{0,1:T(8,128)S(1)}, s32[32,8]{0,1:T(8,128)}, u32[]{:S(2)}) copy-start(s32[32,8]{0,1:T(8,128)} %param.21) | copy-start | bytes 3076
  7.4 164.3 %reduce-scatter.3.cloned.1.call-start = ((), (), s32[]{:S(2)}) async-start(), calls=%async_computation.2 | async-start | bytes 655360 | tf_op jit(solution)/shard_map/reduce_scatter | solution.py:145
  112.9 13.8 %copy-start.4 = (f32[2048]{0:T(1024)S(1)}, f32[2048]{0:T(1024)}, u32[]{:S(2)}) copy-start(f32[2048]{0:T(1024)} %param.14) | copy-start | bytes 24580
  126.5 4.5 %copy-start.2 = (bf16[2,4096,256]{2,1,0:T(8,128)(2,1)S(1)}, bf16[2,4096,256]{2,1,0:T(8,128)(2,1)}, u32[]{:S(2)}) copy-start(bf16[2,4096,256]{2,1,0:T(8,128)(2,1)} %param.19) | copy-start | bytes 12582916
  139.1 7.7 %slice-start = ((s8[6291456]{0:T(1024)(128)(4,1)}), s8[4194304]{0:T(1024)(128)(4,1)S(1)}, s32[]{:S(2)}) async-start(s8[6291456]{0:T(1024)(128)(4,1)} %bitcast.189), calls=%async_computation.5 | async-start | bytes 8388608
  139.1 8.3 %slice-start.1 = ((s8[6291456]{0:T(1024)(128)(4,1)}), s8[2097152]{0:T(1024)(128)(4,1)S(1)}, s32[]{:S(2)}) async-start(s8[6291456]{0:T(1024)(128)(4,1)} %bitcast.189), calls=%async_computation.6 | async-start | bytes 4194304
  139.2 8.3 %copy-start.1 = (f32[2,8,4,1,6,4096]{5,1,0,4,2,3:T(8,128)S(1)}, f32[2,8,4,1,6,4096]{5,1,0,4,2,3:T(8,128)}, u32[]{:S(2)}) copy-start(f32[2,8,4,1,6,4096]{5,1,0,4,2,3:T(8,128)} %convolution_bitcast_fusion) | copy-start | bytes 18874372
  152.1 2.2 copy-start.6
  158.9 124.7 %all-gather.5.cloned.1.call-start = ((), (), s32[]{:S(2)}) async-start(), calls=%async_computation.3 | async-start | bytes 4866048 | tf_op jit(solution)/shard_map/all_gather | solution.py:195
  159.5 212.6 %reduce-scatter.5.cloned.1.call-start = ((), (), s32[]{:S(2)}) async-start(), calls=%async_computation.4 | async-start | bytes 1622016 | tf_op jit(solution)/shard_map/reduce_scatter | solution.py:205
  166.0 3.3 copy-start.7
  283.6 4.4 %copy-start.3 = (bf16[1536,280]{0,1:T(8,128)(2,1)S(1)}, bf16[1536,280]{0,1:T(8,128)(2,1)}, u32[]{:S(2)}) copy-start(bf16[1536,280]{0,1:T(8,128)(2,1)} %param.16) | copy-start | bytes 2580484
Sparse Core Ops, SparseCore 0:
  159.0 12.6 reduce-scatter.2
Sparse Core Ops, SparseCore 1:
  161.6 42.5 all-gather.4
  298.6 73.4 reduce-scatter.4

commit v3 on v2

--- a/solution.py
+++ b/solution.py
@@ -77,12 +77,9 @@
         .set(jnp.arange(requests, dtype=jnp.int32))
     )
 
-    x_plane = lax.all_gather(jnp.swapaxes(step_inputs, 0, 1), ("req", "tpo"), axis=0, tiled=False)
-    my_slots = lax.dynamic_slice_in_dim(x_plane, req_index * group_requests, group_requests, 0)
-    carry = jnp.concatenate([x_plane[inverse[r]][None], my_slots], axis=0)
-    carry = lax.all_gather(carry, "tpi", axis=0, tiled=False)
-    x_req = carry[:, 0].reshape(beams, steps, width)
-    x_group = jnp.swapaxes(carry[:, 1:], 0, 1).reshape(group_rows, steps, width)
+    x_all = lax.all_gather(jnp.swapaxes(step_inputs, 0, 1), ALL, axis=0, tiled=True)
+    x_req = lax.dynamic_slice_in_dim(x_all, inverse[r] * beams, beams, 0)
+    x_group = lax.dynamic_slice_in_dim(x_all, req_index * group_rows, group_rows, 0)
 
     normed = rms_normed(x_req)
     qkv = (
@@ -186,11 +183,11 @@
         (numerator / denominator[..., None]).reshape(owned, steps, attn_width).astype(jnp.bfloat16)
     )
 
-    att_plane = lax.all_gather(attention, ("req", "tpo"), axis=0, tiled=False)
+    att_all = lax.all_gather(attention, ALL, axis=0, tiled=True)
     my_requests = lax.dynamic_slice_in_dim(slot_request, req_index * group_requests, group_requests)
-    att_mine = att_plane[my_requests]
-    att_group = lax.all_gather(att_mine, "tpi", axis=0, tiled=False)
-    att_group = jnp.swapaxes(att_group, 0, 1).reshape(group_rows, steps, attn_width)
+    att_group = att_all.reshape(requests, beams, steps, attn_width)[my_requests].reshape(
+        group_rows, steps, attn_width
+    )
 
     full_out = lax.all_gather(out_weight, TP, axis=0, tiled=True)
     middle = x_group.astype(jnp.float32) + jnp.dot(
@@ -200,10 +197,11 @@
     gate = jnp.dot(mixed_in, gate_weight, preferred_element_type=jnp.float32)
     upward = jnp.dot(mixed_in, up_weight, preferred_element_type=jnp.float32)
     hidden = (jax.nn.silu(gate) * upward).astype(jnp.bfloat16)
-    partial = jnp.dot(hidden, down_weight, preferred_element_type=jnp.float32)
-    partial = partial.reshape(tp_count, rows_dev * steps, width)
+    partial = jnp.dot(hidden, down_weight, preferred_element_type=jnp.float32).astype(jnp.bfloat16)
+    chunk = rows_dev * steps * width
+    partial = partial.reshape(tp_count, 16, chunk // 16)
     lowered = lax.psum_scatter(partial, TP, scatter_dimension=0, tiled=True)
-    lowered = lowered.reshape(rows_dev, steps, width)
+    lowered = lowered.reshape(rows_dev, steps, width).astype(jnp.float32)
     middle_mine = lax.dynamic_slice_in_dim(middle, tp_index * rows_dev, rows_dev, 0)
     result = (middle_mine + lowered).astype(jnp.bfloat16)
     return jnp.swapaxes(result, 0, 1)

time: 382 us -> 331 us (0.87)
  blocking collectives: 216 us -> 0 us
  waiting for transfers between devices: 76.4 us -> 253 us
  matrix products: 23.2 us -> 17.2 us
    all_gather x4 -> x0, blocking collectives: 216 us -> none  [the longest x1 101 us: per_device(): lax.all_gather(jnp.swapaxes(step_inputs, 0, 1), ('req', 'tpo'), axis=0, t...]
    all_gather x0 -> x2, waiting for transfers between devices: none -> 123 us  [the longest x1 65 us: per_device(): att_all = lax.all_gather(attention, ALL, axis=0, tiled=True)]
    all_gather x1, waiting for transfers between devices: 0.03 us -> 38.6 us  [per_device(): full_out = lax.all_gather(out_weight, TP, axis=0, tiled=True)]
    reduce_scatter x1, waiting for transfers between devices: 2.28 us -> 13.5 us  [per_device(): packed = lax.psum_scatter(packed, 'tpi', scatter_dimension=0, tiled=True)[0]]
    dot_general x2, matrix products: 7.35 us -> 2.03 us  [per_device(): jnp.einsum('btgd,cpd->cbtgp', qg[:, :, k], keys_k, preferred_element_type...]
    reduce_max x1, other arithmetic: 6.32 us -> 2.13 us  [per_device(): peak = jnp.max(scores, axis=-1)]
    reduce_scatter x1, waiting for transfers between devices: 73.6 us -> 77.4 us  [per_device(): lowered = lax.psum_scatter(partial, TP, scatter_dimension=0, tiled=True)]
  transfers between devices with their start and end apart: 3 -> 5, of which waited for: 2 -> 5; matrix products, arithmetic and copies ran while one was open for 4% -> 7% of each run, Pallas kernels for 0% -> 0%
where the time goes in v3:
time: 331 us; the launch traced here: 330 us
  waiting for transfers between devices  253 us (76%)
  local copies, waits for them, and re-layouts  31.6 us (10%)
  matrix products  17.2 us (5%)
  between operations  14.3 us (4%)
  other arithmetic  14.2 us (4%)
    reduce_scatter x1, waiting for transfers between devices, per_device(): lowered = lax.psum_scatter(partial, TP, scatter_dimension=0, tiled=True)  77.4 us
    all_gather x1, waiting for transfers between devices, per_device(): att_all = lax.all_gather(attention, ALL, axis=0, tiled=True)  65 us
    all_gather x1, waiting for transfers between devices, per_device(): lax.all_gather(jnp.swapaxes(step_inputs, 0, 1), ALL, axis=0, tiled=True)  57.8 us
    all_gather x1, waiting for transfers between devices, per_device(): full_out = lax.all_gather(out_weight, TP, axis=0, tiled=True)  38.6 us
    reduce_scatter x1, waiting for transfers between devices, per_device(): packed = lax.psum_scatter(packed, 'tpi', scatter_dimension=0, tiled=True)[0]  13.5 us
  transfers between devices with their start and end apart: 5, of which 5 were waited for; matrix products, arithmetic and copies ran while one was open for 7% of the time, Pallas kernels for 0%

profile of v3, /device:TPU:0, one launch (start us, length us, event | category | flops | bytes accessed | tf_op | source)
XLA Modules:
  0.0 330.5 jit_solution(11663422701476200743)
XLA Ops:
  6.5 1.4 copy.160
  8.1 1.0 dynamic-slice_reduce_fusion
  9.1 0.6 gather_fusion.7
  9.7 0.6 gather_fusion.9
  10.4 0.6 gather_fusion.6
  11.0 0.6 gather_fusion
  11.7 0.6 gather_fusion.1
  12.4 0.6 gather_fusion.2
  13.0 0.6 gather_fusion.3
  13.8 0.9 dynamic-slice_reduce_fusion.4
  14.7 0.7 gather_fusion.5
  15.8 0.7 scatter_custom_fusion
  16.5 0.7 dynamic_slice.30
  17.9 0.6 gather_fusion.4
  18.6 0.6 gather_fusion.10
  19.3 0.6 gather_fusion.11
  20.0 0.6 gather_fusion.8
  21.0 57.8 %all-gather.4.cloned.1.call-done = bf16[256,4,1536]{2,1,0:T(4,128)(2,1)} async-done(((bf16[2,4,1536]{2,1,0:T(4,128)(2,1)}), bf16[256,4,1536]{2,1,0:T(4,128)(2,1)}) %all-gather.4.cloned.1.call-update) | async-done | bytes 3145744 | tf_op jit(solution)/shard_map/all_gather | solution.py:80
  78.8 1.2 fusion.56
  80.0 1.1 fusion.57
  81.1 3.9 %fusion.18 = bf16[8,4,2048]{2,0,1:T(8,128)(2,1)S(1)} fusion(bf16[1536,2048]{1,0:T(8,128)(2,1)} %param.13, f32[2048]{0:T(1024)S(1)} %copy-done.3, bf16[8,4,1536]{2,1,0:T(4,128)(2,1)S(1)} %fusion.57), kind=kOutput, calls=%fused_computation.37 | convolution fusion | flops 201457664 | bytes 6529024 | tf_op jit(solution)/shard_map/dot_general | solution.py:86
  85.2 1.0 convolution_bitcast_fusion.1
  86.3 1.0 convolution_bitcast_fusion
  87.3 2.1 fusion.5
  89.4 4.6 %fusion.2 = (bf16[2,8,4,2,6,4096]{5,1,0,4,2,3:T(8,128)(2,1)S(1)}, f32[2,8,4,2,6]{1,0,4,2,3:T(2,128)S(1)}) fusion(f32[2,8,4,2,6]{1,0,4,2,3:T(2,128)S(1)} %fusion.5, pred[2,4096]{1,0:T(4,128)(4,1)S(1)} %iota_compare_fusion, f32[2,8,4,1,6,4096]{5,1,0,4,2,3:T(8,128)S(1)} %convolution_bitcast_fusion, f32[2,8,4,1,6,4096]{5,1,0,4,2,3:T(8,128)S(1)} %convolution_bitcast_fusion.1), kind=kLoop, calls=%fused_computation.20 | loop fusion | flops 22019328 | bytes 18888704 | tf_op jit(solution)/shard_map/convert_element_type | solution.py:123
  94.1 0.8 slice_bitcast_fusion.1
  94.9 1.4 copy-done.4
  96.3 1.0 fusion.30
  97.3 1.0 fusion.35
  99.8 1.0 pad_maximum_fusion
  101.1 0.7 gather_fusion.12
  102.2 0.7 gather_fusion.13
  102.9 13.5 %reduce-scatter.3.cloned.1.call-done = f32[1,2,4,2,6,130]{5,4,3,2,1,0:T(8,128)} async-done(((f32[4,2,4,2,6,130]{5,4,3,2,1,0:T(8,128)}), f32[1,2,4,2,6,130]{5,4,3,2,1,0:T(8,128)}) %reduce-scatter.3.cloned.1.call-update) | async-done | bytes 49936 | tf_op jit(solution)/shard_map/reduce_scatter | solution.py:142
  116.4 0.9 fusion.71
  117.7 1.1 fusion.83
  118.8 1.2 fusion.41
  121.5 1.4 constant_dynamic-slice_fusion
  122.9 65.0 %all-gather.6.cloned.1.call-done = bf16[256,4,1536]{2,1,0:T(4,128)(2,1)} async-done(((bf16[2,4,1536]{2,1,0:T(4,128)(2,1)}), bf16[256,4,1536]{2,1,0:T(4,128)(2,1)}) %all-gather.6.cloned.1.call-update) | async-done | bytes 3145744 | tf_op jit(solution)/shard_map/all_gather | solution.py:186
  187.9 4.4 %copy.99 = bf16[32,8,4,1536]{3,1,2,0:T(8,128)(2,1)} copy(bf16[32,8,4,1536]{3,2,1,0:T(4,128)(2,1)} %bitcast.180) | data formatting | bytes 6291456 | tf_op jit(solution)/shard_map/reshape | solution.py:188
  192.3 3.4 %gather_fusion.14 = bf16[8,8,4,1536]{3,1,2,0:T(8,128)(2,1)} fusion(bf16[32,8,4,1536]{3,1,2,0:T(8,128)(2,1)} %copy.99, s32[1024]{0:T(1024)S(1)} %pad_clamp_fusion), kind=kCustom, calls=%fused_computation.14 | custom fusion | bytes 1572896 | tf_op jit(solution)/shard_map/gather | solution.py:188
  195.7 38.6 %all-gather.8.cloned.1.call-done = bf16[1536,1536]{1,0:T(8,128)(2,1)} async-done(((bf16[48,1536]{1,0:T(8,128)(2,1)}), bf16[1536,1536]{1,0:T(8,128)(2,1)}) %all-gather.8.cloned.1.call-update) | async-done | bytes 4718608 | tf_op jit(solution)/shard_map/all_gather | solution.py:192
  234.3 4.1 %multiply_reduce_fusion = (f32[64,4]{0,1:T(4,128)S(1)}, f32[64,4,1536]{2,0,1:T(8,128)S(1)}) fusion(bf16[1536,1536]{1,0:T(8,128)(2,1)} %all-gather.8.cloned.1.call-done, bf16[8,8,4,1536]{3,1,2,0:T(8,128)(2,1)} %gather_fusion.14, bf16[64,4,1536]{2,1,0:T(4,128)(2,1)S(1)} %constant_dynamic-slice_fusion), kind=kOutput, calls=%fused_computation.47 | convolution fusion | flops 1209532160 | bytes 7865344 | tf_op jit(solution)/shard_map/dot_general | solution.py:193
  239.1 3.2 convolution_convert_fusion
  242.3 1.7 copy.101
  244.0 1.1 reshape.452
  245.1 77.4 %reduce-scatter.5.cloned.1.call-done = bf16[1,16,768]{2,1,0:T(8,128)(2,1)} async-done(((bf16[32,16,768]{2,1,0:T(8,128)(2,1)}), bf16[1,16,768]{2,1,0:T(8,128)(2,1)}) %reduce-scatter.5.cloned.1.call-update) | async-done | bytes 24592 | tf_op jit(solution)/shard_map/reduce_scatter | solution.py:203
  322.5 0.8 reshape.455
  323.3 0.6 fusion.73
  (87 shorter events, 6.1 us)
Async XLA Ops:
  6.5 232.5 %copy-start = (bf16[280,1536]{1,0:T(8,128)(2,1)S(1)}, bf16[280,1536]{1,0:T(8,128)(2,1)}, u32[]{:S(2)}) copy-start(bf16[280,1536]{1,0:T(8,128)(2,1)} %param.18) | copy-start | bytes 2580484
  6.5 9.2 %copy-start.5 = (s32[32]{0:T(128)S(1)}, s32[32]{0:T(128)}, u32[]{:S(2)}) copy-start(s32[32]{0:T(128)} %param.23) | copy-start | bytes 388
  6.5 72.3 %all-gather.4.cloned.1.call-start = ((), (), s32[]{:S(2)}) async-start(), calls=%async_computation.2 | async-start | bytes 3170304 | tf_op jit(solution)/shard_map/all_gather | solution.py:80
  8.0 108.4 %reduce-scatter.3.cloned.1.call-start = ((), (), s32[]{:S(2)}) async-start(), calls=%async_computation.3 | async-start | bytes 655360 | tf_op jit(solution)/shard_map/reduce_scatter | solution.py:142
  11.7 69.4 %copy-start.3 = (f32[2048]{0:T(1024)S(1)}, f32[2048]{0:T(1024)}, u32[]{:S(2)}) copy-start(f32[2048]{0:T(1024)} %param.14) | copy-start | bytes 24580
  78.8 6.4 %copy-start.1 = (bf16[2,4096,256]{2,1,0:T(8,128)(2,1)S(1)}, bf16[2,4096,256]{2,1,0:T(8,128)(2,1)}, u32[]{:S(2)}) copy-start(bf16[2,4096,256]{2,1,0:T(8,128)(2,1)} %param.19) | copy-start | bytes 12582916
  94.1 2.2 copy-start.4
  100.8 87.1 %all-gather.6.cloned.1.call-start = ((), (), s32[]{:S(2)}) async-start(), calls=%async_computation.4 | async-start | bytes 3170304 | tf_op jit(solution)/shard_map/all_gather | solution.py:186
  120.6 113.7 %all-gather.8.cloned.1.call-start = ((), (), s32[]{:S(2)}) async-start(), calls=%async_computation.5 | async-start | bytes 4866048 | tf_op jit(solution)/shard_map/all_gather | solution.py:192
  121.2 201.3 %reduce-scatter.5.cloned.1.call-start = ((), (), s32[]{:S(2)}) async-start(), calls=%async_computation.6 | async-start | bytes 811008 | tf_op jit(solution)/shard_map/reduce_scatter | solution.py:203
  234.3 4.2 %copy-start.2 = (bf16[1536,280]{0,1:T(8,128)(2,1)S(1)}, bf16[1536,280]{0,1:T(8,128)(2,1)}, u32[]{:S(2)}) copy-start(bf16[1536,280]{0,1:T(8,128)(2,1)} %param.16) | copy-start | bytes 2580484
Sparse Core Ops, SparseCore 0:
  10.4 68.3 all-gather.3
  100.9 15.4 reduce-scatter.2
  120.8 67.1 all-gather.5
  190.0 44.2 all-gather.7
  245.2 77.2 reduce-scatter.4

commit v4 on v3

--- a/solution.py
+++ b/solution.py
@@ -77,7 +77,20 @@
         .set(jnp.arange(requests, dtype=jnp.int32))
     )
 
-    x_all = lax.all_gather(jnp.swapaxes(step_inputs, 0, 1), ALL, axis=0, tiled=True)
+    column_rows = out_weight.shape[0]
+    share = column_rows // n_req
+    w_share = lax.dynamic_slice_in_dim(out_weight, req_index * share, share, 0)
+    carry = jnp.concatenate(
+        [jnp.swapaxes(step_inputs, 0, 1).reshape(rows_dev * steps, width), w_share], axis=0
+    )
+    carry = lax.all_gather(carry, ALL, axis=0, tiled=False)
+    x_all = carry[:, : rows_dev * steps].reshape(requests * beams, steps, width)
+    full_out = (
+        carry[:, rows_dev * steps :]
+        .reshape(n_req, tp_count, share, width)
+        .transpose(1, 0, 2, 3)
+        .reshape(tp_count * column_rows, width)
+    )
     x_req = lax.dynamic_slice_in_dim(x_all, inverse[r] * beams, beams, 0)
     x_group = lax.dynamic_slice_in_dim(x_all, req_index * group_rows, group_rows, 0)
 
@@ -189,7 +202,6 @@
         group_rows, steps, attn_width
     )
 
-    full_out = lax.all_gather(out_weight, TP, axis=0, tiled=True)
     middle = x_group.astype(jnp.float32) + jnp.dot(
         att_group, full_out, preferred_element_type=jnp.float32
     )

time: 331 us -> 306 us (0.924)
  waiting for transfers between devices: 253 us -> 202 us
  local copies, waits for them, and re-layouts: 31.6 us -> 55.9 us
    all_gather x2 -> x1, waiting for transfers between devices: 96.4 us -> 60.8 us  [per_device(): carry = lax.all_gather(carry, ALL, axis=0, tiled=False)]
    reshape x0 -> x4, local copies, waits for them, and re-layouts: none -> 17.6 us  [the longest x2 11.4 us: per_device(): full_out = carry[:, rows_dev * steps:].reshape(n_req, tp_count, share, wi...]
    all_gather x1, waiting for transfers between devices: 65 us -> 51.6 us  [per_device(): att_all = lax.all_gather(attention, ALL, axis=0, tiled=True)]
    slice x0 -> x3, local copies, waits for them, and re-layouts: none -> 6.51 us  [the longest x1 3.72 us: per_device(): x_all = carry[:, :rows_dev * steps].reshape(requests * beams, steps, width)]
  transfers between devices with their start and end apart: 5 -> 4, of which waited for: 5 -> 4; matrix products, arithmetic and copies ran while one was open for 7% -> 9% of each run, Pallas kernels for 0% -> 0%
where the time goes in v4:
time: 306 us; the launch traced here: 305 us
  waiting for transfers between devices  202 us (66%)
  local copies, waits for them, and re-layouts  55.9 us (18%)
  matrix products  17.2 us (6%)
  other arithmetic  15.4 us (5%)
  between operations  14.2 us (5%)
    reduce_scatter x1, waiting for transfers between devices, per_device(): lowered = lax.psum_scatter(partial, TP, scatter_dimension=0, tiled=True)  75.5 us
    all_gather x1, waiting for transfers between devices, per_device(): carry = lax.all_gather(carry, ALL, axis=0, tiled=False)  60.8 us
    all_gather x1, waiting for transfers between devices, per_device(): att_all = lax.all_gather(attention, ALL, axis=0, tiled=True)  51.6 us
    reduce_scatter x1, waiting for transfers between devices, per_device(): packed = lax.psum_scatter(packed, 'tpi', scatter_dimension=0, tiled=True)[0]  13.6 us
    reshape x2, local copies, waits for them, and re-layouts, per_device(): full_out = carry[:, rows_dev * steps:].reshape(n_req, tp_count, share, wi...  11.4 us
  transfers between devices with their start and end apart: 4, of which 4 were waited for; matrix products, arithmetic and copies ran while one was open for 9% of the time, Pallas kernels for 0%

profile of v4, /device:TPU:0, one launch (start us, length us, event | category | flops | bytes accessed | tf_op | source)
XLA Modules:
  0.0 304.6 jit_solution(18016615249455211079)
XLA Ops:
  6.5 0.8 copy.81
  7.4 0.9 constant_dynamic-slice_fusion.1
  9.0 0.9 dynamic-slice_reduce_fusion.4
  9.9 0.7 compare_select_fusion.6
  10.6 0.7 scatter_custom_fusion
  12.5 1.0 dynamic-slice_reduce_fusion
  13.5 0.6 gather_fusion.9
  14.8 0.7 gather_fusion.6
  16.1 0.6 gather_fusion.10
  16.8 0.6 gather_fusion.11
  17.8 0.6 gather_fusion
  19.1 0.6 gather_fusion.2
  21.4 0.7 gather_fusion.5
  22.5 60.8 %all-gather.7.cloned.1.call-done = bf16[128,20,1536]{2,1,0:T(8,128)(2,1)} async-done(((bf16[1,20,1536]{2,1,0:T(8,128)(2,1)}), bf16[128,20,1536]{2,1,0:T(8,128)(2,1)}) %all-gather.7.cloned.1.call-update) | async-done | bytes 7864336 | tf_op jit(solution)/shard_map/all_gather | solution.py:86
  83.3 3.7 %slice.136 = bf16[128,8,1536]{2,1,0:T(8,128)(2,1)} slice(bf16[128,20,1536]{2,1,0:T(8,128)(2,1)} %all-gather.7.cloned.1.call-done), slice={[0:128], [0:8], [0:1536]} | slice | bytes 6291456 | tf_op jit(solution)/shard_map/slice | solution.py:87
  87.1 6.1 %reshape.462 = bf16[256,4,1536]{2,1,0:T(4,128)(2,1)} reshape(bf16[128,8,1536]{2,1,0:T(8,128)(2,1)} %slice.136) | data formatting | bytes 6291456 | tf_op jit(solution)/shard_map/reshape | solution.py:87
  93.2 1.2 fusion.51
  94.4 1.1 fusion.52
  95.5 3.9 %fusion.13 = bf16[8,4,2048]{2,0,1:T(8,128)(2,1)S(1)} fusion(bf16[1536,2048]{1,0:T(8,128)(2,1)} %param.13, f32[2048]{0:T(1024)S(1)} %copy-done.3, bf16[8,4,1536]{2,1,0:T(4,128)(2,1)S(1)} %fusion.52), kind=kOutput, calls=%fused_computation.36 | convolution fusion | flops 201457664 | bytes 6529024 | tf_op jit(solution)/shard_map/dot_general | solution.py:99
  99.6 1.0 convolution_bitcast_fusion.1
  100.6 1.0 convolution_bitcast_fusion
  101.8 2.1 fusion.5
  103.9 4.6 %fusion.2 = (bf16[2,8,4,2,6,4096]{5,1,0,4,2,3:T(8,128)(2,1)S(1)}, f32[2,8,4,2,6]{1,0,4,2,3:T(2,128)S(1)}) fusion(f32[2,8,4,2,6]{1,0,4,2,3:T(2,128)S(1)} %fusion.5, pred[2,4096]{1,0:T(4,128)(4,1)S(1)} %iota_compare_fusion, f32[2,8,4,1,6,4096]{5,1,0,4,2,3:T(8,128)S(1)} %convolution_bitcast_fusion, f32[2,8,4,1,6,4096]{5,1,0,4,2,3:T(8,128)S(1)} %convolution_bitcast_fusion.1), kind=kLoop, calls=%fused_computation.20 | loop fusion | flops 22019328 | bytes 18888704 | tf_op jit(solution)/shard_map/convert_element_type | solution.py:136
  108.5 0.8 slice_bitcast_fusion.1
  109.3 1.4 copy-done.4
  110.7 1.0 fusion.25
  111.7 1.0 fusion.30
  114.2 0.9 pad_maximum_fusion
  115.4 0.7 gather_fusion.13
  116.2 0.7 gather_fusion.12
  117.4 13.6 %reduce-scatter.3.cloned.1.call-done = f32[1,2,4,2,6,130]{5,4,3,2,1,0:T(8,128)} async-done(((f32[4,2,4,2,6,130]{5,4,3,2,1,0:T(8,128)}), f32[1,2,4,2,6,130]{5,4,3,2,1,0:T(8,128)}) %reduce-scatter.3.cloned.1.call-update) | async-done | bytes 49936 | tf_op jit(solution)/shard_map/reduce_scatter | solution.py:155
  131.0 0.9 fusion.66
  132.2 1.1 fusion.78
  133.3 1.2 fusion.36
  135.4 2.8 slice-done
  138.1 3.2 %copy.171 = bf16[4,32,12,1536]{3,2,0,1:T(8,128)(2,1)} copy(bf16[4,32,12,1536]{3,2,1,0:T(8,128)(2,1)S(1)} %bitcast.179) | data formatting | bytes 9437184 | tf_op jit(solution)/shard_map/reshape | solution.py:90
  141.3 8.2 %reshape.615 = bf16[1536,1536,1]{1,0,2:T(8,128)(2,1)} reshape(bf16[32,4,12,1536]{3,2,1,0:T(8,128)(2,1)} %bitcast.180) | data formatting | bytes 9437184 | tf_op jit(solution)/shard_map/reshape | solution.py:92
  149.6 1.4 constant_dynamic-slice_fusion
  151.0 51.6 %all-gather.5.cloned.1.call-done = bf16[256,4,1536]{2,1,0:T(4,128)(2,1)} async-done(((bf16[2,4,1536]{2,1,0:T(4,128)(2,1)}), bf16[256,4,1536]{2,1,0:T(4,128)(2,1)}) %all-gather.5.cloned.1.call-update) | async-done | bytes 3145744 | tf_op jit(solution)/shard_map/all_gather | solution.py:199
  202.5 4.4 %copy.109 = bf16[32,8,4,1536]{3,1,2,0:T(8,128)(2,1)} copy(bf16[32,8,4,1536]{3,2,1,0:T(4,128)(2,1)} %bitcast.181) | data formatting | bytes 6291456 | tf_op jit(solution)/shard_map/reshape | solution.py:201
  207.0 3.4 %gather_fusion.14 = bf16[8,8,4,1536]{3,1,2,0:T(8,128)(2,1)} fusion(bf16[32,8,4,1536]{3,1,2,0:T(8,128)(2,1)} %copy.109, s32[1024]{0:T(1024)S(1)} %pad_clamp_fusion), kind=kCustom, calls=%fused_computation.14 | custom fusion | bytes 1572896 | tf_op jit(solution)/shard_map/gather | solution.py:201
  210.3 4.1 %multiply_reduce_fusion = (f32[64,4]{0,1:T(4,128)S(1)}, f32[64,4,1536]{2,0,1:T(8,128)S(1)}) fusion(bf16[1536,1536,1]{1,0,2:T(8,128)(2,1)} %reshape.615, bf16[8,8,4,1536]{3,1,2,0:T(8,128)(2,1)} %gather_fusion.14, bf16[64,4,1536]{2,1,0:T(4,128)(2,1)S(1)} %constant_dynamic-slice_fusion), kind=kOutput, calls=%fused_computation.46 | convolution fusion | flops 1209532160 | bytes 7865344 | tf_op jit(solution)/shard_map/dot_general | solution.py:205
  215.1 3.2 %convolution_convert_fusion = bf16[64,4,1536]{2,0,1:T(8,128)(2,1)} fusion(bf16[280,1536]{1,0:T(8,128)(2,1)S(1)} %copy-done, bf16[1536,280]{0,1:T(8,128)(2,1)} %param.17, f32[64,4,280]{2,0,1:T(8,128)S(1)} %fusion.41, f32[64,4,1536]{2,0,1:T(8,128)S(1)} %get-tuple-element.32, f32[64,4]{0,1:T(4,128)S(1)} %add_rsqrt_fusion.1), kind=kOutput, calls=%fused_computation.34 | convolution fusion | flops 442011648 | bytes 4367360 | tf_op jit(solution)/shard_map/dot_general | solution.py:212
  218.3 1.7 copy.112
  220.1 1.1 reshape.468
  221.2 75.5 %reduce-scatter.5.cloned.1.call-done = bf16[1,16,768]{2,1,0:T(8,128)(2,1)} async-done(((bf16[32,16,768]{2,1,0:T(8,128)(2,1)}), bf16[1,16,768]{2,1,0:T(8,128)(2,1)}) %reduce-scatter.5.cloned.1.call-update) | async-done | bytes 24592 | tf_op jit(solution)/shard_map/reduce_scatter | solution.py:215
  296.7 0.8 reshape.471
  297.4 0.6 fusion.68
  (93 shorter events, 10.0 us)
Async XLA Ops:
  6.5 208.6 %copy-start = (bf16[280,1536]{1,0:T(8,128)(2,1)S(1)}, bf16[280,1536]{1,0:T(8,128)(2,1)}, u32[]{:S(2)}) copy-start(bf16[280,1536]{1,0:T(8,128)(2,1)} %param.18) | copy-start | bytes 2580484
  6.5 76.8 %all-gather.7.cloned.1.call-start = ((), (), s32[]{:S(2)}) async-start(), calls=%async_computation.5 | async-start | bytes 9510912 | tf_op jit(solution)/shard_map/all_gather | solution.py:86
  9.0 122.0 %reduce-scatter.3.cloned.1.call-start = ((), (), s32[]{:S(2)}) async-start(), calls=%async_computation.2 | async-start | bytes 655360 | tf_op jit(solution)/shard_map/reduce_scatter | solution.py:155
  87.1 8.4 %copy-start.3 = (f32[2048]{0:T(1024)S(1)}, f32[2048]{0:T(1024)}, u32[]{:S(2)}) copy-start(f32[2048]{0:T(1024)} %param.14) | copy-start | bytes 24580
  93.2 6.4 %copy-start.1 = (bf16[2,4096,256]{2,1,0:T(8,128)(2,1)S(1)}, bf16[2,4096,256]{2,1,0:T(8,128)(2,1)}, u32[]{:S(2)}) copy-start(bf16[2,4096,256]{2,1,0:T(8,128)(2,1)} %param.19) | copy-start | bytes 12582916
  108.5 2.2 copy-start.4
  112.7 22.6 %copy-start.5 = (s32[32]{0:T(128)S(1)}, s32[32]{0:T(128)}, u32[]{:S(2)}) copy-start(s32[32]{0:T(128)} %param.23) | copy-start | bytes 388
  115.2 87.3 %all-gather.5.cloned.1.call-start = ((), (), s32[]{:S(2)}) async-start(), calls=%async_computation.3 | async-start | bytes 3170304 | tf_op jit(solution)/shard_map/all_gather | solution.py:199
  135.2 161.5 %reduce-scatter.5.cloned.1.call-start = ((), (), s32[]{:S(2)}) async-start(), calls=%async_computation.4 | async-start | bytes 811008 | tf_op jit(solution)/shard_map/reduce_scatter | solution.py:215
  135.4 2.8 slice-start
  210.3 4.2 %copy-start.2 = (bf16[1536,280]{0,1:T(8,128)(2,1)S(1)}, bf16[1536,280]{0,1:T(8,128)(2,1)}, u32[]{:S(2)}) copy-start(bf16[1536,280]{0,1:T(8,128)(2,1)} %param.16) | copy-start | bytes 2580484
Sparse Core Ops, SparseCore 0:
  10.4 72.8 all-gather.6
  115.3 15.5 reduce-scatter.2
  135.3 67.1 all-gather.4
  221.3 75.3 reduce-scatter.4

commit v5 on v4

--- a/solution.py
+++ b/solution.py
@@ -150,12 +150,7 @@
     peak = jnp.sum(jnp.where(chosen, peak, 0.0), axis=0)
     total = jnp.sum(jnp.where(chosen, total, 0.0), axis=0)
     output = jnp.sum(jnp.where(chosen[..., None], output, 0.0), axis=0)
-    packed = jnp.concatenate([output, peak[..., None], total[..., None]], axis=-1)
-    packed = packed.reshape(n_i, owned, steps, KV_HEADS, group, head_dim + 2)
-    packed = lax.psum_scatter(packed, "tpi", scatter_dimension=0, tiled=True)[0]
-    part_output = packed[..., :head_dim]
-    part_peak = packed[..., head_dim]
-    part_total = packed[..., head_dim + 1]
+    part_output, part_peak, part_total = output, peak, total
 
     anc = []
     for t in range(steps):
@@ -168,15 +163,12 @@
         for u in range(t + 1, steps):
             row[u] = jnp.arange(beams, dtype=jnp.int32)
         anc.append(jnp.stack(row, axis=0))
-    anc = jnp.stack(anc, axis=0)
-    anc_mine = lax.dynamic_slice_in_dim(anc, j * owned, owned, 2)
-    anc_mine = jnp.transpose(anc_mine, (2, 0, 1))
-    u_index = jnp.broadcast_to(jnp.arange(steps, dtype=jnp.int32), anc_mine.shape)
-    hist_keys = new_keys[anc_mine, u_index]
-    hist_values = new_values[anc_mine, u_index]
-    q_mine = lax.dynamic_slice_in_dim(qg, j * owned, owned, 0)
+    anc = jnp.transpose(jnp.stack(anc, axis=0), (2, 0, 1))
+    u_index = jnp.broadcast_to(jnp.arange(steps, dtype=jnp.int32), anc.shape)
+    hist_keys = new_keys[anc, u_index]
+    hist_values = new_values[anc, u_index]
     recent_scores = jnp.einsum(
-        "ctkgd,ctukd->ctkgu", q_mine, hist_keys, preferred_element_type=jnp.float32
+        "btkgd,btukd->btkgu", qg, hist_keys, preferred_element_type=jnp.float32
     ) * scale
     causal = (
         jnp.arange(steps, dtype=jnp.int32)[None, :] <= jnp.arange(steps, dtype=jnp.int32)[:, None]
@@ -187,20 +179,27 @@
     recent_weights = jnp.where(causal, jnp.exp(recent_scores - top[..., None]), 0.0)
     denominator = part_total * factor + jnp.sum(recent_weights, axis=-1)
     numerator = part_output * factor[..., None] + jnp.einsum(
-        "ctkgu,ctukd->ctkgd",
+        "btkgu,btukd->btkgd",
         recent_weights.astype(jnp.bfloat16),
         hist_values,
         preferred_element_type=jnp.float32,
     )
     attention = (
-        (numerator / denominator[..., None]).reshape(owned, steps, attn_width).astype(jnp.bfloat16)
-    )
-
-    att_all = lax.all_gather(attention, ALL, axis=0, tiled=True)
+        (numerator / denominator[..., None]).reshape(beams, steps, attn_width).astype(jnp.bfloat16)
+    )
+
+    att_all = lax.all_gather(attention, ALL, axis=0, tiled=False)
+    root_all = jnp.broadcast_to(jnp.arange(beams, dtype=jnp.int32), (requests, beams))
+    root_steps = []
+    for t in range(steps):
+        root_all = jnp.take_along_axis(root_all, parents[t], axis=1)
+        root_steps.append(root_all)
+    root_steps = jnp.stack(root_steps, axis=2)
     my_requests = lax.dynamic_slice_in_dim(slot_request, req_index * group_requests, group_requests)
-    att_group = att_all.reshape(requests, beams, steps, attn_width)[my_requests].reshape(
-        group_rows, steps, attn_width
-    )
+    source = my_requests[:, None, None] * n_i + root_steps[my_requests] // owned
+    b_index = jnp.broadcast_to(jnp.arange(beams, dtype=jnp.int32)[None, :, None], source.shape)
+    t_index = jnp.broadcast_to(jnp.arange(steps, dtype=jnp.int32)[None, None, :], source.shape)
+    att_group = att_all[source, b_index, t_index].reshape(group_rows, steps, attn_width)
 
     middle = x_group.astype(jnp.float32) + jnp.dot(
         att_group, full_out, preferred_element_type=jnp.float32

time: 306 us -> 318 us (1.039)
  local copies, waits for them, and re-layouts: 55.9 us -> 78.9 us
  waiting for transfers between devices: 202 us -> 184 us
  matrix products: 17.2 us -> 22.1 us
    reduce_scatter x1 -> x0, waiting for transfers between devices: 13.6 us -> none  [per_device(): packed = lax.psum_scatter(packed, 'tpi', scatter_dimension=0, tiled=True)[0]]
    all_gather x0 -> x1, local copies, waits for them, and re-layouts: none -> 13.1 us  [per_device(): att_all = lax.all_gather(attention, ALL, axis=0, tiled=False)]
    gather x3 -> x24, local copies, waits for them, and re-layouts: 4.66 us -> 13.9 us  [the longest x20 7.54 us: per_device(): root_all = jnp.take_along_axis(root_all, parents[t], axis=1)]
    all_gather x1, waiting for transfers between devices: 51.6 us -> 45.3 us  [per_device(): att_all = lax.all_gather(attention, ALL, axis=0, tiled=False)]
    reduce_sum x1 -> x2, other arithmetic: 0.14 us -> 6.06 us  [the longest x1 5.92 us: per_device(): total = jnp.sum(weights, axis=-1)]
    dot_general x2, matrix products: 2.03 us -> 7.35 us  [per_device(): jnp.einsum('btgd,cpd->cbtgp', qg[:, :, k], keys_k, preferred_element_type...]
    convert_element_type x1 -> x0, other arithmetic: 4.63 us -> none  [per_device(): weights = weights.astype(jnp.bfloat16)]
    reduce_max x1, other arithmetic: 2.13 us -> 6.31 us  [per_device(): peak = jnp.max(scores, axis=-1)]
  transfers between devices with their start and end apart: 4 -> 3, of which waited for: 4 -> 3; matrix products, arithmetic and copies ran while one was open for 9% -> 11% of each run, Pallas kernels for 0% -> 0%
where the time goes in v5:
time: 318 us; the launch traced here: 317 us
  waiting for transfers between devices  184 us (58%)
  local copies, waits for them, and re-layouts  78.9 us (25%)
  matrix products  22.1 us (7%)
  other arithmetic  18.1 us (6%)
  between operations  14.3 us (4%)
    reduce_scatter x1, waiting for transfers between devices, per_device(): lowered = lax.psum_scatter(partial, TP, scatter_dimension=0, tiled=True)  77.6 us
    all_gather x1, waiting for transfers between devices, per_device(): carry = lax.all_gather(carry, ALL, axis=0, tiled=False)  60.9 us
    all_gather x1, waiting for transfers between devices, per_device(): att_all = lax.all_gather(attention, ALL, axis=0, tiled=False)  45.3 us
    all_gather x1, local copies, waits for them, and re-layouts, per_device(): att_all = lax.all_gather(attention, ALL, axis=0, tiled=False)  13.1 us
    reshape x2, local copies, waits for them, and re-layouts, per_device(): full_out = carry[:, rows_dev * steps:].reshape(n_req, tp_count, share, wi...  11.4 us
    gather x20, local copies, waits for them, and re-layouts, per_device(): root_all = jnp.take_along_axis(root_all, parents[t], axis=1)  7.54 us
    dot_general x2, matrix products, per_device(): jnp.einsum('btgd,cpd->cbtgp', qg[:, :, k], keys_k, preferred_element_type...  7.35 us
  transfers between devices with their start and end apart: 3, of which 3 were waited for; matrix products, arithmetic and copies ran while one was open for 11% of the time, Pallas kernels for 0%

profile of v5, /device:TPU:0, one launch (start us, length us, event | category | flops | bytes accessed | tf_op | source)
XLA Modules:
  0.0 317.5 jit_solution(14603928869895128765)
XLA Ops:
  6.5 0.8 copy.99
  7.4 0.9 constant_dynamic-slice_fusion.1
  9.0 0.9 dynamic-slice_reduce_fusion.4
  9.9 0.7 compare_select_fusion.11
  10.6 0.7 scatter_custom_fusion
  12.5 1.0 dynamic-slice_reduce_fusion
  13.5 0.6 gather_fusion.9
  16.1 0.6 gather_fusion.10
  16.8 0.6 gather_fusion.11
  18.1 0.7 gather_fusion.1
  21.0 0.7 gather_fusion.5
  22.4 60.9 %all-gather.7.cloned.1.call-done = bf16[128,20,1536]{2,1,0:T(8,128)(2,1)} async-done(((bf16[1,20,1536]{2,1,0:T(8,128)(2,1)}), bf16[128,20,1536]{2,1,0:T(8,128)(2,1)}) %all-gather.7.cloned.1.call-update) | async-done | bytes 7864336 | tf_op jit(solution)/shard_map/all_gather | solution.py:86
  83.3 3.8 %slice.151 = bf16[128,8,1536]{2,1,0:T(8,128)(2,1)} slice(bf16[128,20,1536]{2,1,0:T(8,128)(2,1)} %all-gather.7.cloned.1.call-done), slice={[0:128], [0:8], [0:1536]} | slice | bytes 6291456 | tf_op jit(solution)/shard_map/slice | solution.py:87
  87.1 6.1 %reshape.551 = bf16[256,4,1536]{2,1,0:T(4,128)(2,1)} reshape(bf16[128,8,1536]{2,1,0:T(8,128)(2,1)} %slice.151) | data formatting | bytes 6291456 | tf_op jit(solution)/shard_map/reshape | solution.py:87
  93.3 1.2 fusion.50
  94.4 1.1 fusion.51
  95.6 3.9 %fusion.13 = bf16[8,4,2048]{2,0,1:T(8,128)(2,1)S(1)} fusion(bf16[1536,2048]{1,0:T(8,128)(2,1)} %param.15, f32[2048]{0:T(1024)S(1)} %copy-done.5, bf16[8,4,1536]{2,1,0:T(4,128)(2,1)S(1)} %fusion.51), kind=kOutput, calls=%fused_computation.41 | convolution fusion | flops 201457664 | bytes 6529024 | tf_op jit(solution)/shard_map/dot_general | solution.py:99
  99.8 3.7 %convolution_bitcast_fusion.1 = f32[2,8,4,1,6,4096]{5,1,0,4,2,3:T(8,128)} fusion(bf16[2,4096,256]{2,1,0:T(8,128)(2,1)S(1)} %copy-done.2, bf16[8,4,2,6,64]{4,0,3,2,1:T(8,128)(2,1)S(1)} %bitcast.245, bf16[8,4,2,6,64]{4,0,3,2,1:T(8,128)(2,1)S(1)} %bitcast.242), kind=kOutput, calls=%fused_computation.30 | convolution fusion | flops 402751488 | bytes 8585216 | tf_op jit(solution)/shard_map/btgd,cpd->cbtgp/dot_general | solution.py:124
  103.5 3.7 %convolution_bitcast_fusion = f32[2,8,4,1,6,4096]{5,1,0,4,2,3:T(8,128)} fusion(bf16[2,4096,256]{2,1,0:T(8,128)(2,1)S(1)} %copy-done.2, bf16[8,4,2,6,64]{4,0,3,2,1:T(8,128)(2,1)S(1)} %bitcast.246, bf16[8,4,2,6,64]{4,0,3,2,1:T(8,128)(2,1)S(1)} %bitcast.243), kind=kOutput, calls=%fused_computation.29 | convolution fusion | flops 402751488 | bytes 8585216 | tf_op jit(solution)/shard_map/btgd,cpd->cbtgp/dot_general | solution.py:124
  107.2 0.9 gather_fusion.13
  108.3 0.9 gather_fusion.12
  109.6 6.3 %fusion.5 = f32[2,8,4,2,6]{1,0,4,2,3:T(2,128)S(1)} fusion(f32[2,8,4,1,6,4096]{5,1,0,4,2,3:T(8,128)} %convolution_bitcast_fusion, f32[2,8,4,1,6,4096]{5,1,0,4,2,3:T(8,128)} %convolution_bitcast_fusion.1, pred[2,4096]{1,0:T(4,128)(4,1)S(1)} %iota_compare_fusion), kind=kLoop, calls=%fused_computation.31 | loop fusion | flops 12582144 | bytes 12594176 | tf_op jit(solution)/shard_map/reduce_max | solution.py:133
  115.9 0.6 slice-done
  116.5 1.3 slice-done.1
  117.8 5.9 %fusion.1 = (f32[2,8,4,2,6]{1,0,4,2,3:T(2,128)S(1)}, bf16[2,8,4,2,6,4096]{5,1,0,4,2,3:T(8,128)(2,1)}) fusion(f32[2,8,4,2,6]{1,0,4,2,3:T(2,128)S(1)} %fusion.5, pred[2,4096]{1,0:T(4,128)(4,1)S(1)} %iota_compare_fusion, f32[2,8,4,1,6,4096]{5,1,0,4,2,3:T(8,128)S(1)} %copy-done.1, f32[2,8,4,1,6,4096]{5,1,0,4,2,3:T(8,128)S(1)} %bitcast.238), kind=kLoop, calls=%fused_computation.24 | loop fusion | flops 22019328 | bytes 18888704 | tf_op jit(solution)/shard_map/reduce_sum | solution.py:135
  124.6 3.4 %slice_bitcast_fusion.1 = (bf16[2,8,4,6,4096]{4,1,0,3,2:T(8,128)(2,1)S(1)}, bf16[2,8,4,6,4096]{4,1,0,3,2:T(8,128)(2,1)S(1)}) fusion(bf16[2,8,4,2,6,4096]{5,1,0,4,2,3:T(8,128)(2,1)} %get-tuple-element.15), kind=kLoop, calls=%fused_computation.33 | loop fusion | bytes 12582912 | tf_op jit(solution)/shard_map/squeeze | solution.py:141
  128.7 1.0 fusion.27
  129.6 1.0 fusion.32
  131.2 0.7 copy.153
  132.7 1.9 gather_fusion.16
  134.8 1.4 gather_fusion.17
  136.6 1.4 gather_fusion.18
  138.2 1.4 gather_fusion.19
  140.9 2.8 slice-done.2
  143.7 3.1 copy.197
  146.9 8.2 %reshape.777 = bf16[1536,1536,1]{1,0,2:T(8,128)(2,1)} reshape(bf16[32,4,12,1536]{3,2,1,0:T(8,128)(2,1)} %bitcast.240) | data formatting | bytes 9437184 | tf_op jit(solution)/shard_map/reshape | solution.py:92
  155.1 2.3 constant_dynamic-slice_fusion
  157.4 45.3 %all-gather.5.cloned.1.call-done = bf16[128,8,4,1536]{3,1,2,0:T(8,128)(2,1)} async-done(((bf16[1,8,4,1536]{3,1,2,0:T(8,128)(2,1)}), bf16[128,8,4,1536]{3,1,2,0:T(8,128)(2,1)}) %all-gather.5.cloned.1.call-update) | async-done | bytes 12582928 | tf_op jit(solution)/shard_map/all_gather | solution.py:191
  202.7 13.1 %copy.136 = bf16[128,8,4,1536]{3,2,1,0:T(4,128)(2,1)} copy(bf16[128,8,4,1536]{3,1,2,0:T(8,128)(2,1)} %all-gather.5.cloned.1.call-done) | data formatting | bytes 25165824 | tf_op jit(solution)/shard_map/all_gather | solution.py:191
  215.9 4.0 %gather_fusion.15 = bf16[256,1536]{1,0:T(8,128)(2,1)S(1)} fusion(bf16[128,8,4,1536]{3,2,1,0:T(4,128)(2,1)} %copy.136, s32[256]{0:T(256)S(1)} %reshape.703), kind=kCustom, calls=%fused_computation.19 | custom fusion | bytes 1575936 | tf_op jit(solution)/shard_map/gather | solution.py:202
  219.9 1.1 reshape.553
  220.9 4.3 %multiply_reduce_fusion = (f32[64,4]{0,1:T(4,128)S(1)}, f32[64,4,1536]{2,0,1:T(8,128)S(1)}) fusion(bf16[1536,1536,1]{1,0,2:T(8,128)(2,1)} %reshape.777, bf16[64,4,1536]{2,1,0:T(4,128)(2,1)} %reshape.553, bf16[64,4,1536]{2,1,0:T(4,128)(2,1)} %constant_dynamic-slice_fusion), kind=kOutput, calls=%fused_computation.51 | convolution fusion | flops 1209532160 | bytes 7865344 | tf_op jit(solution)/shard_map/dot_general | solution.py:204
  225.9 3.2 %convolution_convert_fusion = bf16[64,4,1536]{2,0,1:T(8,128)(2,1)} fusion(bf16[280,1536]{1,0:T(8,128)(2,1)S(1)} %copy-done, bf16[1536,280]{0,1:T(8,128)(2,1)} %param.19, f32[64,4,280]{2,0,1:T(8,128)S(1)} %fusion.41, f32[64,4,1536]{2,0,1:T(8,128)S(1)} %get-tuple-element.40, f32[64,4]{0,1:T(4,128)S(1)} %add_rsqrt_fusion.1), kind=kOutput, calls=%fused_computation.39 | convolution fusion | flops 442011648 | bytes 4367360 | tf_op jit(solution)/shard_map/dot_general | solution.py:211
  229.1 1.7 copy.139
  230.9 1.1 reshape.556
  232.0 77.6 %reduce-scatter.2.cloned.1.call-done = bf16[1,16,768]{2,1,0:T(8,128)(2,1)} async-done(((bf16[32,16,768]{2,1,0:T(8,128)(2,1)}), bf16[1,16,768]{2,1,0:T(8,128)(2,1)}) %reduce-scatter.2.cloned.1.call-update) | async-done | bytes 24592 | tf_op jit(solution)/shard_map/reduce_scatter | solution.py:214
  309.5 0.8 reshape.562
  310.3 0.6 fusion.71
  (129 shorter events, 13.1 us)
Async XLA Ops:
  6.5 219.4 %copy-start = (bf16[280,1536]{1,0:T(8,128)(2,1)S(1)}, bf16[280,1536]{1,0:T(8,128)(2,1)}, u32[]{:S(2)}) copy-start(bf16[280,1536]{1,0:T(8,128)(2,1)} %param.20) | copy-start | bytes 2580484
  6.5 76.8 %all-gather.7.cloned.1.call-start = ((), (), s32[]{:S(2)}) async-start(), calls=%async_computation.3 | async-start | bytes 9510912 | tf_op jit(solution)/shard_map/all_gather | solution.py:86
  9.0 193.8 %all-gather.5.cloned.1.call-start = ((), (), s32[]{:S(2)}) async-start(), calls=%async_computation.1 | async-start | bytes 12681216 | tf_op jit(solution)/shard_map/all_gather | solution.py:191
  87.1 8.5 %copy-start.5 = (f32[2048]{0:T(1024)S(1)}, f32[2048]{0:T(1024)}, u32[]{:S(2)}) copy-start(f32[2048]{0:T(1024)} %param.16) | copy-start | bytes 24580
  93.3 6.5 %copy-start.2 = (bf16[2,4096,256]{2,1,0:T(8,128)(2,1)S(1)}, bf16[2,4096,256]{2,1,0:T(8,128)(2,1)}, u32[]{:S(2)}) copy-start(bf16[2,4096,256]{2,1,0:T(8,128)(2,1)} %param.21) | copy-start | bytes 12582916
  109.4 7.1 %slice-start = ((s8[6291456]{0:T(1024)(128)(4,1)}), s8[2097152]{0:T(1024)(128)(4,1)S(1)}, s32[]{:S(2)}) async-start(s8[6291456]{0:T(1024)(128)(4,1)} %bitcast.237), calls=%async_computation.4 | async-start | bytes 4194304
  109.6 8.2 %slice-start.1 = ((s8[6291456]{0:T(1024)(128)(4,1)}), s8[4194304]{0:T(1024)(128)(4,1)S(1)}, s32[]{:S(2)}) async-start(s8[6291456]{0:T(1024)(128)(4,1)} %bitcast.237), calls=%async_computation.5 | async-start | bytes 8388608
  109.6 8.2 %copy-start.1 = (f32[2,8,4,1,6,4096]{5,1,0,4,2,3:T(8,128)S(1)}, f32[2,8,4,1,6,4096]{5,1,0,4,2,3:T(8,128)}, u32[]{:S(2)}) copy-start(f32[2,8,4,1,6,4096]{5,1,0,4,2,3:T(8,128)} %convolution_bitcast_fusion) | copy-start | bytes 18874372
  124.6 4.0 %copy-start.7 = (bf16[2,4096,256]{2,1,0:T(8,128)(2,1)S(1)}, bf16[2,4096,256]{2,1,0:T(8,128)(2,1)}, u32[]{:S(2)}) copy-start(bf16[2,4096,256]{2,1,0:T(8,128)(2,1)} %param.22) | copy-start | bytes 12582916
  129.6 2.5 copy-start.4
  131.9 177.6 %reduce-scatter.2.cloned.1.call-start = ((), (), s32[]{:S(2)}) async-start(), calls=%async_computation.2 | async-start | bytes 811008 | tf_op jit(solution)/shard_map/reduce_scatter | solution.py:214
  138.2 1.7 copy-start.6
  140.9 2.8 slice-start.2
  220.9 4.4 %copy-start.3 = (bf16[1536,280]{0,1:T(8,128)(2,1)S(1)}, bf16[1536,280]{0,1:T(8,128)(2,1)}, u32[]{:S(2)}) copy-start(bf16[1536,280]{0,1:T(8,128)(2,1)} %param.18) | copy-start | bytes 2580484
Sparse Core Ops, SparseCore 0:
  10.4 72.8 all-gather.6
  132.0 70.6 all-gather.4
  232.1 77.4 reduce-scatter.1

commit v6 on v4

--- a/solution.py
+++ b/solution.py
@@ -210,9 +210,11 @@
     upward = jnp.dot(mixed_in, up_weight, preferred_element_type=jnp.float32)
     hidden = (jax.nn.silu(gate) * upward).astype(jnp.bfloat16)
     partial = jnp.dot(hidden, down_weight, preferred_element_type=jnp.float32).astype(jnp.bfloat16)
-    chunk = rows_dev * steps * width
-    partial = partial.reshape(tp_count, 16, chunk // 16)
-    lowered = lax.psum_scatter(partial, TP, scatter_dimension=0, tiled=True)
+    partial = partial.reshape(n_o, n_i, rows_dev * steps, width)
+    partial = jnp.swapaxes(partial, 0, 1).reshape(n_i, n_o * rows_dev * steps, width)
+    partial = lax.psum_scatter(partial, "tpi", scatter_dimension=0, tiled=True)
+    partial = partial.reshape(n_o, 16, rows_dev * steps * width // 16)
+    lowered = lax.psum_scatter(partial, "tpo", scatter_dimension=0, tiled=True)
     lowered = lowered.reshape(rows_dev, steps, width).astype(jnp.float32)
     middle_mine = lax.dynamic_slice_in_dim(middle, tp_index * rows_dev, rows_dev, 0)
     result = (middle_mine + lowered).astype(jnp.bfloat16)

time: 306 us -> 322 us (1.052)
  waiting for transfers between devices: 202 us -> 216 us
    reduce_scatter x1 -> x2, waiting for transfers between devices: 75.5 us -> 90.1 us  [the longest x1 73.3 us: per_device(): lowered = lax.psum_scatter(partial, 'tpo', scatter_dimension=0, tiled=True)]
  transfers between devices with their start and end apart: 4 -> 5, of which waited for: 4 -> 5; matrix products, arithmetic and copies ran while one was open for 9% -> 9% of each run, Pallas kernels for 0% -> 0%
where the time goes in v6:
time: 322 us; the launch traced here: 321 us
  waiting for transfers between devices  216 us (67%)
  local copies, waits for them, and re-layouts  56.5 us (18%)
  matrix products  17.2 us (5%)
  other arithmetic  16.4 us (5%)
  between operations  14.2 us (4%)
    reduce_scatter x1, waiting for transfers between devices, per_device(): lowered = lax.psum_scatter(partial, 'tpo', scatter_dimension=0, tiled=True)  73.3 us
    all_gather x1, waiting for transfers between devices, per_device(): carry = lax.all_gather(carry, ALL, axis=0, tiled=False)  60.8 us
    all_gather x1, waiting for transfers between devices, per_device(): att_all = lax.all_gather(attention, ALL, axis=0, tiled=True)  51.6 us
    reduce_scatter x1, waiting for transfers between devices, per_device(): partial = lax.psum_scatter(partial, 'tpi', scatter_dimension=0, tiled=True)  16.8 us
    reduce_scatter x1, waiting for transfers between devices, per_device(): packed = lax.psum_scatter(packed, 'tpi', scatter_dimension=0, tiled=True)[0]  13.6 us
    reshape x2, local copies, waits for them, and re-layouts, per_device(): full_out = carry[:, rows_dev * steps:].reshape(n_req, tp_count, share, wi...  11.4 us
  transfers between devices with their start and end apart: 5, of which 5 were waited for; matrix products, arithmetic and copies ran while one was open for 9% of the time, Pallas kernels for 0%

profile of v6, /device:TPU:0, one launch (start us, length us, event | category | flops | bytes accessed | tf_op | source)
XLA Modules:
  0.0 320.7 jit_solution(3180695503694674593)
XLA Ops:
  6.5 0.8 copy.83
  7.4 0.9 constant_dynamic-slice_fusion.1
  9.0 0.9 dynamic-slice_reduce_fusion.4
  9.9 0.7 compare_select_fusion.6
  10.6 0.7 scatter_custom_fusion
  12.5 1.0 dynamic-slice_reduce_fusion
  13.5 0.6 gather_fusion.9
  14.8 0.7 gather_fusion.6
  16.1 0.6 gather_fusion.10
  17.8 0.6 gather_fusion
  21.4 0.7 gather_fusion.5
  22.5 60.8 %all-gather.7.cloned.1.call-done = bf16[128,20,1536]{2,1,0:T(8,128)(2,1)} async-done(((bf16[1,20,1536]{2,1,0:T(8,128)(2,1)}), bf16[128,20,1536]{2,1,0:T(8,128)(2,1)}) %all-gather.7.cloned.1.call-update) | async-done | bytes 7864336 | tf_op jit(solution)/shard_map/all_gather | solution.py:86
  83.3 3.7 %slice.136 = bf16[128,8,1536]{2,1,0:T(8,128)(2,1)} slice(bf16[128,20,1536]{2,1,0:T(8,128)(2,1)} %all-gather.7.cloned.1.call-done), slice={[0:128], [0:8], [0:1536]} | slice | bytes 6291456 | tf_op jit(solution)/shard_map/slice | solution.py:87
  87.1 6.1 %reshape.468 = bf16[256,4,1536]{2,1,0:T(4,128)(2,1)} reshape(bf16[128,8,1536]{2,1,0:T(8,128)(2,1)} %slice.136) | data formatting | bytes 6291456 | tf_op jit(solution)/shard_map/reshape | solution.py:87
  93.2 1.2 fusion.51
  94.4 1.1 fusion.52
  95.5 3.9 %fusion.13 = bf16[8,4,2048]{2,0,1:T(8,128)(2,1)S(1)} fusion(bf16[1536,2048]{1,0:T(8,128)(2,1)} %param.13, f32[2048]{0:T(1024)S(1)} %copy-done.4, bf16[8,4,1536]{2,1,0:T(4,128)(2,1)S(1)} %fusion.52), kind=kOutput, calls=%fused_computation.36 | convolution fusion | flops 201457664 | bytes 6529024 | tf_op jit(solution)/shard_map/dot_general | solution.py:99
  99.6 1.0 convolution_bitcast_fusion.1
  100.6 1.0 convolution_bitcast_fusion
  101.8 2.1 fusion.5
  103.9 4.6 %fusion.2 = (bf16[2,8,4,2,6,4096]{5,1,0,4,2,3:T(8,128)(2,1)S(1)}, f32[2,8,4,2,6]{1,0,4,2,3:T(2,128)S(1)}) fusion(f32[2,8,4,2,6]{1,0,4,2,3:T(2,128)S(1)} %fusion.5, pred[2,4096]{1,0:T(4,128)(4,1)S(1)} %iota_compare_fusion, f32[2,8,4,1,6,4096]{5,1,0,4,2,3:T(8,128)S(1)} %convolution_bitcast_fusion, f32[2,8,4,1,6,4096]{5,1,0,4,2,3:T(8,128)S(1)} %convolution_bitcast_fusion.1), kind=kLoop, calls=%fused_computation.20 | loop fusion | flops 22019328 | bytes 18888704 | tf_op jit(solution)/shard_map/convert_element_type | solution.py:136
  108.5 0.8 slice_bitcast_fusion.1
  109.3 1.4 copy-done.5
  110.7 1.0 fusion.25
  111.7 1.0 fusion.30
  114.2 0.9 pad_maximum_fusion
  115.4 0.7 gather_fusion.13
  116.2 0.7 gather_fusion.12
  117.4 13.6 %reduce-scatter.4.cloned.1.call-done = f32[1,2,4,2,6,130]{5,4,3,2,1,0:T(8,128)} async-done(((f32[4,2,4,2,6,130]{5,4,3,2,1,0:T(8,128)}), f32[1,2,4,2,6,130]{5,4,3,2,1,0:T(8,128)}) %reduce-scatter.4.cloned.1.call-update) | async-done | bytes 49936 | tf_op jit(solution)/shard_map/reduce_scatter | solution.py:155
  131.0 0.9 fusion.66
  132.2 1.1 fusion.78
  133.3 1.2 fusion.36
  135.4 2.8 slice-done
  138.1 3.2 copy.175
  141.3 8.2 %reshape.623 = bf16[1536,1536,1]{1,0,2:T(8,128)(2,1)} reshape(bf16[32,4,12,1536]{3,2,1,0:T(8,128)(2,1)} %bitcast.185) | data formatting | bytes 9437184 | tf_op jit(solution)/shard_map/reshape | solution.py:92
  149.6 1.4 constant_dynamic-slice_fusion
  151.0 51.6 %all-gather.5.cloned.1.call-done = bf16[256,4,1536]{2,1,0:T(4,128)(2,1)} async-done(((bf16[2,4,1536]{2,1,0:T(4,128)(2,1)}), bf16[256,4,1536]{2,1,0:T(4,128)(2,1)}) %all-gather.5.cloned.1.call-update) | async-done | bytes 3145744 | tf_op jit(solution)/shard_map/all_gather | solution.py:199
  202.5 4.4 %copy.111 = bf16[32,8,4,1536]{3,1,2,0:T(8,128)(2,1)} copy(bf16[32,8,4,1536]{3,2,1,0:T(4,128)(2,1)} %bitcast.186) | data formatting | bytes 6291456 | tf_op jit(solution)/shard_map/reshape | solution.py:201
  207.0 3.4 %gather_fusion.14 = bf16[8,8,4,1536]{3,1,2,0:T(8,128)(2,1)} fusion(bf16[32,8,4,1536]{3,1,2,0:T(8,128)(2,1)} %copy.111, s32[1024]{0:T(1024)S(1)} %pad_clamp_fusion), kind=kCustom, calls=%fused_computation.14 | custom fusion | bytes 1572896 | tf_op jit(solution)/shard_map/gather | solution.py:201
  210.3 4.1 %multiply_reduce_fusion = (f32[64,4]{0,1:T(4,128)S(1)}, f32[64,4,1536]{2,0,1:T(8,128)S(1)}) fusion(bf16[1536,1536,1]{1,0,2:T(8,128)(2,1)} %reshape.623, bf16[8,8,4,1536]{3,1,2,0:T(8,128)(2,1)} %gather_fusion.14, bf16[64,4,1536]{2,1,0:T(4,128)(2,1)S(1)} %constant_dynamic-slice_fusion), kind=kOutput, calls=%fused_computation.46 | convolution fusion | flops 1209532160 | bytes 7865344 | tf_op jit(solution)/shard_map/dot_general | solution.py:205
  214.5 1.3 fusion.41
  215.9 2.4 convolution_convert_fusion
  219.1 1.0 copy_bitcast_fusion.1
  220.1 16.8 %reduce-scatter.6.cloned.1.call-done = bf16[1,64,1536]{2,1,0:T(8,128)(2,1)} async-done(((bf16[4,64,1536]{2,1,0:T(8,128)(2,1)}), bf16[1,64,1536]{2,1,0:T(8,128)(2,1)}) %reduce-scatter.6.cloned.1.call-update) | async-done | bytes 196624 | tf_op jit(solution)/shard_map/reduce_scatter | solution.py:215
  236.9 1.7 reshape.476
  238.6 73.3 %reduce-scatter.8.cloned.1.call-done = bf16[1,16,768]{2,1,0:T(8,128)(2,1)} async-done(((bf16[8,16,768]{2,1,0:T(8,128)(2,1)}), bf16[1,16,768]{2,1,0:T(8,128)(2,1)}) %reduce-scatter.8.cloned.1.call-update) | async-done | bytes 24592 | tf_op jit(solution)/shard_map/reduce_scatter | solution.py:217
  311.9 0.8 reshape.479
  312.6 1.6 fusion.68
  (100 shorter events, 11.6 us)
Async XLA Ops:
  6.5 209.3 %copy-start = (bf16[280,1536]{1,0:T(8,128)(2,1)S(1)}, bf16[280,1536]{1,0:T(8,128)(2,1)}, u32[]{:S(2)}) copy-start(bf16[280,1536]{1,0:T(8,128)(2,1)} %param.18) | copy-start | bytes 2580484
  6.5 76.8 %all-gather.7.cloned.1.call-start = ((), (), s32[]{:S(2)}) async-start(), calls=%async_computation.7 | async-start | bytes 9510912 | tf_op jit(solution)/shard_map/all_gather | solution.py:86
  9.0 122.0 %reduce-scatter.4.cloned.1.call-start = ((), (), s32[]{:S(2)}) async-start(), calls=%async_computation.3 | async-start | bytes 655360 | tf_op jit(solution)/shard_map/reduce_scatter | solution.py:155
  87.1 8.4 %copy-start.4 = (f32[2048]{0:T(1024)S(1)}, f32[2048]{0:T(1024)}, u32[]{:S(2)}) copy-start(f32[2048]{0:T(1024)} %param.14) | copy-start | bytes 24580
  93.2 6.4 %copy-start.1 = (bf16[2,4096,256]{2,1,0:T(8,128)(2,1)S(1)}, bf16[2,4096,256]{2,1,0:T(8,128)(2,1)}, u32[]{:S(2)}) copy-start(bf16[2,4096,256]{2,1,0:T(8,128)(2,1)} %param.19) | copy-start | bytes 12582916
  108.5 2.2 copy-start.5
  112.7 22.6 %copy-start.6 = (s32[32]{0:T(128)S(1)}, s32[32]{0:T(128)}, u32[]{:S(2)}) copy-start(s32[32]{0:T(128)} %param.23) | copy-start | bytes 388
  115.2 87.3 %all-gather.5.cloned.1.call-start = ((), (), s32[]{:S(2)}) async-start(), calls=%async_computation.4 | async-start | bytes 3170304 | tf_op jit(solution)/shard_map/all_gather | solution.py:199
  135.2 101.7 %reduce-scatter.6.cloned.1.call-start = ((), (), s32[]{:S(2)}) async-start(), calls=%async_computation.5 | async-start | bytes 983040 | tf_op jit(solution)/shard_map/reduce_scatter | solution.py:215
  135.4 2.8 slice-start
  210.3 4.2 %copy-start.3 = (bf16[1536,280]{0,1:T(8,128)(2,1)S(1)}, bf16[1536,280]{0,1:T(8,128)(2,1)}, u32[]{:S(2)}) copy-start(bf16[1536,280]{0,1:T(8,128)(2,1)} %param.16) | copy-start | bytes 2580484
  214.5 1.4 copy-start.2
  220.1 91.8 %reduce-scatter.8.cloned.1.call-start = ((), (), s32[]{:S(2)}) async-start(), calls=%async_computation.6 | async-start | bytes 221184 | tf_op jit(solution)/shard_map/reduce_scatter | solution.py:217
Sparse Core Ops, SparseCore 0:
  10.4 72.8 all-gather.6
  115.3 15.5 reduce-scatter.3
  135.3 67.1 all-gather.4
  220.2 16.6 reduce-scatter.5
  240.2 71.6 reduce-scatter.7

commit v7 on v4

--- a/solution.py
+++ b/solution.py
@@ -209,11 +209,18 @@
     gate = jnp.dot(mixed_in, gate_weight, preferred_element_type=jnp.float32)
     upward = jnp.dot(mixed_in, up_weight, preferred_element_type=jnp.float32)
     hidden = (jax.nn.silu(gate) * upward).astype(jnp.bfloat16)
-    partial = jnp.dot(hidden, down_weight, preferred_element_type=jnp.float32).astype(jnp.bfloat16)
-    chunk = rows_dev * steps * width
-    partial = partial.reshape(tp_count, 16, chunk // 16)
-    lowered = lax.psum_scatter(partial, TP, scatter_dimension=0, tiled=True)
-    lowered = lowered.reshape(rows_dev, steps, width).astype(jnp.float32)
+    partial = jnp.dot(hidden, down_weight, preferred_element_type=jnp.float32)
+    partial = partial.reshape(tp_count, rows_dev * steps, width)
+    bit = 1
+    while bit < tp_count:
+        pairs = partial.reshape(partial.shape[0] // 2, 2, rows_dev * steps, width)
+        mine = (tp_index // bit) % 2
+        keep = jnp.where(mine == 0, pairs[:, 0], pairs[:, 1])
+        send = jnp.where(mine == 0, pairs[:, 1], pairs[:, 0])
+        perm = [(i, i ^ bit) for i in range(tp_count)]
+        partial = keep + lax.ppermute(send, TP, perm)
+        bit *= 2
+    lowered = partial.reshape(rows_dev, steps, width)
     middle_mine = lax.dynamic_slice_in_dim(middle, tp_index * rows_dev, rows_dev, 0)
     result = (middle_mine + lowered).astype(jnp.bfloat16)
     return jnp.swapaxes(result, 0, 1)

time: 306 us -> 267 us (0.87)
  waiting for transfers between devices: 202 us -> 155 us
  starting transfers between devices: 0.31 us -> 3.5 us
    reduce_scatter x1 -> x0, waiting for transfers between devices: 75.5 us -> none  [per_device(): lowered = lax.psum_scatter(partial, TP, scatter_dimension=0, tiled=True)]
    ppermute x0 -> x5, waiting for transfers between devices: none -> 29 us  [per_device(): partial = keep + lax.ppermute(send, TP, perm)]
    dot_general x0 -> x1, local copies, waits for them, and re-layouts: none -> 3.56 us  [per_device(): partial = jnp.dot(hidden, down_weight, preferred_element_type=jnp.float32)]
    ppermute x0 -> x5, starting transfers between devices: none -> 3.23 us  [per_device(): partial = keep + lax.ppermute(send, TP, perm)]
  transfers between devices with their start and end apart: 4 -> 8, of which waited for: 4 -> 8; matrix products, arithmetic and copies ran while one was open for 9% -> 10% of each run, Pallas kernels for 0% -> 0%
where the time goes in v7:
time: 267 us; the launch traced here: 266 us
  waiting for transfers between devices  155 us (58%)
  local copies, waits for them, and re-layouts  57.7 us (22%)
  other arithmetic  18 us (7%)
  matrix products  17.5 us (7%)
  between operations  14.3 us (5%)
  starting transfers between devices  3.5 us (1%)
    all_gather x1, waiting for transfers between devices, per_device(): carry = lax.all_gather(carry, ALL, axis=0, tiled=False)  60.8 us
    all_gather x1, waiting for transfers between devices, per_device(): att_all = lax.all_gather(attention, ALL, axis=0, tiled=True)  51.6 us
    ppermute x5, waiting for transfers between devices, per_device(): partial = keep + lax.ppermute(send, TP, perm)  29 us
    reduce_scatter x1, waiting for transfers between devices, per_device(): packed = lax.psum_scatter(packed, 'tpi', scatter_dimension=0, tiled=True)[0]  13.6 us
    reshape x2, local copies, waits for them, and re-layouts, per_device(): full_out = carry[:, rows_dev * steps:].reshape(n_req, tp_count, share, wi...  11.4 us
    reshape x1, local copies, waits for them, and re-layouts, per_device(): x_all = carry[:, :rows_dev * steps].reshape(requests * beams, steps, width)  6.12 us
  transfers between devices with their start and end apart: 8, of which 8 were waited for; matrix products, arithmetic and copies ran while one was open for 10% of the time, Pallas kernels for 0%

profile of v7, /device:TPU:0, one launch (start us, length us, event | category | flops | bytes accessed | tf_op | source)
XLA Modules:
  0.0 266.1 jit_solution(2415146657036589586)
XLA Ops:
  6.5 0.8 copy.122
  7.4 0.9 constant_dynamic-slice_fusion.1
  9.0 0.9 dynamic-slice_reduce_fusion.4
  9.9 0.7 compare_select_fusion.6
  10.6 0.7 scatter_custom_fusion
  12.5 1.0 dynamic-slice_reduce_fusion
  14.8 0.7 gather_fusion.6
  21.4 0.7 gather_fusion.5
  22.5 60.8 %all-gather.7.cloned.1.call-done = bf16[128,20,1536]{2,1,0:T(8,128)(2,1)} async-done(((bf16[1,20,1536]{2,1,0:T(8,128)(2,1)}), bf16[128,20,1536]{2,1,0:T(8,128)(2,1)}) %all-gather.7.cloned.1.call-update) | async-done | bytes 7864336 | tf_op jit(solution)/shard_map/all_gather | solution.py:86
  83.3 3.7 %slice.186 = bf16[128,8,1536]{2,1,0:T(8,128)(2,1)} slice(bf16[128,20,1536]{2,1,0:T(8,128)(2,1)} %all-gather.7.cloned.1.call-done), slice={[0:128], [0:8], [0:1536]} | slice | bytes 6291456 | tf_op jit(solution)/shard_map/slice | solution.py:87
  87.1 6.1 %reshape.531 = bf16[256,4,1536]{2,1,0:T(4,128)(2,1)} reshape(bf16[128,8,1536]{2,1,0:T(8,128)(2,1)} %slice.186) | data formatting | bytes 6291456 | tf_op jit(solution)/shard_map/reshape | solution.py:87
  93.2 1.2 fusion.56
  94.4 1.1 fusion.57
  95.5 3.9 %fusion.13 = bf16[8,4,2048]{2,0,1:T(8,128)(2,1)S(1)} fusion(bf16[1536,2048]{1,0:T(8,128)(2,1)} %param.13, f32[2048]{0:T(1024)S(1)} %copy-done.4, bf16[8,4,1536]{2,1,0:T(4,128)(2,1)S(1)} %fusion.57), kind=kOutput, calls=%fused_computation.35 | convolution fusion | flops 201457664 | bytes 6529024 | tf_op jit(solution)/shard_map/dot_general | solution.py:99
  99.6 1.0 convolution_bitcast_fusion.1
  100.6 1.0 convolution_bitcast_fusion
  101.8 2.1 fusion.5
  103.9 4.6 %fusion.2 = (bf16[2,8,4,2,6,4096]{5,1,0,4,2,3:T(8,128)(2,1)S(1)}, f32[2,8,4,2,6]{1,0,4,2,3:T(2,128)S(1)}) fusion(f32[2,8,4,2,6]{1,0,4,2,3:T(2,128)S(1)} %fusion.5, pred[2,4096]{1,0:T(4,128)(4,1)S(1)} %iota_compare_fusion, f32[2,8,4,1,6,4096]{5,1,0,4,2,3:T(8,128)S(1)} %convolution_bitcast_fusion, f32[2,8,4,1,6,4096]{5,1,0,4,2,3:T(8,128)S(1)} %convolution_bitcast_fusion.1), kind=kLoop, calls=%fused_computation.20 | loop fusion | flops 22019328 | bytes 18888704 | tf_op jit(solution)/shard_map/convert_element_type | solution.py:136
  108.5 0.8 slice_bitcast_fusion.1
  109.3 1.4 copy-done.5
  110.7 1.0 fusion.25
  111.7 1.0 fusion.30
  114.2 0.9 pad_maximum_fusion
  115.4 0.7 gather_fusion.13
  117.4 13.6 %reduce-scatter.2.cloned.1.call-done = f32[1,2,4,2,6,130]{5,4,3,2,1,0:T(8,128)} async-done(((f32[4,2,4,2,6,130]{5,4,3,2,1,0:T(8,128)}), f32[1,2,4,2,6,130]{5,4,3,2,1,0:T(8,128)}) %reduce-scatter.2.cloned.1.call-update) | async-done | bytes 49936 | tf_op jit(solution)/shard_map/reduce_scatter | solution.py:155
  131.0 0.9 fusion.76
  132.2 1.1 fusion.88
  133.3 1.2 fusion.37
  135.3 2.8 %slice-done = bf16[128,12,1536]{2,1,0:T(8,128)(2,1)S(1)} async-done(((bf16[128,20,1536]{2,1,0:T(8,128)(2,1)}), bf16[128,12,1536]{2,1,0:T(8,128)(2,1)S(1)}, s32[]{:S(2)}) %slice-start) | async-done | bytes 4718616 | tf_op jit(solution)/shard_map/slice | solution.py:89
  138.1 3.2 %copy.232 = bf16[4,32,12,1536]{3,2,0,1:T(8,128)(2,1)} copy(bf16[4,32,12,1536]{3,2,1,0:T(8,128)(2,1)S(1)} %bitcast.264) | data formatting | bytes 9437184 | tf_op jit(solution)/shard_map/reshape | solution.py:90
  141.3 8.2 %reshape.687 = bf16[1536,1536,1]{1,0,2:T(8,128)(2,1)} reshape(bf16[32,4,12,1536]{3,2,1,0:T(8,128)(2,1)} %bitcast.265) | data formatting | bytes 9437184 | tf_op jit(solution)/shard_map/reshape | solution.py:92
  149.5 1.4 constant_dynamic-slice_fusion
  150.9 51.6 %all-gather.5.cloned.1.call-done = bf16[256,4,1536]{2,1,0:T(4,128)(2,1)} async-done(((bf16[2,4,1536]{2,1,0:T(4,128)(2,1)}), bf16[256,4,1536]{2,1,0:T(4,128)(2,1)}) %all-gather.5.cloned.1.call-update) | async-done | bytes 3145744 | tf_op jit(solution)/shard_map/all_gather | solution.py:199
  202.5 4.4 %copy.150 = bf16[32,8,4,1536]{3,1,2,0:T(8,128)(2,1)} copy(bf16[32,8,4,1536]{3,2,1,0:T(4,128)(2,1)} %bitcast.270) | data formatting | bytes 6291456 | tf_op jit(solution)/shard_map/reshape | solution.py:201
  207.0 3.4 %gather_fusion.14 = bf16[8,8,4,1536]{3,1,2,0:T(8,128)(2,1)} fusion(bf16[32,8,4,1536]{3,1,2,0:T(8,128)(2,1)} %copy.150, s32[1024]{0:T(1024)S(1)} %pad_clamp_fusion), kind=kCustom, calls=%fused_computation.14 | custom fusion | bytes 1572896 | tf_op jit(solution)/shard_map/gather | solution.py:201
  210.3 4.1 %multiply_reduce_fusion = (f32[64,4]{0,1:T(4,128)S(1)}, f32[64,4,1536]{2,0,1:T(8,128)S(1)}) fusion(bf16[1536,1536,1]{1,0,2:T(8,128)(2,1)} %reshape.687, bf16[8,8,4,1536]{3,1,2,0:T(8,128)(2,1)} %gather_fusion.14, bf16[64,4,1536]{2,1,0:T(4,128)(2,1)S(1)} %constant_dynamic-slice_fusion), kind=kOutput, calls=%fused_computation.45 | convolution fusion | flops 1209532160 | bytes 7865344 | tf_op jit(solution)/shard_map/dot_general | solution.py:205
  215.1 3.5 %fusion.35 = f32[64,4,1536]{2,0,1:T(8,128)} fusion(bf16[280,1536]{1,0:T(8,128)(2,1)S(1)} %copy-done, bf16[1536,280]{0,1:T(8,128)(2,1)} %param.17, f32[64,4,280]{2,0,1:T(8,128)S(1)} %fusion.42, f32[64,4,1536]{2,0,1:T(8,128)S(1)} %get-tuple-element.32, f32[64,4]{0,1:T(4,128)S(1)} %add_rsqrt_fusion.1), kind=kOutput, calls=%fused_computation.50 | convolution fusion | flops 441618432 | bytes 5153792 | tf_op jit(solution)/shard_map/dot_general | solution.py:212
  218.6 3.6 %copy.153 = f32[64,4,1536]{2,1,0:T(4,128)} copy(f32[64,4,1536]{2,0,1:T(8,128)} %fusion.35) | data formatting | bytes 3145728 | tf_op jit(solution)/shard_map/dot_general | solution.py:212
  222.2 1.8 reshape_reshape.3
  224.4 2.2 collective-permute-done
  226.6 1.3 fusion.45
  228.3 11.0 %collective-permute-done.1 = f32[8,8,1536]{2,1,0:T(8,128)S(1)} collective-permute-done((f32[8,8,1536]{2,1,0:T(8,128)S(1)}, f32[8,8,1536]{2,1,0:T(8,128)S(1)}, u32[]{:S(2)}, u32[]{:S(2)}) %collective-permute-start.1) | collective-permute-done | bytes 393248 | tf_op jit(solution)/shard_map/ppermute | solution.py:221
  239.4 1.5 collective-permute-start.2
  241.0 6.2 %collective-permute-done.2 = f32[4,8,1536]{2,1,0:T(8,128)S(1)} collective-permute-done((f32[4,8,1536]{2,1,0:T(8,128)S(1)}, f32[4,8,1536]{2,1,0:T(8,128)S(1)}, u32[]{:S(2)}, u32[]{:S(2)}) %collective-permute-start.2) | collective-permute-done | bytes 196640 | tf_op jit(solution)/shard_map/ppermute | solution.py:221
  247.4 4.9 %collective-permute-done.3 = f32[2,8,1536]{2,1,0:T(8,128)S(1)} collective-permute-done((f32[2,8,1536]{2,1,0:T(8,128)S(1)}, f32[2,8,1536]{2,1,0:T(8,128)S(1)}, u32[]{:S(2)}, u32[]{:S(2)}) %collective-permute-start.3) | collective-permute-done | bytes 98336 | tf_op jit(solution)/shard_map/ppermute | solution.py:221
  252.3 1.0 collective-permute-start.4
  253.3 4.7 %collective-permute-done.4 = f32[1,8,1536]{2,1,0:T(8,128)S(1)} collective-permute-done((f32[1,8,1536]{2,1,0:T(8,128)S(1)}, f32[1,8,1536]{2,1,0:T(8,128)S(1)}, u32[]{:S(2)}, u32[]{:S(2)}) %collective-permute-start.4) | collective-permute-done | bytes 49184 | tf_op jit(solution)/shard_map/ppermute | solution.py:221
  258.0 1.6 fusion.78
  (112 shorter events, 14.9 us)
Async XLA Ops:
  6.5 208.6 %copy-start = (bf16[280,1536]{1,0:T(8,128)(2,1)S(1)}, bf16[280,1536]{1,0:T(8,128)(2,1)}, u32[]{:S(2)}) copy-start(bf16[280,1536]{1,0:T(8,128)(2,1)} %param.18) | copy-start | bytes 2580484
  6.5 76.8 %all-gather.7.cloned.1.call-start = ((), (), s32[]{:S(2)}) async-start(), calls=%async_computation.3 | async-start | bytes 9510912 | tf_op jit(solution)/shard_map/all_gather | solution.py:86
  9.0 122.0 %reduce-scatter.2.cloned.1.call-start = ((), (), s32[]{:S(2)}) async-start(), calls=%async_computation.1 | async-start | bytes 655360 | tf_op jit(solution)/shard_map/reduce_scatter | solution.py:155
  87.1 8.4 %copy-start.4 = (f32[2048]{0:T(1024)S(1)}, f32[2048]{0:T(1024)}, u32[]{:S(2)}) copy-start(f32[2048]{0:T(1024)} %param.14) | copy-start | bytes 24580
  93.2 6.4 %copy-start.2 = (bf16[2,4096,256]{2,1,0:T(8,128)(2,1)S(1)}, bf16[2,4096,256]{2,1,0:T(8,128)(2,1)}, u32[]{:S(2)}) copy-start(bf16[2,4096,256]{2,1,0:T(8,128)(2,1)} %param.19) | copy-start | bytes 12582916
  108.5 2.2 copy-start.5
  112.7 22.5 %copy-start.6 = (s32[32]{0:T(128)S(1)}, s32[32]{0:T(128)}, u32[]{:S(2)}) copy-start(s32[32]{0:T(128)} %param.23) | copy-start | bytes 388
  115.2 87.3 %all-gather.5.cloned.1.call-start = ((), (), s32[]{:S(2)}) async-start(), calls=%async_computation.2 | async-start | bytes 3170304 | tf_op jit(solution)/shard_map/all_gather | solution.py:199
  135.3 2.8 %slice-start = ((bf16[128,20,1536]{2,1,0:T(8,128)(2,1)}), bf16[128,12,1536]{2,1,0:T(8,128)(2,1)S(1)}, s32[]{:S(2)}) async-start(bf16[128,20,1536]{2,1,0:T(8,128)(2,1)} %all-gather.7.cloned.1.call-done), calls=%async_computation.4 | async-start | bytes 12582912 | tf_op jit(solution)/shard_map/slice | solution.py:89
  210.3 4.2 %copy-start.3 = (bf16[1536,280]{0,1:T(8,128)(2,1)S(1)}, bf16[1536,280]{0,1:T(8,128)(2,1)}, u32[]{:S(2)}) copy-start(bf16[1536,280]{0,1:T(8,128)(2,1)} %param.16) | copy-start | bytes 2580484
  214.5 4.1 %copy-start.1 = (f32[64,4,1536]{2,0,1:T(8,128)}, f32[64,4,1536]{2,0,1:T(8,128)S(1)}, u32[]{:S(2)}) copy-start(f32[64,4,1536]{2,0,1:T(8,128)S(1)} %get-tuple-element.32) | copy-start | bytes 4718596
  224.1 2.5 collective-permute-start
  228.0 11.3 %collective-permute-start.1 = (f32[8,8,1536]{2,1,0:T(8,128)S(1)}, f32[8,8,1536]{2,1,0:T(8,128)S(1)}, u32[]{:S(2)}, u32[]{:S(2)}) collective-permute-start(f32[8,8,1536]{2,1,0:T(8,128)S(1)} %select_bitcast_fusion.1), channel_id=1, source_target_pairs={{0,2},{1,3},{2,0},{3,1},{4,6},{5,7},{6,4},{7,5},{8,10},{9,11},{10,... | collective-permute-start | bytes 1179656 | tf_op jit(solution)/shard_map/ppermute | solution.py:221
  239.4 7.8 %collective-permute-start.2 = (f32[4,8,1536]{2,1,0:T(8,128)S(1)}, f32[4,8,1536]{2,1,0:T(8,128)S(1)}, u32[]{:S(2)}, u32[]{:S(2)}) collective-permute-start(f32[4,8,1536]{2,1,0:T(8,128)S(1)} %select_bitcast_fusion.2), channel_id=1, source_target_pairs={{0,4},{1,5},{2,6},{3,7},{4,0},{5,1},{6,2},{7,3},{8,12},{9,13},{10,... | collective-permute-start | bytes 589832 | tf_op jit(solution)/shard_map/ppermute | solution.py:221
  247.2 5.0 %collective-permute-start.3 = (f32[2,8,1536]{2,1,0:T(8,128)S(1)}, f32[2,8,1536]{2,1,0:T(8,128)S(1)}, u32[]{:S(2)}, u32[]{:S(2)}) collective-permute-start(f32[2,8,1536]{2,1,0:T(8,128)S(1)} %select_bitcast_fusion.3), channel_id=1, source_target_pairs={{0,8},{1,9},{2,10},{3,11},{4,12},{5,13},{6,14},{7,15},{8,0},{9,1},... | collective-permute-start | bytes 294920 | tf_op jit(solution)/shard_map/ppermute | solution.py:221
  252.3 5.7 %collective-permute-start.4 = (f32[1,8,1536]{2,1,0:T(8,128)S(1)}, f32[1,8,1536]{2,1,0:T(8,128)S(1)}, u32[]{:S(2)}, u32[]{:S(2)}) collective-permute-start(f32[1,8,1536]{2,1,0:T(8,128)S(1)} %select_bitcast_fusion.4), channel_id=1, source_target_pairs={{0,16},{1,17},{2,18},{3,19},{4,20},{5,21},{6,22},{7,23},{8,24},{9,... | collective-permute-start | bytes 147464 | tf_op jit(solution)/shard_map/ppermute | solution.py:221
Sparse Core Ops, SparseCore 0:
  10.4 72.8 all-gather.6
  115.3 15.5 reduce-scatter.1
  135.3 67.1 all-gather.4

commit v8 on v3

--- a/solution.py
+++ b/solution.py
@@ -33,6 +33,50 @@
     return jnp.concatenate(
         [first * cosine - second * sine, second * cosine + first * sine], axis=-1
     ).astype(jnp.bfloat16)
+
+
+def gather_rounds(x, axes, index, masks):
+    count = 1 << len(masks)
+    buf = x
+    bits = []
+    for mask in masks:
+        low = mask & (-mask)
+        bit = low if mask == low else mask - low
+        perm = [(i, i ^ mask) for i in range(count)]
+        recv = lax.ppermute(buf, axes, perm)
+        mine = (index // bit) % 2
+        buf = jnp.where(mine == 0, jnp.stack([buf, recv]), jnp.stack([recv, buf]))
+        bits.append(bit)
+    depth = len(bits)
+    order = sorted(range(depth), key=lambda a: -bits[depth - 1 - a])
+    buf = jnp.transpose(buf, tuple(order) + tuple(range(depth, buf.ndim)))
+    return buf.reshape((count,) + x.shape)
+
+
+def scatter_rounds(x, axes, index):
+    count = x.shape[0]
+    buf = x
+    bit = 1
+    while bit < count:
+        pairs = buf.reshape((buf.shape[0] // 2, 2) + buf.shape[1:])
+        mine = (index // bit) % 2
+        keep = jnp.where(mine == 0, pairs[:, 0], pairs[:, 1])
+        send = jnp.where(mine == 0, pairs[:, 1], pairs[:, 0])
+        perm = [(i, i ^ bit) for i in range(count)]
+        buf = keep + lax.ppermute(send, axes, perm)
+        bit *= 2
+    return buf[0]
+
+
+def gather_masks(n_req, tp_count):
+    masks = []
+    for shift, size in ((tp_count.bit_length() - 1, n_req), (3, 4), (1, 4)):
+        low = 1 << shift
+        masks.append(low)
+        if size == 4:
+            masks.append(3 * low)
+    masks.append(1)
+    return masks
 
 
 def per_device(
@@ -77,7 +121,11 @@
         .set(jnp.arange(requests, dtype=jnp.int32))
     )
 
-    x_all = lax.all_gather(jnp.swapaxes(step_inputs, 0, 1), ALL, axis=0, tiled=True)
+    flat_masks = gather_masks(n_req, tp_count)
+    x_all = gather_rounds(
+        jnp.swapaxes(step_inputs, 0, 1).reshape(rows_dev * steps, width), ALL, flat, flat_masks
+    ).reshape(requests * beams, steps, width)
+    full_out = lax.all_gather(out_weight, TP, axis=0, tiled=True)
     x_req = lax.dynamic_slice_in_dim(x_all, inverse[r] * beams, beams, 0)
     x_group = lax.dynamic_slice_in_dim(x_all, req_index * group_rows, group_rows, 0)
 
@@ -139,7 +187,7 @@
     output = jnp.sum(jnp.where(chosen[..., None], output, 0.0), axis=0)
     packed = jnp.concatenate([output, peak[..., None], total[..., None]], axis=-1)
     packed = packed.reshape(n_i, owned, steps, KV_HEADS, group, head_dim + 2)
-    packed = lax.psum_scatter(packed, "tpi", scatter_dimension=0, tiled=True)[0]
+    packed = scatter_rounds(packed, "tpi", j)
     part_output = packed[..., :head_dim]
     part_peak = packed[..., head_dim]
     part_total = packed[..., head_dim + 1]
@@ -183,13 +231,14 @@
         (numerator / denominator[..., None]).reshape(owned, steps, attn_width).astype(jnp.bfloat16)
     )
 
-    att_all = lax.all_gather(attention, ALL, axis=0, tiled=True)
+    att_all = gather_rounds(attention, ALL, flat, flat_masks).reshape(
+        requests * beams, steps, attn_width
+    )
     my_requests = lax.dynamic_slice_in_dim(slot_request, req_index * group_requests, group_requests)
     att_group = att_all.reshape(requests, beams, steps, attn_width)[my_requests].reshape(
         group_rows, steps, attn_width
     )
 
-    full_out = lax.all_gather(out_weight, TP, axis=0, tiled=True)
     middle = x_group.astype(jnp.float32) + jnp.dot(
         att_group, full_out, preferred_element_type=jnp.float32
     )
@@ -197,11 +246,9 @@
     gate = jnp.dot(mixed_in, gate_weight, preferred_element_type=jnp.float32)
     upward = jnp.dot(mixed_in, up_weight, preferred_element_type=jnp.float32)
     hidden = (jax.nn.silu(gate) * upward).astype(jnp.bfloat16)
-    partial = jnp.dot(hidden, down_weight, preferred_element_type=jnp.float32).astype(jnp.bfloat16)
-    chunk = rows_dev * steps * width
-    partial = partial.reshape(tp_count, 16, chunk // 16)
-    lowered = lax.psum_scatter(partial, TP, scatter_dimension=0, tiled=True)
-    lowered = lowered.reshape(rows_dev, steps, width).astype(jnp.float32)
+    partial = jnp.dot(hidden, down_weight, preferred_element_type=jnp.float32)
+    partial = scatter_rounds(partial.reshape(tp_count, rows_dev * steps, width), TP, tp_index)
+    lowered = partial.reshape(rows_dev, steps, width)
     middle_mine = lax.dynamic_slice_in_dim(middle, tp_index * rows_dev, rows_dev, 0)
     result = (middle_mine + lowered).astype(jnp.bfloat16)
     return jnp.swapaxes(result, 0, 1)

time: 331 us -> 236 us (0.71)
  waiting for transfers between devices: 253 us -> 103 us
  starting transfers between devices: 0.35 us -> 29.8 us
  other arithmetic: 14.2 us -> 30.6 us
  local copies, waits for them, and re-layouts: 31.6 us -> 40 us
    all_gather x2 -> x0, waiting for transfers between devices: 123 us -> none  [the longest x1 65 us: per_device(): att_all = lax.all_gather(attention, ALL, axis=0, tiled=True)]
    ppermute x0 -> x21, waiting for transfers between devices: none -> 103 us  [the longest x14 70.8 us: gather_rounds(): recv = lax.ppermute(buf, axes, perm)]
    reduce_scatter x2 -> x0, waiting for transfers between devices: 90.9 us -> none  [the longest x1 77.4 us: per_device(): lowered = lax.psum_scatter(partial, TP, scatter_dimension=0, tiled=True)]
    all_gather x1, waiting for transfers between devices: 38.6 us -> 0.01 us  [per_device(): full_out = lax.all_gather(out_weight, TP, axis=0, tiled=True)]
    ppermute x0 -> x21, starting transfers between devices: none -> 29.8 us  [the longest x14 25 us: gather_rounds(): recv = lax.ppermute(buf, axes, perm)]
    another operation x0 -> x7, local copies, waits for them, and re-layouts: none -> 10.5 us  [the longest x1 6.14 us: per_device(): x_all = gather_rounds(jnp.swapaxes(step_inputs, 0, 1).reshape(rows_dev *...]
    select_n x0 -> x31, other arithmetic: none -> 7.87 us  [the longest x24 7.63 us: gather_rounds(): buf = jnp.where(mine == 0, jnp.stack([buf, recv]), jnp.stack([recv, buf]))]
    transpose x0 -> x2, other arithmetic: none -> 6.99 us  [gather_rounds(): buf = jnp.transpose(buf, tuple(order) + tuple(range(depth, buf.ndim)))]
  transfers between devices with their start and end apart: 5 -> 22, of which waited for: 5 -> 20; matrix products, arithmetic and copies ran while one was open for 7% -> 29% of each run, Pallas kernels for 0% -> 0%
where the time goes in v8:
time: 236 us; the launch traced here: 235 us
  waiting for transfers between devices  103 us (44%)
  local copies, waits for them, and re-layouts  40 us (17%)
  other arithmetic  30.6 us (13%)
  starting transfers between devices  29.8 us (13%)
  matrix products  16.8 us (7%)
  between operations  15 us (6%)
    ppermute x14, waiting for transfers between devices, gather_rounds(): recv = lax.ppermute(buf, axes, perm)  70.8 us
    ppermute x7, waiting for transfers between devices, scatter_rounds(): buf = keep + lax.ppermute(send, axes, perm)  32.1 us
    ppermute x14, starting transfers between devices, gather_rounds(): recv = lax.ppermute(buf, axes, perm)  25 us
    select_n x24, other arithmetic, gather_rounds(): buf = jnp.where(mine == 0, jnp.stack([buf, recv]), jnp.stack([recv, buf]))  7.63 us
    transpose x2, other arithmetic, gather_rounds(): buf = jnp.transpose(buf, tuple(order) + tuple(range(depth, buf.ndim)))  6.99 us
    another operation x1, local copies, waits for them, and re-layouts, per_device(): x_all = gather_rounds(jnp.swapaxes(step_inputs, 0, 1).reshape(rows_dev *...  6.14 us
    ppermute x7, starting transfers between devices, scatter_rounds(): buf = keep + lax.ppermute(send, axes, perm)  4.86 us
  transfers between devices with their start and end apart: 22, of which 20 were waited for; matrix products, arithmetic and copies ran while one was open for 29% of the time, Pallas kernels for 0%

profile of v8, /device:TPU:0, one launch (start us, length us, event | category | flops | bytes accessed | tf_op | source)
XLA Modules:
  0.0 235.2 jit_solution(6121027551177841261)
XLA Ops:
  7.4 1.7 collective-permute-start
  19.1 2.2 collective-permute-start.1
  21.4 3.2 %collective-permute-done.1 = bf16[2,8,1536]{2,1,0:T(8,128)(2,1)S(1)} collective-permute-done((bf16[2,8,1536]{2,1,0:T(8,128)(2,1)S(1)}, bf16[2,8,1536]{2,1,0:T(8,128)(2,1)S(1)}, u32[]{:S(2)}, u32[]{:S(2)}) %collective-permute-start.1) | collective-permute-done | bytes 49184 | tf_op jit(solution)/shard_map/ppermute | solution.py:46
  24.5 2.0 collective-permute-start.2
  26.6 3.1 %collective-permute-done.2 = bf16[2,2,8,1536]{3,2,1,0:T(8,128)(2,1)S(1)} collective-permute-done((bf16[2,2,8,1536]{3,2,1,0:T(8,128)(2,1)S(1)}, bf16[2,2,8,1536]{3,2,1,0:T(8,128)(2,1)S(1)}, u32[]{:S(2)}, u32[]{:S(2)}) %collective-permute-start.2) | collective-permute-done | bytes 98336 | tf_op jit(solution)/shard_map/ppermute | solution.py:46
  29.7 4.1 %collective-permute-start.3 = (bf16[2,2,2,8,1536]{4,3,2,1,0:T(8,128)(2,1)S(1)}, bf16[2,2,2,8,1536]{4,3,2,1,0:T(8,128)(2,1)S(1)}, u32[]{:S(2)}, u32[]{:S(2)}) collective-permute-start(bf16[2,2,2,8,1536]{4,3,2,1,0:T(8,128)(2,1)S(1)} %maximum_select_fusion.16), channel_id=1, source_target_pairs={{0,24},{1,25},{2,26},{3,27},{4,28},{5,29},{6,30},{7,31},{8,16},{9,... | collective-permute-start | bytes 589832 | tf_op jit(solution)/shard_map/ppermute | solution.py:46
  33.8 3.6 %collective-permute-done.3 = bf16[2,2,2,8,1536]{4,3,2,1,0:T(8,128)(2,1)S(1)} collective-permute-done((bf16[2,2,2,8,1536]{4,3,2,1,0:T(8,128)(2,1)S(1)}, bf16[2,2,2,8,1536]{4,3,2,1,0:T(8,128)(2,1)S(1)}, u32[]{:S(2)}, u32[]{:S(2)}) %collective-permute-start.3) | collective-permute-done | bytes 196640 | tf_op jit(solution)/shard_map/ppermute | solution.py:46
  37.5 1.6 collective-permute-start.4
  39.2 11.9 %collective-permute-done.4 = bf16[2,2,2,2,8,1536]{5,4,3,2,1,0:T(8,128)(2,1)S(1)} collective-permute-done((bf16[2,2,2,2,8,1536]{5,4,3,2,1,0:T(8,128)(2,1)S(1)}, bf16[2,2,2,2,8,1536]{5,4,3,2,1,0:T(8,128)(2,1)S(1)}, u32[]{:S(2)}, u32[]{:S(2)}) %collective-permute-start.4) | collective-permute-done | bytes 393248 | tf_op jit(solution)/shard_map/ppermute | solution.py:46
  51.2 3.3 %collective-permute-start.5 = (bf16[2,2,2,2,2,8,1536]{6,5,4,3,2,1,0:T(8,128)(2,1)S(1)}, bf16[2,2,2,2,2,8,1536]{6,5,4,3,2,1,0:T(8,128)(2,1)S(1)}, u32[]{:S(2)}, u32[]{:S(2)}) collective-permute-start(bf16[2,2,2,2,2,8,1536]{6,5,4,3,2,1,0:T(8,128)(2,1)S(1)} %maximum_select_fusion.7), channel_id=1, source_target_pairs={{0,6},{1,7},{2,4},{3,5},{4,2},{5,3},{6,0},{7,1},{8,14},{9,15},{10,... | collective-permute-start | bytes 2359304 | tf_op jit(solution)/shard_map/ppermute | solution.py:46
  55.0 16.7 %collective-permute-done.5 = bf16[2,2,2,2,2,8,1536]{6,5,4,3,2,1,0:T(8,128)(2,1)S(1)} collective-permute-done((bf16[2,2,2,2,2,8,1536]{6,5,4,3,2,1,0:T(8,128)(2,1)S(1)}, bf16[2,2,2,2,2,8,1536]{6,5,4,3,2,1,0:T(8,128)(2,1)S(1)}, u32[]{:S(2)}, u32[]{:S(2)}) %collective-permute-start.5) | collective-permute-done | bytes 786464 | tf_op jit(solution)/shard_map/ppermute | solution.py:46
  71.6 1.4 maximum_select_fusion.3
  76.8 2.3 fusion.8
  79.1 2.2 copy.131
  81.4 6.1 %reshape_reshape.7 = bf16[256,4,1536]{2,1,0:T(4,128)(2,1)} reshape(bf16[2,2,2,2,2,2,2,8,1536]{8,7,6,5,4,3,2,1,0:T(8,128)(2,1)} %copy.131) | data formatting | bytes 6291456 | tf_op jit(solution)/shard_map/reshape;reshape | solution.py:127
  89.6 4.1 %fusion.20 = bf16[8,4,2048]{2,0,1:T(8,128)(2,1)S(1)} fusion(bf16[1536,2048]{1,0:T(8,128)(2,1)} %param.13, f32[2048]{0:T(1024)S(1)} %copy-done.4, bf16[8,4,1536]{2,1,0:T(4,128)(2,1)S(1)} %fusion.63), kind=kOutput, calls=%fused_computation.40 | convolution fusion | flops 201457664 | bytes 6529024 | tf_op jit(solution)/shard_map/dot_general | solution.py:134
  95.9 2.1 fusion.5
  98.0 4.6 %fusion.2 = (bf16[2,8,4,2,6,4096]{5,1,0,4,2,3:T(8,128)(2,1)S(1)}, f32[2,8,4,2,6]{1,0,4,2,3:T(2,128)S(1)}) fusion(f32[2,8,4,2,6]{1,0,4,2,3:T(2,128)S(1)} %fusion.5, pred[2,4096]{1,0:T(4,128)(4,1)S(1)} %iota_compare_fusion, f32[2,8,4,1,6,4096]{5,1,0,4,2,3:T(8,128)S(1)} %convolution_bitcast_fusion, f32[2,8,4,1,6,4096]{5,1,0,4,2,3:T(8,128)S(1)} %convolution_bitcast_fusion.1), kind=kLoop, calls=%fused_computation.20 | loop fusion | flops 22019328 | bytes 18888704 | tf_op jit(solution)/shard_map/convert_element_type | solution.py:171
  103.4 1.4 copy-done.6
  111.6 4.3 %collective-permute-done.8 = f32[1,2,4,2,6,130]{5,4,3,2,1,0:T(8,128)S(1)} collective-permute-done((f32[1,2,4,2,6,130]{5,4,3,2,1,0:T(8,128)S(1)}, f32[1,2,4,2,6,130]{5,4,3,2,1,0:T(8,128)S(1)}, u32[]{:S(2)}, u32[]{:S(2)}) %collective-permute-start.8) | collective-permute-done | bytes 49952 | tf_op jit(solution)/shard_map/ppermute | solution.py:66
  118.1 2.9 %collective-permute-done.9 = bf16[2,4,1536]{2,1,0:T(4,128)(2,1)S(1)} collective-permute-done((bf16[2,4,1536]{2,1,0:T(4,128)(2,1)S(1)}, bf16[2,4,1536]{2,1,0:T(4,128)(2,1)S(1)}, u32[]{:S(2)}, u32[]{:S(2)}) %collective-permute-start.9) | collective-permute-done | bytes 24608 | tf_op jit(solution)/shard_map/ppermute | solution.py:46
  121.1 2.8 %collective-permute-start.10 = (bf16[2,2,4,1536]{3,2,1,0:T(4,128)(2,1)S(1)}, bf16[2,2,4,1536]{3,2,1,0:T(4,128)(2,1)S(1)}, u32[]{:S(2)}, u32[]{:S(2)}) collective-permute-start(bf16[2,2,4,1536]{3,2,1,0:T(4,128)(2,1)S(1)} %maximum_select_fusion.26), channel_id=1, source_target_pairs={{0,96},{1,97},{2,98},{3,99},{4,100},{5,101},{6,102},{7,103},{8,104... | collective-permute-start | bytes 147464 | tf_op jit(solution)/shard_map/ppermute | solution.py:46
  123.9 2.5 %collective-permute-done.10 = bf16[2,2,4,1536]{3,2,1,0:T(4,128)(2,1)S(1)} collective-permute-done((bf16[2,2,4,1536]{3,2,1,0:T(4,128)(2,1)S(1)}, bf16[2,2,4,1536]{3,2,1,0:T(4,128)(2,1)S(1)}, u32[]{:S(2)}, u32[]{:S(2)}) %collective-permute-start.10) | collective-permute-done | bytes 49184 | tf_op jit(solution)/shard_map/ppermute | solution.py:46
  127.8 3.4 %collective-permute-done.11 = bf16[2,2,2,4,1536]{4,3,2,1,0:T(4,128)(2,1)S(1)} collective-permute-done((bf16[2,2,2,4,1536]{4,3,2,1,0:T(4,128)(2,1)S(1)}, bf16[2,2,2,4,1536]{4,3,2,1,0:T(4,128)(2,1)S(1)}, u32[]{:S(2)}, u32[]{:S(2)}) %collective-permute-start.11) | collective-permute-done | bytes 98336 | tf_op jit(solution)/shard_map/ppermute | solution.py:46
  131.4 3.0 %collective-permute-start.12 = (bf16[2,2,2,2,4,1536]{5,4,3,2,1,0:T(4,128)(2,1)S(1)}, bf16[2,2,2,2,4,1536]{5,4,3,2,1,0:T(4,128)(2,1)S(1)}, u32[]{:S(2)}, u32[]{:S(2)}) collective-permute-start(bf16[2,2,2,2,4,1536]{5,4,3,2,1,0:T(4,128)(2,1)S(1)} %maximum_select_fusion.18), channel_id=1, source_target_pairs={{0,24},{1,25},{2,26},{3,27},{4,28},{5,29},{6,30},{7,31},{8,16},{9,... | collective-permute-start | bytes 589832 | tf_op jit(solution)/shard_map/ppermute | solution.py:46
  134.5 3.8 %collective-permute-done.12 = bf16[2,2,2,2,4,1536]{5,4,3,2,1,0:T(4,128)(2,1)S(1)} collective-permute-done((bf16[2,2,2,2,4,1536]{5,4,3,2,1,0:T(4,128)(2,1)S(1)}, bf16[2,2,2,2,4,1536]{5,4,3,2,1,0:T(4,128)(2,1)S(1)}, u32[]{:S(2)}, u32[]{:S(2)}) %collective-permute-start.12) | collective-permute-done | bytes 196640 | tf_op jit(solution)/shard_map/ppermute | solution.py:46
  139.4 7.0 %collective-permute-done.13 = bf16[2,2,2,2,2,4,1536]{6,5,4,3,2,1,0:T(4,128)(2,1)S(1)} collective-permute-done((bf16[2,2,2,2,2,4,1536]{6,5,4,3,2,1,0:T(4,128)(2,1)S(1)}, bf16[2,2,2,2,2,4,1536]{6,5,4,3,2,1,0:T(4,128)(2,1)S(1)}, u32[]{:S(2)}, u32[]{:S(2)}) %collective-permute-start.13) | collective-permute-done | bytes 393248 | tf_op jit(solution)/shard_map/ppermute | solution.py:46
  147.1 1.6 collective-permute-start.14
  149.5 11.9 %collective-permute-done.14 = bf16[2,2,2,2,2,2,4,1536]{7,6,5,4,3,2,1,0:T(4,128)(2,1)S(1)} collective-permute-done((bf16[2,2,2,2,2,2,4,1536]{7,6,5,4,3,2,1,0:T(4,128)(2,1)S(1)}, bf16[2,2,2,2,2,2,4,1536]{7,6,5,4,3,2,1,0:T(4,128)(2,1)S(1)}, u32[]{:S(2)}, u32[]{:S(2)}) %collective-permute-start.14) | collective-permute-done | bytes 786464 | tf_op jit(solution)/shard_map/ppermute | solution.py:46
  161.3 2.1 maximum_select_fusion.5
  163.5 1.4 constant_dynamic-slice_fusion
  167.2 4.7 %fusion.9 = bf16[2,2,2,2,2,2,2,2,4,1536]{9,8,7,1,0,3,2,5,4,6:T(4,128)(2,1)S(1)} fusion(bf16[1,2,2,2,2,2,2,2,4,1536]{9,8,7,6,5,4,3,2,1,0:T(4,128)(2,1)} %bitcast.111, bf16[1,2,2,2,2,2,2,2,4,1536]{9,8,7,6,5,4,3,2,1,0:T(4,128)(2,1)S(1)} %maximum_select_fusion.4, pred[]{:T(512)S(6)} %eq.99), kind=kLoop, calls=%fused_computation.33 | loop fusion | flops 4718592 | bytes 6291457 | tf_op jit(solution)/shard_map/transpose | solution.py:52
  171.9 1.8 copy.159
  173.7 2.5 %copy.160 = bf16[32,8,4,1536]{3,1,2,0:T(8,128)(2,1)} copy(bf16[32,8,4,1536]{3,2,1,0:T(4,128)(2,1)S(1)} %bitcast.330) | data formatting | bytes 6291456 | tf_op jit(solution)/shard_map/reshape;reshape;reshape | solution.py:238
  176.2 3.4 %gather_fusion.14 = bf16[8,8,4,1536]{3,1,2,0:T(8,128)(2,1)} fusion(bf16[32,8,4,1536]{3,1,2,0:T(8,128)(2,1)} %copy.160, s32[1024]{0:T(1024)S(1)} %pad_clamp_fusion), kind=kCustom, calls=%fused_computation.14 | custom fusion | bytes 1572896 | tf_op jit(solution)/shard_map/gather | solution.py:238
  179.6 4.1 %multiply_reduce_fusion = (f32[64,4]{0,1:T(4,128)S(1)}, f32[64,4,1536]{2,0,1:T(8,128)S(1)}) fusion(bf16[1536,1536]{1,0:T(8,128)(2,1)} %all-gather.2.cloned.1.call-done, bf16[8,8,4,1536]{3,1,2,0:T(8,128)(2,1)} %gather_fusion.14, bf16[64,4,1536]{2,1,0:T(4,128)(2,1)S(1)} %constant_dynamic-slice_fusion), kind=kOutput, calls=%fused_computation.54 | convolution fusion | flops 1209532160 | bytes 7865344 | tf_op jit(solution)/shard_map/dot_general | solution.py:242
  184.4 3.5 %fusion.42 = f32[64,4,1536]{2,0,1:T(8,128)} fusion(bf16[280,1536]{1,0:T(8,128)(2,1)S(1)} %copy-done, bf16[1536,280]{0,1:T(8,128)(2,1)} %param.17, f32[64,4,280]{2,0,1:T(8,128)S(1)} %fusion.47, f32[64,4,1536]{2,0,1:T(8,128)S(1)} %get-tuple-element.32, f32[64,4]{0,1:T(4,128)S(1)} %add_rsqrt_fusion.1), kind=kOutput, calls=%fused_computation.59 | convolution fusion | flops 441618432 | bytes 5153792 | tf_op jit(solution)/shard_map/dot_general | solution.py:249
  187.9 3.6 %copy.162 = f32[64,4,1536]{2,1,0:T(4,128)} copy(f32[64,4,1536]{2,0,1:T(8,128)} %fusion.42) | data formatting | bytes 3145728 | tf_op jit(solution)/shard_map/dot_general | solution.py:249
  191.4 1.8 reshape_reshape.8
  193.6 2.3 collective-permute-done.16
  195.9 1.3 fusion.50
  197.4 11.1 %collective-permute-done.17 = f32[8,8,1536]{2,1,0:T(8,128)S(1)} collective-permute-done((f32[8,8,1536]{2,1,0:T(8,128)S(1)}, f32[8,8,1536]{2,1,0:T(8,128)S(1)}, u32[]{:S(2)}, u32[]{:S(2)}) %collective-permute-start.17) | collective-permute-done | bytes 393248 | tf_op jit(solution)/shard_map/ppermute | solution.py:66
  208.6 1.3 collective-permute-start.18
  209.9 6.4 %collective-permute-done.18 = f32[4,8,1536]{2,1,0:T(8,128)S(1)} collective-permute-done((f32[4,8,1536]{2,1,0:T(8,128)S(1)}, f32[4,8,1536]{2,1,0:T(8,128)S(1)}, u32[]{:S(2)}, u32[]{:S(2)}) %collective-permute-start.18) | collective-permute-done | bytes 196640 | tf_op jit(solution)/shard_map/ppermute | solution.py:66
  216.6 4.5 %collective-permute-done.19 = f32[2,8,1536]{2,1,0:T(8,128)S(1)} collective-permute-done((f32[2,8,1536]{2,1,0:T(8,128)S(1)}, f32[2,8,1536]{2,1,0:T(8,128)S(1)}, u32[]{:S(2)}, u32[]{:S(2)}) %collective-permute-start.19) | collective-permute-done | bytes 98336 | tf_op jit(solution)/shard_map/ppermute | solution.py:66
  221.1 2.5 %collective-permute-start.20 = (f32[1,8,1536]{2,1,0:T(8,128)S(1)}, f32[1,8,1536]{2,1,0:T(8,128)S(1)}, u32[]{:S(2)}, u32[]{:S(2)}) collective-permute-start(f32[1,8,1536]{2,1,0:T(8,128)S(1)} %select_bitcast_fusion.6), channel_id=1, source_target_pairs={{0,16},{1,17},{2,18},{3,19},{4,20},{5,21},{6,22},{7,23},{8,24},{9,... | collective-permute-start | bytes 147464 | tf_op jit(solution)/shard_map/ppermute | solution.py:66
  223.6 3.1 %collective-permute-done.20 = f32[1,8,1536]{2,1,0:T(8,128)S(1)} collective-permute-done((f32[1,8,1536]{2,1,0:T(8,128)S(1)}, f32[1,8,1536]{2,1,0:T(8,128)S(1)}, u32[]{:S(2)}, u32[]{:S(2)}) %collective-permute-start.20) | collective-permute-done | bytes 49184 | tf_op jit(solution)/shard_map/ppermute | solution.py:66
  226.8 1.6 fusion.88
  (179 shorter events, 36.3 us)
Async XLA Ops:
  6.5 177.9 %copy-start = (bf16[280,1536]{1,0:T(8,128)(2,1)S(1)}, bf16[280,1536]{1,0:T(8,128)(2,1)}, u32[]{:S(2)}) copy-start(bf16[280,1536]{1,0:T(8,128)(2,1)} %param.18) | copy-start | bytes 2580484
  6.5 9.1 %copy-start.5 = (s32[32,8]{0,1:T(8,128)S(1)}, s32[32,8]{0,1:T(8,128)}, u32[]{:S(2)}) copy-start(s32[32,8]{0,1:T(8,128)} %param.21) | copy-start | bytes 3076
  6.5 173.1 %all-gather.2.cloned.1.call-start = ((), (), s32[]{:S(2)}) async-start(), calls=%async_computation | async-start | bytes 4866048 | tf_op jit(solution)/shard_map/all_gather | solution.py:128
  7.4 11.7 %collective-permute-start = (bf16[8,1536]{1,0:T(8,128)(2,1)S(1)}, bf16[8,1536]{1,0:T(8,128)(2,1)S(1)}, u32[]{:S(2)}, u32[]{:S(2)}) collective-permute-start(bf16[8,1536]{1,0:T(8,128)(2,1)S(1)} %reshape.1860), channel_id=1, source_target_pairs={{0,32},{1,33},{2,34},{3,35},{4,36},{5,37},{6,38},{7,39},{8,40},{9,... | collective-permute-start | bytes 73736 | tf_op jit(solution)/shard_map/ppermute | solution.py:46
  19.1 5.4 %collective-permute-start.1 = (bf16[2,8,1536]{2,1,0:T(8,128)(2,1)S(1)}, bf16[2,8,1536]{2,1,0:T(8,128)(2,1)S(1)}, u32[]{:S(2)}, u32[]{:S(2)}) collective-permute-start(bf16[2,8,1536]{2,1,0:T(8,128)(2,1)S(1)} %maximum_select_fusion.24), channel_id=1, source_target_pairs={{0,96},{1,97},{2,98},{3,99},{4,100},{5,101},{6,102},{7,103},{8,104... | collective-permute-start | bytes 147464 | tf_op jit(solution)/shard_map/ppermute | solution.py:46
  24.5 5.1 %collective-permute-start.2 = (bf16[2,2,8,1536]{3,2,1,0:T(8,128)(2,1)S(1)}, bf16[2,2,8,1536]{3,2,1,0:T(8,128)(2,1)S(1)}, u32[]{:S(2)}, u32[]{:S(2)}) collective-permute-start(bf16[2,2,8,1536]{3,2,1,0:T(8,128)(2,1)S(1)} %maximum_select_fusion.20), channel_id=1, source_target_pairs={{0,8},{1,9},{2,10},{3,11},{4,12},{5,13},{6,14},{7,15},{8,0},{9,1},... | collective-permute-start | bytes 294920 | tf_op jit(solution)/shard_map/ppermute | solution.py:46
  29.7 7.8 %collective-permute-start.3 = (bf16[2,2,2,8,1536]{4,3,2,1,0:T(8,128)(2,1)S(1)}, bf16[2,2,2,8,1536]{4,3,2,1,0:T(8,128)(2,1)S(1)}, u32[]{:S(2)}, u32[]{:S(2)}) collective-permute-start(bf16[2,2,2,8,1536]{4,3,2,1,0:T(8,128)(2,1)S(1)} %maximum_select_fusion.16), channel_id=1, source_target_pairs={{0,24},{1,25},{2,26},{3,27},{4,28},{5,29},{6,30},{7,31},{8,16},{9,... | collective-permute-start | bytes 589832 | tf_op jit(solution)/shard_map/ppermute | solution.py:46
  37.5 13.6 %collective-permute-start.4 = (bf16[2,2,2,2,8,1536]{5,4,3,2,1,0:T(8,128)(2,1)S(1)}, bf16[2,2,2,2,8,1536]{5,4,3,2,1,0:T(8,128)(2,1)S(1)}, u32[]{:S(2)}, u32[]{:S(2)}) collective-permute-start(bf16[2,2,2,2,8,1536]{5,4,3,2,1,0:T(8,128)(2,1)S(1)} %maximum_select_fusion.11), channel_id=1, source_target_pairs={{0,2},{1,3},{2,0},{3,1},{4,6},{5,7},{6,4},{7,5},{8,10},{9,11},{10,... | collective-permute-start | bytes 1179656 | tf_op jit(solution)/shard_map/ppermute | solution.py:46
  51.2 20.4 %collective-permute-start.5 = (bf16[2,2,2,2,2,8,1536]{6,5,4,3,2,1,0:T(8,128)(2,1)S(1)}, bf16[2,2,2,2,2,8,1536]{6,5,4,3,2,1,0:T(8,128)(2,1)S(1)}, u32[]{:S(2)}, u32[]{:S(2)}) collective-permute-start(bf16[2,2,2,2,2,8,1536]{6,5,4,3,2,1,0:T(8,128)(2,1)S(1)} %maximum_select_fusion.7), channel_id=1, source_target_pairs={{0,6},{1,7},{2,4},{3,5},{4,2},{5,3},{6,0},{7,1},{8,14},{9,15},{10,... | collective-permute-start | bytes 2359304 | tf_op jit(solution)/shard_map/ppermute | solution.py:46
  73.1 3.8 %collective-permute-start.6 = (bf16[2,2,2,2,2,2,8,1536]{7,6,5,4,3,2,1,0:T(8,128)(2,1)}, bf16[2,2,2,2,2,2,8,1536]{7,6,5,4,3,2,1,0:T(8,128)(2,1)}, u32[]{:S(2)}, u32[]{:S(2)}) collective-permute-start(bf16[2,2,2,2,2,2,8,1536]{7,6,5,4,3,2,1,0:T(8,128)(2,1)} %maximum_select_fusion.3), channel_id=1, source_target_pairs={{0,1},{1,0},{2,3},{3,2},{4,5},{5,4},{6,7},{7,6},{8,9},{9,8},{10,11... | collective-permute-start | bytes 4718600 | tf_op jit(solution)/shard_map/ppermute | solution.py:46
  81.4 8.2 %copy-start.4 = (f32[2048]{0:T(1024)S(1)}, f32[2048]{0:T(1024)}, u32[]{:S(2)}) copy-start(f32[2048]{0:T(1024)} %param.14) | copy-start | bytes 24580
  89.5 4.3 %copy-start.2 = (bf16[2,4096,256]{2,1,0:T(8,128)(2,1)S(1)}, bf16[2,4096,256]{2,1,0:T(8,128)(2,1)}, u32[]{:S(2)}) copy-start(bf16[2,4096,256]{2,1,0:T(8,128)(2,1)} %param.19) | copy-start | bytes 12582916
  102.6 2.2 copy-start.6
  108.5 1.6 collective-permute-start.7
  110.2 5.6 %collective-permute-start.8 = (f32[1,2,4,2,6,130]{5,4,3,2,1,0:T(8,128)S(1)}, f32[1,2,4,2,6,130]{5,4,3,2,1,0:T(8,128)S(1)}, u32[]{:S(2)}, u32[]{:S(2)}) collective-permute-start(f32[1,2,4,2,6,130]{5,4,3,2,1,0:T(8,128)S(1)} %select_bitcast_fusion.4), channel_id=1, source_target_pairs={{0,2},{1,3},{2,0},{3,1},{4,6},{5,7},{6,4},{7,5},{8,10},{9,11},{10,... | collective-permute-start | bytes 149768 | tf_op jit(solution)/shard_map/ppermute | solution.py:66
  116.9 4.1 %collective-permute-start.9 = (bf16[2,4,1536]{2,1,0:T(4,128)(2,1)S(1)}, bf16[2,4,1536]{2,1,0:T(4,128)(2,1)S(1)}, u32[]{:S(2)}, u32[]{:S(2)}) collective-permute-start(bf16[2,4,1536]{2,1,0:T(4,128)(2,1)S(1)} %convert_element_type.87), channel_id=1, source_target_pairs={{0,32},{1,33},{2,34},{3,35},{4,36},{5,37},{6,38},{7,39},{8,40},{9,... | collective-permute-start | bytes 73736 | tf_op jit(solution)/shard_map/ppermute | solution.py:46
  121.1 5.4 %collective-permute-start.10 = (bf16[2,2,4,1536]{3,2,1,0:T(4,128)(2,1)S(1)}, bf16[2,2,4,1536]{3,2,1,0:T(4,128)(2,1)S(1)}, u32[]{:S(2)}, u32[]{:S(2)}) collective-permute-start(bf16[2,2,4,1536]{3,2,1,0:T(4,128)(2,1)S(1)} %maximum_select_fusion.26), channel_id=1, source_target_pairs={{0,96},{1,97},{2,98},{3,99},{4,100},{5,101},{6,102},{7,103},{8,104... | collective-permute-start | bytes 147464 | tf_op jit(solution)/shard_map/ppermute | solution.py:46
  126.5 4.7 %collective-permute-start.11 = (bf16[2,2,2,4,1536]{4,3,2,1,0:T(4,128)(2,1)S(1)}, bf16[2,2,2,4,1536]{4,3,2,1,0:T(4,128)(2,1)S(1)}, u32[]{:S(2)}, u32[]{:S(2)}) collective-permute-start(bf16[2,2,2,4,1536]{4,3,2,1,0:T(4,128)(2,1)S(1)} %maximum_select_fusion.22), channel_id=1, source_target_pairs={{0,8},{1,9},{2,10},{3,11},{4,12},{5,13},{6,14},{7,15},{8,0},{9,1},... | collective-permute-start | bytes 294920 | tf_op jit(solution)/shard_map/ppermute | solution.py:46
  131.4 7.0 %collective-permute-start.12 = (bf16[2,2,2,2,4,1536]{5,4,3,2,1,0:T(4,128)(2,1)S(1)}, bf16[2,2,2,2,4,1536]{5,4,3,2,1,0:T(4,128)(2,1)S(1)}, u32[]{:S(2)}, u32[]{:S(2)}) collective-permute-start(bf16[2,2,2,2,4,1536]{5,4,3,2,1,0:T(4,128)(2,1)S(1)} %maximum_select_fusion.18), channel_id=1, source_target_pairs={{0,24},{1,25},{2,26},{3,27},{4,28},{5,29},{6,30},{7,31},{8,16},{9,... | collective-permute-start | bytes 589832 | tf_op jit(solution)/shard_map/ppermute | solution.py:46
  138.6 7.9 %collective-permute-start.13 = (bf16[2,2,2,2,2,4,1536]{6,5,4,3,2,1,0:T(4,128)(2,1)S(1)}, bf16[2,2,2,2,2,4,1536]{6,5,4,3,2,1,0:T(4,128)(2,1)S(1)}, u32[]{:S(2)}, u32[]{:S(2)}) collective-permute-start(bf16[2,2,2,2,2,4,1536]{6,5,4,3,2,1,0:T(4,128)(2,1)S(1)} %maximum_select_fusion.14), channel_id=1, source_target_pairs={{0,2},{1,3},{2,0},{3,1},{4,6},{5,7},{6,4},{7,5},{8,10},{9,11},{10,... | collective-permute-start | bytes 1179656 | tf_op jit(solution)/shard_map/ppermute | solution.py:46
  147.0 16.4 %copy-start.7 = (s32[32]{0:T(128)S(1)}, s32[32]{0:T(128)}, u32[]{:S(2)}) copy-start(s32[32]{0:T(128)} %param.23) | copy-start | bytes 388
  147.1 14.3 %collective-permute-start.14 = (bf16[2,2,2,2,2,2,4,1536]{7,6,5,4,3,2,1,0:T(4,128)(2,1)S(1)}, bf16[2,2,2,2,2,2,4,1536]{7,6,5,4,3,2,1,0:T(4,128)(2,1)S(1)}, u32[]{:S(2)}, u32[]{:S(2)}) collective-permute-start(bf16[2,2,2,2,2,2,4,1536]{7,6,5,4,3,2,1,0:T(4,128)(2,1)S(1)} %maximum_select_fusion.9), channel_id=1, source_target_pairs={{0,6},{1,7},{2,4},{3,5},{4,2},{5,3},{6,0},{7,1},{8,14},{9,15},{10,... | collective-permute-start | bytes 2359304 | tf_op jit(solution)/shard_map/ppermute | solution.py:46
  163.4 3.8 %collective-permute-start.15 = (bf16[2,2,2,2,2,2,2,4,1536]{8,7,6,5,4,3,2,1,0:T(4,128)(2,1)}, bf16[2,2,2,2,2,2,2,4,1536]{8,7,6,5,4,3,2,1,0:T(4,128)(2,1)}, u32[]{:S(2)}, u32[]{:S(2)}) collective-permute-start(bf16[2,2,2,2,2,2,2,4,1536]{8,7,6,5,4,3,2,1,0:T(4,128)(2,1)} %maximum_select_fusion.5), channel_id=1, source_target_pairs={{0,1},{1,0},{2,3},{3,2},{4,5},{5,4},{6,7},{7,6},{8,9},{9,8},{10,11... | collective-permute-start | bytes 4718600 | tf_op jit(solution)/shard_map/ppermute | solution.py:46
  179.6 4.2 %copy-start.3 = (bf16[1536,280]{0,1:T(8,128)(2,1)S(1)}, bf16[1536,280]{0,1:T(8,128)(2,1)}, u32[]{:S(2)}) copy-start(bf16[1536,280]{0,1:T(8,128)(2,1)} %param.16) | copy-start | bytes 2580484
  183.8 4.1 %copy-start.1 = (f32[64,4,1536]{2,0,1:T(8,128)}, f32[64,4,1536]{2,0,1:T(8,128)S(1)}, u32[]{:S(2)}) copy-start(f32[64,4,1536]{2,0,1:T(8,128)S(1)} %get-tuple-element.32) | copy-start | bytes 4718596
  193.4 2.5 %collective-permute-start.16 = (f32[16,8,1536]{2,1,0:T(8,128)S(1)}, f32[16,8,1536]{2,1,0:T(8,128)}, u32[]{:S(2)}, u32[]{:S(2)}) collective-permute-start(f32[16,8,1536]{2,1,0:T(8,128)S(1)} %select_bitcast_fusion), channel_id=1, source_target_pairs={{0,1},{1,0},{2,3},{3,2},{4,5},{5,4},{6,7},{7,6},{8,9},{9,8},{10,11... | collective-permute-start | bytes 2359304 | tf_op jit(solution)/shard_map/ppermute | solution.py:66
  197.3 11.2 %collective-permute-start.17 = (f32[8,8,1536]{2,1,0:T(8,128)S(1)}, f32[8,8,1536]{2,1,0:T(8,128)S(1)}, u32[]{:S(2)}, u32[]{:S(2)}) collective-permute-start(f32[8,8,1536]{2,1,0:T(8,128)S(1)} %select_bitcast_fusion.1), channel_id=1, source_target_pairs={{0,2},{1,3},{2,0},{3,1},{4,6},{5,7},{6,4},{7,5},{8,10},{9,11},{10,... | collective-permute-start | bytes 1179656 | tf_op jit(solution)/shard_map/ppermute | solution.py:66
  208.6 7.7 %collective-permute-start.18 = (f32[4,8,1536]{2,1,0:T(8,128)S(1)}, f32[4,8,1536]{2,1,0:T(8,128)S(1)}, u32[]{:S(2)}, u32[]{:S(2)}) collective-permute-start(f32[4,8,1536]{2,1,0:T(8,128)S(1)} %select_bitcast_fusion.3), channel_id=1, source_target_pairs={{0,4},{1,5},{2,6},{3,7},{4,0},{5,1},{6,2},{7,3},{8,12},{9,13},{10,... | collective-permute-start | bytes 589832 | tf_op jit(solution)/shard_map/ppermute | solution.py:66
  216.3 4.7 %collective-permute-start.19 = (f32[2,8,1536]{2,1,0:T(8,128)S(1)}, f32[2,8,1536]{2,1,0:T(8,128)S(1)}, u32[]{:S(2)}, u32[]{:S(2)}) collective-permute-start(f32[2,8,1536]{2,1,0:T(8,128)S(1)} %select_bitcast_fusion.5), channel_id=1, source_target_pairs={{0,8},{1,9},{2,10},{3,11},{4,12},{5,13},{6,14},{7,15},{8,0},{9,1},... | collective-permute-start | bytes 294920 | tf_op jit(solution)/shard_map/ppermute | solution.py:66
  221.1 5.7 %collective-permute-start.20 = (f32[1,8,1536]{2,1,0:T(8,128)S(1)}, f32[1,8,1536]{2,1,0:T(8,128)S(1)}, u32[]{:S(2)}, u32[]{:S(2)}) collective-permute-start(f32[1,8,1536]{2,1,0:T(8,128)S(1)} %select_bitcast_fusion.6), channel_id=1, source_target_pairs={{0,16},{1,17},{2,18},{3,19},{4,20},{5,21},{6,22},{7,23},{8,24},{9,... | collective-permute-start | bytes 147464 | tf_op jit(solution)/shard_map/ppermute | solution.py:66
Sparse Core Ops, SparseCore 0:
  9.6 53.4 all-gather.1

commit v9 on v8

--- a/solution.py
+++ b/solution.py
@@ -125,7 +125,8 @@
     x_all = gather_rounds(
         jnp.swapaxes(step_inputs, 0, 1).reshape(rows_dev * steps, width), ALL, flat, flat_masks
     ).reshape(requests * beams, steps, width)
-    full_out = lax.all_gather(out_weight, TP, axis=0, tiled=True)
+    after_rows = (x_all[0, 0, 0] * 0).astype(out_weight.dtype)
+    full_out = lax.all_gather(out_weight + after_rows, TP, axis=0, tiled=True)
     x_req = lax.dynamic_slice_in_dim(x_all, inverse[r] * beams, beams, 0)
     x_group = lax.dynamic_slice_in_dim(x_all, req_index * group_rows, group_rows, 0)
 

time: 236 us -> 237 us (level)
  transfers between devices with their start and end apart: 22 -> 22, of which waited for: 20 -> 20; matrix products, arithmetic and copies ran while one was open for 29% -> 16% of each run, Pallas kernels for 0% -> 0%
where the time goes in v9:
time: 237 us; the launch traced here: 236 us
  waiting for transfers between devices  103 us (43%)
  local copies, waits for them, and re-layouts  41.1 us (17%)
  other arithmetic  31.3 us (13%)
  starting transfers between devices  27.7 us (12%)
  matrix products  16.8 us (7%)
  between operations  15.7 us (7%)
    ppermute x14, waiting for transfers between devices, gather_rounds(): recv = lax.ppermute(buf, axes, perm)  70 us
    ppermute x7, waiting for transfers between devices, scatter_rounds(): buf = keep + lax.ppermute(send, axes, perm)  33.4 us
    ppermute x14, starting transfers between devices, gather_rounds(): recv = lax.ppermute(buf, axes, perm)  24.2 us
    select_n x24, other arithmetic, gather_rounds(): buf = jnp.where(mine == 0, jnp.stack([buf, recv]), jnp.stack([recv, buf]))  7.61 us
    transpose x2, other arithmetic, gather_rounds(): buf = jnp.transpose(buf, tuple(order) + tuple(range(depth, buf.ndim)))  7 us
    another operation x1, local copies, waits for them, and re-layouts, per_device(): x_all = gather_rounds(jnp.swapaxes(step_inputs, 0, 1).reshape(rows_dev *...  6.14 us
  transfers between devices with their start and end apart: 22, of which 20 were waited for; matrix products, arithmetic and copies ran while one was open for 16% of the time, Pallas kernels for 0%

profile of v9, /device:TPU:0, one launch (start us, length us, event | category | flops | bytes accessed | tf_op | source)
XLA Modules:
  0.0 236.0 jit_solution(17524776015158971671)
XLA Ops:
  7.4 1.7 collective-permute-start
  19.1 2.2 collective-permute-start.1
  21.3 3.2 %collective-permute-done.1 = bf16[2,8,1536]{2,1,0:T(8,128)(2,1)S(1)} collective-permute-done((bf16[2,8,1536]{2,1,0:T(8,128)(2,1)S(1)}, bf16[2,8,1536]{2,1,0:T(8,128)(2,1)S(1)}, u32[]{:S(2)}, u32[]{:S(2)}) %collective-permute-start.1) | collective-permute-done | bytes 49184 | tf_op jit(solution)/shard_map/ppermute | solution.py:46
  24.5 2.0 collective-permute-start.2
  26.5 2.7 %collective-permute-done.2 = bf16[2,2,8,1536]{3,2,1,0:T(8,128)(2,1)S(1)} collective-permute-done((bf16[2,2,8,1536]{3,2,1,0:T(8,128)(2,1)S(1)}, bf16[2,2,8,1536]{3,2,1,0:T(8,128)(2,1)S(1)}, u32[]{:S(2)}, u32[]{:S(2)}) %collective-permute-start.2) | collective-permute-done | bytes 98336 | tf_op jit(solution)/shard_map/ppermute | solution.py:46
  29.2 4.1 %collective-permute-start.3 = (bf16[2,2,2,8,1536]{4,3,2,1,0:T(8,128)(2,1)S(1)}, bf16[2,2,2,8,1536]{4,3,2,1,0:T(8,128)(2,1)S(1)}, u32[]{:S(2)}, u32[]{:S(2)}) collective-permute-start(bf16[2,2,2,8,1536]{4,3,2,1,0:T(8,128)(2,1)S(1)} %maximum_select_fusion.16), channel_id=1, source_target_pairs={{0,24},{1,25},{2,26},{3,27},{4,28},{5,29},{6,30},{7,31},{8,16},{9,... | collective-permute-start | bytes 589832 | tf_op jit(solution)/shard_map/ppermute | solution.py:46
  33.3 3.6 %collective-permute-done.3 = bf16[2,2,2,8,1536]{4,3,2,1,0:T(8,128)(2,1)S(1)} collective-permute-done((bf16[2,2,2,8,1536]{4,3,2,1,0:T(8,128)(2,1)S(1)}, bf16[2,2,2,8,1536]{4,3,2,1,0:T(8,128)(2,1)S(1)}, u32[]{:S(2)}, u32[]{:S(2)}) %collective-permute-start.3) | collective-permute-done | bytes 196640 | tf_op jit(solution)/shard_map/ppermute | solution.py:46
  37.0 1.7 collective-permute-start.4
  38.7 6.1 %collective-permute-done.4 = bf16[2,2,2,2,8,1536]{5,4,3,2,1,0:T(8,128)(2,1)S(1)} collective-permute-done((bf16[2,2,2,2,8,1536]{5,4,3,2,1,0:T(8,128)(2,1)S(1)}, bf16[2,2,2,2,8,1536]{5,4,3,2,1,0:T(8,128)(2,1)S(1)}, u32[]{:S(2)}, u32[]{:S(2)}) %collective-permute-start.4) | collective-permute-done | bytes 393248 | tf_op jit(solution)/shard_map/ppermute | solution.py:46
  45.0 3.1 %collective-permute-start.5 = (bf16[2,2,2,2,2,8,1536]{6,5,4,3,2,1,0:T(8,128)(2,1)S(1)}, bf16[2,2,2,2,2,8,1536]{6,5,4,3,2,1,0:T(8,128)(2,1)S(1)}, u32[]{:S(2)}, u32[]{:S(2)}) collective-permute-start(bf16[2,2,2,2,2,8,1536]{6,5,4,3,2,1,0:T(8,128)(2,1)S(1)} %maximum_select_fusion.7), channel_id=1, source_target_pairs={{0,6},{1,7},{2,4},{3,5},{4,2},{5,3},{6,0},{7,1},{8,14},{9,15},{10,... | collective-permute-start | bytes 2359304 | tf_op jit(solution)/shard_map/ppermute | solution.py:46
  48.5 12.5 %collective-permute-done.5 = bf16[2,2,2,2,2,8,1536]{6,5,4,3,2,1,0:T(8,128)(2,1)S(1)} collective-permute-done((bf16[2,2,2,2,2,8,1536]{6,5,4,3,2,1,0:T(8,128)(2,1)S(1)}, bf16[2,2,2,2,2,8,1536]{6,5,4,3,2,1,0:T(8,128)(2,1)S(1)}, u32[]{:S(2)}, u32[]{:S(2)}) %collective-permute-start.5) | collective-permute-done | bytes 786464 | tf_op jit(solution)/shard_map/ppermute | solution.py:46
  61.0 1.4 maximum_select_fusion.3
  66.2 2.3 fusion.8
  68.5 2.1 copy.131
  70.7 6.1 %reshape_reshape.7 = bf16[256,4,1536]{2,1,0:T(4,128)(2,1)} reshape(bf16[2,2,2,2,2,2,2,8,1536]{8,7,6,5,4,3,2,1,0:T(8,128)(2,1)} %copy.131) | data formatting | bytes 6291456 | tf_op jit(solution)/shard_map/reshape;reshape | solution.py:127
  78.9 4.1 %fusion.20 = bf16[8,4,2048]{2,0,1:T(8,128)(2,1)S(1)} fusion(bf16[1536,2048]{1,0:T(8,128)(2,1)} %param.13, f32[2048]{0:T(1024)S(1)} %copy-done.5, bf16[8,4,1536]{2,1,0:T(4,128)(2,1)S(1)} %fusion.63), kind=kOutput, calls=%fused_computation.40 | convolution fusion | flops 201457664 | bytes 6529024 | tf_op jit(solution)/shard_map/dot_general | solution.py:135
  86.3 2.1 fusion.5
  88.5 4.6 %fusion.2 = (bf16[2,8,4,2,6,4096]{5,1,0,4,2,3:T(8,128)(2,1)S(1)}, f32[2,8,4,2,6]{1,0,4,2,3:T(2,128)S(1)}) fusion(f32[2,8,4,2,6]{1,0,4,2,3:T(2,128)S(1)} %fusion.5, pred[2,4096]{1,0:T(4,128)(4,1)S(1)} %iota_compare_fusion, f32[2,8,4,1,6,4096]{5,1,0,4,2,3:T(8,128)S(1)} %convolution_bitcast_fusion, f32[2,8,4,1,6,4096]{5,1,0,4,2,3:T(8,128)S(1)} %convolution_bitcast_fusion.1), kind=kLoop, calls=%fused_computation.20 | loop fusion | flops 22019328 | bytes 18888704 | tf_op jit(solution)/shard_map/convert_element_type | solution.py:172
  93.9 1.4 copy-done.7
  103.5 4.2 %collective-permute-done.8 = f32[1,2,4,2,6,130]{5,4,3,2,1,0:T(8,128)S(1)} collective-permute-done((f32[1,2,4,2,6,130]{5,4,3,2,1,0:T(8,128)S(1)}, f32[1,2,4,2,6,130]{5,4,3,2,1,0:T(8,128)S(1)}, u32[]{:S(2)}, u32[]{:S(2)}) %collective-permute-start.8) | collective-permute-done | bytes 49952 | tf_op jit(solution)/shard_map/ppermute | solution.py:66
  109.1 3.8 %collective-permute-done.9 = bf16[2,4,1536]{2,1,0:T(4,128)(2,1)S(1)} collective-permute-done((bf16[2,4,1536]{2,1,0:T(4,128)(2,1)S(1)}, bf16[2,4,1536]{2,1,0:T(4,128)(2,1)S(1)}, u32[]{:S(2)}, u32[]{:S(2)}) %collective-permute-start.9) | collective-permute-done | bytes 24608 | tf_op jit(solution)/shard_map/ppermute | solution.py:46
  112.9 2.2 collective-permute-start.10
  115.2 3.1 %collective-permute-done.10 = bf16[2,2,4,1536]{3,2,1,0:T(4,128)(2,1)S(1)} collective-permute-done((bf16[2,2,4,1536]{3,2,1,0:T(4,128)(2,1)S(1)}, bf16[2,2,4,1536]{3,2,1,0:T(4,128)(2,1)S(1)}, u32[]{:S(2)}, u32[]{:S(2)}) %collective-permute-start.10) | collective-permute-done | bytes 49184 | tf_op jit(solution)/shard_map/ppermute | solution.py:46
  118.6 4.6 %collective-permute-done.11 = bf16[2,2,2,4,1536]{4,3,2,1,0:T(4,128)(2,1)S(1)} collective-permute-done((bf16[2,2,2,4,1536]{4,3,2,1,0:T(4,128)(2,1)S(1)}, bf16[2,2,2,4,1536]{4,3,2,1,0:T(4,128)(2,1)S(1)}, u32[]{:S(2)}, u32[]{:S(2)}) %collective-permute-start.11) | collective-permute-done | bytes 98336 | tf_op jit(solution)/shard_map/ppermute | solution.py:46
  123.4 2.9 %collective-permute-start.12 = (bf16[2,2,2,2,4,1536]{5,4,3,2,1,0:T(4,128)(2,1)S(1)}, bf16[2,2,2,2,4,1536]{5,4,3,2,1,0:T(4,128)(2,1)S(1)}, u32[]{:S(2)}, u32[]{:S(2)}) collective-permute-start(bf16[2,2,2,2,4,1536]{5,4,3,2,1,0:T(4,128)(2,1)S(1)} %maximum_select_fusion.18), channel_id=1, source_target_pairs={{0,24},{1,25},{2,26},{3,27},{4,28},{5,29},{6,30},{7,31},{8,16},{9,... | collective-permute-start | bytes 589832 | tf_op jit(solution)/shard_map/ppermute | solution.py:46
  126.4 3.9 %collective-permute-done.12 = bf16[2,2,2,2,4,1536]{5,4,3,2,1,0:T(4,128)(2,1)S(1)} collective-permute-done((bf16[2,2,2,2,4,1536]{5,4,3,2,1,0:T(4,128)(2,1)S(1)}, bf16[2,2,2,2,4,1536]{5,4,3,2,1,0:T(4,128)(2,1)S(1)}, u32[]{:S(2)}, u32[]{:S(2)}) %collective-permute-start.12) | collective-permute-done | bytes 196640 | tf_op jit(solution)/shard_map/ppermute | solution.py:46
  131.7 14.7 %collective-permute-done.13 = bf16[2,2,2,2,2,4,1536]{6,5,4,3,2,1,0:T(4,128)(2,1)S(1)} collective-permute-done((bf16[2,2,2,2,2,4,1536]{6,5,4,3,2,1,0:T(4,128)(2,1)S(1)}, bf16[2,2,2,2,2,4,1536]{6,5,4,3,2,1,0:T(4,128)(2,1)S(1)}, u32[]{:S(2)}, u32[]{:S(2)}) %collective-permute-start.13) | collective-permute-done | bytes 393248 | tf_op jit(solution)/shard_map/ppermute | solution.py:46
  146.9 3.4 %collective-permute-start.14 = (bf16[2,2,2,2,2,2,4,1536]{7,6,5,4,3,2,1,0:T(4,128)(2,1)S(1)}, bf16[2,2,2,2,2,2,4,1536]{7,6,5,4,3,2,1,0:T(4,128)(2,1)S(1)}, u32[]{:S(2)}, u32[]{:S(2)}) collective-permute-start(bf16[2,2,2,2,2,2,4,1536]{7,6,5,4,3,2,1,0:T(4,128)(2,1)S(1)} %maximum_select_fusion.9), channel_id=1, source_target_pairs={{0,6},{1,7},{2,4},{3,5},{4,2},{5,3},{6,0},{7,1},{8,14},{9,15},{10,... | collective-permute-start | bytes 2359304 | tf_op jit(solution)/shard_map/ppermute | solution.py:46
  151.2 10.9 %collective-permute-done.14 = bf16[2,2,2,2,2,2,4,1536]{7,6,5,4,3,2,1,0:T(4,128)(2,1)S(1)} collective-permute-done((bf16[2,2,2,2,2,2,4,1536]{7,6,5,4,3,2,1,0:T(4,128)(2,1)S(1)}, bf16[2,2,2,2,2,2,4,1536]{7,6,5,4,3,2,1,0:T(4,128)(2,1)S(1)}, u32[]{:S(2)}, u32[]{:S(2)}) %collective-permute-start.14) | collective-permute-done | bytes 786464 | tf_op jit(solution)/shard_map/ppermute | solution.py:46
  162.2 2.1 maximum_select_fusion.5
  164.4 1.4 constant_dynamic-slice_fusion
  168.0 4.7 %fusion.9 = bf16[2,2,2,2,2,2,2,2,4,1536]{9,8,7,1,0,3,2,5,4,6:T(4,128)(2,1)S(1)} fusion(bf16[1,2,2,2,2,2,2,2,4,1536]{9,8,7,6,5,4,3,2,1,0:T(4,128)(2,1)} %bitcast.111, bf16[1,2,2,2,2,2,2,2,4,1536]{9,8,7,6,5,4,3,2,1,0:T(4,128)(2,1)S(1)} %maximum_select_fusion.4, pred[]{:T(512)S(6)} %eq.99), kind=kLoop, calls=%fused_computation.33 | loop fusion | flops 4718592 | bytes 6291457 | tf_op jit(solution)/shard_map/transpose | solution.py:52
  172.7 1.8 copy.159
  174.5 2.5 %copy.160 = bf16[32,8,4,1536]{3,1,2,0:T(8,128)(2,1)} copy(bf16[32,8,4,1536]{3,2,1,0:T(4,128)(2,1)S(1)} %bitcast.331) | data formatting | bytes 6291456 | tf_op jit(solution)/shard_map/reshape;reshape;reshape | solution.py:239
  177.0 3.4 %gather_fusion.14 = bf16[8,8,4,1536]{3,1,2,0:T(8,128)(2,1)} fusion(bf16[32,8,4,1536]{3,1,2,0:T(8,128)(2,1)} %copy.160, s32[1024]{0:T(1024)S(1)} %pad_clamp_fusion), kind=kCustom, calls=%fused_computation.14 | custom fusion | bytes 1572896 | tf_op jit(solution)/shard_map/gather | solution.py:239
  180.4 4.1 %multiply_reduce_fusion = (f32[64,4]{0,1:T(4,128)S(1)}, f32[64,4,1536]{2,0,1:T(8,128)S(1)}) fusion(bf16[1536,1536]{1,0:T(8,128)(2,1)} %all-gather.2.cloned.1.call-done, bf16[8,8,4,1536]{3,1,2,0:T(8,128)(2,1)} %gather_fusion.14, bf16[64,4,1536]{2,1,0:T(4,128)(2,1)S(1)} %constant_dynamic-slice_fusion), kind=kOutput, calls=%fused_computation.54 | convolution fusion | flops 1209532160 | bytes 7865344 | tf_op jit(solution)/shard_map/dot_general | solution.py:243
  185.2 3.5 %fusion.42 = f32[64,4,1536]{2,0,1:T(8,128)} fusion(bf16[280,1536]{1,0:T(8,128)(2,1)S(1)} %copy-done, bf16[1536,280]{0,1:T(8,128)(2,1)} %param.17, f32[64,4,280]{2,0,1:T(8,128)S(1)} %fusion.47, f32[64,4,1536]{2,0,1:T(8,128)S(1)} %get-tuple-element.32, f32[64,4]{0,1:T(4,128)S(1)} %add_rsqrt_fusion.1), kind=kOutput, calls=%fused_computation.59 | convolution fusion | flops 441618432 | bytes 5153792 | tf_op jit(solution)/shard_map/dot_general | solution.py:250
  188.7 3.6 %copy.162 = f32[64,4,1536]{2,1,0:T(4,128)} copy(f32[64,4,1536]{2,0,1:T(8,128)} %fusion.42) | data formatting | bytes 3145728 | tf_op jit(solution)/shard_map/dot_general | solution.py:250
  192.3 1.8 reshape_reshape.8
  194.4 2.3 collective-permute-done.16
  196.7 1.3 fusion.50
  198.3 11.1 %collective-permute-done.17 = f32[8,8,1536]{2,1,0:T(8,128)S(1)} collective-permute-done((f32[8,8,1536]{2,1,0:T(8,128)S(1)}, f32[8,8,1536]{2,1,0:T(8,128)S(1)}, u32[]{:S(2)}, u32[]{:S(2)}) %collective-permute-start.17) | collective-permute-done | bytes 393248 | tf_op jit(solution)/shard_map/ppermute | solution.py:66
  209.4 1.2 collective-permute-start.18
  210.6 6.5 %collective-permute-done.18 = f32[4,8,1536]{2,1,0:T(8,128)S(1)} collective-permute-done((f32[4,8,1536]{2,1,0:T(8,128)S(1)}, f32[4,8,1536]{2,1,0:T(8,128)S(1)}, u32[]{:S(2)}, u32[]{:S(2)}) %collective-permute-start.18) | collective-permute-done | bytes 196640 | tf_op jit(solution)/shard_map/ppermute | solution.py:66
  217.3 4.6 %collective-permute-done.19 = f32[2,8,1536]{2,1,0:T(8,128)S(1)} collective-permute-done((f32[2,8,1536]{2,1,0:T(8,128)S(1)}, f32[2,8,1536]{2,1,0:T(8,128)S(1)}, u32[]{:S(2)}, u32[]{:S(2)}) %collective-permute-start.19) | collective-permute-done | bytes 98336 | tf_op jit(solution)/shard_map/ppermute | solution.py:66
  221.9 1.3 collective-permute-start.20
  223.2 4.4 %collective-permute-done.20 = f32[1,8,1536]{2,1,0:T(8,128)S(1)} collective-permute-done((f32[1,8,1536]{2,1,0:T(8,128)S(1)}, f32[1,8,1536]{2,1,0:T(8,128)S(1)}, u32[]{:S(2)}, u32[]{:S(2)}) %collective-permute-start.20) | collective-permute-done | bytes 49184 | tf_op jit(solution)/shard_map/ppermute | solution.py:66
  227.6 1.6 fusion.88
  (183 shorter events, 36.5 us)
Async XLA Ops:
  6.5 178.7 %copy-start = (bf16[280,1536]{1,0:T(8,128)(2,1)S(1)}, bf16[280,1536]{1,0:T(8,128)(2,1)}, u32[]{:S(2)}) copy-start(bf16[280,1536]{1,0:T(8,128)(2,1)} %param.18) | copy-start | bytes 2580484
  6.5 9.0 %copy-start.6 = (s32[32,8]{0,1:T(8,128)S(1)}, s32[32,8]{0,1:T(8,128)}, u32[]{:S(2)}) copy-start(s32[32,8]{0,1:T(8,128)} %param.21) | copy-start | bytes 3076
  6.5 173.9 %all-gather.2.cloned.1.call-start = ((), (), s32[]{:S(2)}) async-start(), calls=%async_computation | async-start | bytes 4866048 | tf_op jit(solution)/shard_map/all_gather | solution.py:129
  7.4 11.6 %collective-permute-start = (bf16[8,1536]{1,0:T(8,128)(2,1)S(1)}, bf16[8,1536]{1,0:T(8,128)(2,1)S(1)}, u32[]{:S(2)}, u32[]{:S(2)}) collective-permute-start(bf16[8,1536]{1,0:T(8,128)(2,1)S(1)} %reshape.1862), channel_id=1, source_target_pairs={{0,32},{1,33},{2,34},{3,35},{4,36},{5,37},{6,38},{7,39},{8,40},{9,... | collective-permute-start | bytes 73736 | tf_op jit(solution)/shard_map/ppermute | solution.py:46
  19.1 5.4 %collective-permute-start.1 = (bf16[2,8,1536]{2,1,0:T(8,128)(2,1)S(1)}, bf16[2,8,1536]{2,1,0:T(8,128)(2,1)S(1)}, u32[]{:S(2)}, u32[]{:S(2)}) collective-permute-start(bf16[2,8,1536]{2,1,0:T(8,128)(2,1)S(1)} %maximum_select_fusion.24), channel_id=1, source_target_pairs={{0,96},{1,97},{2,98},{3,99},{4,100},{5,101},{6,102},{7,103},{8,104... | collective-permute-start | bytes 147464 | tf_op jit(solution)/shard_map/ppermute | solution.py:46
  24.5 4.7 %collective-permute-start.2 = (bf16[2,2,8,1536]{3,2,1,0:T(8,128)(2,1)S(1)}, bf16[2,2,8,1536]{3,2,1,0:T(8,128)(2,1)S(1)}, u32[]{:S(2)}, u32[]{:S(2)}) collective-permute-start(bf16[2,2,8,1536]{3,2,1,0:T(8,128)(2,1)S(1)} %maximum_select_fusion.20), channel_id=1, source_target_pairs={{0,8},{1,9},{2,10},{3,11},{4,12},{5,13},{6,14},{7,15},{8,0},{9,1},... | collective-permute-start | bytes 294920 | tf_op jit(solution)/shard_map/ppermute | solution.py:46
  29.2 7.8 %collective-permute-start.3 = (bf16[2,2,2,8,1536]{4,3,2,1,0:T(8,128)(2,1)S(1)}, bf16[2,2,2,8,1536]{4,3,2,1,0:T(8,128)(2,1)S(1)}, u32[]{:S(2)}, u32[]{:S(2)}) collective-permute-start(bf16[2,2,2,8,1536]{4,3,2,1,0:T(8,128)(2,1)S(1)} %maximum_select_fusion.16), channel_id=1, source_target_pairs={{0,24},{1,25},{2,26},{3,27},{4,28},{5,29},{6,30},{7,31},{8,16},{9,... | collective-permute-start | bytes 589832 | tf_op jit(solution)/shard_map/ppermute | solution.py:46
  37.0 7.9 %collective-permute-start.4 = (bf16[2,2,2,2,8,1536]{5,4,3,2,1,0:T(8,128)(2,1)S(1)}, bf16[2,2,2,2,8,1536]{5,4,3,2,1,0:T(8,128)(2,1)S(1)}, u32[]{:S(2)}, u32[]{:S(2)}) collective-permute-start(bf16[2,2,2,2,8,1536]{5,4,3,2,1,0:T(8,128)(2,1)S(1)} %maximum_select_fusion.11), channel_id=1, source_target_pairs={{0,2},{1,3},{2,0},{3,1},{4,6},{5,7},{6,4},{7,5},{8,10},{9,11},{10,... | collective-permute-start | bytes 1179656 | tf_op jit(solution)/shard_map/ppermute | solution.py:46
  45.0 16.0 %collective-permute-start.5 = (bf16[2,2,2,2,2,8,1536]{6,5,4,3,2,1,0:T(8,128)(2,1)S(1)}, bf16[2,2,2,2,2,8,1536]{6,5,4,3,2,1,0:T(8,128)(2,1)S(1)}, u32[]{:S(2)}, u32[]{:S(2)}) collective-permute-start(bf16[2,2,2,2,2,8,1536]{6,5,4,3,2,1,0:T(8,128)(2,1)S(1)} %maximum_select_fusion.7), channel_id=1, source_target_pairs={{0,6},{1,7},{2,4},{3,5},{4,2},{5,3},{6,0},{7,1},{8,14},{9,15},{10,... | collective-permute-start | bytes 2359304 | tf_op jit(solution)/shard_map/ppermute | solution.py:46
  62.4 3.8 %collective-permute-start.6 = (bf16[2,2,2,2,2,2,8,1536]{7,6,5,4,3,2,1,0:T(8,128)(2,1)}, bf16[2,2,2,2,2,2,8,1536]{7,6,5,4,3,2,1,0:T(8,128)(2,1)}, u32[]{:S(2)}, u32[]{:S(2)}) collective-permute-start(bf16[2,2,2,2,2,2,8,1536]{7,6,5,4,3,2,1,0:T(8,128)(2,1)} %maximum_select_fusion.3), channel_id=1, source_target_pairs={{0,1},{1,0},{2,3},{3,2},{4,5},{5,4},{6,7},{7,6},{8,9},{9,8},{10,11... | collective-permute-start | bytes 4718600 | tf_op jit(solution)/shard_map/ppermute | solution.py:46
  70.7 8.2 %copy-start.5 = (f32[2048]{0:T(1024)S(1)}, f32[2048]{0:T(1024)}, u32[]{:S(2)}) copy-start(f32[2048]{0:T(1024)} %param.14) | copy-start | bytes 24580
  78.9 4.3 %copy-start.2 = (bf16[2,4096,256]{2,1,0:T(8,128)(2,1)S(1)}, bf16[2,4096,256]{2,1,0:T(8,128)(2,1)}, u32[]{:S(2)}) copy-start(bf16[2,4096,256]{2,1,0:T(8,128)(2,1)} %param.19) | copy-start | bytes 12582916
  93.1 2.2 copy-start.7
  96.3 3.2 %copy-start.4 = (bf16[48,1536]{1,0:T(8,128)(2,1)S(1)}, bf16[48,1536]{1,0:T(8,128)(2,1)}, u32[]{:S(2)}) copy-start(bf16[48,1536]{1,0:T(8,128)(2,1)} %param.15) | copy-start | bytes 442372
  100.4 1.6 collective-permute-start.7
  102.1 5.6 %collective-permute-start.8 = (f32[1,2,4,2,6,130]{5,4,3,2,1,0:T(8,128)S(1)}, f32[1,2,4,2,6,130]{5,4,3,2,1,0:T(8,128)S(1)}, u32[]{:S(2)}, u32[]{:S(2)}) collective-permute-start(f32[1,2,4,2,6,130]{5,4,3,2,1,0:T(8,128)S(1)} %select_bitcast_fusion.4), channel_id=1, source_target_pairs={{0,2},{1,3},{2,0},{3,1},{4,6},{5,7},{6,4},{7,5},{8,10},{9,11},{10,... | collective-permute-start | bytes 149768 | tf_op jit(solution)/shard_map/ppermute | solution.py:66
  108.7 4.1 %collective-permute-start.9 = (bf16[2,4,1536]{2,1,0:T(4,128)(2,1)S(1)}, bf16[2,4,1536]{2,1,0:T(4,128)(2,1)S(1)}, u32[]{:S(2)}, u32[]{:S(2)}) collective-permute-start(bf16[2,4,1536]{2,1,0:T(4,128)(2,1)S(1)} %convert_element_type.87), channel_id=1, source_target_pairs={{0,32},{1,33},{2,34},{3,35},{4,36},{5,37},{6,38},{7,39},{8,40},{9,... | collective-permute-start | bytes 73736 | tf_op jit(solution)/shard_map/ppermute | solution.py:46
  112.9 5.4 %collective-permute-start.10 = (bf16[2,2,4,1536]{3,2,1,0:T(4,128)(2,1)S(1)}, bf16[2,2,4,1536]{3,2,1,0:T(4,128)(2,1)S(1)}, u32[]{:S(2)}, u32[]{:S(2)}) collective-permute-start(bf16[2,2,4,1536]{3,2,1,0:T(4,128)(2,1)S(1)} %maximum_select_fusion.26), channel_id=1, source_target_pairs={{0,96},{1,97},{2,98},{3,99},{4,100},{5,101},{6,102},{7,103},{8,104... | collective-permute-start | bytes 147464 | tf_op jit(solution)/shard_map/ppermute | solution.py:46
  118.4 4.9 %collective-permute-start.11 = (bf16[2,2,2,4,1536]{4,3,2,1,0:T(4,128)(2,1)S(1)}, bf16[2,2,2,4,1536]{4,3,2,1,0:T(4,128)(2,1)S(1)}, u32[]{:S(2)}, u32[]{:S(2)}) collective-permute-start(bf16[2,2,2,4,1536]{4,3,2,1,0:T(4,128)(2,1)S(1)} %maximum_select_fusion.22), channel_id=1, source_target_pairs={{0,8},{1,9},{2,10},{3,11},{4,12},{5,13},{6,14},{7,15},{8,0},{9,1},... | collective-permute-start | bytes 294920 | tf_op jit(solution)/shard_map/ppermute | solution.py:46
  123.4 7.0 %collective-permute-start.12 = (bf16[2,2,2,2,4,1536]{5,4,3,2,1,0:T(4,128)(2,1)S(1)}, bf16[2,2,2,2,4,1536]{5,4,3,2,1,0:T(4,128)(2,1)S(1)}, u32[]{:S(2)}, u32[]{:S(2)}) collective-permute-start(bf16[2,2,2,2,4,1536]{5,4,3,2,1,0:T(4,128)(2,1)S(1)} %maximum_select_fusion.18), channel_id=1, source_target_pairs={{0,24},{1,25},{2,26},{3,27},{4,28},{5,29},{6,30},{7,31},{8,16},{9,... | collective-permute-start | bytes 589832 | tf_op jit(solution)/shard_map/ppermute | solution.py:46
  130.6 15.7 %collective-permute-start.13 = (bf16[2,2,2,2,2,4,1536]{6,5,4,3,2,1,0:T(4,128)(2,1)S(1)}, bf16[2,2,2,2,2,4,1536]{6,5,4,3,2,1,0:T(4,128)(2,1)S(1)}, u32[]{:S(2)}, u32[]{:S(2)}) collective-permute-start(bf16[2,2,2,2,2,4,1536]{6,5,4,3,2,1,0:T(4,128)(2,1)S(1)} %maximum_select_fusion.14), channel_id=1, source_target_pairs={{0,2},{1,3},{2,0},{3,1},{4,6},{5,7},{6,4},{7,5},{8,10},{9,11},{10,... | collective-permute-start | bytes 1179656 | tf_op jit(solution)/shard_map/ppermute | solution.py:46
  146.9 17.3 %copy-start.8 = (s32[32]{0:T(128)S(1)}, s32[32]{0:T(128)}, u32[]{:S(2)}) copy-start(s32[32]{0:T(128)} %param.23) | copy-start | bytes 388
  146.9 15.2 %collective-permute-start.14 = (bf16[2,2,2,2,2,2,4,1536]{7,6,5,4,3,2,1,0:T(4,128)(2,1)S(1)}, bf16[2,2,2,2,2,2,4,1536]{7,6,5,4,3,2,1,0:T(4,128)(2,1)S(1)}, u32[]{:S(2)}, u32[]{:S(2)}) collective-permute-start(bf16[2,2,2,2,2,2,4,1536]{7,6,5,4,3,2,1,0:T(4,128)(2,1)S(1)} %maximum_select_fusion.9), channel_id=1, source_target_pairs={{0,6},{1,7},{2,4},{3,5},{4,2},{5,3},{6,0},{7,1},{8,14},{9,15},{10,... | collective-permute-start | bytes 2359304 | tf_op jit(solution)/shard_map/ppermute | solution.py:46
  164.3 3.8 %collective-permute-start.15 = (bf16[2,2,2,2,2,2,2,4,1536]{8,7,6,5,4,3,2,1,0:T(4,128)(2,1)}, bf16[2,2,2,2,2,2,2,4,1536]{8,7,6,5,4,3,2,1,0:T(4,128)(2,1)}, u32[]{:S(2)}, u32[]{:S(2)}) collective-permute-start(bf16[2,2,2,2,2,2,2,4,1536]{8,7,6,5,4,3,2,1,0:T(4,128)(2,1)} %maximum_select_fusion.5), channel_id=1, source_target_pairs={{0,1},{1,0},{2,3},{3,2},{4,5},{5,4},{6,7},{7,6},{8,9},{9,8},{10,11... | collective-permute-start | bytes 4718600 | tf_op jit(solution)/shard_map/ppermute | solution.py:46
  180.4 4.2 %copy-start.3 = (bf16[1536,280]{0,1:T(8,128)(2,1)S(1)}, bf16[1536,280]{0,1:T(8,128)(2,1)}, u32[]{:S(2)}) copy-start(bf16[1536,280]{0,1:T(8,128)(2,1)} %param.16) | copy-start | bytes 2580484
  184.6 4.1 %copy-start.1 = (f32[64,4,1536]{2,0,1:T(8,128)}, f32[64,4,1536]{2,0,1:T(8,128)S(1)}, u32[]{:S(2)}) copy-start(f32[64,4,1536]{2,0,1:T(8,128)S(1)} %get-tuple-element.32) | copy-start | bytes 4718596
  194.2 2.5 %collective-permute-start.16 = (f32[16,8,1536]{2,1,0:T(8,128)S(1)}, f32[16,8,1536]{2,1,0:T(8,128)}, u32[]{:S(2)}, u32[]{:S(2)}) collective-permute-start(f32[16,8,1536]{2,1,0:T(8,128)S(1)} %select_bitcast_fusion), channel_id=1, source_target_pairs={{0,1},{1,0},{2,3},{3,2},{4,5},{5,4},{6,7},{7,6},{8,9},{9,8},{10,11... | collective-permute-start | bytes 2359304 | tf_op jit(solution)/shard_map/ppermute | solution.py:66
  198.1 11.2 %collective-permute-start.17 = (f32[8,8,1536]{2,1,0:T(8,128)S(1)}, f32[8,8,1536]{2,1,0:T(8,128)S(1)}, u32[]{:S(2)}, u32[]{:S(2)}) collective-permute-start(f32[8,8,1536]{2,1,0:T(8,128)S(1)} %select_bitcast_fusion.1), channel_id=1, source_target_pairs={{0,2},{1,3},{2,0},{3,1},{4,6},{5,7},{6,4},{7,5},{8,10},{9,11},{10,... | collective-permute-start | bytes 1179656 | tf_op jit(solution)/shard_map/ppermute | solution.py:66
  209.4 7.7 %collective-permute-start.18 = (f32[4,8,1536]{2,1,0:T(8,128)S(1)}, f32[4,8,1536]{2,1,0:T(8,128)S(1)}, u32[]{:S(2)}, u32[]{:S(2)}) collective-permute-start(f32[4,8,1536]{2,1,0:T(8,128)S(1)} %select_bitcast_fusion.3), channel_id=1, source_target_pairs={{0,4},{1,5},{2,6},{3,7},{4,0},{5,1},{6,2},{7,3},{8,12},{9,13},{10,... | collective-permute-start | bytes 589832 | tf_op jit(solution)/shard_map/ppermute | solution.py:66
  217.2 4.7 %collective-permute-start.19 = (f32[2,8,1536]{2,1,0:T(8,128)S(1)}, f32[2,8,1536]{2,1,0:T(8,128)S(1)}, u32[]{:S(2)}, u32[]{:S(2)}) collective-permute-start(f32[2,8,1536]{2,1,0:T(8,128)S(1)} %select_bitcast_fusion.5), channel_id=1, source_target_pairs={{0,8},{1,9},{2,10},{3,11},{4,12},{5,13},{6,14},{7,15},{8,0},{9,1},... | collective-permute-start | bytes 294920 | tf_op jit(solution)/shard_map/ppermute | solution.py:66
  221.9 5.7 %collective-permute-start.20 = (f32[1,8,1536]{2,1,0:T(8,128)S(1)}, f32[1,8,1536]{2,1,0:T(8,128)S(1)}, u32[]{:S(2)}, u32[]{:S(2)}) collective-permute-start(f32[1,8,1536]{2,1,0:T(8,128)S(1)} %select_bitcast_fusion.6), channel_id=1, source_target_pairs={{0,16},{1,17},{2,18},{3,19},{4,20},{5,21},{6,22},{7,23},{8,24},{9,... | collective-permute-start | bytes 147464 | tf_op jit(solution)/shard_map/ppermute | solution.py:66
Sparse Core Ops, SparseCore 0:
  100.3 49.0 all-gather.1

commit v10 on v9

--- a/solution.py
+++ b/solution.py
@@ -1,6 +1,10 @@
 import jax
 import jax.numpy as jnp
 from jax import lax
+import functools
+
+from jax.experimental import pallas as pl
+from jax.experimental.pallas import tpu as pltpu
 from jax.sharding import Mesh
 from jax.sharding import PartitionSpec as P
 
@@ -33,6 +37,52 @@
     return jnp.concatenate(
         [first * cosine - second * sine, second * cosine + first * sine], axis=-1
     ).astype(jnp.bfloat16)
+
+
+def _prefix_kernel(limits_ref, q_ref, k_ref, v_ref, o_ref, m_ref, l_ref, *, scale, masked):
+    c = pl.program_id(0)
+    q = q_ref[0]
+    keys = k_ref[0]
+    s = lax.dot_general(q, keys, (((1,), (1,)), ((), ())), preferred_element_type=jnp.float32) * scale
+    col = lax.broadcasted_iota(jnp.int32, s.shape, 1)
+    live = col < limits_ref[c]
+    s = jnp.where(live, s, masked)
+    m = jnp.max(s, axis=1, keepdims=True)
+    w = jnp.where(live, jnp.exp(s - m), 0.0)
+    l = jnp.sum(w, axis=1, keepdims=True)
+    o = jnp.dot(w.astype(jnp.bfloat16), v_ref[0], preferred_element_type=jnp.float32)
+    o_ref[0, 0] = o
+    m_ref[0, 0] = m
+    l_ref[0, 0] = l
+
+
+def prefix_attention(q, keys, values, limits, scale, masked, interpret=False):
+    kvh, rows, d = q.shape
+    cache_rows, ctx, _ = keys.shape
+    kern = functools.partial(_prefix_kernel, scale=scale, masked=masked)
+    return pl.pallas_call(
+        kern,
+        out_shape=(
+            jax.ShapeDtypeStruct((cache_rows, kvh, rows, d), jnp.float32),
+            jax.ShapeDtypeStruct((cache_rows, kvh, rows, 1), jnp.float32),
+            jax.ShapeDtypeStruct((cache_rows, kvh, rows, 1), jnp.float32),
+        ),
+        grid_spec=pltpu.PrefetchScalarGridSpec(
+            num_scalar_prefetch=1,
+            grid=(cache_rows, kvh),
+            in_specs=[
+                pl.BlockSpec((1, rows, d), lambda c, k, lim: (k, 0, 0)),
+                pl.BlockSpec((1, ctx, d), lambda c, k, lim: (c, 0, k)),
+                pl.BlockSpec((1, ctx, d), lambda c, k, lim: (c, 0, k)),
+            ],
+            out_specs=[
+                pl.BlockSpec((1, 1, rows, d), lambda c, k, lim: (c, k, 0, 0)),
+                pl.BlockSpec((1, 1, rows, 1), lambda c, k, lim: (c, k, 0, 0)),
+                pl.BlockSpec((1, 1, rows, 1), lambda c, k, lim: (c, k, 0, 0)),
+            ],
+        ),
+        interpret=interpret,
+    )(limits, q, keys, values)
 
 
 def gather_rounds(x, axes, index, masks):
@@ -153,35 +203,15 @@
     new_values = qkv[..., attn_width + kv_width :].reshape(beams, steps, KV_HEADS, head_dim)
 
     qg = queries.reshape(beams, steps, KV_HEADS, group, head_dim)
-    score_parts = []
-    for k in range(KV_HEADS):
-        keys_k = cache_keys[:, :, k * head_dim : (k + 1) * head_dim]
-        score_parts.append(
-            jnp.einsum("btgd,cpd->cbtgp", qg[:, :, k], keys_k, preferred_element_type=jnp.float32)
-        )
-    scores = jnp.stack(score_parts, axis=3) * scale
     my_beams = j * owned + jnp.arange(owned, dtype=jnp.int32)
     limits = len_r[my_beams]
-    live = (jnp.arange(context, dtype=jnp.int32)[None, :] < limits[:, None])[
-        :, None, None, None, None, :
-    ]
-    scores = jnp.where(live, scores, masked_score)
-    peak = jnp.max(scores, axis=-1)
-    weights = jnp.where(live, jnp.exp(scores - peak[..., None]), 0.0)
-    total = jnp.sum(weights, axis=-1)
-    weights = weights.astype(jnp.bfloat16)
-    output = jnp.stack(
-        [
-            jnp.einsum(
-                "cbtgp,cpd->cbtgd",
-                weights[:, :, :, k],
-                cache_values[:, :, k * head_dim : (k + 1) * head_dim],
-                preferred_element_type=jnp.float32,
-            )
-            for k in range(KV_HEADS)
-        ],
-        axis=3,
-    )
+    q_heads = jnp.transpose(qg, (2, 0, 1, 3, 4)).reshape(KV_HEADS, beams * steps * group, head_dim)
+    output, peak, total = prefix_attention(
+        q_heads, cache_keys, cache_values, limits, scale, masked_score
+    )
+    output = output.reshape(owned, KV_HEADS, beams, steps, group, head_dim).transpose(0, 2, 3, 1, 4, 5)
+    peak = peak.reshape(owned, KV_HEADS, beams, steps, group).transpose(0, 2, 3, 1, 4)
+    total = total.reshape(owned, KV_HEADS, beams, steps, group).transpose(0, 2, 3, 1, 4)
     chosen = (roots[None, :, :] == my_beams[:, None, None])[..., None, None]
     peak = jnp.sum(jnp.where(chosen, peak, 0.0), axis=0)
     total = jnp.sum(jnp.where(chosen, total, 0.0), axis=0)

time: 237 us -> 242 us (1.021)
  Pallas kernels: 0 us -> 10 us
  matrix products: 16.8 us -> 12.8 us
  other arithmetic: 31.3 us -> 28 us
    pallas_call x0 -> x1, Pallas kernels: none -> 10 us  [prefix_attention(): pl.pallas_call(kern, out_shape=(jax.ShapeDtypeStruct((cache_rows, kvh, ro...]
    convert_element_type x1 -> x0, other arithmetic: 4.63 us -> none  [per_device(): weights = weights.astype(jnp.bfloat16)]
    dot_general x4 -> x0, matrix products: 3.98 us -> none  [the longest x2 2.03 us: per_device(): jnp.einsum('btgd,cpd->cbtgp', qg[:, :, k], keys_k, preferred_element_type...]
  transfers between devices with their start and end apart: 22 -> 22, of which waited for: 20 -> 19; matrix products, arithmetic and copies ran while one was open for 16% -> 16% of each run, Pallas kernels for 0% -> 0%
where the time goes in v10:
time: 242 us; the launch traced here: 241 us
  waiting for transfers between devices  105 us (43%)
  local copies, waits for them, and re-layouts  41.4 us (17%)
  other arithmetic  28 us (12%)
  starting transfers between devices  27.8 us (11%)
  between operations  15.7 us (6%)
  matrix products  12.8 us (5%)
  Pallas kernels  10 us (4%)
    ppermute x14, waiting for transfers between devices, gather_rounds(): recv = lax.ppermute(buf, axes, perm)  72.1 us
    ppermute x7, waiting for transfers between devices, scatter_rounds(): buf = keep + lax.ppermute(send, axes, perm)  33.1 us
    ppermute x14, starting transfers between devices, gather_rounds(): recv = lax.ppermute(buf, axes, perm)  23.3 us
    pallas_call x1, Pallas kernels, prefix_attention(): pl.pallas_call(kern, out_shape=(jax.ShapeDtypeStruct((cache_rows, kvh, ro...  10 us
    select_n x24, other arithmetic, gather_rounds(): buf = jnp.where(mine == 0, jnp.stack([buf, recv]), jnp.stack([recv, buf]))  8.48 us
    transpose x2, other arithmetic, gather_rounds(): buf = jnp.transpose(buf, tuple(order) + tuple(range(depth, buf.ndim)))  7.01 us
    another operation x1, local copies, waits for them, and re-layouts, per_device(): x_all = gather_rounds(jnp.swapaxes(step_inputs, 0, 1).reshape(rows_dev *...  6.14 us
  transfers between devices with their start and end apart: 22, of which 19 were waited for; matrix products, arithmetic and copies ran while one was open for 16% of the time, Pallas kernels for 0%

profile of v10, /device:TPU:0, one launch (start us, length us, event | category | flops | bytes accessed | tf_op | source)
XLA Modules:
  0.0 240.9 jit_solution(10738932397160265140)
XLA Ops:
  7.4 1.7 collective-permute-start
  18.1 2.2 collective-permute-start.1
  20.3 3.2 %collective-permute-done.1 = bf16[2,8,1536]{2,1,0:T(8,128)(2,1)S(1)} collective-permute-done((bf16[2,8,1536]{2,1,0:T(8,128)(2,1)S(1)}, bf16[2,8,1536]{2,1,0:T(8,128)(2,1)S(1)}, u32[]{:S(2)}, u32[]{:S(2)}) %collective-permute-start.1) | collective-permute-done | bytes 49184 | tf_op jit(solution)/shard_map/ppermute | solution.py:96
  23.5 2.0 collective-permute-start.2
  25.6 2.7 %collective-permute-done.2 = bf16[2,2,8,1536]{3,2,1,0:T(8,128)(2,1)S(1)} collective-permute-done((bf16[2,2,8,1536]{3,2,1,0:T(8,128)(2,1)S(1)}, bf16[2,2,8,1536]{3,2,1,0:T(8,128)(2,1)S(1)}, u32[]{:S(2)}, u32[]{:S(2)}) %collective-permute-start.2) | collective-permute-done | bytes 98336 | tf_op jit(solution)/shard_map/ppermute | solution.py:96
  28.2 4.1 %collective-permute-start.3 = (bf16[2,2,2,8,1536]{4,3,2,1,0:T(8,128)(2,1)S(1)}, bf16[2,2,2,8,1536]{4,3,2,1,0:T(8,128)(2,1)S(1)}, u32[]{:S(2)}, u32[]{:S(2)}) collective-permute-start(bf16[2,2,2,8,1536]{4,3,2,1,0:T(8,128)(2,1)S(1)} %maximum_select_fusion.15), channel_id=1, source_target_pairs={{0,24},{1,25},{2,26},{3,27},{4,28},{5,29},{6,30},{7,31},{8,16},{9,... | collective-permute-start | bytes 589832 | tf_op jit(solution)/shard_map/ppermute | solution.py:96
  32.4 3.6 %collective-permute-done.3 = bf16[2,2,2,8,1536]{4,3,2,1,0:T(8,128)(2,1)S(1)} collective-permute-done((bf16[2,2,2,8,1536]{4,3,2,1,0:T(8,128)(2,1)S(1)}, bf16[2,2,2,8,1536]{4,3,2,1,0:T(8,128)(2,1)S(1)}, u32[]{:S(2)}, u32[]{:S(2)}) %collective-permute-start.3) | collective-permute-done | bytes 196640 | tf_op jit(solution)/shard_map/ppermute | solution.py:96
  36.1 1.7 collective-permute-start.4
  37.8 6.1 %collective-permute-done.4 = bf16[2,2,2,2,8,1536]{5,4,3,2,1,0:T(8,128)(2,1)S(1)} collective-permute-done((bf16[2,2,2,2,8,1536]{5,4,3,2,1,0:T(8,128)(2,1)S(1)}, bf16[2,2,2,2,8,1536]{5,4,3,2,1,0:T(8,128)(2,1)S(1)}, u32[]{:S(2)}, u32[]{:S(2)}) %collective-permute-start.4) | collective-permute-done | bytes 393248 | tf_op jit(solution)/shard_map/ppermute | solution.py:96
  44.9 3.0 %collective-permute-start.5 = (bf16[2,2,2,2,2,8,1536]{6,5,4,3,2,1,0:T(8,128)(2,1)}, bf16[2,2,2,2,2,8,1536]{6,5,4,3,2,1,0:T(8,128)(2,1)S(1)}, u32[]{:S(2)}, u32[]{:S(2)}) collective-permute-start(bf16[2,2,2,2,2,8,1536]{6,5,4,3,2,1,0:T(8,128)(2,1)} %maximum_select_fusion.7), channel_id=1, source_target_pairs={{0,6},{1,7},{2,4},{3,5},{4,2},{5,3},{6,0},{7,1},{8,14},{9,15},{10,... | collective-permute-start | bytes 2359304 | tf_op jit(solution)/shard_map/ppermute | solution.py:96
  48.9 12.2 %collective-permute-done.5 = bf16[2,2,2,2,2,8,1536]{6,5,4,3,2,1,0:T(8,128)(2,1)S(1)} collective-permute-done((bf16[2,2,2,2,2,8,1536]{6,5,4,3,2,1,0:T(8,128)(2,1)}, bf16[2,2,2,2,2,8,1536]{6,5,4,3,2,1,0:T(8,128)(2,1)S(1)}, u32[]{:S(2)}, u32[]{:S(2)}) %collective-permute-start.5) | collective-permute-done | bytes 786464 | tf_op jit(solution)/shard_map/ppermute | solution.py:96
  61.1 1.4 maximum_select_fusion.3
  66.5 2.3 fusion.4
  68.9 2.1 copy.131
  71.0 6.1 %reshape_reshape.7 = bf16[256,4,1536]{2,1,0:T(4,128)(2,1)} reshape(bf16[2,2,2,2,2,2,2,8,1536]{8,7,6,5,4,3,2,1,0:T(8,128)(2,1)} %copy.131) | data formatting | bytes 6291456 | tf_op jit(solution)/shard_map/reshape;reshape | solution.py:177
  80.4 3.9 %fusion.12 = bf16[8,4,2048]{2,0,1:T(8,128)(2,1)S(1)} fusion(bf16[1536,2048]{1,0:T(8,128)(2,1)} %param.13, f32[2048]{0:T(1024)S(1)} %copy-done.4, bf16[8,4,1536]{2,1,0:T(4,128)(2,1)S(1)} %fusion.36), kind=kOutput, calls=%fused_computation.26 | convolution fusion | flops 201457664 | bytes 6529024 | tf_op jit(solution)/shard_map/dot_general | solution.py:185
  85.4 10.0 %shard_map.118 = (f32[2,2,192,128]{3,2,1,0:T(8,128)}, f32[2,2,192,1]{3,2,1,0:T(8,128)}, f32[2,2,192,1]{3,2,1,0:T(8,128)}) custom-call(s32[2]{0:T(128)} %gather_fusion.4, bf16[2,192,128]{2,1,0:T(8,128)(2,1)} %copy.141.q_ref, bf16[2,4096,256]{2,1,0:T(8,128)(2,1)} %k_ref.1, bf16[2,4096,256]{2,1,0:T(8,128)(2,1)} %v_ref.1), custom_call_target="tpu_custom_call" | custom-call | tf_op jit(solution)/shard_map/pallas_call | solution.py:63
  95.4 1.3 copy.142
  96.8 1.2 reduce.8
  98.1 1.2 reduce.9
  106.0 4.3 %collective-permute-done.8 = f32[1,2,4,2,6,130]{5,4,3,2,1,0:T(8,128)S(1)} collective-permute-done((f32[1,2,4,2,6,130]{5,4,3,2,1,0:T(8,128)S(1)}, f32[1,2,4,2,6,130]{5,4,3,2,1,0:T(8,128)S(1)}, u32[]{:S(2)}, u32[]{:S(2)}) %collective-permute-start.8) | collective-permute-done | bytes 49952 | tf_op jit(solution)/shard_map/ppermute | solution.py:116
  111.5 3.8 %collective-permute-done.9 = bf16[2,4,1536]{2,1,0:T(4,128)(2,1)S(1)} collective-permute-done((bf16[2,4,1536]{2,1,0:T(4,128)(2,1)S(1)}, bf16[2,4,1536]{2,1,0:T(4,128)(2,1)S(1)}, u32[]{:S(2)}, u32[]{:S(2)}) %collective-permute-start.9) | collective-permute-done | bytes 24608 | tf_op jit(solution)/shard_map/ppermute | solution.py:96
  115.3 2.2 collective-permute-start.10
  117.6 3.1 %collective-permute-done.10 = bf16[2,2,4,1536]{3,2,1,0:T(4,128)(2,1)S(1)} collective-permute-done((bf16[2,2,4,1536]{3,2,1,0:T(4,128)(2,1)S(1)}, bf16[2,2,4,1536]{3,2,1,0:T(4,128)(2,1)S(1)}, u32[]{:S(2)}, u32[]{:S(2)}) %collective-permute-start.10) | collective-permute-done | bytes 49184 | tf_op jit(solution)/shard_map/ppermute | solution.py:96
  121.1 4.4 %collective-permute-done.11 = bf16[2,2,2,4,1536]{4,3,2,1,0:T(4,128)(2,1)S(1)} collective-permute-done((bf16[2,2,2,4,1536]{4,3,2,1,0:T(4,128)(2,1)S(1)}, bf16[2,2,2,4,1536]{4,3,2,1,0:T(4,128)(2,1)S(1)}, u32[]{:S(2)}, u32[]{:S(2)}) %collective-permute-start.11) | collective-permute-done | bytes 98336 | tf_op jit(solution)/shard_map/ppermute | solution.py:96
  125.6 3.0 %collective-permute-start.12 = (bf16[2,2,2,2,4,1536]{5,4,3,2,1,0:T(4,128)(2,1)S(1)}, bf16[2,2,2,2,4,1536]{5,4,3,2,1,0:T(4,128)(2,1)S(1)}, u32[]{:S(2)}, u32[]{:S(2)}) collective-permute-start(bf16[2,2,2,2,4,1536]{5,4,3,2,1,0:T(4,128)(2,1)S(1)} %maximum_select_fusion.17), channel_id=1, source_target_pairs={{0,24},{1,25},{2,26},{3,27},{4,28},{5,29},{6,30},{7,31},{8,16},{9,... | collective-permute-start | bytes 589832 | tf_op jit(solution)/shard_map/ppermute | solution.py:96
  128.8 4.0 %collective-permute-done.12 = bf16[2,2,2,2,4,1536]{5,4,3,2,1,0:T(4,128)(2,1)S(1)} collective-permute-done((bf16[2,2,2,2,4,1536]{5,4,3,2,1,0:T(4,128)(2,1)S(1)}, bf16[2,2,2,2,4,1536]{5,4,3,2,1,0:T(4,128)(2,1)S(1)}, u32[]{:S(2)}, u32[]{:S(2)}) %collective-permute-start.12) | collective-permute-done | bytes 196640 | tf_op jit(solution)/shard_map/ppermute | solution.py:96
  133.7 16.2 %collective-permute-done.13 = bf16[2,2,2,2,2,4,1536]{6,5,4,3,2,1,0:T(4,128)(2,1)S(1)} collective-permute-done((bf16[2,2,2,2,2,4,1536]{6,5,4,3,2,1,0:T(4,128)(2,1)S(1)}, bf16[2,2,2,2,2,4,1536]{6,5,4,3,2,1,0:T(4,128)(2,1)S(1)}, u32[]{:S(2)}, u32[]{:S(2)}) %collective-permute-start.13) | collective-permute-done | bytes 393248 | tf_op jit(solution)/shard_map/ppermute | solution.py:96
  150.4 3.1 %collective-permute-start.14 = (bf16[2,2,2,2,2,2,4,1536]{7,6,5,4,3,2,1,0:T(4,128)(2,1)S(1)}, bf16[2,2,2,2,2,2,4,1536]{7,6,5,4,3,2,1,0:T(4,128)(2,1)S(1)}, u32[]{:S(2)}, u32[]{:S(2)}) collective-permute-start(bf16[2,2,2,2,2,2,4,1536]{7,6,5,4,3,2,1,0:T(4,128)(2,1)S(1)} %maximum_select_fusion.9), channel_id=1, source_target_pairs={{0,6},{1,7},{2,4},{3,5},{4,2},{5,3},{6,0},{7,1},{8,14},{9,15},{10,... | collective-permute-start | bytes 2359304 | tf_op jit(solution)/shard_map/ppermute | solution.py:96
  154.4 12.5 %collective-permute-done.14 = bf16[2,2,2,2,2,2,4,1536]{7,6,5,4,3,2,1,0:T(4,128)(2,1)S(1)} collective-permute-done((bf16[2,2,2,2,2,2,4,1536]{7,6,5,4,3,2,1,0:T(4,128)(2,1)S(1)}, bf16[2,2,2,2,2,2,4,1536]{7,6,5,4,3,2,1,0:T(4,128)(2,1)S(1)}, u32[]{:S(2)}, u32[]{:S(2)}) %collective-permute-start.14) | collective-permute-done | bytes 786464 | tf_op jit(solution)/shard_map/ppermute | solution.py:96
  166.9 2.1 maximum_select_fusion.5
  169.0 1.4 constant_dynamic-slice_fusion
  172.7 4.7 %fusion.5 = bf16[2,2,2,2,2,2,2,2,4,1536]{9,8,7,1,0,3,2,5,4,6:T(4,128)(2,1)S(1)} fusion(bf16[1,2,2,2,2,2,2,2,4,1536]{9,8,7,6,5,4,3,2,1,0:T(4,128)(2,1)} %bitcast.95, bf16[1,2,2,2,2,2,2,2,4,1536]{9,8,7,6,5,4,3,2,1,0:T(4,128)(2,1)S(1)} %maximum_select_fusion.4, pred[]{:T(512)S(6)} %eq.99), kind=kLoop, calls=%fused_computation.23 | loop fusion | flops 4718592 | bytes 6291457 | tf_op jit(solution)/shard_map/transpose | solution.py:102
  177.4 1.8 copy.159
  179.2 2.5 %copy.160 = bf16[32,8,4,1536]{3,1,2,0:T(8,128)(2,1)} copy(bf16[32,8,4,1536]{3,2,1,0:T(4,128)(2,1)S(1)} %bitcast.285) | data formatting | bytes 6291456 | tf_op jit(solution)/shard_map/reshape;reshape;reshape | solution.py:269
  181.7 3.4 %gather_fusion.14 = bf16[8,8,4,1536]{3,1,2,0:T(8,128)(2,1)} fusion(bf16[32,8,4,1536]{3,1,2,0:T(8,128)(2,1)} %copy.160, s32[1024]{0:T(1024)S(1)} %pad_clamp_fusion), kind=kCustom, calls=%fused_computation.14 | custom fusion | bytes 1572896 | tf_op jit(solution)/shard_map/gather | solution.py:269
  185.1 4.1 %multiply_reduce_fusion = (f32[64,4]{0,1:T(4,128)S(1)}, f32[64,4,1536]{2,0,1:T(8,128)S(1)}) fusion(bf16[1536,1536]{1,0:T(8,128)(2,1)} %all-gather.2.cloned.1.call-done, bf16[8,8,4,1536]{3,1,2,0:T(8,128)(2,1)} %gather_fusion.14, bf16[64,4,1536]{2,1,0:T(4,128)(2,1)S(1)} %constant_dynamic-slice_fusion), kind=kOutput, calls=%fused_computation.32 | convolution fusion | flops 1209532160 | bytes 7865344 | tf_op jit(solution)/shard_map/dot_general | solution.py:273
  189.9 3.5 %fusion.16 = f32[64,4,1536]{2,0,1:T(8,128)} fusion(bf16[280,1536]{1,0:T(8,128)(2,1)S(1)} %copy-done, bf16[1536,280]{0,1:T(8,128)(2,1)} %param.17, f32[64,4,280]{2,0,1:T(8,128)S(1)} %fusion.21, f32[64,4,1536]{2,0,1:T(8,128)S(1)} %get-tuple-element.34, f32[64,4]{0,1:T(4,128)S(1)} %add_rsqrt_fusion.1), kind=kOutput, calls=%fused_computation.35 | convolution fusion | flops 441618432 | bytes 5153792 | tf_op jit(solution)/shard_map/dot_general | solution.py:280
  193.4 3.6 %copy.162 = f32[64,4,1536]{2,1,0:T(4,128)} copy(f32[64,4,1536]{2,0,1:T(8,128)} %fusion.16) | data formatting | bytes 3145728 | tf_op jit(solution)/shard_map/dot_general | solution.py:280
  197.0 1.8 reshape_reshape.8
  199.1 2.3 collective-permute-done.16
  201.4 1.3 fusion.24
  202.9 11.1 %collective-permute-done.17 = f32[8,8,1536]{2,1,0:T(8,128)S(1)} collective-permute-done((f32[8,8,1536]{2,1,0:T(8,128)S(1)}, f32[8,8,1536]{2,1,0:T(8,128)S(1)}, u32[]{:S(2)}, u32[]{:S(2)}) %collective-permute-start.17) | collective-permute-done | bytes 393248 | tf_op jit(solution)/shard_map/ppermute | solution.py:116
  214.1 2.7 %collective-permute-start.18 = (f32[4,8,1536]{2,1,0:T(8,128)S(1)}, f32[4,8,1536]{2,1,0:T(8,128)S(1)}, u32[]{:S(2)}, u32[]{:S(2)}) collective-permute-start(f32[4,8,1536]{2,1,0:T(8,128)S(1)} %select_bitcast_fusion.3), channel_id=1, source_target_pairs={{0,4},{1,5},{2,6},{3,7},{4,0},{5,1},{6,2},{7,3},{8,12},{9,13},{10,... | collective-permute-start | bytes 589832 | tf_op jit(solution)/shard_map/ppermute | solution.py:116
  216.8 5.0 %collective-permute-done.18 = f32[4,8,1536]{2,1,0:T(8,128)S(1)} collective-permute-done((f32[4,8,1536]{2,1,0:T(8,128)S(1)}, f32[4,8,1536]{2,1,0:T(8,128)S(1)}, u32[]{:S(2)}, u32[]{:S(2)}) %collective-permute-start.18) | collective-permute-done | bytes 196640 | tf_op jit(solution)/shard_map/ppermute | solution.py:116
  222.0 4.8 %collective-permute-done.19 = f32[2,8,1536]{2,1,0:T(8,128)S(1)} collective-permute-done((f32[2,8,1536]{2,1,0:T(8,128)S(1)}, f32[2,8,1536]{2,1,0:T(8,128)S(1)}, u32[]{:S(2)}, u32[]{:S(2)}) %collective-permute-start.19) | collective-permute-done | bytes 98336 | tf_op jit(solution)/shard_map/ppermute | solution.py:116
  227.1 5.3 %collective-permute-done.20 = f32[1,8,1536]{2,1,0:T(8,128)S(1)} collective-permute-done((f32[1,8,1536]{2,1,0:T(8,128)S(1)}, f32[1,8,1536]{2,1,0:T(8,128)S(1)}, u32[]{:S(2)}, u32[]{:S(2)}) %collective-permute-start.20) | collective-permute-done | bytes 49184 | tf_op jit(solution)/shard_map/ppermute | solution.py:116
  232.5 1.6 fusion.55
  (179 shorter events, 33.6 us)
Async XLA Ops:
  6.5 183.4 %copy-start = (bf16[280,1536]{1,0:T(8,128)(2,1)S(1)}, bf16[280,1536]{1,0:T(8,128)(2,1)}, u32[]{:S(2)}) copy-start(bf16[280,1536]{1,0:T(8,128)(2,1)} %param.18) | copy-start | bytes 2580484
  6.5 178.6 %all-gather.2.cloned.1.call-start = ((), (), s32[]{:S(2)}) async-start(), calls=%async_computation | async-start | bytes 4866048 | tf_op jit(solution)/shard_map/all_gather | solution.py:179
  7.4 10.7 %collective-permute-start = (bf16[8,1536]{1,0:T(8,128)(2,1)S(1)}, bf16[8,1536]{1,0:T(8,128)(2,1)S(1)}, u32[]{:S(2)}, u32[]{:S(2)}) collective-permute-start(bf16[8,1536]{1,0:T(8,128)(2,1)S(1)} %reshape.1856), channel_id=1, source_target_pairs={{0,32},{1,33},{2,34},{3,35},{4,36},{5,37},{6,38},{7,39},{8,40},{9,... | collective-permute-start | bytes 73736 | tf_op jit(solution)/shard_map/ppermute | solution.py:96
  14.0 4.0 %copy-start.5 = (s32[32,8]{0,1:T(8,128)S(1)}, s32[32,8]{0,1:T(8,128)}, u32[]{:S(2)}) copy-start(s32[32,8]{0,1:T(8,128)} %param.21) | copy-start | bytes 3076
  18.1 5.4 %collective-permute-start.1 = (bf16[2,8,1536]{2,1,0:T(8,128)(2,1)S(1)}, bf16[2,8,1536]{2,1,0:T(8,128)(2,1)S(1)}, u32[]{:S(2)}, u32[]{:S(2)}) collective-permute-start(bf16[2,8,1536]{2,1,0:T(8,128)(2,1)S(1)} %maximum_select_fusion.23), channel_id=1, source_target_pairs={{0,96},{1,97},{2,98},{3,99},{4,100},{5,101},{6,102},{7,103},{8,104... | collective-permute-start | bytes 147464 | tf_op jit(solution)/shard_map/ppermute | solution.py:96
  23.5 4.7 %collective-permute-start.2 = (bf16[2,2,8,1536]{3,2,1,0:T(8,128)(2,1)S(1)}, bf16[2,2,8,1536]{3,2,1,0:T(8,128)(2,1)S(1)}, u32[]{:S(2)}, u32[]{:S(2)}) collective-permute-start(bf16[2,2,8,1536]{3,2,1,0:T(8,128)(2,1)S(1)} %maximum_select_fusion.19), channel_id=1, source_target_pairs={{0,8},{1,9},{2,10},{3,11},{4,12},{5,13},{6,14},{7,15},{8,0},{9,1},... | collective-permute-start | bytes 294920 | tf_op jit(solution)/shard_map/ppermute | solution.py:96
  28.2 7.8 %collective-permute-start.3 = (bf16[2,2,2,8,1536]{4,3,2,1,0:T(8,128)(2,1)S(1)}, bf16[2,2,2,8,1536]{4,3,2,1,0:T(8,128)(2,1)S(1)}, u32[]{:S(2)}, u32[]{:S(2)}) collective-permute-start(bf16[2,2,2,8,1536]{4,3,2,1,0:T(8,128)(2,1)S(1)} %maximum_select_fusion.15), channel_id=1, source_target_pairs={{0,24},{1,25},{2,26},{3,27},{4,28},{5,29},{6,30},{7,31},{8,16},{9,... | collective-permute-start | bytes 589832 | tf_op jit(solution)/shard_map/ppermute | solution.py:96
  36.1 7.9 %collective-permute-start.4 = (bf16[2,2,2,2,8,1536]{5,4,3,2,1,0:T(8,128)(2,1)S(1)}, bf16[2,2,2,2,8,1536]{5,4,3,2,1,0:T(8,128)(2,1)S(1)}, u32[]{:S(2)}, u32[]{:S(2)}) collective-permute-start(bf16[2,2,2,2,8,1536]{5,4,3,2,1,0:T(8,128)(2,1)S(1)} %maximum_select_fusion.11), channel_id=1, source_target_pairs={{0,2},{1,3},{2,0},{3,1},{4,6},{5,7},{6,4},{7,5},{8,10},{9,11},{10,... | collective-permute-start | bytes 1179656 | tf_op jit(solution)/shard_map/ppermute | solution.py:96
  44.9 16.2 %collective-permute-start.5 = (bf16[2,2,2,2,2,8,1536]{6,5,4,3,2,1,0:T(8,128)(2,1)}, bf16[2,2,2,2,2,8,1536]{6,5,4,3,2,1,0:T(8,128)(2,1)S(1)}, u32[]{:S(2)}, u32[]{:S(2)}) collective-permute-start(bf16[2,2,2,2,2,8,1536]{6,5,4,3,2,1,0:T(8,128)(2,1)} %maximum_select_fusion.7), channel_id=1, source_target_pairs={{0,6},{1,7},{2,4},{3,5},{4,2},{5,3},{6,0},{7,1},{8,14},{9,15},{10,... | collective-permute-start | bytes 2359304 | tf_op jit(solution)/shard_map/ppermute | solution.py:96
  62.5 4.0 %collective-permute-start.6 = (bf16[2,2,2,2,2,2,8,1536]{7,6,5,4,3,2,1,0:T(8,128)(2,1)}, bf16[2,2,2,2,2,2,8,1536]{7,6,5,4,3,2,1,0:T(8,128)(2,1)}, u32[]{:S(2)}, u32[]{:S(2)}) collective-permute-start(bf16[2,2,2,2,2,2,8,1536]{7,6,5,4,3,2,1,0:T(8,128)(2,1)} %maximum_select_fusion.3), channel_id=1, source_target_pairs={{0,1},{1,0},{2,3},{3,2},{4,5},{5,4},{6,7},{7,6},{8,9},{9,8},{10,11... | collective-permute-start | bytes 4718600 | tf_op jit(solution)/shard_map/ppermute | solution.py:96
  71.0 9.3 %copy-start.4 = (f32[2048]{0:T(1024)S(1)}, f32[2048]{0:T(1024)}, u32[]{:S(2)}) copy-start(f32[2048]{0:T(1024)} %param.14) | copy-start | bytes 24580
  95.4 4.7 %copy-start.3 = (bf16[48,1536]{1,0:T(8,128)(2,1)S(1)}, bf16[48,1536]{1,0:T(8,128)(2,1)}, u32[]{:S(2)}) copy-start(bf16[48,1536]{1,0:T(8,128)(2,1)} %param.15) | copy-start | bytes 442372
  102.5 1.7 collective-permute-start.7
  104.3 6.0 %collective-permute-start.8 = (f32[1,2,4,2,6,130]{5,4,3,2,1,0:T(8,128)S(1)}, f32[1,2,4,2,6,130]{5,4,3,2,1,0:T(8,128)S(1)}, u32[]{:S(2)}, u32[]{:S(2)}) collective-permute-start(f32[1,2,4,2,6,130]{5,4,3,2,1,0:T(8,128)S(1)} %select_bitcast_fusion.4), channel_id=1, source_target_pairs={{0,2},{1,3},{2,0},{3,1},{4,6},{5,7},{6,4},{7,5},{8,10},{9,11},{10,... | collective-permute-start | bytes 149768 | tf_op jit(solution)/shard_map/ppermute | solution.py:116
  111.4 3.9 %collective-permute-start.9 = (bf16[2,4,1536]{2,1,0:T(4,128)(2,1)S(1)}, bf16[2,4,1536]{2,1,0:T(4,128)(2,1)S(1)}, u32[]{:S(2)}, u32[]{:S(2)}) collective-permute-start(bf16[2,4,1536]{2,1,0:T(4,128)(2,1)S(1)} %convert_element_type.83), channel_id=1, source_target_pairs={{0,32},{1,33},{2,34},{3,35},{4,36},{5,37},{6,38},{7,39},{8,40},{9,... | collective-permute-start | bytes 73736 | tf_op jit(solution)/shard_map/ppermute | solution.py:96
  115.3 5.4 %collective-permute-start.10 = (bf16[2,2,4,1536]{3,2,1,0:T(4,128)(2,1)S(1)}, bf16[2,2,4,1536]{3,2,1,0:T(4,128)(2,1)S(1)}, u32[]{:S(2)}, u32[]{:S(2)}) collective-permute-start(bf16[2,2,4,1536]{3,2,1,0:T(4,128)(2,1)S(1)} %maximum_select_fusion.25), channel_id=1, source_target_pairs={{0,96},{1,97},{2,98},{3,99},{4,100},{5,101},{6,102},{7,103},{8,104... | collective-permute-start | bytes 147464 | tf_op jit(solution)/shard_map/ppermute | solution.py:96
  120.8 4.7 %collective-permute-start.11 = (bf16[2,2,2,4,1536]{4,3,2,1,0:T(4,128)(2,1)S(1)}, bf16[2,2,2,4,1536]{4,3,2,1,0:T(4,128)(2,1)S(1)}, u32[]{:S(2)}, u32[]{:S(2)}) collective-permute-start(bf16[2,2,2,4,1536]{4,3,2,1,0:T(4,128)(2,1)S(1)} %maximum_select_fusion.21), channel_id=1, source_target_pairs={{0,8},{1,9},{2,10},{3,11},{4,12},{5,13},{6,14},{7,15},{8,0},{9,1},... | collective-permute-start | bytes 294920 | tf_op jit(solution)/shard_map/ppermute | solution.py:96
  125.6 7.1 %collective-permute-start.12 = (bf16[2,2,2,2,4,1536]{5,4,3,2,1,0:T(4,128)(2,1)S(1)}, bf16[2,2,2,2,4,1536]{5,4,3,2,1,0:T(4,128)(2,1)S(1)}, u32[]{:S(2)}, u32[]{:S(2)}) collective-permute-start(bf16[2,2,2,2,4,1536]{5,4,3,2,1,0:T(4,128)(2,1)S(1)} %maximum_select_fusion.17), channel_id=1, source_target_pairs={{0,24},{1,25},{2,26},{3,27},{4,28},{5,29},{6,30},{7,31},{8,16},{9,... | collective-permute-start | bytes 589832 | tf_op jit(solution)/shard_map/ppermute | solution.py:96
  133.1 16.8 %collective-permute-start.13 = (bf16[2,2,2,2,2,4,1536]{6,5,4,3,2,1,0:T(4,128)(2,1)S(1)}, bf16[2,2,2,2,2,4,1536]{6,5,4,3,2,1,0:T(4,128)(2,1)S(1)}, u32[]{:S(2)}, u32[]{:S(2)}) collective-permute-start(bf16[2,2,2,2,2,4,1536]{6,5,4,3,2,1,0:T(4,128)(2,1)S(1)} %maximum_select_fusion.13), channel_id=1, source_target_pairs={{0,2},{1,3},{2,0},{3,1},{4,6},{5,7},{6,4},{7,5},{8,10},{9,11},{10,... | collective-permute-start | bytes 1179656 | tf_op jit(solution)/shard_map/ppermute | solution.py:96
  150.4 16.4 %collective-permute-start.14 = (bf16[2,2,2,2,2,2,4,1536]{7,6,5,4,3,2,1,0:T(4,128)(2,1)S(1)}, bf16[2,2,2,2,2,2,4,1536]{7,6,5,4,3,2,1,0:T(4,128)(2,1)S(1)}, u32[]{:S(2)}, u32[]{:S(2)}) collective-permute-start(bf16[2,2,2,2,2,2,4,1536]{7,6,5,4,3,2,1,0:T(4,128)(2,1)S(1)} %maximum_select_fusion.9), channel_id=1, source_target_pairs={{0,6},{1,7},{2,4},{3,5},{4,2},{5,3},{6,0},{7,1},{8,14},{9,15},{10,... | collective-permute-start | bytes 2359304 | tf_op jit(solution)/shard_map/ppermute | solution.py:96
  166.9 2.1 copy-start.6
  169.0 3.8 %collective-permute-start.15 = (bf16[2,2,2,2,2,2,2,4,1536]{8,7,6,5,4,3,2,1,0:T(4,128)(2,1)}, bf16[2,2,2,2,2,2,2,4,1536]{8,7,6,5,4,3,2,1,0:T(4,128)(2,1)}, u32[]{:S(2)}, u32[]{:S(2)}) collective-permute-start(bf16[2,2,2,2,2,2,2,4,1536]{8,7,6,5,4,3,2,1,0:T(4,128)(2,1)} %maximum_select_fusion.5), channel_id=1, source_target_pairs={{0,1},{1,0},{2,3},{3,2},{4,5},{5,4},{6,7},{7,6},{8,9},{9,8},{10,11... | collective-permute-start | bytes 4718600 | tf_op jit(solution)/shard_map/ppermute | solution.py:96
  185.1 4.2 %copy-start.2 = (bf16[1536,280]{0,1:T(8,128)(2,1)S(1)}, bf16[1536,280]{0,1:T(8,128)(2,1)}, u32[]{:S(2)}) copy-start(bf16[1536,280]{0,1:T(8,128)(2,1)} %param.16) | copy-start | bytes 2580484
  189.3 4.1 %copy-start.1 = (f32[64,4,1536]{2,0,1:T(8,128)}, f32[64,4,1536]{2,0,1:T(8,128)S(1)}, u32[]{:S(2)}) copy-start(f32[64,4,1536]{2,0,1:T(8,128)S(1)} %get-tuple-element.34) | copy-start | bytes 4718596
  198.9 2.5 %collective-permute-start.16 = (f32[16,8,1536]{2,1,0:T(8,128)S(1)}, f32[16,8,1536]{2,1,0:T(8,128)}, u32[]{:S(2)}, u32[]{:S(2)}) collective-permute-start(f32[16,8,1536]{2,1,0:T(8,128)S(1)} %select_bitcast_fusion), channel_id=1, source_target_pairs={{0,1},{1,0},{2,3},{3,2},{4,5},{5,4},{6,7},{7,6},{8,9},{9,8},{10,11... | collective-permute-start | bytes 2359304 | tf_op jit(solution)/shard_map/ppermute | solution.py:116
  202.8 11.2 %collective-permute-start.17 = (f32[8,8,1536]{2,1,0:T(8,128)S(1)}, f32[8,8,1536]{2,1,0:T(8,128)S(1)}, u32[]{:S(2)}, u32[]{:S(2)}) collective-permute-start(f32[8,8,1536]{2,1,0:T(8,128)S(1)} %select_bitcast_fusion.1), channel_id=1, source_target_pairs={{0,2},{1,3},{2,0},{3,1},{4,6},{5,7},{6,4},{7,5},{8,10},{9,11},{10,... | collective-permute-start | bytes 1179656 | tf_op jit(solution)/shard_map/ppermute | solution.py:116
  214.1 7.7 %collective-permute-start.18 = (f32[4,8,1536]{2,1,0:T(8,128)S(1)}, f32[4,8,1536]{2,1,0:T(8,128)S(1)}, u32[]{:S(2)}, u32[]{:S(2)}) collective-permute-start(f32[4,8,1536]{2,1,0:T(8,128)S(1)} %select_bitcast_fusion.3), channel_id=1, source_target_pairs={{0,4},{1,5},{2,6},{3,7},{4,0},{5,1},{6,2},{7,3},{8,12},{9,13},{10,... | collective-permute-start | bytes 589832 | tf_op jit(solution)/shard_map/ppermute | solution.py:116
  221.8 4.9 %collective-permute-start.19 = (f32[2,8,1536]{2,1,0:T(8,128)S(1)}, f32[2,8,1536]{2,1,0:T(8,128)S(1)}, u32[]{:S(2)}, u32[]{:S(2)}) collective-permute-start(f32[2,8,1536]{2,1,0:T(8,128)S(1)} %select_bitcast_fusion.5), channel_id=1, source_target_pairs={{0,8},{1,9},{2,10},{3,11},{4,12},{5,13},{6,14},{7,15},{8,0},{9,1},... | collective-permute-start | bytes 294920 | tf_op jit(solution)/shard_map/ppermute | solution.py:116
  226.8 5.7 %collective-permute-start.20 = (f32[1,8,1536]{2,1,0:T(8,128)S(1)}, f32[1,8,1536]{2,1,0:T(8,128)S(1)}, u32[]{:S(2)}, u32[]{:S(2)}) collective-permute-start(f32[1,8,1536]{2,1,0:T(8,128)S(1)} %select_bitcast_fusion.6), channel_id=1, source_target_pairs={{0,16},{1,17},{2,18},{3,19},{4,20},{5,21},{6,22},{7,23},{8,24},{9,... | collective-permute-start | bytes 147464 | tf_op jit(solution)/shard_map/ppermute | solution.py:116
Sparse Core Ops, SparseCore 0:
  101.0 50.7 all-gather.1

commit v11 on v9

--- a/solution.py
+++ b/solution.py
@@ -48,9 +48,15 @@
         buf = jnp.where(mine == 0, jnp.stack([buf, recv]), jnp.stack([recv, buf]))
         bits.append(bit)
     depth = len(bits)
-    order = sorted(range(depth), key=lambda a: -bits[depth - 1 - a])
-    buf = jnp.transpose(buf, tuple(order) + tuple(range(depth, buf.ndim)))
-    return buf.reshape((count,) + x.shape)
+    flat_buf = buf.reshape((count,) + x.shape)
+
+    def position(device):
+        pos = jnp.zeros_like(device)
+        for a in range(depth):
+            pos = pos + ((device // bits[depth - 1 - a]) % 2) * (1 << (depth - 1 - a))
+        return pos
+
+    return flat_buf, position
 
 
 def scatter_rounds(x, axes, index):
@@ -122,13 +128,16 @@
     )
 
     flat_masks = gather_masks(n_req, tp_count)
-    x_all = gather_rounds(
+    x_blocks, x_position = gather_rounds(
         jnp.swapaxes(step_inputs, 0, 1).reshape(rows_dev * steps, width), ALL, flat, flat_masks
-    ).reshape(requests * beams, steps, width)
-    after_rows = (x_all[0, 0, 0] * 0).astype(out_weight.dtype)
+    )
+    x_blocks = x_blocks.reshape(x_blocks.shape[0], rows_dev, steps, width)
+    slot_devices = inverse[r] * n_i + jnp.arange(n_i, dtype=jnp.int32)
+    x_req = x_blocks[x_position(slot_devices)].reshape(beams, steps, width)
+    group_devices = req_index * tp_count + jnp.arange(tp_count, dtype=jnp.int32)
+    x_group = x_blocks[x_position(group_devices)].reshape(group_rows, steps, width)
+    after_rows = (x_blocks[0, 0, 0, 0] * 0).astype(out_weight.dtype)
     full_out = lax.all_gather(out_weight + after_rows, TP, axis=0, tiled=True)
-    x_req = lax.dynamic_slice_in_dim(x_all, inverse[r] * beams, beams, 0)
-    x_group = lax.dynamic_slice_in_dim(x_all, req_index * group_rows, group_rows, 0)
 
     normed = rms_normed(x_req)
     qkv = (
@@ -232,13 +241,10 @@
         (numerator / denominator[..., None]).reshape(owned, steps, attn_width).astype(jnp.bfloat16)
     )
 
-    att_all = gather_rounds(attention, ALL, flat, flat_masks).reshape(
-        requests * beams, steps, attn_width
-    )
+    att_blocks, att_position = gather_rounds(attention, ALL, flat, flat_masks)
     my_requests = lax.dynamic_slice_in_dim(slot_request, req_index * group_requests, group_requests)
-    att_group = att_all.reshape(requests, beams, steps, attn_width)[my_requests].reshape(
-        group_rows, steps, attn_width
-    )
+    owner_devices = (my_requests[:, None] * n_i + jnp.arange(n_i, dtype=jnp.int32)[None, :]).reshape(-1)
+    att_group = att_blocks[att_position(owner_devices)].reshape(group_rows, steps, attn_width)
 
     middle = x_group.astype(jnp.float32) + jnp.dot(
         att_group, full_out, preferred_element_type=jnp.float32

time: 237 us -> 240 us (1.013)
    select_n x24 -> x26, other arithmetic: 7.61 us -> 18.2 us  [gather_rounds(): buf = jnp.where(mine == 0, jnp.stack([buf, recv]), jnp.stack([recv, buf]))]
    another operation x2 -> x0, local copies, waits for them, and re-layouts: 8.61 us -> none  [the longest x1 6.14 us: per_device(): x_all = gather_rounds(jnp.swapaxes(step_inputs, 0, 1).reshape(rows_dev *...]
    transpose x2 -> x0, other arithmetic: 7 us -> none  [gather_rounds(): buf = jnp.transpose(buf, tuple(order) + tuple(range(depth, buf.ndim)))]
    select_n x0 -> x1, local copies, waits for them, and re-layouts: none -> 6.14 us  [gather_rounds(): buf = jnp.where(mine == 0, jnp.stack([buf, recv]), jnp.stack([recv, buf]))]
    gather x1 -> x3, local copies, waits for them, and re-layouts: 3.42 us -> 8.73 us  [the longest x1 3.11 us: per_device(): x_blocks[x_position(group_devices)].reshape(group_rows, steps, width)]
    transpose x2 -> x0, local copies, waits for them, and re-layouts: 3.96 us -> none  [gather_rounds(): buf = jnp.transpose(buf, tuple(order) + tuple(range(depth, buf.ndim)))]
  transfers between devices with their start and end apart: 22 -> 22, of which waited for: 20 -> 19; matrix products, arithmetic and copies ran while one was open for 16% -> 16% of each run, Pallas kernels for 0% -> 0%
where the time goes in v11:
time: 240 us
  waiting for transfers between devices  103 us (43%)
  local copies, waits for them, and re-layouts  40.8 us (17%)
  other arithmetic  33.4 us (14%)
  starting transfers between devices  29.3 us (12%)
  matrix products  17.3 us (7%)
  between operations  15.8 us (7%)
    ppermute x14, waiting for transfers between devices, gather_rounds(): recv = lax.ppermute(buf, axes, perm)  70.7 us
    ppermute x7, waiting for transfers between devices, scatter_rounds(): buf = keep + lax.ppermute(send, axes, perm)  32.4 us
    ppermute x14, starting transfers between devices, gather_rounds(): recv = lax.ppermute(buf, axes, perm)  24.1 us
    select_n x26, other arithmetic, gather_rounds(): buf = jnp.where(mine == 0, jnp.stack([buf, recv]), jnp.stack([recv, buf]))  18.2 us
    select_n x1, local copies, waits for them, and re-layouts, gather_rounds(): buf = jnp.where(mine == 0, jnp.stack([buf, recv]), jnp.stack([recv, buf]))  6.14 us
    ppermute x7, starting transfers between devices, scatter_rounds(): buf = keep + lax.ppermute(send, axes, perm)  5.19 us
  transfers between devices with their start and end apart: 22, of which 19 were waited for; matrix products, arithmetic and copies ran while one was open for 16% of the time, Pallas kernels for 0%

profile of v11, /device:TPU:0, one launch (start us, length us, event | category | flops | bytes accessed | tf_op | source)
XLA Modules:
  0.0 239.7 jit_solution(9754597962009704931)
XLA Ops:
  7.4 1.7 collective-permute-start
  21.0 2.2 collective-permute-start.1
  23.2 3.2 %collective-permute-done.1 = bf16[2,8,1536]{2,1,0:T(8,128)(2,1)S(1)} collective-permute-done((bf16[2,8,1536]{2,1,0:T(8,128)(2,1)S(1)}, bf16[2,8,1536]{2,1,0:T(8,128)(2,1)S(1)}, u32[]{:S(2)}, u32[]{:S(2)}) %collective-permute-start.1) | collective-permute-done | bytes 49184 | tf_op jit(solution)/shard_map/ppermute | solution.py:46
  26.4 2.0 collective-permute-start.2
  28.5 2.7 %collective-permute-done.2 = bf16[2,2,8,1536]{3,2,1,0:T(8,128)(2,1)S(1)} collective-permute-done((bf16[2,2,8,1536]{3,2,1,0:T(8,128)(2,1)S(1)}, bf16[2,2,8,1536]{3,2,1,0:T(8,128)(2,1)S(1)}, u32[]{:S(2)}, u32[]{:S(2)}) %collective-permute-start.2) | collective-permute-done | bytes 98336 | tf_op jit(solution)/shard_map/ppermute | solution.py:46
  31.1 4.1 %collective-permute-start.3 = (bf16[2,2,2,8,1536]{4,3,2,1,0:T(8,128)(2,1)S(1)}, bf16[2,2,2,8,1536]{4,3,2,1,0:T(8,128)(2,1)S(1)}, u32[]{:S(2)}, u32[]{:S(2)}) collective-permute-start(bf16[2,2,2,8,1536]{4,3,2,1,0:T(8,128)(2,1)S(1)} %maximum_select_fusion.16), channel_id=1, source_target_pairs={{0,24},{1,25},{2,26},{3,27},{4,28},{5,29},{6,30},{7,31},{8,16},{9,... | collective-permute-start | bytes 589832 | tf_op jit(solution)/shard_map/ppermute | solution.py:46
  35.3 3.6 %collective-permute-done.3 = bf16[2,2,2,8,1536]{4,3,2,1,0:T(8,128)(2,1)S(1)} collective-permute-done((bf16[2,2,2,8,1536]{4,3,2,1,0:T(8,128)(2,1)S(1)}, bf16[2,2,2,8,1536]{4,3,2,1,0:T(8,128)(2,1)S(1)}, u32[]{:S(2)}, u32[]{:S(2)}) %collective-permute-start.3) | collective-permute-done | bytes 196640 | tf_op jit(solution)/shard_map/ppermute | solution.py:46
  39.0 1.7 collective-permute-start.4
  40.7 6.1 %collective-permute-done.4 = bf16[2,2,2,2,8,1536]{5,4,3,2,1,0:T(8,128)(2,1)S(1)} collective-permute-done((bf16[2,2,2,2,8,1536]{5,4,3,2,1,0:T(8,128)(2,1)S(1)}, bf16[2,2,2,2,8,1536]{5,4,3,2,1,0:T(8,128)(2,1)S(1)}, u32[]{:S(2)}, u32[]{:S(2)}) %collective-permute-start.4) | collective-permute-done | bytes 393248 | tf_op jit(solution)/shard_map/ppermute | solution.py:46
  47.0 3.1 %collective-permute-start.5 = (bf16[2,2,2,2,2,8,1536]{6,5,4,3,2,1,0:T(8,128)(2,1)S(1)}, bf16[2,2,2,2,2,8,1536]{6,5,4,3,2,1,0:T(8,128)(2,1)S(1)}, u32[]{:S(2)}, u32[]{:S(2)}) collective-permute-start(bf16[2,2,2,2,2,8,1536]{6,5,4,3,2,1,0:T(8,128)(2,1)S(1)} %maximum_select_fusion.7), channel_id=1, source_target_pairs={{0,6},{1,7},{2,4},{3,5},{4,2},{5,3},{6,0},{7,1},{8,14},{9,15},{10,... | collective-permute-start | bytes 2359304 | tf_op jit(solution)/shard_map/ppermute | solution.py:46
  50.5 12.5 %collective-permute-done.5 = bf16[2,2,2,2,2,8,1536]{6,5,4,3,2,1,0:T(8,128)(2,1)S(1)} collective-permute-done((bf16[2,2,2,2,2,8,1536]{6,5,4,3,2,1,0:T(8,128)(2,1)S(1)}, bf16[2,2,2,2,2,8,1536]{6,5,4,3,2,1,0:T(8,128)(2,1)S(1)}, u32[]{:S(2)}, u32[]{:S(2)}) %collective-permute-start.5) | collective-permute-done | bytes 786464 | tf_op jit(solution)/shard_map/ppermute | solution.py:46
  63.0 1.4 maximum_select_fusion.3
  65.7 2.4 %collective-permute-done.6 = bf16[2,2,2,2,2,2,8,1536]{7,6,5,4,3,2,1,0:T(8,128)(2,1)} collective-permute-done((bf16[2,2,2,2,2,2,8,1536]{7,6,5,4,3,2,1,0:T(8,128)(2,1)}, bf16[2,2,2,2,2,2,8,1536]{7,6,5,4,3,2,1,0:T(8,128)(2,1)}, u32[]{:S(2)}, u32[]{:S(2)}) %collective-permute-start.6) | collective-permute-done | bytes 1572896 | tf_op jit(solution)/shard_map/ppermute | solution.py:46
  68.1 3.7 %maximum_select_fusion = bf16[2,2,2,2,2,2,2,8,1536]{8,7,6,5,4,3,2,1,0:T(8,128)(2,1)} fusion(bf16[1,2,2,2,2,2,2,8,1536]{8,7,6,5,4,3,2,1,0:T(8,128)(2,1)} %bitcast.18, bf16[1,2,2,2,2,2,2,8,1536]{8,7,6,5,4,3,2,1,0:T(8,128)(2,1)S(1)} %maximum_select_fusion.2, pred[]{:T(512)S(6)} %eq.122), kind=kLoop, calls=%fused_computation.32 | loop fusion | flops 4718592 | bytes 6291457 | tf_op jit(solution)/shard_map/jit(_where)/select_n | solution.py:48
  71.8 6.1 %select_n.1256 = bf16[128,2,4,1536]{3,2,1,0:T(4,128)(2,1)} reshape(bf16[2,2,2,2,2,2,2,8,1536]{8,7,6,5,4,3,2,1,0:T(8,128)(2,1)} %maximum_select_fusion) | data formatting | bytes 6291456 | tf_op jit(solution)/shard_map/jit(_where)/select_n | solution.py:48
  78.0 2.5 %gather_fusion.6 = bf16[4,2,4,1536]{3,2,1,0:T(4,128)(2,1)S(1)} fusion(bf16[128,2,4,1536]{3,2,1,0:T(4,128)(2,1)} %select_n.1256, s32[1024]{0:T(1024)S(1)} %pad_clamp_fusion.6), kind=kCustom, calls=%fused_computation.6 | custom fusion | bytes 196624 | tf_op jit(solution)/shard_map/gather | solution.py:136
  80.8 4.1 %fusion.18 = bf16[8,4,2048]{2,0,1:T(8,128)(2,1)S(1)} fusion(bf16[1536,2048]{1,0:T(8,128)(2,1)} %param.13, f32[2048]{0:T(1024)S(1)} %copy-done.5, f32[8,4,1536]{2,1,0:T(4,128)S(1)} %bitcast_convert_fusion, f32[8,4]{0,1:T(4,128)S(1)} %copy.184), kind=kOutput, calls=%fused_computation.40 | convolution fusion | flops 201555968 | bytes 6627456 | tf_op jit(solution)/shard_map/dot_general | solution.py:144
  88.3 2.1 fusion.5
  90.4 4.6 %fusion.2 = (bf16[2,8,4,2,6,4096]{5,1,0,4,2,3:T(8,128)(2,1)S(1)}, f32[2,8,4,2,6]{1,0,4,2,3:T(2,128)S(1)}) fusion(f32[2,8,4,2,6]{1,0,4,2,3:T(2,128)S(1)} %fusion.5, pred[2,4096]{1,0:T(4,128)(4,1)S(1)} %iota_compare_fusion, f32[2,8,4,1,6,4096]{5,1,0,4,2,3:T(8,128)S(1)} %convolution_bitcast_fusion, f32[2,8,4,1,6,4096]{5,1,0,4,2,3:T(8,128)S(1)} %convolution_bitcast_fusion.1), kind=kLoop, calls=%fused_computation.22 | loop fusion | flops 22019328 | bytes 18888704 | tf_op jit(solution)/shard_map/convert_element_type | solution.py:181
  95.9 1.4 copy-done.7
  105.5 4.2 %collective-permute-done.8 = f32[1,2,4,2,6,130]{5,4,3,2,1,0:T(8,128)S(1)} collective-permute-done((f32[1,2,4,2,6,130]{5,4,3,2,1,0:T(8,128)S(1)}, f32[1,2,4,2,6,130]{5,4,3,2,1,0:T(8,128)S(1)}, u32[]{:S(2)}, u32[]{:S(2)}) %collective-permute-start.8) | collective-permute-done | bytes 49952 | tf_op jit(solution)/shard_map/ppermute | solution.py:72
  111.1 3.8 %collective-permute-done.9 = bf16[2,4,1536]{2,1,0:T(4,128)(2,1)S(1)} collective-permute-done((bf16[2,4,1536]{2,1,0:T(4,128)(2,1)S(1)}, bf16[2,4,1536]{2,1,0:T(4,128)(2,1)S(1)}, u32[]{:S(2)}, u32[]{:S(2)}) %collective-permute-start.9) | collective-permute-done | bytes 24608 | tf_op jit(solution)/shard_map/ppermute | solution.py:46
  114.9 2.2 collective-permute-start.10
  117.2 3.1 %collective-permute-done.10 = bf16[2,2,4,1536]{3,2,1,0:T(4,128)(2,1)S(1)} collective-permute-done((bf16[2,2,4,1536]{3,2,1,0:T(4,128)(2,1)S(1)}, bf16[2,2,4,1536]{3,2,1,0:T(4,128)(2,1)S(1)}, u32[]{:S(2)}, u32[]{:S(2)}) %collective-permute-start.10) | collective-permute-done | bytes 49184 | tf_op jit(solution)/shard_map/ppermute | solution.py:46
  120.6 4.6 %collective-permute-done.11 = bf16[2,2,2,4,1536]{4,3,2,1,0:T(4,128)(2,1)S(1)} collective-permute-done((bf16[2,2,2,4,1536]{4,3,2,1,0:T(4,128)(2,1)S(1)}, bf16[2,2,2,4,1536]{4,3,2,1,0:T(4,128)(2,1)S(1)}, u32[]{:S(2)}, u32[]{:S(2)}) %collective-permute-start.11) | collective-permute-done | bytes 98336 | tf_op jit(solution)/shard_map/ppermute | solution.py:46
  125.3 2.9 %collective-permute-start.12 = (bf16[2,2,2,2,4,1536]{5,4,3,2,1,0:T(4,128)(2,1)S(1)}, bf16[2,2,2,2,4,1536]{5,4,3,2,1,0:T(4,128)(2,1)S(1)}, u32[]{:S(2)}, u32[]{:S(2)}) collective-permute-start(bf16[2,2,2,2,4,1536]{5,4,3,2,1,0:T(4,128)(2,1)S(1)} %maximum_select_fusion.18), channel_id=1, source_target_pairs={{0,24},{1,25},{2,26},{3,27},{4,28},{5,29},{6,30},{7,31},{8,16},{9,... | collective-permute-start | bytes 589832 | tf_op jit(solution)/shard_map/ppermute | solution.py:46
  128.4 3.9 %collective-permute-done.12 = bf16[2,2,2,2,4,1536]{5,4,3,2,1,0:T(4,128)(2,1)S(1)} collective-permute-done((bf16[2,2,2,2,4,1536]{5,4,3,2,1,0:T(4,128)(2,1)S(1)}, bf16[2,2,2,2,4,1536]{5,4,3,2,1,0:T(4,128)(2,1)S(1)}, u32[]{:S(2)}, u32[]{:S(2)}) %collective-permute-start.12) | collective-permute-done | bytes 196640 | tf_op jit(solution)/shard_map/ppermute | solution.py:46
  133.7 14.7 %collective-permute-done.13 = bf16[2,2,2,2,2,4,1536]{6,5,4,3,2,1,0:T(4,128)(2,1)S(1)} collective-permute-done((bf16[2,2,2,2,2,4,1536]{6,5,4,3,2,1,0:T(4,128)(2,1)S(1)}, bf16[2,2,2,2,2,4,1536]{6,5,4,3,2,1,0:T(4,128)(2,1)S(1)}, u32[]{:S(2)}, u32[]{:S(2)}) %collective-permute-start.13) | collective-permute-done | bytes 393248 | tf_op jit(solution)/shard_map/ppermute | solution.py:46
  148.3 1.5 maximum_select_fusion.9
  149.8 3.3 %collective-permute-start.14 = (bf16[2,2,2,2,2,2,4,1536]{7,6,5,4,3,2,1,0:T(4,128)(2,1)}, bf16[2,2,2,2,2,2,4,1536]{7,6,5,4,3,2,1,0:T(4,128)(2,1)S(1)}, u32[]{:S(2)}, u32[]{:S(2)}) collective-permute-start(bf16[2,2,2,2,2,2,4,1536]{7,6,5,4,3,2,1,0:T(4,128)(2,1)} %maximum_select_fusion.9), channel_id=1, source_target_pairs={{0,6},{1,7},{2,4},{3,5},{4,2},{5,3},{6,0},{7,1},{8,14},{9,15},{10,... | collective-permute-start | bytes 2359304 | tf_op jit(solution)/shard_map/ppermute | solution.py:46
  154.3 10.1 %collective-permute-done.14 = bf16[2,2,2,2,2,2,4,1536]{7,6,5,4,3,2,1,0:T(4,128)(2,1)S(1)} collective-permute-done((bf16[2,2,2,2,2,2,4,1536]{7,6,5,4,3,2,1,0:T(4,128)(2,1)}, bf16[2,2,2,2,2,2,4,1536]{7,6,5,4,3,2,1,0:T(4,128)(2,1)S(1)}, u32[]{:S(2)}, u32[]{:S(2)}) %collective-permute-start.14) | collective-permute-done | bytes 786464 | tf_op jit(solution)/shard_map/ppermute | solution.py:46
  164.4 2.0 maximum_select_fusion.5
  166.5 3.1 %gather_fusion = bf16[32,2,4,1536]{3,2,1,0:T(4,128)(2,1)S(1)} fusion(bf16[128,2,4,1536]{3,2,1,0:T(4,128)(2,1)} %select_n.1256, s32[1024]{0:T(1024)S(1)} %pad_clamp_fusion.12), kind=kCustom, calls=%fused_computation | custom fusion | bytes 1572992 | tf_op jit(solution)/shard_map/gather | solution.py:138
  169.9 2.2 copy.183
  173.9 6.0 %maximum_select_fusion.1 = bf16[2,2,2,2,2,2,2,2,4,1536]{9,8,7,6,5,4,3,2,1,0:T(4,128)(2,1)} fusion(bf16[1,2,2,2,2,2,2,2,4,1536]{9,8,7,6,5,4,3,2,1,0:T(4,128)(2,1)} %bitcast.115, bf16[1,2,2,2,2,2,2,2,4,1536]{9,8,7,6,5,4,3,2,1,0:T(4,128)(2,1)S(1)} %maximum_select_fusion.4, pred[]{:T(512)S(6)} %eq.122), kind=kLoop, calls=%fused_computation.33 | loop fusion | flops 4718592 | bytes 6291457 | tf_op jit(solution)/shard_map/jit(_where)/select_n | solution.py:48
  179.9 3.1 %gather_fusion.16 = bf16[32,2,4,1536]{3,2,1,0:T(4,128)(2,1)S(1)} fusion(bf16[128,2,4,1536]{3,2,1,0:T(4,128)(2,1)} %bitcast.336, s32[1024]{0:T(1024)S(1)} %pad_clamp_fusion), kind=kCustom, calls=%fused_computation.16 | custom fusion | bytes 1572992 | tf_op jit(solution)/shard_map/gather | solution.py:247
  183.0 4.6 %multiply_reduce_fusion = (f32[64,4]{0,1:T(4,128)S(1)}, f32[64,4,1536]{2,0,1:T(8,128)S(1)}) fusion(bf16[1536,1536]{1,0:T(8,128)(2,1)} %all-gather.2.cloned.1.call-done, bf16[64,4,1536]{2,1,0:T(4,128)(2,1)S(1)} %bitcast.370, f32[64,4,1536]{2,1,0:T(4,128)} %bitcast.363), kind=kOutput, calls=%fused_computation.54 | convolution fusion | flops 1209138944 | bytes 8651776 | tf_op jit(solution)/shard_map/dot_general | solution.py:249
  188.3 3.5 %fusion.40 = f32[64,4,1536]{2,0,1:T(8,128)} fusion(bf16[280,1536]{1,0:T(8,128)(2,1)S(1)} %copy-done, bf16[1536,280]{0,1:T(8,128)(2,1)} %param.17, f32[64,4,280]{2,0,1:T(8,128)S(1)} %fusion.45, f32[64,4,1536]{2,0,1:T(8,128)S(1)} %get-tuple-element.32, f32[64,4]{0,1:T(4,128)S(1)} %add_rsqrt_fusion.1), kind=kOutput, calls=%fused_computation.59 | convolution fusion | flops 441618432 | bytes 5153792 | tf_op jit(solution)/shard_map/dot_general | solution.py:256
  191.8 3.6 %copy.213 = f32[64,4,1536]{2,1,0:T(4,128)} copy(f32[64,4,1536]{2,0,1:T(8,128)} %fusion.40) | data formatting | bytes 3145728 | tf_op jit(solution)/shard_map/dot_general | solution.py:256
  195.3 1.8 reshape_reshape.2
  197.9 2.0 collective-permute-done.16
  201.5 11.2 %collective-permute-done.17 = f32[8,8,1536]{2,1,0:T(8,128)S(1)} collective-permute-done((f32[8,8,1536]{2,1,0:T(8,128)S(1)}, f32[8,8,1536]{2,1,0:T(8,128)S(1)}, u32[]{:S(2)}, u32[]{:S(2)}) %collective-permute-start.17) | collective-permute-done | bytes 393248 | tf_op jit(solution)/shard_map/ppermute | solution.py:72
  212.9 2.0 collective-permute-start.18
  214.9 5.9 %collective-permute-done.18 = f32[4,8,1536]{2,1,0:T(8,128)S(1)} collective-permute-done((f32[4,8,1536]{2,1,0:T(8,128)S(1)}, f32[4,8,1536]{2,1,0:T(8,128)S(1)}, u32[]{:S(2)}, u32[]{:S(2)}) %collective-permute-start.18) | collective-permute-done | bytes 196640 | tf_op jit(solution)/shard_map/ppermute | solution.py:72
  221.0 4.6 %collective-permute-done.19 = f32[2,8,1536]{2,1,0:T(8,128)S(1)} collective-permute-done((f32[2,8,1536]{2,1,0:T(8,128)S(1)}, f32[2,8,1536]{2,1,0:T(8,128)S(1)}, u32[]{:S(2)}, u32[]{:S(2)}) %collective-permute-start.19) | collective-permute-done | bytes 98336 | tf_op jit(solution)/shard_map/ppermute | solution.py:72
  225.6 1.7 collective-permute-start.20
  227.3 4.0 %collective-permute-done.20 = f32[1,8,1536]{2,1,0:T(8,128)S(1)} collective-permute-done((f32[1,8,1536]{2,1,0:T(8,128)S(1)}, f32[1,8,1536]{2,1,0:T(8,128)S(1)}, u32[]{:S(2)}, u32[]{:S(2)}) %collective-permute-start.20) | collective-permute-done | bytes 49184 | tf_op jit(solution)/shard_map/ppermute | solution.py:72
  231.3 1.6 fusion.85
  (191 shorter events, 35.5 us)
Async XLA Ops:
  6.5 181.8 %copy-start = (bf16[280,1536]{1,0:T(8,128)(2,1)S(1)}, bf16[280,1536]{1,0:T(8,128)(2,1)}, u32[]{:S(2)}) copy-start(bf16[280,1536]{1,0:T(8,128)(2,1)} %param.18) | copy-start | bytes 2580484
  6.5 9.0 %copy-start.6 = (s32[32,8]{0,1:T(8,128)S(1)}, s32[32,8]{0,1:T(8,128)}, u32[]{:S(2)}) copy-start(s32[32,8]{0,1:T(8,128)} %param.21) | copy-start | bytes 3076
  6.5 176.5 %all-gather.2.cloned.1.call-start = ((), (), s32[]{:S(2)}) async-start(), calls=%async_computation | async-start | bytes 4866048 | tf_op jit(solution)/shard_map/all_gather | solution.py:140
  7.4 13.6 %collective-permute-start = (bf16[8,1536]{1,0:T(8,128)(2,1)S(1)}, bf16[8,1536]{1,0:T(8,128)(2,1)S(1)}, u32[]{:S(2)}, u32[]{:S(2)}) collective-permute-start(bf16[8,1536]{1,0:T(8,128)(2,1)S(1)} %reshape.3294), channel_id=1, source_target_pairs={{0,32},{1,33},{2,34},{3,35},{4,36},{5,37},{6,38},{7,39},{8,40},{9,... | collective-permute-start | bytes 73736 | tf_op jit(solution)/shard_map/ppermute | solution.py:46
  21.0 5.4 %collective-permute-start.1 = (bf16[2,8,1536]{2,1,0:T(8,128)(2,1)S(1)}, bf16[2,8,1536]{2,1,0:T(8,128)(2,1)S(1)}, u32[]{:S(2)}, u32[]{:S(2)}) collective-permute-start(bf16[2,8,1536]{2,1,0:T(8,128)(2,1)S(1)} %maximum_select_fusion.24), channel_id=1, source_target_pairs={{0,96},{1,97},{2,98},{3,99},{4,100},{5,101},{6,102},{7,103},{8,104... | collective-permute-start | bytes 147464 | tf_op jit(solution)/shard_map/ppermute | solution.py:46
  26.4 4.7 %collective-permute-start.2 = (bf16[2,2,8,1536]{3,2,1,0:T(8,128)(2,1)S(1)}, bf16[2,2,8,1536]{3,2,1,0:T(8,128)(2,1)S(1)}, u32[]{:S(2)}, u32[]{:S(2)}) collective-permute-start(bf16[2,2,8,1536]{3,2,1,0:T(8,128)(2,1)S(1)} %maximum_select_fusion.20), channel_id=1, source_target_pairs={{0,8},{1,9},{2,10},{3,11},{4,12},{5,13},{6,14},{7,15},{8,0},{9,1},... | collective-permute-start | bytes 294920 | tf_op jit(solution)/shard_map/ppermute | solution.py:46
  31.1 7.8 %collective-permute-start.3 = (bf16[2,2,2,8,1536]{4,3,2,1,0:T(8,128)(2,1)S(1)}, bf16[2,2,2,8,1536]{4,3,2,1,0:T(8,128)(2,1)S(1)}, u32[]{:S(2)}, u32[]{:S(2)}) collective-permute-start(bf16[2,2,2,8,1536]{4,3,2,1,0:T(8,128)(2,1)S(1)} %maximum_select_fusion.16), channel_id=1, source_target_pairs={{0,24},{1,25},{2,26},{3,27},{4,28},{5,29},{6,30},{7,31},{8,16},{9,... | collective-permute-start | bytes 589832 | tf_op jit(solution)/shard_map/ppermute | solution.py:46
  39.0 7.9 %collective-permute-start.4 = (bf16[2,2,2,2,8,1536]{5,4,3,2,1,0:T(8,128)(2,1)S(1)}, bf16[2,2,2,2,8,1536]{5,4,3,2,1,0:T(8,128)(2,1)S(1)}, u32[]{:S(2)}, u32[]{:S(2)}) collective-permute-start(bf16[2,2,2,2,8,1536]{5,4,3,2,1,0:T(8,128)(2,1)S(1)} %maximum_select_fusion.11), channel_id=1, source_target_pairs={{0,2},{1,3},{2,0},{3,1},{4,6},{5,7},{6,4},{7,5},{8,10},{9,11},{10,... | collective-permute-start | bytes 1179656 | tf_op jit(solution)/shard_map/ppermute | solution.py:46
  47.0 16.0 %collective-permute-start.5 = (bf16[2,2,2,2,2,8,1536]{6,5,4,3,2,1,0:T(8,128)(2,1)S(1)}, bf16[2,2,2,2,2,8,1536]{6,5,4,3,2,1,0:T(8,128)(2,1)S(1)}, u32[]{:S(2)}, u32[]{:S(2)}) collective-permute-start(bf16[2,2,2,2,2,8,1536]{6,5,4,3,2,1,0:T(8,128)(2,1)S(1)} %maximum_select_fusion.7), channel_id=1, source_target_pairs={{0,6},{1,7},{2,4},{3,5},{4,2},{5,3},{6,0},{7,1},{8,14},{9,15},{10,... | collective-permute-start | bytes 2359304 | tf_op jit(solution)/shard_map/ppermute | solution.py:46
  64.4 3.8 %collective-permute-start.6 = (bf16[2,2,2,2,2,2,8,1536]{7,6,5,4,3,2,1,0:T(8,128)(2,1)}, bf16[2,2,2,2,2,2,8,1536]{7,6,5,4,3,2,1,0:T(8,128)(2,1)}, u32[]{:S(2)}, u32[]{:S(2)}) collective-permute-start(bf16[2,2,2,2,2,2,8,1536]{7,6,5,4,3,2,1,0:T(8,128)(2,1)} %maximum_select_fusion.3), channel_id=1, source_target_pairs={{0,1},{1,0},{2,3},{3,2},{4,5},{5,4},{6,7},{7,6},{8,9},{9,8},{10,11... | collective-permute-start | bytes 4718600 | tf_op jit(solution)/shard_map/ppermute | solution.py:46
  71.8 8.9 %copy-start.5 = (f32[2048]{0:T(1024)S(1)}, f32[2048]{0:T(1024)}, u32[]{:S(2)}) copy-start(f32[2048]{0:T(1024)} %param.14) | copy-start | bytes 24580
  80.8 4.3 %copy-start.2 = (bf16[2,4096,256]{2,1,0:T(8,128)(2,1)S(1)}, bf16[2,4096,256]{2,1,0:T(8,128)(2,1)}, u32[]{:S(2)}) copy-start(bf16[2,4096,256]{2,1,0:T(8,128)(2,1)} %param.19) | copy-start | bytes 12582916
  95.1 2.2 copy-start.7
  98.2 3.2 %copy-start.4 = (bf16[48,1536]{1,0:T(8,128)(2,1)S(1)}, bf16[48,1536]{1,0:T(8,128)(2,1)}, u32[]{:S(2)}) copy-start(bf16[48,1536]{1,0:T(8,128)(2,1)} %param.15) | copy-start | bytes 442372
  102.3 1.6 collective-permute-start.7
  104.0 5.6 %collective-permute-start.8 = (f32[1,2,4,2,6,130]{5,4,3,2,1,0:T(8,128)S(1)}, f32[1,2,4,2,6,130]{5,4,3,2,1,0:T(8,128)S(1)}, u32[]{:S(2)}, u32[]{:S(2)}) collective-permute-start(f32[1,2,4,2,6,130]{5,4,3,2,1,0:T(8,128)S(1)} %select_bitcast_fusion.4), channel_id=1, source_target_pairs={{0,2},{1,3},{2,0},{3,1},{4,6},{5,7},{6,4},{7,5},{8,10},{9,11},{10,... | collective-permute-start | bytes 149768 | tf_op jit(solution)/shard_map/ppermute | solution.py:72
  110.3 42.9 %copy-start.8 = (s32[32]{0:T(128)S(1)}, s32[32]{0:T(128)}, u32[]{:S(2)}) copy-start(s32[32]{0:T(128)} %param.23) | copy-start | bytes 388
  110.7 4.1 %collective-permute-start.9 = (bf16[2,4,1536]{2,1,0:T(4,128)(2,1)S(1)}, bf16[2,4,1536]{2,1,0:T(4,128)(2,1)S(1)}, u32[]{:S(2)}, u32[]{:S(2)}) collective-permute-start(bf16[2,4,1536]{2,1,0:T(4,128)(2,1)S(1)} %convert_element_type.99), channel_id=1, source_target_pairs={{0,32},{1,33},{2,34},{3,35},{4,36},{5,37},{6,38},{7,39},{8,40},{9,... | collective-permute-start | bytes 73736 | tf_op jit(solution)/shard_map/ppermute | solution.py:46
  114.9 5.4 %collective-permute-start.10 = (bf16[2,2,4,1536]{3,2,1,0:T(4,128)(2,1)S(1)}, bf16[2,2,4,1536]{3,2,1,0:T(4,128)(2,1)S(1)}, u32[]{:S(2)}, u32[]{:S(2)}) collective-permute-start(bf16[2,2,4,1536]{3,2,1,0:T(4,128)(2,1)S(1)} %maximum_select_fusion.26), channel_id=1, source_target_pairs={{0,96},{1,97},{2,98},{3,99},{4,100},{5,101},{6,102},{7,103},{8,104... | collective-permute-start | bytes 147464 | tf_op jit(solution)/shard_map/ppermute | solution.py:46
  120.3 4.9 %collective-permute-start.11 = (bf16[2,2,2,4,1536]{4,3,2,1,0:T(4,128)(2,1)S(1)}, bf16[2,2,2,4,1536]{4,3,2,1,0:T(4,128)(2,1)S(1)}, u32[]{:S(2)}, u32[]{:S(2)}) collective-permute-start(bf16[2,2,2,4,1536]{4,3,2,1,0:T(4,128)(2,1)S(1)} %maximum_select_fusion.22), channel_id=1, source_target_pairs={{0,8},{1,9},{2,10},{3,11},{4,12},{5,13},{6,14},{7,15},{8,0},{9,1},... | collective-permute-start | bytes 294920 | tf_op jit(solution)/shard_map/ppermute | solution.py:46
  125.3 7.0 %collective-permute-start.12 = (bf16[2,2,2,2,4,1536]{5,4,3,2,1,0:T(4,128)(2,1)S(1)}, bf16[2,2,2,2,4,1536]{5,4,3,2,1,0:T(4,128)(2,1)S(1)}, u32[]{:S(2)}, u32[]{:S(2)}) collective-permute-start(bf16[2,2,2,2,4,1536]{5,4,3,2,1,0:T(4,128)(2,1)S(1)} %maximum_select_fusion.18), channel_id=1, source_target_pairs={{0,24},{1,25},{2,26},{3,27},{4,28},{5,29},{6,30},{7,31},{8,16},{9,... | collective-permute-start | bytes 589832 | tf_op jit(solution)/shard_map/ppermute | solution.py:46
  132.6 15.7 %collective-permute-start.13 = (bf16[2,2,2,2,2,4,1536]{6,5,4,3,2,1,0:T(4,128)(2,1)S(1)}, bf16[2,2,2,2,2,4,1536]{6,5,4,3,2,1,0:T(4,128)(2,1)S(1)}, u32[]{:S(2)}, u32[]{:S(2)}) collective-permute-start(bf16[2,2,2,2,2,4,1536]{6,5,4,3,2,1,0:T(4,128)(2,1)S(1)} %maximum_select_fusion.14), channel_id=1, source_target_pairs={{0,2},{1,3},{2,0},{3,1},{4,6},{5,7},{6,4},{7,5},{8,10},{9,11},{10,... | collective-permute-start | bytes 1179656 | tf_op jit(solution)/shard_map/ppermute | solution.py:46
  149.8 14.5 %collective-permute-start.14 = (bf16[2,2,2,2,2,2,4,1536]{7,6,5,4,3,2,1,0:T(4,128)(2,1)}, bf16[2,2,2,2,2,2,4,1536]{7,6,5,4,3,2,1,0:T(4,128)(2,1)S(1)}, u32[]{:S(2)}, u32[]{:S(2)}) collective-permute-start(bf16[2,2,2,2,2,2,4,1536]{7,6,5,4,3,2,1,0:T(4,128)(2,1)} %maximum_select_fusion.9), channel_id=1, source_target_pairs={{0,6},{1,7},{2,4},{3,5},{4,2},{5,3},{6,0},{7,1},{8,14},{9,15},{10,... | collective-permute-start | bytes 2359304 | tf_op jit(solution)/shard_map/ppermute | solution.py:46
  166.4 7.5 %collective-permute-start.15 = (bf16[2,2,2,2,2,2,2,4,1536]{8,7,6,5,4,3,2,1,0:T(4,128)(2,1)}, bf16[2,2,2,2,2,2,2,4,1536]{8,7,6,5,4,3,2,1,0:T(4,128)(2,1)}, u32[]{:S(2)}, u32[]{:S(2)}) collective-permute-start(bf16[2,2,2,2,2,2,2,4,1536]{8,7,6,5,4,3,2,1,0:T(4,128)(2,1)} %maximum_select_fusion.5), channel_id=1, source_target_pairs={{0,1},{1,0},{2,3},{3,2},{4,5},{5,4},{6,7},{7,6},{8,9},{9,8},{10,11... | collective-permute-start | bytes 4718600 | tf_op jit(solution)/shard_map/ppermute | solution.py:46
  183.0 4.6 %copy-start.3 = (bf16[1536,280]{0,1:T(8,128)(2,1)S(1)}, bf16[1536,280]{0,1:T(8,128)(2,1)}, u32[]{:S(2)}) copy-start(bf16[1536,280]{0,1:T(8,128)(2,1)} %param.16) | copy-start | bytes 2580484
  187.7 4.1 %copy-start.1 = (f32[64,4,1536]{2,0,1:T(8,128)}, f32[64,4,1536]{2,0,1:T(8,128)S(1)}, u32[]{:S(2)}) copy-start(f32[64,4,1536]{2,0,1:T(8,128)S(1)} %get-tuple-element.32) | copy-start | bytes 4718596
  197.3 2.6 %collective-permute-start.16 = (f32[16,8,1536]{2,1,0:T(8,128)S(1)}, f32[16,8,1536]{2,1,0:T(8,128)}, u32[]{:S(2)}, u32[]{:S(2)}) collective-permute-start(f32[16,8,1536]{2,1,0:T(8,128)S(1)} %select_bitcast_fusion), channel_id=1, source_target_pairs={{0,1},{1,0},{2,3},{3,2},{4,5},{5,4},{6,7},{7,6},{8,9},{9,8},{10,11... | collective-permute-start | bytes 2359304 | tf_op jit(solution)/shard_map/ppermute | solution.py:72
  201.3 11.5 %collective-permute-start.17 = (f32[8,8,1536]{2,1,0:T(8,128)S(1)}, f32[8,8,1536]{2,1,0:T(8,128)S(1)}, u32[]{:S(2)}, u32[]{:S(2)}) collective-permute-start(f32[8,8,1536]{2,1,0:T(8,128)S(1)} %select_bitcast_fusion.1), channel_id=1, source_target_pairs={{0,2},{1,3},{2,0},{3,1},{4,6},{5,7},{6,4},{7,5},{8,10},{9,11},{10,... | collective-permute-start | bytes 1179656 | tf_op jit(solution)/shard_map/ppermute | solution.py:72
  212.9 7.9 %collective-permute-start.18 = (f32[4,8,1536]{2,1,0:T(8,128)S(1)}, f32[4,8,1536]{2,1,0:T(8,128)S(1)}, u32[]{:S(2)}, u32[]{:S(2)}) collective-permute-start(f32[4,8,1536]{2,1,0:T(8,128)S(1)} %select_bitcast_fusion.3), channel_id=1, source_target_pairs={{0,4},{1,5},{2,6},{3,7},{4,0},{5,1},{6,2},{7,3},{8,12},{9,13},{10,... | collective-permute-start | bytes 589832 | tf_op jit(solution)/shard_map/ppermute | solution.py:72
  220.8 4.7 %collective-permute-start.19 = (f32[2,8,1536]{2,1,0:T(8,128)S(1)}, f32[2,8,1536]{2,1,0:T(8,128)S(1)}, u32[]{:S(2)}, u32[]{:S(2)}) collective-permute-start(f32[2,8,1536]{2,1,0:T(8,128)S(1)} %select_bitcast_fusion.5), channel_id=1, source_target_pairs={{0,8},{1,9},{2,10},{3,11},{4,12},{5,13},{6,14},{7,15},{8,0},{9,1},... | collective-permute-start | bytes 294920 | tf_op jit(solution)/shard_map/ppermute | solution.py:72
  225.6 5.7 %collective-permute-start.20 = (f32[1,8,1536]{2,1,0:T(8,128)S(1)}, f32[1,8,1536]{2,1,0:T(8,128)S(1)}, u32[]{:S(2)}, u32[]{:S(2)}) collective-permute-start(f32[1,8,1536]{2,1,0:T(8,128)S(1)} %select_bitcast_fusion.6), channel_id=1, source_target_pairs={{0,16},{1,17},{2,18},{3,19},{4,20},{5,21},{6,22},{7,23},{8,24},{9,... | collective-permute-start | bytes 147464 | tf_op jit(solution)/shard_map/ppermute | solution.py:72
Sparse Core Ops, SparseCore 0:
  102.3 49.0 all-gather.1

commit v12 on v11

--- a/solution.py
+++ b/solution.py
@@ -44,8 +44,9 @@
         bit = low if mask == low else mask - low
         perm = [(i, i ^ mask) for i in range(count)]
         recv = lax.ppermute(buf, axes, perm)
-        mine = (index // bit) % 2
-        buf = jnp.where(mine == 0, jnp.stack([buf, recv]), jnp.stack([recv, buf]))
+        if mask != low:
+            recv = jnp.flip(recv, axis=0)
+        buf = jnp.stack([buf, recv])
         bits.append(bit)
     depth = len(bits)
     flat_buf = buf.reshape((count,) + x.shape)
@@ -53,7 +54,9 @@
     def position(device):
         pos = jnp.zeros_like(device)
         for a in range(depth):
-            pos = pos + ((device // bits[depth - 1 - a]) % 2) * (1 << (depth - 1 - a))
+            bit = bits[depth - 1 - a]
+            slot = ((device // bit) % 2) ^ ((index // bit) % 2)
+            pos = pos + slot * (1 << (depth - 1 - a))
         return pos
 
     return flat_buf, position

time: 240 us -> 240 us (level)
  other arithmetic: 33.4 us -> 27.3 us
  matrix products: 17.3 us -> 21.6 us
    select_n x26 -> x0, other arithmetic: 18.2 us -> none  [gather_rounds(): buf = jnp.where(mine == 0, jnp.stack([buf, recv]), jnp.stack([recv, buf]))]
    another operation x12 -> x16, other arithmetic: 1.51 us -> 14.2 us  [the longest x14 14 us: gather_rounds(): buf = jnp.stack([buf, recv])]
    another operation x3 -> x8, local copies, waits for them, and re-layouts: 0.05 us -> 6.63 us  [the longest x1 6.13 us: per_device(): x_blocks = x_blocks.reshape(x_blocks.shape[0], rows_dev, steps, width)]
    select_n x1 -> x0, local copies, waits for them, and re-layouts: 6.14 us -> none  [gather_rounds(): buf = jnp.where(mine == 0, jnp.stack([buf, recv]), jnp.stack([recv, buf]))]
    dot_general x2, matrix products: 1.95 us -> 6.24 us  [per_device(): jnp.einsum('cbtgp,cpd->cbtgd', weights[:, :, :, k], cache_values[:, :, k...]
  transfers between devices with their start and end apart: 22 -> 22, of which waited for: 19 -> 19; matrix products, arithmetic and copies ran while one was open for 16% -> 17% of each run, Pallas kernels for 0% -> 0%
where the time goes in v12:
time: 240 us; the launch traced here: 239 us
  waiting for transfers between devices  102 us (42%)
  local copies, waits for them, and re-layouts  42.4 us (18%)
  starting transfers between devices  29.4 us (12%)
  other arithmetic  27.3 us (11%)
  matrix products  21.6 us (9%)
  between operations  15.6 us (6%)
    ppermute x14, waiting for transfers between devices, gather_rounds(): recv = lax.ppermute(buf, axes, perm)  69.6 us
    ppermute x7, waiting for transfers between devices, scatter_rounds(): buf = keep + lax.ppermute(send, axes, perm)  32.8 us
    ppermute x14, starting transfers between devices, gather_rounds(): recv = lax.ppermute(buf, axes, perm)  23.7 us
    another operation x14, other arithmetic, gather_rounds(): buf = jnp.stack([buf, recv])  14 us
    dot_general x2, matrix products, per_device(): jnp.einsum('cbtgp,cpd->cbtgd', weights[:, :, :, k], cache_values[:, :, k...  6.24 us
    another operation x1, local copies, waits for them, and re-layouts, per_device(): x_blocks = x_blocks.reshape(x_blocks.shape[0], rows_dev, steps, width)  6.13 us
    ppermute x7, starting transfers between devices, scatter_rounds(): buf = keep + lax.ppermute(send, axes, perm)  5.68 us
  transfers between devices with their start and end apart: 22, of which 19 were waited for; matrix products, arithmetic and copies ran while one was open for 17% of the time, Pallas kernels for 0%

profile of v12, /device:TPU:0, one launch (start us, length us, event | category | flops | bytes accessed | tf_op | source)
XLA Modules:
  0.0 238.7 jit_solution(3134100380400845605)
XLA Ops:
  7.4 1.7 collective-permute-start
  15.6 2.2 collective-permute-start.1
  19.2 1.8 collective-permute-done.1
  21.0 2.0 collective-permute-start.2
  23.0 2.7 %collective-permute-done.2 = bf16[2,2,8,1536]{3,2,1,0:T(8,128)(2,1)S(1)} collective-permute-done((bf16[2,2,8,1536]{3,2,1,0:T(8,128)(2,1)S(1)}, bf16[2,2,8,1536]{3,2,1,0:T(8,128)(2,1)S(1)}, u32[]{:S(2)}, u32[]{:S(2)}) %collective-permute-start.2) | collective-permute-done | bytes 98336 | tf_op jit(solution)/shard_map/ppermute | solution.py:46
  25.7 4.1 %collective-permute-start.3 = (bf16[2,2,2,8,1536]{4,3,2,1,0:T(8,128)(2,1)S(1)}, bf16[2,2,2,8,1536]{4,3,2,1,0:T(8,128)(2,1)S(1)}, u32[]{:S(2)}, u32[]{:S(2)}) collective-permute-start(bf16[2,2,2,8,1536]{4,3,2,1,0:T(8,128)(2,1)S(1)} %get-tuple-element.34), channel_id=1, source_target_pairs={{0,24},{1,25},{2,26},{3,27},{4,28},{5,29},{6,30},{7,31},{8,16},{9,... | collective-permute-start | bytes 589832 | tf_op jit(solution)/shard_map/ppermute | solution.py:46
  29.9 3.6 %collective-permute-done.3 = bf16[2,2,2,8,1536]{4,3,2,1,0:T(8,128)(2,1)S(1)} collective-permute-done((bf16[2,2,2,8,1536]{4,3,2,1,0:T(8,128)(2,1)S(1)}, bf16[2,2,2,8,1536]{4,3,2,1,0:T(8,128)(2,1)S(1)}, u32[]{:S(2)}, u32[]{:S(2)}) %collective-permute-start.3) | collective-permute-done | bytes 196640 | tf_op jit(solution)/shard_map/ppermute | solution.py:46
  33.6 1.7 collective-permute-start.4
  35.3 6.1 %collective-permute-done.4 = bf16[2,2,2,2,8,1536]{5,4,3,2,1,0:T(8,128)(2,1)S(1)} collective-permute-done((bf16[2,2,2,2,8,1536]{5,4,3,2,1,0:T(8,128)(2,1)S(1)}, bf16[2,2,2,2,8,1536]{5,4,3,2,1,0:T(8,128)(2,1)S(1)}, u32[]{:S(2)}, u32[]{:S(2)}) %collective-permute-start.4) | collective-permute-done | bytes 393248 | tf_op jit(solution)/shard_map/ppermute | solution.py:46
  41.5 3.1 %collective-permute-start.5 = (bf16[2,2,2,2,2,8,1536]{6,5,4,3,2,1,0:T(8,128)(2,1)S(1)}, bf16[2,2,2,2,2,8,1536]{6,5,4,3,2,1,0:T(8,128)(2,1)S(1)}, u32[]{:S(2)}, u32[]{:S(2)}) collective-permute-start(bf16[2,2,2,2,2,8,1536]{6,5,4,3,2,1,0:T(8,128)(2,1)S(1)} %get-tuple-element.24), channel_id=1, source_target_pairs={{0,6},{1,7},{2,4},{3,5},{4,2},{5,3},{6,0},{7,1},{8,14},{9,15},{10,... | collective-permute-start | bytes 2359304 | tf_op jit(solution)/shard_map/ppermute | solution.py:46
  45.9 11.6 %collective-permute-done.5 = bf16[2,2,2,2,2,8,1536]{6,5,4,3,2,1,0:T(8,128)(2,1)S(1)} collective-permute-done((bf16[2,2,2,2,2,8,1536]{6,5,4,3,2,1,0:T(8,128)(2,1)S(1)}, bf16[2,2,2,2,2,8,1536]{6,5,4,3,2,1,0:T(8,128)(2,1)S(1)}, u32[]{:S(2)}, u32[]{:S(2)}) %collective-permute-start.5) | collective-permute-done | bytes 786464 | tf_op jit(solution)/shard_map/ppermute | solution.py:46
  57.6 1.4 fusion.207
  62.7 3.3 %pad_maximum_fusion = bf16[2,2,2,2,2,2,2,8,1536]{8,7,6,5,4,3,2,1,0:T(8,128)(2,1)} fusion(bf16[1,2,2,2,2,2,2,8,1536]{8,7,6,5,4,3,2,1,0:T(8,128)(2,1)} %bitcast.13, bf16[1,2,2,2,2,2,2,8,1536]{8,7,6,5,4,3,2,1,0:T(8,128)(2,1)S(1)} %get-tuple-element.19), kind=kLoop, calls=%fused_computation.32 | loop fusion | flops 1572864 | bytes 6291456 | tf_op jit(solution)/shard_map/stack | solution.py:49
  66.1 6.1 %reshape_reshape.7 = bf16[128,2,4,1536]{3,2,1,0:T(4,128)(2,1)} reshape(bf16[2,2,2,2,2,2,2,8,1536]{8,7,6,5,4,3,2,1,0:T(8,128)(2,1)} %pad_maximum_fusion) | data formatting | bytes 6291456 | tf_op jit(solution)/shard_map/reshape;reshape | solution.py:137
  72.2 2.5 %gather_fusion.6 = bf16[4,2,4,1536]{3,2,1,0:T(4,128)(2,1)S(1)} fusion(bf16[128,2,4,1536]{3,2,1,0:T(4,128)(2,1)} %reshape_reshape.7, s32[1024]{0:T(1024)S(1)} %pad_clamp_fusion.6), kind=kCustom, calls=%fused_computation.6 | custom fusion | bytes 196624 | tf_op jit(solution)/shard_map/gather | solution.py:139
  75.0 4.1 %fusion.18 = bf16[8,4,2048]{2,0,1:T(8,128)(2,1)S(1)} fusion(bf16[1536,2048]{1,0:T(8,128)(2,1)} %param.13, f32[2048]{0:T(1024)S(1)} %copy-done.6, f32[8,4,1536]{2,1,0:T(4,128)S(1)} %bitcast_convert_fusion, f32[8,4]{0,1:T(4,128)S(1)} %copy.180), kind=kOutput, calls=%fused_computation.40 | convolution fusion | flops 201555968 | bytes 6627456 | tf_op jit(solution)/shard_map/dot_general | solution.py:147
  82.6 2.1 fusion.5
  84.7 4.6 %fusion.2 = (bf16[2,8,4,2,6,4096]{5,1,0,4,2,3:T(8,128)(2,1)S(1)}, f32[2,8,4,2,6]{1,0,4,2,3:T(2,128)S(1)}) fusion(f32[2,8,4,2,6]{1,0,4,2,3:T(2,128)S(1)} %fusion.5, pred[2,4096]{1,0:T(4,128)(4,1)S(1)} %iota_compare_fusion, f32[2,8,4,1,6,4096]{5,1,0,4,2,3:T(8,128)S(1)} %convolution_bitcast_fusion, f32[2,8,4,1,6,4096]{5,1,0,4,2,3:T(8,128)S(1)} %convolution_bitcast_fusion.1), kind=kLoop, calls=%fused_computation.22 | loop fusion | flops 22019328 | bytes 18888704 | tf_op jit(solution)/shard_map/convert_element_type | solution.py:184
  89.4 3.1 %slice_bitcast_fusion.1 = (bf16[2,8,4,6,4096]{4,1,0,3,2:T(8,128)(2,1)}, bf16[2,8,4,6,4096]{4,1,0,3,2:T(8,128)(2,1)}) fusion(bf16[2,8,4,2,6,4096]{5,1,0,4,2,3:T(8,128)(2,1)S(1)} %get-tuple-element.13), kind=kLoop, calls=%fused_computation.31 | loop fusion | bytes 12582912 | tf_op jit(solution)/shard_map/squeeze | solution.py:189
  93.8 3.7 %fusion.30 = f32[2,8,4,1,6,128]{5,1,4,2,0,3:T(8,128)S(1)} fusion(bf16[2,4096,256]{2,1,0:T(8,128)(2,1)} %param.20, bf16[2,8,4,6,4096]{4,1,0,3,2:T(8,128)(2,1)} %get-tuple-element.15), kind=kOutput, calls=%fused_computation.55 | convolution fusion | flops 402653184 | bytes 5439488 | tf_op jit(solution)/shard_map/cbtgp,cpd->cbtgd/dot_general | solution.py:187
  97.5 2.6 %fusion.35 = f32[2,8,4,1,6,128]{5,1,4,2,0,3:T(8,128)S(1)} fusion(bf16[2,4096,256]{2,1,0:T(8,128)(2,1)} %param.20, bf16[2,8,4,6,4096]{4,1,0,3,2:T(8,128)(2,1)S(1)} %copy-done.3), kind=kOutput, calls=%fused_computation.56 | convolution fusion | flops 402653184 | bytes 5439488 | tf_op jit(solution)/shard_map/cbtgp,cpd->cbtgd/dot_general | solution.py:187
  105.0 5.1 %collective-permute-done.8 = f32[1,2,4,2,6,130]{5,4,3,2,1,0:T(8,128)S(1)} collective-permute-done((f32[1,2,4,2,6,130]{5,4,3,2,1,0:T(8,128)S(1)}, f32[1,2,4,2,6,130]{5,4,3,2,1,0:T(8,128)S(1)}, u32[]{:S(2)}, u32[]{:S(2)}) %collective-permute-start.8) | collective-permute-done | bytes 49952 | tf_op jit(solution)/shard_map/ppermute | solution.py:75
  111.2 3.8 %collective-permute-done.9 = bf16[2,4,1536]{2,1,0:T(4,128)(2,1)S(1)} collective-permute-done((bf16[2,4,1536]{2,1,0:T(4,128)(2,1)S(1)}, bf16[2,4,1536]{2,1,0:T(4,128)(2,1)S(1)}, u32[]{:S(2)}, u32[]{:S(2)}) %collective-permute-start.9) | collective-permute-done | bytes 24608 | tf_op jit(solution)/shard_map/ppermute | solution.py:46
  115.1 2.1 collective-permute-start.10
  117.1 3.3 %collective-permute-done.10 = bf16[2,2,4,1536]{3,2,1,0:T(4,128)(2,1)S(1)} collective-permute-done((bf16[2,2,4,1536]{3,2,1,0:T(4,128)(2,1)S(1)}, bf16[2,2,4,1536]{3,2,1,0:T(4,128)(2,1)S(1)}, u32[]{:S(2)}, u32[]{:S(2)}) %collective-permute-start.10) | collective-permute-done | bytes 49184 | tf_op jit(solution)/shard_map/ppermute | solution.py:46
  120.9 4.6 %collective-permute-done.11 = bf16[2,2,2,4,1536]{4,3,2,1,0:T(4,128)(2,1)S(1)} collective-permute-done((bf16[2,2,2,4,1536]{4,3,2,1,0:T(4,128)(2,1)S(1)}, bf16[2,2,2,4,1536]{4,3,2,1,0:T(4,128)(2,1)S(1)}, u32[]{:S(2)}, u32[]{:S(2)}) %collective-permute-start.11) | collective-permute-done | bytes 98336 | tf_op jit(solution)/shard_map/ppermute | solution.py:46
  125.6 3.5 %collective-permute-start.12 = (bf16[2,2,2,2,4,1536]{5,4,3,2,1,0:T(4,128)(2,1)S(1)}, bf16[2,2,2,2,4,1536]{5,4,3,2,1,0:T(4,128)(2,1)S(1)}, u32[]{:S(2)}, u32[]{:S(2)}) collective-permute-start(bf16[2,2,2,2,4,1536]{5,4,3,2,1,0:T(4,128)(2,1)S(1)} %get-tuple-element.32), channel_id=1, source_target_pairs={{0,24},{1,25},{2,26},{3,27},{4,28},{5,29},{6,30},{7,31},{8,16},{9,... | collective-permute-start | bytes 589832 | tf_op jit(solution)/shard_map/ppermute | solution.py:46
  129.1 7.6 %collective-permute-done.12 = bf16[2,2,2,2,4,1536]{5,4,3,2,1,0:T(4,128)(2,1)S(1)} collective-permute-done((bf16[2,2,2,2,4,1536]{5,4,3,2,1,0:T(4,128)(2,1)S(1)}, bf16[2,2,2,2,4,1536]{5,4,3,2,1,0:T(4,128)(2,1)S(1)}, u32[]{:S(2)}, u32[]{:S(2)}) %collective-permute-start.12) | collective-permute-done | bytes 196640 | tf_op jit(solution)/shard_map/ppermute | solution.py:46
  137.5 8.8 %collective-permute-done.13 = bf16[2,2,2,2,2,4,1536]{6,5,4,3,2,1,0:T(4,128)(2,1)S(1)} collective-permute-done((bf16[2,2,2,2,2,4,1536]{6,5,4,3,2,1,0:T(4,128)(2,1)S(1)}, bf16[2,2,2,2,2,4,1536]{6,5,4,3,2,1,0:T(4,128)(2,1)S(1)}, u32[]{:S(2)}, u32[]{:S(2)}) %collective-permute-start.13) | collective-permute-done | bytes 393248 | tf_op jit(solution)/shard_map/ppermute | solution.py:46
  146.9 2.7 %collective-permute-start.14 = (bf16[2,2,2,2,2,2,4,1536]{7,6,5,4,3,2,1,0:T(4,128)(2,1)S(1)}, bf16[2,2,2,2,2,2,4,1536]{7,6,5,4,3,2,1,0:T(4,128)(2,1)S(1)}, u32[]{:S(2)}, u32[]{:S(2)}) collective-permute-start(bf16[2,2,2,2,2,2,4,1536]{7,6,5,4,3,2,1,0:T(4,128)(2,1)S(1)} %get-tuple-element.22), channel_id=1, source_target_pairs={{0,6},{1,7},{2,4},{3,5},{4,2},{5,3},{6,0},{7,1},{8,14},{9,15},{10,... | collective-permute-start | bytes 2359304 | tf_op jit(solution)/shard_map/ppermute | solution.py:46
  149.6 15.1 %collective-permute-done.14 = bf16[2,2,2,2,2,2,4,1536]{7,6,5,4,3,2,1,0:T(4,128)(2,1)S(1)} collective-permute-done((bf16[2,2,2,2,2,2,4,1536]{7,6,5,4,3,2,1,0:T(4,128)(2,1)S(1)}, bf16[2,2,2,2,2,2,4,1536]{7,6,5,4,3,2,1,0:T(4,128)(2,1)S(1)}, u32[]{:S(2)}, u32[]{:S(2)}) %collective-permute-start.14) | collective-permute-done | bytes 786464 | tf_op jit(solution)/shard_map/ppermute | solution.py:46
  165.0 2.5 %fusion.208 = (bf16[1,2,2,2,2,2,2,2,4,1536]{9,8,7,6,5,4,3,2,1,0:T(4,128)(2,1)S(1)}, bf16[2,2,2,2,2,2,2,4,1536]{8,7,6,5,4,3,2,1,0:T(4,128)(2,1)}) fusion(bf16[1,2,2,2,2,2,2,4,1536]{8,7,6,5,4,3,2,1,0:T(4,128)(2,1)S(1)} %reverse_bitcast_fusion, bf16[1,2,2,2,2,2,2,4,1536]{8,7,6,5,4,3,2,1,0:T(4,128)(2,1)S(1)} %get-tuple-element.21), kind=kLoop, calls=%fused_computation.445 | loop fusion | flops 786432 | bytes 4718592 | tf_op jit(solution)/shard_map/stack | solution.py:49
  167.8 3.1 %gather_fusion = bf16[32,2,4,1536]{3,2,1,0:T(4,128)(2,1)S(1)} fusion(bf16[128,2,4,1536]{3,2,1,0:T(4,128)(2,1)} %reshape_reshape.7, s32[1024]{0:T(1024)S(1)} %pad_clamp_fusion.12), kind=kCustom, calls=%fused_computation | custom fusion | bytes 1572992 | tf_op jit(solution)/shard_map/gather | solution.py:141
  171.2 2.3 copy.179
  173.4 5.4 %pad_maximum_fusion.1 = bf16[2,2,2,2,2,2,2,2,4,1536]{9,8,7,6,5,4,3,2,1,0:T(4,128)(2,1)} fusion(bf16[1,2,2,2,2,2,2,2,4,1536]{9,8,7,6,5,4,3,2,1,0:T(4,128)(2,1)} %bitcast.105, bf16[1,2,2,2,2,2,2,2,4,1536]{9,8,7,6,5,4,3,2,1,0:T(4,128)(2,1)S(1)} %get-tuple-element.17), kind=kLoop, calls=%fused_computation.33 | loop fusion | flops 1572864 | bytes 6291456 | tf_op jit(solution)/shard_map/stack | solution.py:49
  178.8 3.1 %gather_fusion.16 = bf16[32,2,4,1536]{3,2,1,0:T(4,128)(2,1)S(1)} fusion(bf16[128,2,4,1536]{3,2,1,0:T(4,128)(2,1)} %bitcast.334, s32[1024]{0:T(1024)S(1)} %pad_clamp_fusion), kind=kCustom, calls=%fused_computation.16 | custom fusion | bytes 1572992 | tf_op jit(solution)/shard_map/gather | solution.py:250
  182.0 4.6 %multiply_reduce_fusion = (f32[64,4]{0,1:T(4,128)S(1)}, f32[64,4,1536]{2,0,1:T(8,128)S(1)}) fusion(bf16[1536,1536]{1,0:T(8,128)(2,1)} %all-gather.2.cloned.1.call-done, bf16[64,4,1536]{2,1,0:T(4,128)(2,1)S(1)} %bitcast.346, f32[64,4,1536]{2,1,0:T(4,128)} %bitcast.345), kind=kOutput, calls=%fused_computation.52 | convolution fusion | flops 1209138944 | bytes 8651776 | tf_op jit(solution)/shard_map/dot_general | solution.py:252
  187.3 3.5 %fusion.40 = f32[64,4,1536]{2,0,1:T(8,128)} fusion(bf16[280,1536]{1,0:T(8,128)(2,1)S(1)} %copy-done, bf16[1536,280]{0,1:T(8,128)(2,1)} %param.17, f32[64,4,280]{2,0,1:T(8,128)S(1)} %fusion.45, f32[64,4,1536]{2,0,1:T(8,128)S(1)} %get-tuple-element.56, f32[64,4]{0,1:T(4,128)S(1)} %add_rsqrt_fusion.1), kind=kOutput, calls=%fused_computation.57 | convolution fusion | flops 441618432 | bytes 5153792 | tf_op jit(solution)/shard_map/dot_general | solution.py:259
  190.7 3.6 %copy.209 = f32[64,4,1536]{2,1,0:T(4,128)} copy(f32[64,4,1536]{2,0,1:T(8,128)} %fusion.40) | data formatting | bytes 3145728 | tf_op jit(solution)/shard_map/dot_general | solution.py:259
  194.3 1.8 reshape_reshape.8
  196.8 2.0 collective-permute-done.16
  200.6 11.2 %collective-permute-done.17 = f32[8,8,1536]{2,1,0:T(8,128)S(1)} collective-permute-done((f32[8,8,1536]{2,1,0:T(8,128)S(1)}, f32[8,8,1536]{2,1,0:T(8,128)S(1)}, u32[]{:S(2)}, u32[]{:S(2)}) %collective-permute-start.17) | collective-permute-done | bytes 393248 | tf_op jit(solution)/shard_map/ppermute | solution.py:75
  211.9 2.1 collective-permute-start.18
  213.9 5.8 %collective-permute-done.18 = f32[4,8,1536]{2,1,0:T(8,128)S(1)} collective-permute-done((f32[4,8,1536]{2,1,0:T(8,128)S(1)}, f32[4,8,1536]{2,1,0:T(8,128)S(1)}, u32[]{:S(2)}, u32[]{:S(2)}) %collective-permute-start.18) | collective-permute-done | bytes 196640 | tf_op jit(solution)/shard_map/ppermute | solution.py:75
  220.3 4.3 %collective-permute-done.19 = f32[2,8,1536]{2,1,0:T(8,128)S(1)} collective-permute-done((f32[2,8,1536]{2,1,0:T(8,128)S(1)}, f32[2,8,1536]{2,1,0:T(8,128)S(1)}, u32[]{:S(2)}, u32[]{:S(2)}) %collective-permute-start.19) | collective-permute-done | bytes 98336 | tf_op jit(solution)/shard_map/ppermute | solution.py:75
  224.6 1.6 collective-permute-start.20
  226.2 4.0 %collective-permute-done.20 = f32[1,8,1536]{2,1,0:T(8,128)S(1)} collective-permute-done((f32[1,8,1536]{2,1,0:T(8,128)S(1)}, f32[1,8,1536]{2,1,0:T(8,128)S(1)}, u32[]{:S(2)}, u32[]{:S(2)}) %collective-permute-start.20) | collective-permute-done | bytes 49184 | tf_op jit(solution)/shard_map/ppermute | solution.py:75
  230.3 1.6 fusion.85
  (173 shorter events, 30.0 us)
Async XLA Ops:
  6.5 180.7 %copy-start = (bf16[280,1536]{1,0:T(8,128)(2,1)S(1)}, bf16[280,1536]{1,0:T(8,128)(2,1)}, u32[]{:S(2)}) copy-start(bf16[280,1536]{1,0:T(8,128)(2,1)} %param.18) | copy-start | bytes 2580484
  6.5 175.4 %all-gather.2.cloned.1.call-start = ((), (), s32[]{:S(2)}) async-start(), calls=%async_computation | async-start | bytes 4866048 | tf_op jit(solution)/shard_map/all_gather | solution.py:143
  7.4 8.2 %collective-permute-start = (bf16[8,1536]{1,0:T(8,128)(2,1)S(1)}, bf16[8,1536]{1,0:T(8,128)(2,1)S(1)}, u32[]{:S(2)}, u32[]{:S(2)}) collective-permute-start(bf16[8,1536]{1,0:T(8,128)(2,1)S(1)} %reshape.2067), channel_id=1, source_target_pairs={{0,32},{1,33},{2,34},{3,35},{4,36},{5,37},{6,38},{7,39},{8,40},{9,... | collective-permute-start | bytes 73736 | tf_op jit(solution)/shard_map/ppermute | solution.py:46
  12.7 22.6 %copy-start.8 = (s32[32]{0:T(128)S(1)}, s32[32]{0:T(128)}, u32[]{:S(2)}) copy-start(s32[32]{0:T(128)} %param.23) | copy-start | bytes 388
  15.6 29.1 %copy-start.7 = (s32[32,8]{0,1:T(8,128)S(1)}, s32[32,8]{0,1:T(8,128)}, u32[]{:S(2)}) copy-start(s32[32,8]{0,1:T(8,128)} %param.21) | copy-start | bytes 3076
  15.6 5.4 %collective-permute-start.1 = (bf16[2,8,1536]{2,1,0:T(8,128)(2,1)S(1)}, bf16[2,8,1536]{2,1,0:T(8,128)(2,1)S(1)}, u32[]{:S(2)}, u32[]{:S(2)}) collective-permute-start(bf16[2,8,1536]{2,1,0:T(8,128)(2,1)S(1)} %get-tuple-element.46), channel_id=1, source_target_pairs={{0,96},{1,97},{2,98},{3,99},{4,100},{5,101},{6,102},{7,103},{8,104... | collective-permute-start | bytes 147464 | tf_op jit(solution)/shard_map/ppermute | solution.py:46
  21.0 4.7 %collective-permute-start.2 = (bf16[2,2,8,1536]{3,2,1,0:T(8,128)(2,1)S(1)}, bf16[2,2,8,1536]{3,2,1,0:T(8,128)(2,1)S(1)}, u32[]{:S(2)}, u32[]{:S(2)}) collective-permute-start(bf16[2,2,8,1536]{3,2,1,0:T(8,128)(2,1)S(1)} %get-tuple-element.42), channel_id=1, source_target_pairs={{0,8},{1,9},{2,10},{3,11},{4,12},{5,13},{6,14},{7,15},{8,0},{9,1},... | collective-permute-start | bytes 294920 | tf_op jit(solution)/shard_map/ppermute | solution.py:46
  25.7 7.8 %collective-permute-start.3 = (bf16[2,2,2,8,1536]{4,3,2,1,0:T(8,128)(2,1)S(1)}, bf16[2,2,2,8,1536]{4,3,2,1,0:T(8,128)(2,1)S(1)}, u32[]{:S(2)}, u32[]{:S(2)}) collective-permute-start(bf16[2,2,2,8,1536]{4,3,2,1,0:T(8,128)(2,1)S(1)} %get-tuple-element.34), channel_id=1, source_target_pairs={{0,24},{1,25},{2,26},{3,27},{4,28},{5,29},{6,30},{7,31},{8,16},{9,... | collective-permute-start | bytes 589832 | tf_op jit(solution)/shard_map/ppermute | solution.py:46
  33.6 7.9 %collective-permute-start.4 = (bf16[2,2,2,2,8,1536]{5,4,3,2,1,0:T(8,128)(2,1)S(1)}, bf16[2,2,2,2,8,1536]{5,4,3,2,1,0:T(8,128)(2,1)S(1)}, u32[]{:S(2)}, u32[]{:S(2)}) collective-permute-start(bf16[2,2,2,2,8,1536]{5,4,3,2,1,0:T(8,128)(2,1)S(1)} %get-tuple-element.28), channel_id=1, source_target_pairs={{0,2},{1,3},{2,0},{3,1},{4,6},{5,7},{6,4},{7,5},{8,10},{9,11},{10,... | collective-permute-start | bytes 1179656 | tf_op jit(solution)/shard_map/ppermute | solution.py:46
  41.5 16.0 %collective-permute-start.5 = (bf16[2,2,2,2,2,8,1536]{6,5,4,3,2,1,0:T(8,128)(2,1)S(1)}, bf16[2,2,2,2,2,8,1536]{6,5,4,3,2,1,0:T(8,128)(2,1)S(1)}, u32[]{:S(2)}, u32[]{:S(2)}) collective-permute-start(bf16[2,2,2,2,2,8,1536]{6,5,4,3,2,1,0:T(8,128)(2,1)S(1)} %get-tuple-element.24), channel_id=1, source_target_pairs={{0,6},{1,7},{2,4},{3,5},{4,2},{5,3},{6,0},{7,1},{8,14},{9,15},{10,... | collective-permute-start | bytes 2359304 | tf_op jit(solution)/shard_map/ppermute | solution.py:46
  59.0 3.8 %collective-permute-start.6 = (bf16[2,2,2,2,2,2,8,1536]{7,6,5,4,3,2,1,0:T(8,128)(2,1)}, bf16[2,2,2,2,2,2,8,1536]{7,6,5,4,3,2,1,0:T(8,128)(2,1)}, u32[]{:S(2)}, u32[]{:S(2)}) collective-permute-start(bf16[2,2,2,2,2,2,8,1536]{7,6,5,4,3,2,1,0:T(8,128)(2,1)} %get-tuple-element.20), channel_id=1, source_target_pairs={{0,1},{1,0},{2,3},{3,2},{4,5},{5,4},{6,7},{7,6},{8,9},{9,8},{10,11... | collective-permute-start | bytes 4718600 | tf_op jit(solution)/shard_map/ppermute | solution.py:46
  66.1 8.9 %copy-start.6 = (f32[2048]{0:T(1024)S(1)}, f32[2048]{0:T(1024)}, u32[]{:S(2)}) copy-start(f32[2048]{0:T(1024)} %param.14) | copy-start | bytes 24580
  75.0 4.3 %copy-start.2 = (bf16[2,4096,256]{2,1,0:T(8,128)(2,1)S(1)}, bf16[2,4096,256]{2,1,0:T(8,128)(2,1)}, u32[]{:S(2)}) copy-start(bf16[2,4096,256]{2,1,0:T(8,128)(2,1)} %param.19) | copy-start | bytes 12582916
  89.3 3.8 %copy-start.5 = (bf16[48,1536]{1,0:T(8,128)(2,1)S(1)}, bf16[48,1536]{1,0:T(8,128)(2,1)}, u32[]{:S(2)}) copy-start(bf16[48,1536]{1,0:T(8,128)(2,1)} %param.15) | copy-start | bytes 442372
  93.8 3.7 %copy-start.3 = (bf16[2,8,4,6,4096]{4,1,0,3,2:T(8,128)(2,1)S(1)}, bf16[2,8,4,6,4096]{4,1,0,3,2:T(8,128)(2,1)}, u32[]{:S(2)}) copy-start(bf16[2,8,4,6,4096]{4,1,0,3,2:T(8,128)(2,1)} %get-tuple-element.16) | copy-start | bytes 9437188
  101.9 1.6 collective-permute-start.7
  103.6 6.5 %collective-permute-start.8 = (f32[1,2,4,2,6,130]{5,4,3,2,1,0:T(8,128)S(1)}, f32[1,2,4,2,6,130]{5,4,3,2,1,0:T(8,128)S(1)}, u32[]{:S(2)}, u32[]{:S(2)}) collective-permute-start(f32[1,2,4,2,6,130]{5,4,3,2,1,0:T(8,128)S(1)} %select_bitcast_fusion.4), channel_id=1, source_target_pairs={{0,2},{1,3},{2,0},{3,1},{4,6},{5,7},{6,4},{7,5},{8,10},{9,11},{10,... | collective-permute-start | bytes 149768 | tf_op jit(solution)/shard_map/ppermute | solution.py:75
  111.1 3.9 %collective-permute-start.9 = (bf16[2,4,1536]{2,1,0:T(4,128)(2,1)S(1)}, bf16[2,4,1536]{2,1,0:T(4,128)(2,1)S(1)}, u32[]{:S(2)}, u32[]{:S(2)}) collective-permute-start(bf16[2,4,1536]{2,1,0:T(4,128)(2,1)S(1)} %convert_element_type.91), channel_id=1, source_target_pairs={{0,32},{1,33},{2,34},{3,35},{4,36},{5,37},{6,38},{7,39},{8,40},{9,... | collective-permute-start | bytes 73736 | tf_op jit(solution)/shard_map/ppermute | solution.py:46
  115.1 5.4 %collective-permute-start.10 = (bf16[2,2,4,1536]{3,2,1,0:T(4,128)(2,1)S(1)}, bf16[2,2,4,1536]{3,2,1,0:T(4,128)(2,1)S(1)}, u32[]{:S(2)}, u32[]{:S(2)}) collective-permute-start(bf16[2,2,4,1536]{3,2,1,0:T(4,128)(2,1)S(1)} %get-tuple-element.44), channel_id=1, source_target_pairs={{0,96},{1,97},{2,98},{3,99},{4,100},{5,101},{6,102},{7,103},{8,104... | collective-permute-start | bytes 147464 | tf_op jit(solution)/shard_map/ppermute | solution.py:46
  120.5 4.9 %collective-permute-start.11 = (bf16[2,2,2,4,1536]{4,3,2,1,0:T(4,128)(2,1)S(1)}, bf16[2,2,2,4,1536]{4,3,2,1,0:T(4,128)(2,1)S(1)}, u32[]{:S(2)}, u32[]{:S(2)}) collective-permute-start(bf16[2,2,2,4,1536]{4,3,2,1,0:T(4,128)(2,1)S(1)} %get-tuple-element.38), channel_id=1, source_target_pairs={{0,8},{1,9},{2,10},{3,11},{4,12},{5,13},{6,14},{7,15},{8,0},{9,1},... | collective-permute-start | bytes 294920 | tf_op jit(solution)/shard_map/ppermute | solution.py:46
  125.6 11.1 %collective-permute-start.12 = (bf16[2,2,2,2,4,1536]{5,4,3,2,1,0:T(4,128)(2,1)S(1)}, bf16[2,2,2,2,4,1536]{5,4,3,2,1,0:T(4,128)(2,1)S(1)}, u32[]{:S(2)}, u32[]{:S(2)}) collective-permute-start(bf16[2,2,2,2,4,1536]{5,4,3,2,1,0:T(4,128)(2,1)S(1)} %get-tuple-element.32), channel_id=1, source_target_pairs={{0,24},{1,25},{2,26},{3,27},{4,28},{5,29},{6,30},{7,31},{8,16},{9,... | collective-permute-start | bytes 589832 | tf_op jit(solution)/shard_map/ppermute | solution.py:46
  137.1 9.1 %collective-permute-start.13 = (bf16[2,2,2,2,2,4,1536]{6,5,4,3,2,1,0:T(4,128)(2,1)S(1)}, bf16[2,2,2,2,2,4,1536]{6,5,4,3,2,1,0:T(4,128)(2,1)S(1)}, u32[]{:S(2)}, u32[]{:S(2)}) collective-permute-start(bf16[2,2,2,2,2,4,1536]{6,5,4,3,2,1,0:T(4,128)(2,1)S(1)} %get-tuple-element.26), channel_id=1, source_target_pairs={{0,2},{1,3},{2,0},{3,1},{4,6},{5,7},{6,4},{7,5},{8,10},{9,11},{10,... | collective-permute-start | bytes 1179656 | tf_op jit(solution)/shard_map/ppermute | solution.py:46
  146.9 17.8 %collective-permute-start.14 = (bf16[2,2,2,2,2,2,4,1536]{7,6,5,4,3,2,1,0:T(4,128)(2,1)S(1)}, bf16[2,2,2,2,2,2,4,1536]{7,6,5,4,3,2,1,0:T(4,128)(2,1)S(1)}, u32[]{:S(2)}, u32[]{:S(2)}) collective-permute-start(bf16[2,2,2,2,2,2,4,1536]{7,6,5,4,3,2,1,0:T(4,128)(2,1)S(1)} %get-tuple-element.22), channel_id=1, source_target_pairs={{0,6},{1,7},{2,4},{3,5},{4,2},{5,3},{6,0},{7,1},{8,14},{9,15},{10,... | collective-permute-start | bytes 2359304 | tf_op jit(solution)/shard_map/ppermute | solution.py:46
  167.4 6.0 %collective-permute-start.15 = (bf16[2,2,2,2,2,2,2,4,1536]{8,7,6,5,4,3,2,1,0:T(4,128)(2,1)}, bf16[2,2,2,2,2,2,2,4,1536]{8,7,6,5,4,3,2,1,0:T(4,128)(2,1)}, u32[]{:S(2)}, u32[]{:S(2)}) collective-permute-start(bf16[2,2,2,2,2,2,2,4,1536]{8,7,6,5,4,3,2,1,0:T(4,128)(2,1)} %get-tuple-element.18), channel_id=1, source_target_pairs={{0,1},{1,0},{2,3},{3,2},{4,5},{5,4},{6,7},{7,6},{8,9},{9,8},{10,11... | collective-permute-start | bytes 4718600 | tf_op jit(solution)/shard_map/ppermute | solution.py:46
  182.0 4.7 %copy-start.4 = (bf16[1536,280]{0,1:T(8,128)(2,1)S(1)}, bf16[1536,280]{0,1:T(8,128)(2,1)}, u32[]{:S(2)}) copy-start(bf16[1536,280]{0,1:T(8,128)(2,1)} %param.16) | copy-start | bytes 2580484
  186.6 4.1 %copy-start.1 = (f32[64,4,1536]{2,0,1:T(8,128)}, f32[64,4,1536]{2,0,1:T(8,128)S(1)}, u32[]{:S(2)}) copy-start(f32[64,4,1536]{2,0,1:T(8,128)S(1)} %get-tuple-element.56) | copy-start | bytes 4718596
  196.3 2.6 %collective-permute-start.16 = (f32[16,8,1536]{2,1,0:T(8,128)S(1)}, f32[16,8,1536]{2,1,0:T(8,128)}, u32[]{:S(2)}, u32[]{:S(2)}) collective-permute-start(f32[16,8,1536]{2,1,0:T(8,128)S(1)} %select_bitcast_fusion), channel_id=1, source_target_pairs={{0,1},{1,0},{2,3},{3,2},{4,5},{5,4},{6,7},{7,6},{8,9},{9,8},{10,11... | collective-permute-start | bytes 2359304 | tf_op jit(solution)/shard_map/ppermute | solution.py:75
  200.3 11.5 %collective-permute-start.17 = (f32[8,8,1536]{2,1,0:T(8,128)S(1)}, f32[8,8,1536]{2,1,0:T(8,128)S(1)}, u32[]{:S(2)}, u32[]{:S(2)}) collective-permute-start(f32[8,8,1536]{2,1,0:T(8,128)S(1)} %select_bitcast_fusion.1), channel_id=1, source_target_pairs={{0,2},{1,3},{2,0},{3,1},{4,6},{5,7},{6,4},{7,5},{8,10},{9,11},{10,... | collective-permute-start | bytes 1179656 | tf_op jit(solution)/shard_map/ppermute | solution.py:75
  211.9 7.9 %collective-permute-start.18 = (f32[4,8,1536]{2,1,0:T(8,128)S(1)}, f32[4,8,1536]{2,1,0:T(8,128)S(1)}, u32[]{:S(2)}, u32[]{:S(2)}) collective-permute-start(f32[4,8,1536]{2,1,0:T(8,128)S(1)} %select_bitcast_fusion.3), channel_id=1, source_target_pairs={{0,4},{1,5},{2,6},{3,7},{4,0},{5,1},{6,2},{7,3},{8,12},{9,13},{10,... | collective-permute-start | bytes 589832 | tf_op jit(solution)/shard_map/ppermute | solution.py:75
  219.8 4.7 %collective-permute-start.19 = (f32[2,8,1536]{2,1,0:T(8,128)S(1)}, f32[2,8,1536]{2,1,0:T(8,128)S(1)}, u32[]{:S(2)}, u32[]{:S(2)}) collective-permute-start(f32[2,8,1536]{2,1,0:T(8,128)S(1)} %select_bitcast_fusion.5), channel_id=1, source_target_pairs={{0,8},{1,9},{2,10},{3,11},{4,12},{5,13},{6,14},{7,15},{8,0},{9,1},... | collective-permute-start | bytes 294920 | tf_op jit(solution)/shard_map/ppermute | solution.py:75
  224.6 5.7 %collective-permute-start.20 = (f32[1,8,1536]{2,1,0:T(8,128)S(1)}, f32[1,8,1536]{2,1,0:T(8,128)S(1)}, u32[]{:S(2)}, u32[]{:S(2)}) collective-permute-start(f32[1,8,1536]{2,1,0:T(8,128)S(1)} %select_bitcast_fusion.6), channel_id=1, source_target_pairs={{0,16},{1,17},{2,18},{3,19},{4,20},{5,21},{6,22},{7,23},{8,24},{9,... | collective-permute-start | bytes 147464 | tf_op jit(solution)/shard_map/ppermute | solution.py:75
Sparse Core Ops, SparseCore 0:
  94.0 49.0 all-gather.1

commit v13 on v8

--- a/solution.py
+++ b/solution.py
@@ -53,7 +53,7 @@
     return buf.reshape((count,) + x.shape)
 
 
-def scatter_rounds(x, axes, index):
+def scatter_rounds(x, axes, index, wire=jnp.float32):
     count = x.shape[0]
     buf = x
     bit = 1
@@ -63,7 +63,8 @@
         keep = jnp.where(mine == 0, pairs[:, 0], pairs[:, 1])
         send = jnp.where(mine == 0, pairs[:, 1], pairs[:, 0])
         perm = [(i, i ^ bit) for i in range(count)]
-        buf = keep + lax.ppermute(send, axes, perm)
+        recv = lax.ppermute(send.astype(wire), axes, perm)
+        buf = keep + recv.astype(keep.dtype)
         bit *= 2
     return buf[0]
 
@@ -247,7 +248,9 @@
     upward = jnp.dot(mixed_in, up_weight, preferred_element_type=jnp.float32)
     hidden = (jax.nn.silu(gate) * upward).astype(jnp.bfloat16)
     partial = jnp.dot(hidden, down_weight, preferred_element_type=jnp.float32)
-    partial = scatter_rounds(partial.reshape(tp_count, rows_dev * steps, width), TP, tp_index)
+    partial = scatter_rounds(
+        partial.reshape(tp_count, rows_dev * steps, width), TP, tp_index, wire=jnp.bfloat16
+    )
     lowered = partial.reshape(rows_dev, steps, width)
     middle_mine = lax.dynamic_slice_in_dim(middle, tp_index * rows_dev, rows_dev, 0)
     result = (middle_mine + lowered).astype(jnp.bfloat16)

time: 236 us -> 229 us (0.970)
  waiting for transfers between devices: 103 us -> 95.9 us
    ppermute x7, waiting for transfers between devices: 32.1 us -> 25.1 us  [scatter_rounds(): recv = lax.ppermute(send.astype(wire), axes, perm)]
  transfers between devices with their start and end apart: 22 -> 22, of which waited for: 20 -> 20; matrix products, arithmetic and copies ran while one was open for 29% -> 30% of each run, Pallas kernels for 0% -> 0%
where the time goes in v13:
time: 229 us; the launch traced here: 228 us
  waiting for transfers between devices  95.9 us (42%)
  local copies, waits for them, and re-layouts  40 us (17%)
  other arithmetic  30.4 us (13%)
  starting transfers between devices  29.8 us (13%)
  matrix products  16.8 us (7%)
  between operations  15 us (7%)
    ppermute x14, waiting for transfers between devices, gather_rounds(): recv = lax.ppermute(buf, axes, perm)  70.8 us
    ppermute x7, waiting for transfers between devices, scatter_rounds(): recv = lax.ppermute(send.astype(wire), axes, perm)  25.1 us
    ppermute x14, starting transfers between devices, gather_rounds(): recv = lax.ppermute(buf, axes, perm)  25 us
    select_n x24, other arithmetic, gather_rounds(): buf = jnp.where(mine == 0, jnp.stack([buf, recv]), jnp.stack([recv, buf]))  7.63 us
    transpose x2, other arithmetic, gather_rounds(): buf = jnp.transpose(buf, tuple(order) + tuple(range(depth, buf.ndim)))  6.99 us
    another operation x1, local copies, waits for them, and re-layouts, per_device(): x_all = gather_rounds(jnp.swapaxes(step_inputs, 0, 1).reshape(rows_dev *...  6.14 us
    ppermute x7, starting transfers between devices, scatter_rounds(): recv = lax.ppermute(send.astype(wire), axes, perm)  4.82 us
    convert_element_type x1, other arithmetic, per_device(): weights = weights.astype(jnp.bfloat16)  4.63 us
  transfers between devices with their start and end apart: 22, of which 20 were waited for; matrix products, arithmetic and copies ran while one was open for 30% of the time, Pallas kernels for 0%

profile of v13, /device:TPU:0, one launch (start us, length us, event | category | flops | bytes accessed | tf_op | source)
XLA Modules:
  0.0 227.9 jit_solution(16904645754737674665)
XLA Ops:
  7.4 1.7 collective-permute-start
  19.1 2.2 collective-permute-start.1
  21.4 3.2 %collective-permute-done.1 = bf16[2,8,1536]{2,1,0:T(8,128)(2,1)S(1)} collective-permute-done((bf16[2,8,1536]{2,1,0:T(8,128)(2,1)S(1)}, bf16[2,8,1536]{2,1,0:T(8,128)(2,1)S(1)}, u32[]{:S(2)}, u32[]{:S(2)}) %collective-permute-start.1) | collective-permute-done | bytes 49184 | tf_op jit(solution)/shard_map/ppermute | solution.py:46
  24.5 2.0 collective-permute-start.2
  26.6 3.1 %collective-permute-done.2 = bf16[2,2,8,1536]{3,2,1,0:T(8,128)(2,1)S(1)} collective-permute-done((bf16[2,2,8,1536]{3,2,1,0:T(8,128)(2,1)S(1)}, bf16[2,2,8,1536]{3,2,1,0:T(8,128)(2,1)S(1)}, u32[]{:S(2)}, u32[]{:S(2)}) %collective-permute-start.2) | collective-permute-done | bytes 98336 | tf_op jit(solution)/shard_map/ppermute | solution.py:46
  29.7 4.1 %collective-permute-start.3 = (bf16[2,2,2,8,1536]{4,3,2,1,0:T(8,128)(2,1)S(1)}, bf16[2,2,2,8,1536]{4,3,2,1,0:T(8,128)(2,1)S(1)}, u32[]{:S(2)}, u32[]{:S(2)}) collective-permute-start(bf16[2,2,2,8,1536]{4,3,2,1,0:T(8,128)(2,1)S(1)} %maximum_select_fusion.16), channel_id=1, source_target_pairs={{0,24},{1,25},{2,26},{3,27},{4,28},{5,29},{6,30},{7,31},{8,16},{9,... | collective-permute-start | bytes 589832 | tf_op jit(solution)/shard_map/ppermute | solution.py:46
  33.8 3.6 %collective-permute-done.3 = bf16[2,2,2,8,1536]{4,3,2,1,0:T(8,128)(2,1)S(1)} collective-permute-done((bf16[2,2,2,8,1536]{4,3,2,1,0:T(8,128)(2,1)S(1)}, bf16[2,2,2,8,1536]{4,3,2,1,0:T(8,128)(2,1)S(1)}, u32[]{:S(2)}, u32[]{:S(2)}) %collective-permute-start.3) | collective-permute-done | bytes 196640 | tf_op jit(solution)/shard_map/ppermute | solution.py:46
  37.5 1.6 collective-permute-start.4
  39.2 11.9 %collective-permute-done.4 = bf16[2,2,2,2,8,1536]{5,4,3,2,1,0:T(8,128)(2,1)S(1)} collective-permute-done((bf16[2,2,2,2,8,1536]{5,4,3,2,1,0:T(8,128)(2,1)S(1)}, bf16[2,2,2,2,8,1536]{5,4,3,2,1,0:T(8,128)(2,1)S(1)}, u32[]{:S(2)}, u32[]{:S(2)}) %collective-permute-start.4) | collective-permute-done | bytes 393248 | tf_op jit(solution)/shard_map/ppermute | solution.py:46
  51.2 3.3 %collective-permute-start.5 = (bf16[2,2,2,2,2,8,1536]{6,5,4,3,2,1,0:T(8,128)(2,1)S(1)}, bf16[2,2,2,2,2,8,1536]{6,5,4,3,2,1,0:T(8,128)(2,1)S(1)}, u32[]{:S(2)}, u32[]{:S(2)}) collective-permute-start(bf16[2,2,2,2,2,8,1536]{6,5,4,3,2,1,0:T(8,128)(2,1)S(1)} %maximum_select_fusion.7), channel_id=1, source_target_pairs={{0,6},{1,7},{2,4},{3,5},{4,2},{5,3},{6,0},{7,1},{8,14},{9,15},{10,... | collective-permute-start | bytes 2359304 | tf_op jit(solution)/shard_map/ppermute | solution.py:46
  55.0 16.7 %collective-permute-done.5 = bf16[2,2,2,2,2,8,1536]{6,5,4,3,2,1,0:T(8,128)(2,1)S(1)} collective-permute-done((bf16[2,2,2,2,2,8,1536]{6,5,4,3,2,1,0:T(8,128)(2,1)S(1)}, bf16[2,2,2,2,2,8,1536]{6,5,4,3,2,1,0:T(8,128)(2,1)S(1)}, u32[]{:S(2)}, u32[]{:S(2)}) %collective-permute-start.5) | collective-permute-done | bytes 786464 | tf_op jit(solution)/shard_map/ppermute | solution.py:46
  71.6 1.4 maximum_select_fusion.3
  76.8 2.3 %fusion.8 = bf16[2,2,2,2,2,2,2,8,1536]{8,7,1,0,3,2,5,4,6:T(8,128)(2,1)S(1)} fusion(bf16[1,2,2,2,2,2,2,8,1536]{8,7,6,5,4,3,2,1,0:T(8,128)(2,1)} %bitcast.18, bf16[1,2,2,2,2,2,2,8,1536]{8,7,6,5,4,3,2,1,0:T(8,128)(2,1)S(1)} %maximum_select_fusion.2, pred[]{:T(512)S(6)} %eq.99), kind=kLoop, calls=%fused_computation.31 | loop fusion | flops 4718592 | bytes 6291457 | tf_op jit(solution)/shard_map/transpose | solution.py:52
  79.1 2.2 copy.131
  81.4 6.1 %reshape_reshape.7 = bf16[256,4,1536]{2,1,0:T(4,128)(2,1)} reshape(bf16[2,2,2,2,2,2,2,8,1536]{8,7,6,5,4,3,2,1,0:T(8,128)(2,1)} %copy.131) | data formatting | bytes 6291456 | tf_op jit(solution)/shard_map/reshape;reshape | solution.py:128
  89.6 4.1 %fusion.20 = bf16[8,4,2048]{2,0,1:T(8,128)(2,1)S(1)} fusion(bf16[1536,2048]{1,0:T(8,128)(2,1)} %param.13, f32[2048]{0:T(1024)S(1)} %copy-done.4, bf16[8,4,1536]{2,1,0:T(4,128)(2,1)S(1)} %fusion.64), kind=kOutput, calls=%fused_computation.40 | convolution fusion | flops 201457664 | bytes 6529024 | tf_op jit(solution)/shard_map/dot_general | solution.py:135
  95.9 2.1 fusion.5
  98.0 4.6 %fusion.2 = (bf16[2,8,4,2,6,4096]{5,1,0,4,2,3:T(8,128)(2,1)S(1)}, f32[2,8,4,2,6]{1,0,4,2,3:T(2,128)S(1)}) fusion(f32[2,8,4,2,6]{1,0,4,2,3:T(2,128)S(1)} %fusion.5, pred[2,4096]{1,0:T(4,128)(4,1)S(1)} %iota_compare_fusion, f32[2,8,4,1,6,4096]{5,1,0,4,2,3:T(8,128)S(1)} %convolution_bitcast_fusion, f32[2,8,4,1,6,4096]{5,1,0,4,2,3:T(8,128)S(1)} %convolution_bitcast_fusion.1), kind=kLoop, calls=%fused_computation.20 | loop fusion | flops 22019328 | bytes 18888704 | tf_op jit(solution)/shard_map/convert_element_type | solution.py:172
  103.4 1.4 copy-done.6
  111.6 4.3 %collective-permute-done.8 = f32[1,2,4,2,6,130]{5,4,3,2,1,0:T(8,128)S(1)} collective-permute-done((f32[1,2,4,2,6,130]{5,4,3,2,1,0:T(8,128)S(1)}, f32[1,2,4,2,6,130]{5,4,3,2,1,0:T(8,128)S(1)}, u32[]{:S(2)}, u32[]{:S(2)}) %collective-permute-start.8) | collective-permute-done | bytes 49952 | tf_op jit(solution)/shard_map/ppermute | solution.py:66
  118.1 2.9 %collective-permute-done.9 = bf16[2,4,1536]{2,1,0:T(4,128)(2,1)S(1)} collective-permute-done((bf16[2,4,1536]{2,1,0:T(4,128)(2,1)S(1)}, bf16[2,4,1536]{2,1,0:T(4,128)(2,1)S(1)}, u32[]{:S(2)}, u32[]{:S(2)}) %collective-permute-start.9) | collective-permute-done | bytes 24608 | tf_op jit(solution)/shard_map/ppermute | solution.py:46
  121.1 2.8 %collective-permute-start.10 = (bf16[2,2,4,1536]{3,2,1,0:T(4,128)(2,1)S(1)}, bf16[2,2,4,1536]{3,2,1,0:T(4,128)(2,1)S(1)}, u32[]{:S(2)}, u32[]{:S(2)}) collective-permute-start(bf16[2,2,4,1536]{3,2,1,0:T(4,128)(2,1)S(1)} %maximum_select_fusion.26), channel_id=1, source_target_pairs={{0,96},{1,97},{2,98},{3,99},{4,100},{5,101},{6,102},{7,103},{8,104... | collective-permute-start | bytes 147464 | tf_op jit(solution)/shard_map/ppermute | solution.py:46
  123.9 2.5 %collective-permute-done.10 = bf16[2,2,4,1536]{3,2,1,0:T(4,128)(2,1)S(1)} collective-permute-done((bf16[2,2,4,1536]{3,2,1,0:T(4,128)(2,1)S(1)}, bf16[2,2,4,1536]{3,2,1,0:T(4,128)(2,1)S(1)}, u32[]{:S(2)}, u32[]{:S(2)}) %collective-permute-start.10) | collective-permute-done | bytes 49184 | tf_op jit(solution)/shard_map/ppermute | solution.py:46
  127.8 3.4 %collective-permute-done.11 = bf16[2,2,2,4,1536]{4,3,2,1,0:T(4,128)(2,1)S(1)} collective-permute-done((bf16[2,2,2,4,1536]{4,3,2,1,0:T(4,128)(2,1)S(1)}, bf16[2,2,2,4,1536]{4,3,2,1,0:T(4,128)(2,1)S(1)}, u32[]{:S(2)}, u32[]{:S(2)}) %collective-permute-start.11) | collective-permute-done | bytes 98336 | tf_op jit(solution)/shard_map/ppermute | solution.py:46
  131.4 3.0 %collective-permute-start.12 = (bf16[2,2,2,2,4,1536]{5,4,3,2,1,0:T(4,128)(2,1)S(1)}, bf16[2,2,2,2,4,1536]{5,4,3,2,1,0:T(4,128)(2,1)S(1)}, u32[]{:S(2)}, u32[]{:S(2)}) collective-permute-start(bf16[2,2,2,2,4,1536]{5,4,3,2,1,0:T(4,128)(2,1)S(1)} %maximum_select_fusion.18), channel_id=1, source_target_pairs={{0,24},{1,25},{2,26},{3,27},{4,28},{5,29},{6,30},{7,31},{8,16},{9,... | collective-permute-start | bytes 589832 | tf_op jit(solution)/shard_map/ppermute | solution.py:46
  134.5 3.8 %collective-permute-done.12 = bf16[2,2,2,2,4,1536]{5,4,3,2,1,0:T(4,128)(2,1)S(1)} collective-permute-done((bf16[2,2,2,2,4,1536]{5,4,3,2,1,0:T(4,128)(2,1)S(1)}, bf16[2,2,2,2,4,1536]{5,4,3,2,1,0:T(4,128)(2,1)S(1)}, u32[]{:S(2)}, u32[]{:S(2)}) %collective-permute-start.12) | collective-permute-done | bytes 196640 | tf_op jit(solution)/shard_map/ppermute | solution.py:46
  139.4 7.0 %collective-permute-done.13 = bf16[2,2,2,2,2,4,1536]{6,5,4,3,2,1,0:T(4,128)(2,1)S(1)} collective-permute-done((bf16[2,2,2,2,2,4,1536]{6,5,4,3,2,1,0:T(4,128)(2,1)S(1)}, bf16[2,2,2,2,2,4,1536]{6,5,4,3,2,1,0:T(4,128)(2,1)S(1)}, u32[]{:S(2)}, u32[]{:S(2)}) %collective-permute-start.13) | collective-permute-done | bytes 393248 | tf_op jit(solution)/shard_map/ppermute | solution.py:46
  147.1 1.6 collective-permute-start.14
  149.5 11.9 %collective-permute-done.14 = bf16[2,2,2,2,2,2,4,1536]{7,6,5,4,3,2,1,0:T(4,128)(2,1)S(1)} collective-permute-done((bf16[2,2,2,2,2,2,4,1536]{7,6,5,4,3,2,1,0:T(4,128)(2,1)S(1)}, bf16[2,2,2,2,2,2,4,1536]{7,6,5,4,3,2,1,0:T(4,128)(2,1)S(1)}, u32[]{:S(2)}, u32[]{:S(2)}) %collective-permute-start.14) | collective-permute-done | bytes 786464 | tf_op jit(solution)/shard_map/ppermute | solution.py:46
  161.3 2.1 maximum_select_fusion.5
  163.5 1.4 constant_dynamic-slice_fusion
  165.5 1.2 maximum_select_fusion.4
  167.2 4.7 %fusion.9 = bf16[2,2,2,2,2,2,2,2,4,1536]{9,8,7,1,0,3,2,5,4,6:T(4,128)(2,1)S(1)} fusion(bf16[1,2,2,2,2,2,2,2,4,1536]{9,8,7,6,5,4,3,2,1,0:T(4,128)(2,1)} %bitcast.111, bf16[1,2,2,2,2,2,2,2,4,1536]{9,8,7,6,5,4,3,2,1,0:T(4,128)(2,1)S(1)} %maximum_select_fusion.4, pred[]{:T(512)S(6)} %eq.99), kind=kLoop, calls=%fused_computation.33 | loop fusion | flops 4718592 | bytes 6291457 | tf_op jit(solution)/shard_map/transpose | solution.py:52
  171.9 1.8 copy.159
  173.7 2.5 %copy.160 = bf16[32,8,4,1536]{3,1,2,0:T(8,128)(2,1)} copy(bf16[32,8,4,1536]{3,2,1,0:T(4,128)(2,1)S(1)} %bitcast.338) | data formatting | bytes 6291456 | tf_op jit(solution)/shard_map/reshape;reshape;reshape | solution.py:239
  176.2 3.4 %gather_fusion.14 = bf16[8,8,4,1536]{3,1,2,0:T(8,128)(2,1)} fusion(bf16[32,8,4,1536]{3,1,2,0:T(8,128)(2,1)} %copy.160, s32[1024]{0:T(1024)S(1)} %pad_clamp_fusion), kind=kCustom, calls=%fused_computation.14 | custom fusion | bytes 1572896 | tf_op jit(solution)/shard_map/gather | solution.py:239
  179.6 4.1 %multiply_reduce_fusion = (f32[64,4]{0,1:T(4,128)S(1)}, f32[64,4,1536]{2,0,1:T(8,128)S(1)}) fusion(bf16[1536,1536]{1,0:T(8,128)(2,1)} %all-gather.2.cloned.1.call-done, bf16[8,8,4,1536]{3,1,2,0:T(8,128)(2,1)} %gather_fusion.14, bf16[64,4,1536]{2,1,0:T(4,128)(2,1)S(1)} %constant_dynamic-slice_fusion), kind=kOutput, calls=%fused_computation.54 | convolution fusion | flops 1209532160 | bytes 7865344 | tf_op jit(solution)/shard_map/dot_general | solution.py:243
  184.4 3.5 %fusion.42 = f32[64,4,1536]{2,0,1:T(8,128)} fusion(bf16[280,1536]{1,0:T(8,128)(2,1)S(1)} %copy-done, bf16[1536,280]{0,1:T(8,128)(2,1)} %param.17, f32[64,4,280]{2,0,1:T(8,128)S(1)} %fusion.47, f32[64,4,1536]{2,0,1:T(8,128)S(1)} %get-tuple-element.32, f32[64,4]{0,1:T(4,128)S(1)} %add_rsqrt_fusion.1), kind=kOutput, calls=%fused_computation.59 | convolution fusion | flops 441618432 | bytes 5153792 | tf_op jit(solution)/shard_map/dot_general | solution.py:250
  187.9 3.6 %copy.162 = f32[64,4,1536]{2,1,0:T(4,128)} copy(f32[64,4,1536]{2,0,1:T(8,128)} %fusion.42) | data formatting | bytes 3145728 | tf_op jit(solution)/shard_map/dot_general | solution.py:250
  191.4 1.8 reshape_reshape.8
  193.6 1.7 collective-permute-done.16
  196.6 6.9 %collective-permute-done.17 = bf16[8,8,1536]{2,1,0:T(8,128)(2,1)S(1)} collective-permute-done((bf16[8,8,1536]{2,1,0:T(8,128)(2,1)S(1)}, bf16[8,8,1536]{2,1,0:T(8,128)(2,1)S(1)}, u32[]{:S(2)}, u32[]{:S(2)}) %collective-permute-start.17) | collective-permute-done | bytes 196640 | tf_op jit(solution)/shard_map/ppermute | solution.py:66
  203.6 1.3 collective-permute-start.18
  204.9 4.9 %collective-permute-done.18 = bf16[4,8,1536]{2,1,0:T(8,128)(2,1)S(1)} collective-permute-done((bf16[4,8,1536]{2,1,0:T(8,128)(2,1)S(1)}, bf16[4,8,1536]{2,1,0:T(8,128)(2,1)S(1)}, u32[]{:S(2)}, u32[]{:S(2)}) %collective-permute-start.18) | collective-permute-done | bytes 98336 | tf_op jit(solution)/shard_map/ppermute | solution.py:66
  210.1 3.9 %collective-permute-done.19 = bf16[2,8,1536]{2,1,0:T(8,128)(2,1)S(1)} collective-permute-done((bf16[2,8,1536]{2,1,0:T(8,128)(2,1)S(1)}, bf16[2,8,1536]{2,1,0:T(8,128)(2,1)S(1)}, u32[]{:S(2)}, u32[]{:S(2)}) %collective-permute-start.19) | collective-permute-done | bytes 49184 | tf_op jit(solution)/shard_map/ppermute | solution.py:66
  214.1 2.5 %collective-permute-start.20 = (bf16[1,8,1536]{2,1,0:T(8,128)(2,1)S(1)}, bf16[1,8,1536]{2,1,0:T(8,128)(2,1)S(1)}, u32[]{:S(2)}, u32[]{:S(2)}) collective-permute-start(bf16[1,8,1536]{2,1,0:T(8,128)(2,1)S(1)} %fusion.91), channel_id=1, source_target_pairs={{0,16},{1,17},{2,18},{3,19},{4,20},{5,21},{6,22},{7,23},{8,24},{9,... | collective-permute-start | bytes 73736 | tf_op jit(solution)/shard_map/ppermute | solution.py:66
  216.6 2.9 %collective-permute-done.20 = bf16[1,8,1536]{2,1,0:T(8,128)(2,1)S(1)} collective-permute-done((bf16[1,8,1536]{2,1,0:T(8,128)(2,1)S(1)}, bf16[1,8,1536]{2,1,0:T(8,128)(2,1)S(1)}, u32[]{:S(2)}, u32[]{:S(2)}) %collective-permute-start.20) | collective-permute-done | bytes 24608 | tf_op jit(solution)/shard_map/ppermute | solution.py:66
  219.5 1.6 fusion.93
  (179 shorter events, 36.2 us)
Async XLA Ops:
  6.5 177.9 %copy-start = (bf16[280,1536]{1,0:T(8,128)(2,1)S(1)}, bf16[280,1536]{1,0:T(8,128)(2,1)}, u32[]{:S(2)}) copy-start(bf16[280,1536]{1,0:T(8,128)(2,1)} %param.18) | copy-start | bytes 2580484
  6.5 9.1 %copy-start.5 = (s32[32,8]{0,1:T(8,128)S(1)}, s32[32,8]{0,1:T(8,128)}, u32[]{:S(2)}) copy-start(s32[32,8]{0,1:T(8,128)} %param.21) | copy-start | bytes 3076
  6.5 173.1 %all-gather.2.cloned.1.call-start = ((), (), s32[]{:S(2)}) async-start(), calls=%async_computation | async-start | bytes 4866048 | tf_op jit(solution)/shard_map/all_gather | solution.py:129
  7.4 11.7 %collective-permute-start = (bf16[8,1536]{1,0:T(8,128)(2,1)S(1)}, bf16[8,1536]{1,0:T(8,128)(2,1)S(1)}, u32[]{:S(2)}, u32[]{:S(2)}) collective-permute-start(bf16[8,1536]{1,0:T(8,128)(2,1)S(1)} %reshape.1869), channel_id=1, source_target_pairs={{0,32},{1,33},{2,34},{3,35},{4,36},{5,37},{6,38},{7,39},{8,40},{9,... | collective-permute-start | bytes 73736 | tf_op jit(solution)/shard_map/ppermute | solution.py:46
  19.1 5.4 %collective-permute-start.1 = (bf16[2,8,1536]{2,1,0:T(8,128)(2,1)S(1)}, bf16[2,8,1536]{2,1,0:T(8,128)(2,1)S(1)}, u32[]{:S(2)}, u32[]{:S(2)}) collective-permute-start(bf16[2,8,1536]{2,1,0:T(8,128)(2,1)S(1)} %maximum_select_fusion.24), channel_id=1, source_target_pairs={{0,96},{1,97},{2,98},{3,99},{4,100},{5,101},{6,102},{7,103},{8,104... | collective-permute-start | bytes 147464 | tf_op jit(solution)/shard_map/ppermute | solution.py:46
  24.5 5.1 %collective-permute-start.2 = (bf16[2,2,8,1536]{3,2,1,0:T(8,128)(2,1)S(1)}, bf16[2,2,8,1536]{3,2,1,0:T(8,128)(2,1)S(1)}, u32[]{:S(2)}, u32[]{:S(2)}) collective-permute-start(bf16[2,2,8,1536]{3,2,1,0:T(8,128)(2,1)S(1)} %maximum_select_fusion.20), channel_id=1, source_target_pairs={{0,8},{1,9},{2,10},{3,11},{4,12},{5,13},{6,14},{7,15},{8,0},{9,1},... | collective-permute-start | bytes 294920 | tf_op jit(solution)/shard_map/ppermute | solution.py:46
  29.7 7.8 %collective-permute-start.3 = (bf16[2,2,2,8,1536]{4,3,2,1,0:T(8,128)(2,1)S(1)}, bf16[2,2,2,8,1536]{4,3,2,1,0:T(8,128)(2,1)S(1)}, u32[]{:S(2)}, u32[]{:S(2)}) collective-permute-start(bf16[2,2,2,8,1536]{4,3,2,1,0:T(8,128)(2,1)S(1)} %maximum_select_fusion.16), channel_id=1, source_target_pairs={{0,24},{1,25},{2,26},{3,27},{4,28},{5,29},{6,30},{7,31},{8,16},{9,... | collective-permute-start | bytes 589832 | tf_op jit(solution)/shard_map/ppermute | solution.py:46
  37.5 13.6 %collective-permute-start.4 = (bf16[2,2,2,2,8,1536]{5,4,3,2,1,0:T(8,128)(2,1)S(1)}, bf16[2,2,2,2,8,1536]{5,4,3,2,1,0:T(8,128)(2,1)S(1)}, u32[]{:S(2)}, u32[]{:S(2)}) collective-permute-start(bf16[2,2,2,2,8,1536]{5,4,3,2,1,0:T(8,128)(2,1)S(1)} %maximum_select_fusion.11), channel_id=1, source_target_pairs={{0,2},{1,3},{2,0},{3,1},{4,6},{5,7},{6,4},{7,5},{8,10},{9,11},{10,... | collective-permute-start | bytes 1179656 | tf_op jit(solution)/shard_map/ppermute | solution.py:46
  51.2 20.4 %collective-permute-start.5 = (bf16[2,2,2,2,2,8,1536]{6,5,4,3,2,1,0:T(8,128)(2,1)S(1)}, bf16[2,2,2,2,2,8,1536]{6,5,4,3,2,1,0:T(8,128)(2,1)S(1)}, u32[]{:S(2)}, u32[]{:S(2)}) collective-permute-start(bf16[2,2,2,2,2,8,1536]{6,5,4,3,2,1,0:T(8,128)(2,1)S(1)} %maximum_select_fusion.7), channel_id=1, source_target_pairs={{0,6},{1,7},{2,4},{3,5},{4,2},{5,3},{6,0},{7,1},{8,14},{9,15},{10,... | collective-permute-start | bytes 2359304 | tf_op jit(solution)/shard_map/ppermute | solution.py:46
  73.1 3.8 %collective-permute-start.6 = (bf16[2,2,2,2,2,2,8,1536]{7,6,5,4,3,2,1,0:T(8,128)(2,1)}, bf16[2,2,2,2,2,2,8,1536]{7,6,5,4,3,2,1,0:T(8,128)(2,1)}, u32[]{:S(2)}, u32[]{:S(2)}) collective-permute-start(bf16[2,2,2,2,2,2,8,1536]{7,6,5,4,3,2,1,0:T(8,128)(2,1)} %maximum_select_fusion.3), channel_id=1, source_target_pairs={{0,1},{1,0},{2,3},{3,2},{4,5},{5,4},{6,7},{7,6},{8,9},{9,8},{10,11... | collective-permute-start | bytes 4718600 | tf_op jit(solution)/shard_map/ppermute | solution.py:46
  81.4 8.2 %copy-start.4 = (f32[2048]{0:T(1024)S(1)}, f32[2048]{0:T(1024)}, u32[]{:S(2)}) copy-start(f32[2048]{0:T(1024)} %param.14) | copy-start | bytes 24580
  89.5 4.3 %copy-start.2 = (bf16[2,4096,256]{2,1,0:T(8,128)(2,1)S(1)}, bf16[2,4096,256]{2,1,0:T(8,128)(2,1)}, u32[]{:S(2)}) copy-start(bf16[2,4096,256]{2,1,0:T(8,128)(2,1)} %param.19) | copy-start | bytes 12582916
  102.6 2.2 copy-start.6
  108.5 1.6 collective-permute-start.7
  110.2 5.6 %collective-permute-start.8 = (f32[1,2,4,2,6,130]{5,4,3,2,1,0:T(8,128)S(1)}, f32[1,2,4,2,6,130]{5,4,3,2,1,0:T(8,128)S(1)}, u32[]{:S(2)}, u32[]{:S(2)}) collective-permute-start(f32[1,2,4,2,6,130]{5,4,3,2,1,0:T(8,128)S(1)} %select_bitcast_fusion.1), channel_id=1, source_target_pairs={{0,2},{1,3},{2,0},{3,1},{4,6},{5,7},{6,4},{7,5},{8,10},{9,11},{10,... | collective-permute-start | bytes 149768 | tf_op jit(solution)/shard_map/ppermute | solution.py:66
  116.9 4.1 %collective-permute-start.9 = (bf16[2,4,1536]{2,1,0:T(4,128)(2,1)S(1)}, bf16[2,4,1536]{2,1,0:T(4,128)(2,1)S(1)}, u32[]{:S(2)}, u32[]{:S(2)}) collective-permute-start(bf16[2,4,1536]{2,1,0:T(4,128)(2,1)S(1)} %convert_element_type.140), channel_id=1, source_target_pairs={{0,32},{1,33},{2,34},{3,35},{4,36},{5,37},{6,38},{7,39},{8,40},{9,... | collective-permute-start | bytes 73736 | tf_op jit(solution)/shard_map/ppermute | solution.py:46
  121.1 5.4 %collective-permute-start.10 = (bf16[2,2,4,1536]{3,2,1,0:T(4,128)(2,1)S(1)}, bf16[2,2,4,1536]{3,2,1,0:T(4,128)(2,1)S(1)}, u32[]{:S(2)}, u32[]{:S(2)}) collective-permute-start(bf16[2,2,4,1536]{3,2,1,0:T(4,128)(2,1)S(1)} %maximum_select_fusion.26), channel_id=1, source_target_pairs={{0,96},{1,97},{2,98},{3,99},{4,100},{5,101},{6,102},{7,103},{8,104... | collective-permute-start | bytes 147464 | tf_op jit(solution)/shard_map/ppermute | solution.py:46
  126.5 4.7 %collective-permute-start.11 = (bf16[2,2,2,4,1536]{4,3,2,1,0:T(4,128)(2,1)S(1)}, bf16[2,2,2,4,1536]{4,3,2,1,0:T(4,128)(2,1)S(1)}, u32[]{:S(2)}, u32[]{:S(2)}) collective-permute-start(bf16[2,2,2,4,1536]{4,3,2,1,0:T(4,128)(2,1)S(1)} %maximum_select_fusion.22), channel_id=1, source_target_pairs={{0,8},{1,9},{2,10},{3,11},{4,12},{5,13},{6,14},{7,15},{8,0},{9,1},... | collective-permute-start | bytes 294920 | tf_op jit(solution)/shard_map/ppermute | solution.py:46
  131.4 7.0 %collective-permute-start.12 = (bf16[2,2,2,2,4,1536]{5,4,3,2,1,0:T(4,128)(2,1)S(1)}, bf16[2,2,2,2,4,1536]{5,4,3,2,1,0:T(4,128)(2,1)S(1)}, u32[]{:S(2)}, u32[]{:S(2)}) collective-permute-start(bf16[2,2,2,2,4,1536]{5,4,3,2,1,0:T(4,128)(2,1)S(1)} %maximum_select_fusion.18), channel_id=1, source_target_pairs={{0,24},{1,25},{2,26},{3,27},{4,28},{5,29},{6,30},{7,31},{8,16},{9,... | collective-permute-start | bytes 589832 | tf_op jit(solution)/shard_map/ppermute | solution.py:46
  138.6 7.9 %collective-permute-start.13 = (bf16[2,2,2,2,2,4,1536]{6,5,4,3,2,1,0:T(4,128)(2,1)S(1)}, bf16[2,2,2,2,2,4,1536]{6,5,4,3,2,1,0:T(4,128)(2,1)S(1)}, u32[]{:S(2)}, u32[]{:S(2)}) collective-permute-start(bf16[2,2,2,2,2,4,1536]{6,5,4,3,2,1,0:T(4,128)(2,1)S(1)} %maximum_select_fusion.14), channel_id=1, source_target_pairs={{0,2},{1,3},{2,0},{3,1},{4,6},{5,7},{6,4},{7,5},{8,10},{9,11},{10,... | collective-permute-start | bytes 1179656 | tf_op jit(solution)/shard_map/ppermute | solution.py:46
  147.0 16.4 %copy-start.7 = (s32[32]{0:T(128)S(1)}, s32[32]{0:T(128)}, u32[]{:S(2)}) copy-start(s32[32]{0:T(128)} %param.23) | copy-start | bytes 388
  147.1 14.3 %collective-permute-start.14 = (bf16[2,2,2,2,2,2,4,1536]{7,6,5,4,3,2,1,0:T(4,128)(2,1)S(1)}, bf16[2,2,2,2,2,2,4,1536]{7,6,5,4,3,2,1,0:T(4,128)(2,1)S(1)}, u32[]{:S(2)}, u32[]{:S(2)}) collective-permute-start(bf16[2,2,2,2,2,2,4,1536]{7,6,5,4,3,2,1,0:T(4,128)(2,1)S(1)} %maximum_select_fusion.9), channel_id=1, source_target_pairs={{0,6},{1,7},{2,4},{3,5},{4,2},{5,3},{6,0},{7,1},{8,14},{9,15},{10,... | collective-permute-start | bytes 2359304 | tf_op jit(solution)/shard_map/ppermute | solution.py:46
  163.4 3.8 %collective-permute-start.15 = (bf16[2,2,2,2,2,2,2,4,1536]{8,7,6,5,4,3,2,1,0:T(4,128)(2,1)}, bf16[2,2,2,2,2,2,2,4,1536]{8,7,6,5,4,3,2,1,0:T(4,128)(2,1)}, u32[]{:S(2)}, u32[]{:S(2)}) collective-permute-start(bf16[2,2,2,2,2,2,2,4,1536]{8,7,6,5,4,3,2,1,0:T(4,128)(2,1)} %maximum_select_fusion.5), channel_id=1, source_target_pairs={{0,1},{1,0},{2,3},{3,2},{4,5},{5,4},{6,7},{7,6},{8,9},{9,8},{10,11... | collective-permute-start | bytes 4718600 | tf_op jit(solution)/shard_map/ppermute | solution.py:46
  179.6 4.2 %copy-start.3 = (bf16[1536,280]{0,1:T(8,128)(2,1)S(1)}, bf16[1536,280]{0,1:T(8,128)(2,1)}, u32[]{:S(2)}) copy-start(bf16[1536,280]{0,1:T(8,128)(2,1)} %param.16) | copy-start | bytes 2580484
  183.8 4.1 %copy-start.1 = (f32[64,4,1536]{2,0,1:T(8,128)}, f32[64,4,1536]{2,0,1:T(8,128)S(1)}, u32[]{:S(2)}) copy-start(f32[64,4,1536]{2,0,1:T(8,128)S(1)} %get-tuple-element.32) | copy-start | bytes 4718596
  193.4 1.9 collective-permute-start.16
  196.5 7.0 %collective-permute-start.17 = (bf16[8,8,1536]{2,1,0:T(8,128)(2,1)S(1)}, bf16[8,8,1536]{2,1,0:T(8,128)(2,1)S(1)}, u32[]{:S(2)}, u32[]{:S(2)}) collective-permute-start(bf16[8,8,1536]{2,1,0:T(8,128)(2,1)S(1)} %fusion.65), channel_id=1, source_target_pairs={{0,2},{1,3},{2,0},{3,1},{4,6},{5,7},{6,4},{7,5},{8,10},{9,11},{10,... | collective-permute-start | bytes 589832 | tf_op jit(solution)/shard_map/ppermute | solution.py:66
  203.6 6.2 %collective-permute-start.18 = (bf16[4,8,1536]{2,1,0:T(8,128)(2,1)S(1)}, bf16[4,8,1536]{2,1,0:T(8,128)(2,1)S(1)}, u32[]{:S(2)}, u32[]{:S(2)}) collective-permute-start(bf16[4,8,1536]{2,1,0:T(8,128)(2,1)S(1)} %fusion.70), channel_id=1, source_target_pairs={{0,4},{1,5},{2,6},{3,7},{4,0},{5,1},{6,2},{7,3},{8,12},{9,13},{10,... | collective-permute-start | bytes 294920 | tf_op jit(solution)/shard_map/ppermute | solution.py:66
  209.9 4.2 %collective-permute-start.19 = (bf16[2,8,1536]{2,1,0:T(8,128)(2,1)S(1)}, bf16[2,8,1536]{2,1,0:T(8,128)(2,1)S(1)}, u32[]{:S(2)}, u32[]{:S(2)}) collective-permute-start(bf16[2,8,1536]{2,1,0:T(8,128)(2,1)S(1)} %fusion.87), channel_id=1, source_target_pairs={{0,8},{1,9},{2,10},{3,11},{4,12},{5,13},{6,14},{7,15},{8,0},{9,1},... | collective-permute-start | bytes 147464 | tf_op jit(solution)/shard_map/ppermute | solution.py:66
  214.1 5.4 %collective-permute-start.20 = (bf16[1,8,1536]{2,1,0:T(8,128)(2,1)S(1)}, bf16[1,8,1536]{2,1,0:T(8,128)(2,1)S(1)}, u32[]{:S(2)}, u32[]{:S(2)}) collective-permute-start(bf16[1,8,1536]{2,1,0:T(8,128)(2,1)S(1)} %fusion.91), channel_id=1, source_target_pairs={{0,16},{1,17},{2,18},{3,19},{4,20},{5,21},{6,22},{7,23},{8,24},{9,... | collective-permute-start | bytes 73736 | tf_op jit(solution)/shard_map/ppermute | solution.py:66
Sparse Core Ops, SparseCore 0:
  9.6 53.4 all-gather.1

commit v14 on v13

--- a/solution.py
+++ b/solution.py
@@ -67,6 +67,27 @@
         buf = keep + recv.astype(keep.dtype)
         bit *= 2
     return buf[0]
+
+
+def scatter_ring(x, axes, index, masks, wire):
+    count = x.shape[0]
+    depth = count.bit_length() - 1
+    buf = x.reshape((2,) * depth + x.shape[1:])
+    axis_bits = [1 << (depth - 1 - a) for a in range(depth)]
+    for mask in masks:
+        low = mask & (-mask)
+        bit = low if mask == low else mask - low
+        ax = axis_bits.index(bit)
+        mine = (index // bit) % 2
+        first = lax.index_in_dim(buf, 0, ax, keepdims=False)
+        second = lax.index_in_dim(buf, 1, ax, keepdims=False)
+        keep = jnp.where(mine == 0, first, second)
+        send = jnp.where(mine == 0, second, first)
+        perm = [(i, i ^ mask) for i in range(count)]
+        recv = lax.ppermute(send.astype(wire), axes, perm)
+        buf = keep + recv.astype(keep.dtype)
+        axis_bits.pop(ax)
+    return buf
 
 
 def gather_masks(n_req, tp_count):
@@ -248,9 +269,9 @@
     upward = jnp.dot(mixed_in, up_weight, preferred_element_type=jnp.float32)
     hidden = (jax.nn.silu(gate) * upward).astype(jnp.bfloat16)
     partial = jnp.dot(hidden, down_weight, preferred_element_type=jnp.float32)
-    partial = scatter_rounds(
-        partial.reshape(tp_count, rows_dev * steps, width), TP, tp_index, wire=jnp.bfloat16
-    )
+    partial = scatter_ring(
+        partial.reshape(tp_count, rows_dev * steps, width), TP, tp_index, [1, 6, 2, 24, 8], jnp.bfloat16
+    )[None]
     lowered = partial.reshape(rows_dev, steps, width)
     middle_mine = lax.dynamic_slice_in_dim(middle, tp_index * rows_dev, rows_dev, 0)
     result = (middle_mine + lowered).astype(jnp.bfloat16)

time: 229 us -> 228 us (level)
    ppermute x7 -> x2, waiting for transfers between devices: 25.1 us -> 4.66 us  [scatter_rounds(): recv = lax.ppermute(send.astype(wire), axes, perm)]
    ppermute x0 -> x5, waiting for transfers between devices: none -> 19.1 us  [scatter_ring(): recv = lax.ppermute(send.astype(wire), axes, perm)]
    ppermute x0 -> x5, starting transfers between devices: none -> 4.96 us  [scatter_ring(): recv = lax.ppermute(send.astype(wire), axes, perm)]
    ppermute x7 -> x2, starting transfers between devices: 4.82 us -> 0.53 us  [scatter_rounds(): recv = lax.ppermute(send.astype(wire), axes, perm)]
where the time goes in v14:
time: 228 us; the launch traced here: 227 us
  waiting for transfers between devices  94.6 us (41%)
  local copies, waits for them, and re-layouts  40 us (18%)
  starting transfers between devices  30.5 us (13%)
  other arithmetic  30.4 us (13%)
  matrix products  16.8 us (7%)
  between operations  15 us (7%)
    ppermute x14, waiting for transfers between devices, gather_rounds(): recv = lax.ppermute(buf, axes, perm)  70.8 us
    ppermute x14, starting transfers between devices, gather_rounds(): recv = lax.ppermute(buf, axes, perm)  25 us
    ppermute x5, waiting for transfers between devices, scatter_ring(): recv = lax.ppermute(send.astype(wire), axes, perm)  19.1 us
    select_n x24, other arithmetic, gather_rounds(): buf = jnp.where(mine == 0, jnp.stack([buf, recv]), jnp.stack([recv, buf]))  7.63 us
    transpose x2, other arithmetic, gather_rounds(): buf = jnp.transpose(buf, tuple(order) + tuple(range(depth, buf.ndim)))  6.99 us
    another operation x1, local copies, waits for them, and re-layouts, per_device(): x_all = gather_rounds(jnp.swapaxes(step_inputs, 0, 1).reshape(rows_dev *...  6.14 us
    ppermute x5, starting transfers between devices, scatter_ring(): recv = lax.ppermute(send.astype(wire), axes, perm)  4.96 us
    ppermute x2, waiting for transfers between devices, scatter_rounds(): recv = lax.ppermute(send.astype(wire), axes, perm)  4.66 us
  transfers between devices with their start and end apart: 22, of which 20 were waited for; matrix products, arithmetic and copies ran while one was open for 30% of the time, Pallas kernels for 0%

profile of v14, /device:TPU:0, one launch (start us, length us, event | category | flops | bytes accessed | tf_op | source)
XLA Modules:
  0.0 227.3 jit_solution(9624468901036852294)
XLA Ops:
  7.4 1.7 collective-permute-start
  19.1 2.2 collective-permute-start.1
  21.4 3.2 %collective-permute-done.1 = bf16[2,8,1536]{2,1,0:T(8,128)(2,1)S(1)} collective-permute-done((bf16[2,8,1536]{2,1,0:T(8,128)(2,1)S(1)}, bf16[2,8,1536]{2,1,0:T(8,128)(2,1)S(1)}, u32[]{:S(2)}, u32[]{:S(2)}) %collective-permute-start.1) | collective-permute-done | bytes 49184 | tf_op jit(solution)/shard_map/ppermute | solution.py:46
  24.5 2.0 collective-permute-start.2
  26.6 3.1 %collective-permute-done.2 = bf16[2,2,8,1536]{3,2,1,0:T(8,128)(2,1)S(1)} collective-permute-done((bf16[2,2,8,1536]{3,2,1,0:T(8,128)(2,1)S(1)}, bf16[2,2,8,1536]{3,2,1,0:T(8,128)(2,1)S(1)}, u32[]{:S(2)}, u32[]{:S(2)}) %collective-permute-start.2) | collective-permute-done | bytes 98336 | tf_op jit(solution)/shard_map/ppermute | solution.py:46
  29.7 4.1 %collective-permute-start.3 = (bf16[2,2,2,8,1536]{4,3,2,1,0:T(8,128)(2,1)S(1)}, bf16[2,2,2,8,1536]{4,3,2,1,0:T(8,128)(2,1)S(1)}, u32[]{:S(2)}, u32[]{:S(2)}) collective-permute-start(bf16[2,2,2,8,1536]{4,3,2,1,0:T(8,128)(2,1)S(1)} %maximum_select_fusion.16), channel_id=1, source_target_pairs={{0,24},{1,25},{2,26},{3,27},{4,28},{5,29},{6,30},{7,31},{8,16},{9,... | collective-permute-start | bytes 589832 | tf_op jit(solution)/shard_map/ppermute | solution.py:46
  33.8 3.6 %collective-permute-done.3 = bf16[2,2,2,8,1536]{4,3,2,1,0:T(8,128)(2,1)S(1)} collective-permute-done((bf16[2,2,2,8,1536]{4,3,2,1,0:T(8,128)(2,1)S(1)}, bf16[2,2,2,8,1536]{4,3,2,1,0:T(8,128)(2,1)S(1)}, u32[]{:S(2)}, u32[]{:S(2)}) %collective-permute-start.3) | collective-permute-done | bytes 196640 | tf_op jit(solution)/shard_map/ppermute | solution.py:46
  37.5 1.6 collective-permute-start.4
  39.2 11.9 %collective-permute-done.4 = bf16[2,2,2,2,8,1536]{5,4,3,2,1,0:T(8,128)(2,1)S(1)} collective-permute-done((bf16[2,2,2,2,8,1536]{5,4,3,2,1,0:T(8,128)(2,1)S(1)}, bf16[2,2,2,2,8,1536]{5,4,3,2,1,0:T(8,128)(2,1)S(1)}, u32[]{:S(2)}, u32[]{:S(2)}) %collective-permute-start.4) | collective-permute-done | bytes 393248 | tf_op jit(solution)/shard_map/ppermute | solution.py:46
  51.2 3.3 %collective-permute-start.5 = (bf16[2,2,2,2,2,8,1536]{6,5,4,3,2,1,0:T(8,128)(2,1)S(1)}, bf16[2,2,2,2,2,8,1536]{6,5,4,3,2,1,0:T(8,128)(2,1)S(1)}, u32[]{:S(2)}, u32[]{:S(2)}) collective-permute-start(bf16[2,2,2,2,2,8,1536]{6,5,4,3,2,1,0:T(8,128)(2,1)S(1)} %maximum_select_fusion.7), channel_id=1, source_target_pairs={{0,6},{1,7},{2,4},{3,5},{4,2},{5,3},{6,0},{7,1},{8,14},{9,15},{10,... | collective-permute-start | bytes 2359304 | tf_op jit(solution)/shard_map/ppermute | solution.py:46
  55.0 16.7 %collective-permute-done.5 = bf16[2,2,2,2,2,8,1536]{6,5,4,3,2,1,0:T(8,128)(2,1)S(1)} collective-permute-done((bf16[2,2,2,2,2,8,1536]{6,5,4,3,2,1,0:T(8,128)(2,1)S(1)}, bf16[2,2,2,2,2,8,1536]{6,5,4,3,2,1,0:T(8,128)(2,1)S(1)}, u32[]{:S(2)}, u32[]{:S(2)}) %collective-permute-start.5) | collective-permute-done | bytes 786464 | tf_op jit(solution)/shard_map/ppermute | solution.py:46
  71.6 1.4 maximum_select_fusion.3
  76.8 2.3 %fusion.8 = bf16[2,2,2,2,2,2,2,8,1536]{8,7,1,0,3,2,5,4,6:T(8,128)(2,1)S(1)} fusion(bf16[1,2,2,2,2,2,2,8,1536]{8,7,6,5,4,3,2,1,0:T(8,128)(2,1)} %bitcast.18, bf16[1,2,2,2,2,2,2,8,1536]{8,7,6,5,4,3,2,1,0:T(8,128)(2,1)S(1)} %maximum_select_fusion.2, pred[]{:T(512)S(6)} %eq.99), kind=kLoop, calls=%fused_computation.31 | loop fusion | flops 4718592 | bytes 6291457 | tf_op jit(solution)/shard_map/transpose | solution.py:52
  79.1 2.2 copy.114
  81.4 6.1 %reshape_reshape.7 = bf16[256,4,1536]{2,1,0:T(4,128)(2,1)} reshape(bf16[2,2,2,2,2,2,2,8,1536]{8,7,6,5,4,3,2,1,0:T(8,128)(2,1)} %copy.114) | data formatting | bytes 6291456 | tf_op jit(solution)/shard_map/reshape;reshape | solution.py:149
  89.6 4.1 %fusion.20 = bf16[8,4,2048]{2,0,1:T(8,128)(2,1)S(1)} fusion(bf16[1536,2048]{1,0:T(8,128)(2,1)} %param.13, f32[2048]{0:T(1024)S(1)} %copy-done.4, bf16[8,4,1536]{2,1,0:T(4,128)(2,1)S(1)} %fusion.64), kind=kOutput, calls=%fused_computation.40 | convolution fusion | flops 201457664 | bytes 6529024 | tf_op jit(solution)/shard_map/dot_general | solution.py:156
  95.9 2.1 fusion.5
  98.0 4.6 %fusion.2 = (bf16[2,8,4,2,6,4096]{5,1,0,4,2,3:T(8,128)(2,1)S(1)}, f32[2,8,4,2,6]{1,0,4,2,3:T(2,128)S(1)}) fusion(f32[2,8,4,2,6]{1,0,4,2,3:T(2,128)S(1)} %fusion.5, pred[2,4096]{1,0:T(4,128)(4,1)S(1)} %iota_compare_fusion, f32[2,8,4,1,6,4096]{5,1,0,4,2,3:T(8,128)S(1)} %convolution_bitcast_fusion, f32[2,8,4,1,6,4096]{5,1,0,4,2,3:T(8,128)S(1)} %convolution_bitcast_fusion.1), kind=kLoop, calls=%fused_computation.20 | loop fusion | flops 22019328 | bytes 18888704 | tf_op jit(solution)/shard_map/convert_element_type | solution.py:193
  103.4 1.4 copy-done.6
  111.6 4.3 %collective-permute-done.8 = f32[1,2,4,2,6,130]{5,4,3,2,1,0:T(8,128)S(1)} collective-permute-done((f32[1,2,4,2,6,130]{5,4,3,2,1,0:T(8,128)S(1)}, f32[1,2,4,2,6,130]{5,4,3,2,1,0:T(8,128)S(1)}, u32[]{:S(2)}, u32[]{:S(2)}) %collective-permute-start.8) | collective-permute-done | bytes 49952 | tf_op jit(solution)/shard_map/ppermute | solution.py:66
  118.1 2.9 %collective-permute-done.9 = bf16[2,4,1536]{2,1,0:T(4,128)(2,1)S(1)} collective-permute-done((bf16[2,4,1536]{2,1,0:T(4,128)(2,1)S(1)}, bf16[2,4,1536]{2,1,0:T(4,128)(2,1)S(1)}, u32[]{:S(2)}, u32[]{:S(2)}) %collective-permute-start.9) | collective-permute-done | bytes 24608 | tf_op jit(solution)/shard_map/ppermute | solution.py:46
  121.1 2.8 %collective-permute-start.10 = (bf16[2,2,4,1536]{3,2,1,0:T(4,128)(2,1)S(1)}, bf16[2,2,4,1536]{3,2,1,0:T(4,128)(2,1)S(1)}, u32[]{:S(2)}, u32[]{:S(2)}) collective-permute-start(bf16[2,2,4,1536]{3,2,1,0:T(4,128)(2,1)S(1)} %maximum_select_fusion.26), channel_id=1, source_target_pairs={{0,96},{1,97},{2,98},{3,99},{4,100},{5,101},{6,102},{7,103},{8,104... | collective-permute-start | bytes 147464 | tf_op jit(solution)/shard_map/ppermute | solution.py:46
  123.9 2.5 %collective-permute-done.10 = bf16[2,2,4,1536]{3,2,1,0:T(4,128)(2,1)S(1)} collective-permute-done((bf16[2,2,4,1536]{3,2,1,0:T(4,128)(2,1)S(1)}, bf16[2,2,4,1536]{3,2,1,0:T(4,128)(2,1)S(1)}, u32[]{:S(2)}, u32[]{:S(2)}) %collective-permute-start.10) | collective-permute-done | bytes 49184 | tf_op jit(solution)/shard_map/ppermute | solution.py:46
  127.8 3.4 %collective-permute-done.11 = bf16[2,2,2,4,1536]{4,3,2,1,0:T(4,128)(2,1)S(1)} collective-permute-done((bf16[2,2,2,4,1536]{4,3,2,1,0:T(4,128)(2,1)S(1)}, bf16[2,2,2,4,1536]{4,3,2,1,0:T(4,128)(2,1)S(1)}, u32[]{:S(2)}, u32[]{:S(2)}) %collective-permute-start.11) | collective-permute-done | bytes 98336 | tf_op jit(solution)/shard_map/ppermute | solution.py:46
  131.4 3.0 %collective-permute-start.12 = (bf16[2,2,2,2,4,1536]{5,4,3,2,1,0:T(4,128)(2,1)S(1)}, bf16[2,2,2,2,4,1536]{5,4,3,2,1,0:T(4,128)(2,1)S(1)}, u32[]{:S(2)}, u32[]{:S(2)}) collective-permute-start(bf16[2,2,2,2,4,1536]{5,4,3,2,1,0:T(4,128)(2,1)S(1)} %maximum_select_fusion.18), channel_id=1, source_target_pairs={{0,24},{1,25},{2,26},{3,27},{4,28},{5,29},{6,30},{7,31},{8,16},{9,... | collective-permute-start | bytes 589832 | tf_op jit(solution)/shard_map/ppermute | solution.py:46
  134.5 3.8 %collective-permute-done.12 = bf16[2,2,2,2,4,1536]{5,4,3,2,1,0:T(4,128)(2,1)S(1)} collective-permute-done((bf16[2,2,2,2,4,1536]{5,4,3,2,1,0:T(4,128)(2,1)S(1)}, bf16[2,2,2,2,4,1536]{5,4,3,2,1,0:T(4,128)(2,1)S(1)}, u32[]{:S(2)}, u32[]{:S(2)}) %collective-permute-start.12) | collective-permute-done | bytes 196640 | tf_op jit(solution)/shard_map/ppermute | solution.py:46
  139.4 7.0 %collective-permute-done.13 = bf16[2,2,2,2,2,4,1536]{6,5,4,3,2,1,0:T(4,128)(2,1)S(1)} collective-permute-done((bf16[2,2,2,2,2,4,1536]{6,5,4,3,2,1,0:T(4,128)(2,1)S(1)}, bf16[2,2,2,2,2,4,1536]{6,5,4,3,2,1,0:T(4,128)(2,1)S(1)}, u32[]{:S(2)}, u32[]{:S(2)}) %collective-permute-start.13) | collective-permute-done | bytes 393248 | tf_op jit(solution)/shard_map/ppermute | solution.py:46
  147.1 1.6 collective-permute-start.14
  149.5 11.9 %collective-permute-done.14 = bf16[2,2,2,2,2,2,4,1536]{7,6,5,4,3,2,1,0:T(4,128)(2,1)S(1)} collective-permute-done((bf16[2,2,2,2,2,2,4,1536]{7,6,5,4,3,2,1,0:T(4,128)(2,1)S(1)}, bf16[2,2,2,2,2,2,4,1536]{7,6,5,4,3,2,1,0:T(4,128)(2,1)S(1)}, u32[]{:S(2)}, u32[]{:S(2)}) %collective-permute-start.14) | collective-permute-done | bytes 786464 | tf_op jit(solution)/shard_map/ppermute | solution.py:46
  161.3 2.1 maximum_select_fusion.5
  163.5 1.4 constant_dynamic-slice_fusion
  165.5 1.2 maximum_select_fusion.4
  167.2 4.7 %fusion.9 = bf16[2,2,2,2,2,2,2,2,4,1536]{9,8,7,1,0,3,2,5,4,6:T(4,128)(2,1)S(1)} fusion(bf16[1,2,2,2,2,2,2,2,4,1536]{9,8,7,6,5,4,3,2,1,0:T(4,128)(2,1)} %bitcast.111, bf16[1,2,2,2,2,2,2,2,4,1536]{9,8,7,6,5,4,3,2,1,0:T(4,128)(2,1)S(1)} %maximum_select_fusion.4, pred[]{:T(512)S(6)} %eq.99), kind=kLoop, calls=%fused_computation.33 | loop fusion | flops 4718592 | bytes 6291457 | tf_op jit(solution)/shard_map/transpose | solution.py:52
  171.9 1.8 copy.142
  173.7 2.5 %copy.143 = bf16[32,8,4,1536]{3,1,2,0:T(8,128)(2,1)} copy(bf16[32,8,4,1536]{3,2,1,0:T(4,128)(2,1)S(1)} %bitcast.313) | data formatting | bytes 6291456 | tf_op jit(solution)/shard_map/reshape;reshape;reshape | solution.py:260
  176.2 3.4 %gather_fusion.14 = bf16[8,8,4,1536]{3,1,2,0:T(8,128)(2,1)} fusion(bf16[32,8,4,1536]{3,1,2,0:T(8,128)(2,1)} %copy.143, s32[1024]{0:T(1024)S(1)} %pad_clamp_fusion), kind=kCustom, calls=%fused_computation.14 | custom fusion | bytes 1572896 | tf_op jit(solution)/shard_map/gather | solution.py:260
  179.6 4.1 %multiply_reduce_fusion = (f32[64,4]{0,1:T(4,128)S(1)}, f32[64,4,1536]{2,0,1:T(8,128)S(1)}) fusion(bf16[1536,1536]{1,0:T(8,128)(2,1)} %all-gather.2.cloned.1.call-done, bf16[8,8,4,1536]{3,1,2,0:T(8,128)(2,1)} %gather_fusion.14, bf16[64,4,1536]{2,1,0:T(4,128)(2,1)S(1)} %constant_dynamic-slice_fusion), kind=kOutput, calls=%fused_computation.54 | convolution fusion | flops 1209532160 | bytes 7865344 | tf_op jit(solution)/shard_map/dot_general | solution.py:264
  184.4 3.5 %fusion.42 = f32[64,4,1536]{2,0,1:T(8,128)} fusion(bf16[280,1536]{1,0:T(8,128)(2,1)S(1)} %copy-done, bf16[1536,280]{0,1:T(8,128)(2,1)} %param.17, f32[64,4,280]{2,0,1:T(8,128)S(1)} %fusion.47, f32[64,4,1536]{2,0,1:T(8,128)S(1)} %get-tuple-element.32, f32[64,4]{0,1:T(4,128)S(1)} %add_rsqrt_fusion.1), kind=kOutput, calls=%fused_computation.59 | convolution fusion | flops 441618432 | bytes 5153792 | tf_op jit(solution)/shard_map/dot_general | solution.py:271
  187.9 3.6 %copy.145 = f32[64,4,1536]{2,1,0:T(4,128)} copy(f32[64,4,1536]{2,0,1:T(8,128)} %fusion.42) | data formatting | bytes 3145728 | tf_op jit(solution)/shard_map/dot_general | solution.py:271
  191.4 1.8 reshape_reshape.8
  193.6 1.7 collective-permute-done.16
  196.5 1.5 collective-permute-start.17
  198.0 6.7 %collective-permute-done.17 = bf16[2,2,2,8,1536]{4,3,2,1,0:T(8,128)(2,1)S(1)} collective-permute-done((bf16[2,2,2,8,1536]{4,3,2,1,0:T(8,128)(2,1)S(1)}, bf16[2,2,2,8,1536]{4,3,2,1,0:T(8,128)(2,1)S(1)}, u32[]{:S(2)}, u32[]{:S(2)}) %collective-permute-start.17) | collective-permute-done | bytes 196640 | tf_op jit(solution)/shard_map/ppermute | solution.py:87
  204.9 4.6 %collective-permute-done.18 = bf16[2,2,8,1536]{3,2,1,0:T(8,128)(2,1)S(1)} collective-permute-done((bf16[2,2,8,1536]{3,2,1,0:T(8,128)(2,1)S(1)}, bf16[2,2,8,1536]{3,2,1,0:T(8,128)(2,1)S(1)}, u32[]{:S(2)}, u32[]{:S(2)}) %collective-permute-start.18) | collective-permute-done | bytes 98336 | tf_op jit(solution)/shard_map/ppermute | solution.py:87
  209.6 3.0 %collective-permute-start.19 = (bf16[2,8,1536]{2,1,0:T(8,128)(2,1)S(1)}, bf16[2,8,1536]{2,1,0:T(8,128)(2,1)S(1)}, u32[]{:S(2)}, u32[]{:S(2)}) collective-permute-start(bf16[2,8,1536]{2,1,0:T(8,128)(2,1)S(1)} %fusion.84), channel_id=1, source_target_pairs={{0,24},{1,25},{2,26},{3,27},{4,28},{5,29},{6,30},{7,31},{8,16},{9,... | collective-permute-start | bytes 147464 | tf_op jit(solution)/shard_map/ppermute | solution.py:87
  212.6 2.4 %collective-permute-done.19 = bf16[2,8,1536]{2,1,0:T(8,128)(2,1)S(1)} collective-permute-done((bf16[2,8,1536]{2,1,0:T(8,128)(2,1)S(1)}, bf16[2,8,1536]{2,1,0:T(8,128)(2,1)S(1)}, u32[]{:S(2)}, u32[]{:S(2)}) %collective-permute-start.19) | collective-permute-done | bytes 49184 | tf_op jit(solution)/shard_map/ppermute | solution.py:87
  215.1 3.8 %collective-permute-done.20 = bf16[8,1536]{1,0:T(8,128)(2,1)S(1)} collective-permute-done((bf16[8,1536]{1,0:T(8,128)(2,1)S(1)}, bf16[8,1536]{1,0:T(8,128)(2,1)S(1)}, u32[]{:S(2)}, u32[]{:S(2)}) %collective-permute-start.20) | collective-permute-done | bytes 24608 | tf_op jit(solution)/shard_map/ppermute | solution.py:87
  218.9 1.6 fusion.90
  (179 shorter events, 36.1 us)
Async XLA Ops:
  6.5 177.9 %copy-start = (bf16[280,1536]{1,0:T(8,128)(2,1)S(1)}, bf16[280,1536]{1,0:T(8,128)(2,1)}, u32[]{:S(2)}) copy-start(bf16[280,1536]{1,0:T(8,128)(2,1)} %param.18) | copy-start | bytes 2580484
  6.5 9.1 %copy-start.5 = (s32[32,8]{0,1:T(8,128)S(1)}, s32[32,8]{0,1:T(8,128)}, u32[]{:S(2)}) copy-start(s32[32,8]{0,1:T(8,128)} %param.21) | copy-start | bytes 3076
  6.5 173.1 %all-gather.2.cloned.1.call-start = ((), (), s32[]{:S(2)}) async-start(), calls=%async_computation | async-start | bytes 4866048 | tf_op jit(solution)/shard_map/all_gather | solution.py:150
  7.4 11.7 %collective-permute-start = (bf16[8,1536]{1,0:T(8,128)(2,1)S(1)}, bf16[8,1536]{1,0:T(8,128)(2,1)S(1)}, u32[]{:S(2)}, u32[]{:S(2)}) collective-permute-start(bf16[8,1536]{1,0:T(8,128)(2,1)S(1)} %reshape.1813), channel_id=1, source_target_pairs={{0,32},{1,33},{2,34},{3,35},{4,36},{5,37},{6,38},{7,39},{8,40},{9,... | collective-permute-start | bytes 73736 | tf_op jit(solution)/shard_map/ppermute | solution.py:46
  19.1 5.4 %collective-permute-start.1 = (bf16[2,8,1536]{2,1,0:T(8,128)(2,1)S(1)}, bf16[2,8,1536]{2,1,0:T(8,128)(2,1)S(1)}, u32[]{:S(2)}, u32[]{:S(2)}) collective-permute-start(bf16[2,8,1536]{2,1,0:T(8,128)(2,1)S(1)} %maximum_select_fusion.24), channel_id=1, source_target_pairs={{0,96},{1,97},{2,98},{3,99},{4,100},{5,101},{6,102},{7,103},{8,104... | collective-permute-start | bytes 147464 | tf_op jit(solution)/shard_map/ppermute | solution.py:46
  24.5 5.1 %collective-permute-start.2 = (bf16[2,2,8,1536]{3,2,1,0:T(8,128)(2,1)S(1)}, bf16[2,2,8,1536]{3,2,1,0:T(8,128)(2,1)S(1)}, u32[]{:S(2)}, u32[]{:S(2)}) collective-permute-start(bf16[2,2,8,1536]{3,2,1,0:T(8,128)(2,1)S(1)} %maximum_select_fusion.20), channel_id=1, source_target_pairs={{0,8},{1,9},{2,10},{3,11},{4,12},{5,13},{6,14},{7,15},{8,0},{9,1},... | collective-permute-start | bytes 294920 | tf_op jit(solution)/shard_map/ppermute | solution.py:46
  29.7 7.8 %collective-permute-start.3 = (bf16[2,2,2,8,1536]{4,3,2,1,0:T(8,128)(2,1)S(1)}, bf16[2,2,2,8,1536]{4,3,2,1,0:T(8,128)(2,1)S(1)}, u32[]{:S(2)}, u32[]{:S(2)}) collective-permute-start(bf16[2,2,2,8,1536]{4,3,2,1,0:T(8,128)(2,1)S(1)} %maximum_select_fusion.16), channel_id=1, source_target_pairs={{0,24},{1,25},{2,26},{3,27},{4,28},{5,29},{6,30},{7,31},{8,16},{9,... | collective-permute-start | bytes 589832 | tf_op jit(solution)/shard_map/ppermute | solution.py:46
  37.5 13.6 %collective-permute-start.4 = (bf16[2,2,2,2,8,1536]{5,4,3,2,1,0:T(8,128)(2,1)S(1)}, bf16[2,2,2,2,8,1536]{5,4,3,2,1,0:T(8,128)(2,1)S(1)}, u32[]{:S(2)}, u32[]{:S(2)}) collective-permute-start(bf16[2,2,2,2,8,1536]{5,4,3,2,1,0:T(8,128)(2,1)S(1)} %maximum_select_fusion.11), channel_id=1, source_target_pairs={{0,2},{1,3},{2,0},{3,1},{4,6},{5,7},{6,4},{7,5},{8,10},{9,11},{10,... | collective-permute-start | bytes 1179656 | tf_op jit(solution)/shard_map/ppermute | solution.py:46
  51.2 20.4 %collective-permute-start.5 = (bf16[2,2,2,2,2,8,1536]{6,5,4,3,2,1,0:T(8,128)(2,1)S(1)}, bf16[2,2,2,2,2,8,1536]{6,5,4,3,2,1,0:T(8,128)(2,1)S(1)}, u32[]{:S(2)}, u32[]{:S(2)}) collective-permute-start(bf16[2,2,2,2,2,8,1536]{6,5,4,3,2,1,0:T(8,128)(2,1)S(1)} %maximum_select_fusion.7), channel_id=1, source_target_pairs={{0,6},{1,7},{2,4},{3,5},{4,2},{5,3},{6,0},{7,1},{8,14},{9,15},{10,... | collective-permute-start | bytes 2359304 | tf_op jit(solution)/shard_map/ppermute | solution.py:46
  73.1 3.8 %collective-permute-start.6 = (bf16[2,2,2,2,2,2,8,1536]{7,6,5,4,3,2,1,0:T(8,128)(2,1)}, bf16[2,2,2,2,2,2,8,1536]{7,6,5,4,3,2,1,0:T(8,128)(2,1)}, u32[]{:S(2)}, u32[]{:S(2)}) collective-permute-start(bf16[2,2,2,2,2,2,8,1536]{7,6,5,4,3,2,1,0:T(8,128)(2,1)} %maximum_select_fusion.3), channel_id=1, source_target_pairs={{0,1},{1,0},{2,3},{3,2},{4,5},{5,4},{6,7},{7,6},{8,9},{9,8},{10,11... | collective-permute-start | bytes 4718600 | tf_op jit(solution)/shard_map/ppermute | solution.py:46
  81.4 8.2 %copy-start.4 = (f32[2048]{0:T(1024)S(1)}, f32[2048]{0:T(1024)}, u32[]{:S(2)}) copy-start(f32[2048]{0:T(1024)} %param.14) | copy-start | bytes 24580
  89.5 4.3 %copy-start.2 = (bf16[2,4096,256]{2,1,0:T(8,128)(2,1)S(1)}, bf16[2,4096,256]{2,1,0:T(8,128)(2,1)}, u32[]{:S(2)}) copy-start(bf16[2,4096,256]{2,1,0:T(8,128)(2,1)} %param.19) | copy-start | bytes 12582916
  102.6 2.2 copy-start.6
  108.5 1.6 collective-permute-start.7
  110.2 5.6 %collective-permute-start.8 = (f32[1,2,4,2,6,130]{5,4,3,2,1,0:T(8,128)S(1)}, f32[1,2,4,2,6,130]{5,4,3,2,1,0:T(8,128)S(1)}, u32[]{:S(2)}, u32[]{:S(2)}) collective-permute-start(f32[1,2,4,2,6,130]{5,4,3,2,1,0:T(8,128)S(1)} %select_bitcast_fusion.1), channel_id=1, source_target_pairs={{0,2},{1,3},{2,0},{3,1},{4,6},{5,7},{6,4},{7,5},{8,10},{9,11},{10,... | collective-permute-start | bytes 149768 | tf_op jit(solution)/shard_map/ppermute | solution.py:66
  116.9 4.1 %collective-permute-start.9 = (bf16[2,4,1536]{2,1,0:T(4,128)(2,1)S(1)}, bf16[2,4,1536]{2,1,0:T(4,128)(2,1)S(1)}, u32[]{:S(2)}, u32[]{:S(2)}) collective-permute-start(bf16[2,4,1536]{2,1,0:T(4,128)(2,1)S(1)} %convert_element_type.132), channel_id=1, source_target_pairs={{0,32},{1,33},{2,34},{3,35},{4,36},{5,37},{6,38},{7,39},{8,40},{9,... | collective-permute-start | bytes 73736 | tf_op jit(solution)/shard_map/ppermute | solution.py:46
  121.1 5.4 %collective-permute-start.10 = (bf16[2,2,4,1536]{3,2,1,0:T(4,128)(2,1)S(1)}, bf16[2,2,4,1536]{3,2,1,0:T(4,128)(2,1)S(1)}, u32[]{:S(2)}, u32[]{:S(2)}) collective-permute-start(bf16[2,2,4,1536]{3,2,1,0:T(4,128)(2,1)S(1)} %maximum_select_fusion.26), channel_id=1, source_target_pairs={{0,96},{1,97},{2,98},{3,99},{4,100},{5,101},{6,102},{7,103},{8,104... | collective-permute-start | bytes 147464 | tf_op jit(solution)/shard_map/ppermute | solution.py:46
  126.5 4.7 %collective-permute-start.11 = (bf16[2,2,2,4,1536]{4,3,2,1,0:T(4,128)(2,1)S(1)}, bf16[2,2,2,4,1536]{4,3,2,1,0:T(4,128)(2,1)S(1)}, u32[]{:S(2)}, u32[]{:S(2)}) collective-permute-start(bf16[2,2,2,4,1536]{4,3,2,1,0:T(4,128)(2,1)S(1)} %maximum_select_fusion.22), channel_id=1, source_target_pairs={{0,8},{1,9},{2,10},{3,11},{4,12},{5,13},{6,14},{7,15},{8,0},{9,1},... | collective-permute-start | bytes 294920 | tf_op jit(solution)/shard_map/ppermute | solution.py:46
  131.4 7.0 %collective-permute-start.12 = (bf16[2,2,2,2,4,1536]{5,4,3,2,1,0:T(4,128)(2,1)S(1)}, bf16[2,2,2,2,4,1536]{5,4,3,2,1,0:T(4,128)(2,1)S(1)}, u32[]{:S(2)}, u32[]{:S(2)}) collective-permute-start(bf16[2,2,2,2,4,1536]{5,4,3,2,1,0:T(4,128)(2,1)S(1)} %maximum_select_fusion.18), channel_id=1, source_target_pairs={{0,24},{1,25},{2,26},{3,27},{4,28},{5,29},{6,30},{7,31},{8,16},{9,... | collective-permute-start | bytes 589832 | tf_op jit(solution)/shard_map/ppermute | solution.py:46
  138.6 7.9 %collective-permute-start.13 = (bf16[2,2,2,2,2,4,1536]{6,5,4,3,2,1,0:T(4,128)(2,1)S(1)}, bf16[2,2,2,2,2,4,1536]{6,5,4,3,2,1,0:T(4,128)(2,1)S(1)}, u32[]{:S(2)}, u32[]{:S(2)}) collective-permute-start(bf16[2,2,2,2,2,4,1536]{6,5,4,3,2,1,0:T(4,128)(2,1)S(1)} %maximum_select_fusion.14), channel_id=1, source_target_pairs={{0,2},{1,3},{2,0},{3,1},{4,6},{5,7},{6,4},{7,5},{8,10},{9,11},{10,... | collective-permute-start | bytes 1179656 | tf_op jit(solution)/shard_map/ppermute | solution.py:46
  147.0 16.4 %copy-start.7 = (s32[32]{0:T(128)S(1)}, s32[32]{0:T(128)}, u32[]{:S(2)}) copy-start(s32[32]{0:T(128)} %param.23) | copy-start | bytes 388
  147.1 14.3 %collective-permute-start.14 = (bf16[2,2,2,2,2,2,4,1536]{7,6,5,4,3,2,1,0:T(4,128)(2,1)S(1)}, bf16[2,2,2,2,2,2,4,1536]{7,6,5,4,3,2,1,0:T(4,128)(2,1)S(1)}, u32[]{:S(2)}, u32[]{:S(2)}) collective-permute-start(bf16[2,2,2,2,2,2,4,1536]{7,6,5,4,3,2,1,0:T(4,128)(2,1)S(1)} %maximum_select_fusion.9), channel_id=1, source_target_pairs={{0,6},{1,7},{2,4},{3,5},{4,2},{5,3},{6,0},{7,1},{8,14},{9,15},{10,... | collective-permute-start | bytes 2359304 | tf_op jit(solution)/shard_map/ppermute | solution.py:46
  163.4 3.8 %collective-permute-start.15 = (bf16[2,2,2,2,2,2,2,4,1536]{8,7,6,5,4,3,2,1,0:T(4,128)(2,1)}, bf16[2,2,2,2,2,2,2,4,1536]{8,7,6,5,4,3,2,1,0:T(4,128)(2,1)}, u32[]{:S(2)}, u32[]{:S(2)}) collective-permute-start(bf16[2,2,2,2,2,2,2,4,1536]{8,7,6,5,4,3,2,1,0:T(4,128)(2,1)} %maximum_select_fusion.5), channel_id=1, source_target_pairs={{0,1},{1,0},{2,3},{3,2},{4,5},{5,4},{6,7},{7,6},{8,9},{9,8},{10,11... | collective-permute-start | bytes 4718600 | tf_op jit(solution)/shard_map/ppermute | solution.py:46
  179.6 4.2 %copy-start.3 = (bf16[1536,280]{0,1:T(8,128)(2,1)S(1)}, bf16[1536,280]{0,1:T(8,128)(2,1)}, u32[]{:S(2)}) copy-start(bf16[1536,280]{0,1:T(8,128)(2,1)} %param.16) | copy-start | bytes 2580484
  183.8 4.1 %copy-start.1 = (f32[64,4,1536]{2,0,1:T(8,128)}, f32[64,4,1536]{2,0,1:T(8,128)S(1)}, u32[]{:S(2)}) copy-start(f32[64,4,1536]{2,0,1:T(8,128)S(1)} %get-tuple-element.32) | copy-start | bytes 4718596
  193.4 1.9 collective-permute-start.16
  196.5 8.2 %collective-permute-start.17 = (bf16[2,2,2,8,1536]{4,3,2,1,0:T(8,128)(2,1)S(1)}, bf16[2,2,2,8,1536]{4,3,2,1,0:T(8,128)(2,1)S(1)}, u32[]{:S(2)}, u32[]{:S(2)}) collective-permute-start(bf16[2,2,2,8,1536]{4,3,2,1,0:T(8,128)(2,1)S(1)} %fusion.65), channel_id=1, source_target_pairs={{0,6},{1,7},{2,4},{3,5},{4,2},{5,3},{6,0},{7,1},{8,14},{9,15},{10,... | collective-permute-start | bytes 589832 | tf_op jit(solution)/shard_map/ppermute | solution.py:87
  204.8 4.7 %collective-permute-start.18 = (bf16[2,2,8,1536]{3,2,1,0:T(8,128)(2,1)S(1)}, bf16[2,2,8,1536]{3,2,1,0:T(8,128)(2,1)S(1)}, u32[]{:S(2)}, u32[]{:S(2)}) collective-permute-start(bf16[2,2,8,1536]{3,2,1,0:T(8,128)(2,1)S(1)} %fusion.70), channel_id=1, source_target_pairs={{0,2},{1,3},{2,0},{3,1},{4,6},{5,7},{6,4},{7,5},{8,10},{9,11},{10,... | collective-permute-start | bytes 294920 | tf_op jit(solution)/shard_map/ppermute | solution.py:87
  209.6 5.4 %collective-permute-start.19 = (bf16[2,8,1536]{2,1,0:T(8,128)(2,1)S(1)}, bf16[2,8,1536]{2,1,0:T(8,128)(2,1)S(1)}, u32[]{:S(2)}, u32[]{:S(2)}) collective-permute-start(bf16[2,8,1536]{2,1,0:T(8,128)(2,1)S(1)} %fusion.84), channel_id=1, source_target_pairs={{0,24},{1,25},{2,26},{3,27},{4,28},{5,29},{6,30},{7,31},{8,16},{9,... | collective-permute-start | bytes 147464 | tf_op jit(solution)/shard_map/ppermute | solution.py:87
  215.0 3.9 %collective-permute-start.20 = (bf16[8,1536]{1,0:T(8,128)(2,1)S(1)}, bf16[8,1536]{1,0:T(8,128)(2,1)S(1)}, u32[]{:S(2)}, u32[]{:S(2)}) collective-permute-start(bf16[8,1536]{1,0:T(8,128)(2,1)S(1)} %fusion.88), channel_id=1, source_target_pairs={{0,8},{1,9},{2,10},{3,11},{4,12},{5,13},{6,14},{7,15},{8,0},{9,1},... | collective-permute-start | bytes 73736 | tf_op jit(solution)/shard_map/ppermute | solution.py:87
Sparse Core Ops, SparseCore 0:
  9.6 53.4 all-gather.1
